TPU v7x, 256 devices: a whole 4x4x8 slice. The times are simulated.
256 devices in a mesh: seq: 32 (over y, x, core), chan: 8 (over z).
Axes of the slice: x: 4, y: 4, z: 8, core: 2. Of those that a mesh axis runs over, the one named last changes fastest.
Arguments:
- inner_input: bfloat16 [32768, 8192], P('seq', 'chan'), may hold values from -6 to 6
- state_maps: bfloat16 [32768, 2, 8, 128], P('seq', None, 'chan'), may hold values from -6 to 6
- gate_input: bfloat16 [32768, 8192], P('seq', 'chan'), may hold values from -6 to 6
- step_input: float32 [32768, 128], P('seq', 'chan'), may hold values from -3 to 12
- log_decay_rate: float32 [128], P('chan'), may hold values from 0 to 2.78
- step_bias: float32 [128], P('chan'), may hold values from -17 to 0
- skip_gain: float32 [128], P('chan'), may hold values from 0.5 to 1.5
- conv_kernel: float32 [4, 8192], P(None, 'chan'), may hold values from -3 to 3
- map_kernel: float32 [4, 2, 8, 128], P(None, None, 'chan'), may hold values from -3 to 3
- norm_gain: float32 [8192], P('chan'), may hold values from 0.1 to 1.9
- out_weight: bfloat16 [8192, 2048], P('chan'), may hold values from -0.09375 to 0.09375
Outputs:
- mixed_out: bfloat16 [32768, 2048], P('seq', 'chan')
All inputs are finite; a program needn't handle non-finite values.
Results may differ from a plain program's by a relative error of at most 0.011.
Values may be sent and summed in bfloat16 or wider, within the bound.
A program may use at most 128 MiB of HBM per device.

v0:
```python
import jax
import jax.numpy as jnp
from jax import lax
from jax.sharding import PartitionSpec as P

HEADS = 128
HEAD_DIM = 64
STATE = 128
NGROUPS = 8
BLOCK = 256


step_limit = 0.5
epsilon = 1e-05


def passed_along(x, axis, by):
    count = lax.axis_size(axis)
    pairs = [(i, i + by) for i in range(count) if 0 <= i + by < count]
    return lax.ppermute(x, axis, pairs)


def conv_silu(padded, kernel, length):
    acc = jnp.zeros((length,) + padded.shape[1:], jnp.float32)
    for offset in range(kernel.shape[0]):
        acc = acc + kernel[offset] * padded[offset : offset + length].astype(jnp.float32)
    return jax.nn.silu(acc).astype(jnp.bfloat16)


def local(
    inner_input,
    state_maps,
    gate_input,
    step_input,
    log_decay_rate,
    step_bias,
    skip_gain,
    conv_kernel,
    map_kernel,
    norm_gain,
    out_weight,
):
    row_count = inner_input.shape[0]
    kernel_remainder = conv_kernel.shape[0] - 1
    groups = state_maps.shape[2]
    per_group = HEADS // NGROUPS
    head_count = groups * per_group
    block_count = row_count // BLOCK
    tail_inner, tail_maps = passed_along(
        (inner_input[row_count - kernel_remainder :], state_maps[row_count - kernel_remainder :]),
        "seq",
        1,
    )
    inner_conv = conv_silu(
        jnp.concatenate((tail_inner, inner_input), axis=0), conv_kernel, row_count
    )
    maps_conv = conv_silu(jnp.concatenate((tail_maps, state_maps), axis=0), map_kernel, row_count)
    step = jnp.minimum(jax.nn.softplus(step_input + step_bias), step_limit)
    log_step = step * -jnp.exp(log_decay_rate)
    step_blocks = step.reshape(block_count, BLOCK, groups, per_group)
    cumul = jnp.cumsum(log_step.reshape(block_count, BLOCK, groups, per_group), axis=1)
    x_blocks = inner_conv.reshape(block_count, BLOCK, groups, per_group, HEAD_DIM)
    b_blocks = maps_conv[:, 0].reshape(block_count, BLOCK, groups, STATE)
    c_blocks = maps_conv[:, 1].reshape(block_count, BLOCK, groups, STATE)
    scores = jnp.einsum("ctgn,csgn->cgts", c_blocks, b_blocks, preferred_element_type=jnp.float32)
    cumul_t = cumul.transpose(0, 2, 3, 1)
    gap = cumul_t[..., :, None] - cumul_t[..., None, :]
    row_ids = lax.broadcasted_iota(jnp.int32, (BLOCK, BLOCK), 0)
    col_ids = lax.broadcasted_iota(jnp.int32, (BLOCK, BLOCK), 1)
    decay = jnp.exp(jnp.where(row_ids >= col_ids, gap, -jnp.inf))
    mixing = (scores[:, :, None] * decay * step_blocks.transpose(0, 2, 3, 1)[..., None, :]).astype(
        jnp.bfloat16
    )
    y_local = jnp.einsum("cgjts,csgjp->ctgjp", mixing, x_blocks, preferred_element_type=jnp.float32)
    weighted = (
        (jnp.exp(cumul[:, -1:] - cumul) * step_blocks)[..., None] * b_blocks[:, :, :, None, :]
    ).astype(jnp.bfloat16)
    block_states = jnp.einsum(
        "csgjp,csgjn->cgjpn", x_blocks, weighted, preferred_element_type=jnp.float32
    )
    block_decay = cumul[:, -1]
    running = jnp.zeros((groups, per_group, HEAD_DIM, STATE), jnp.float32)
    local_in = []
    for block_index in range(block_count):
        local_in.append(running)
        running = (
            jnp.exp(block_decay[block_index])[..., None, None] * running + block_states[block_index]
        )
    slab_decay = jnp.sum(block_decay, axis=0)
    device_index = lax.axis_index("seq")
    decays = lax.all_gather(slab_decay[None], "seq", axis=0, tiled=True)
    before = jnp.cumsum(decays, axis=0) - decays
    through = before + decays
    mine = lax.dynamic_index_in_dim(before, device_index, 0, keepdims=False)
    shard_piece = lax.all_gather(
        running[None].astype(jnp.bfloat16), "seq", axis=0, tiled=True
    ).astype(jnp.float32)
    piece_rows = shard_piece.shape[0]
    owners = lax.broadcasted_iota(jnp.int32, (piece_rows, 1, 1), 0)
    factors = jnp.exp(jnp.where(owners < device_index, mine[None] - through, -jnp.inf))
    entering = jnp.zeros_like(running) + jnp.einsum(
        "rgj,rgjpn->gjpn", factors, shard_piece, precision=lax.Precision.HIGHEST
    )
    leading = jnp.cumsum(block_decay, axis=0) - block_decay
    state_in = (
        jnp.exp(leading)[..., None, None] * entering[None] + jnp.stack(local_in, axis=0)
    ).astype(jnp.bfloat16)
    y_carry = jnp.exp(cumul)[..., None] * jnp.einsum(
        "ctgn,cgjpn->ctgjp", c_blocks, state_in, preferred_element_type=jnp.float32
    )
    y_all = y_local + y_carry + skip_gain.reshape(groups, per_group)[:, :, None] * x_blocks
    width = per_group * HEAD_DIM
    gated = y_all.reshape(row_count, groups, width) * jax.nn.silu(
        gate_input.reshape(row_count, groups, width).astype(jnp.float32)
    )
    square_mean = jnp.mean(gated * gated, axis=-1, keepdims=True)
    normed = (
        (gated * lax.rsqrt(square_mean + epsilon) * norm_gain.reshape(groups, width))
        .astype(jnp.bfloat16)
        .reshape(row_count, head_count * HEAD_DIM)
    )
    shares = lax.psum_scatter(
        lax.dot_general(
            out_weight, normed, (((0,), (1,)), ((), ())), preferred_element_type=jnp.float32
        ),
        "chan",
        scatter_dimension=0,
        tiled=True,
    )
    return shares.T.astype(jnp.bfloat16)


def solution(mesh):
    return jax.shard_map(
        local,
        mesh=mesh,
        in_specs=(
            P("seq", "chan"),
            P("seq", None, "chan", None),
            P("seq", "chan"),
            P("seq", "chan"),
            P("chan"),
            P("chan"),
            P("chan"),
            P(None, "chan"),
            P(None, None, "chan", None),
            P("chan"),
            P("chan", None),
        ),
        out_specs=P("seq", "chan"),
        check_vma=False,
    )
```

profile of v0, /device:TPU:24, one launch (start us, length us, event | category | flops | bytes accessed | tf_op | source)
XLA Modules:
  0.0 251.8 jit_solution(10126762526046400024)
XLA Ops:
  6.5 1.3 copy.71
  7.8 1.9 collective-permute-start.1
  9.7 0.7 slice.101
  10.5 0.9 copy.68
  11.4 3.5 %collective-permute-start = (bf16[3,1024]{0,1:T(8,128)(2,1)}, bf16[3,1024]{0,1:T(8,128)(2,1)S(1)}, u32[]{:S(2)}, u32[]{:S(2)}) collective-permute-start(bf16[3,1024]{0,1:T(8,128)(2,1)} %copy.68), channel_id=1, source_target_pairs={{0,8},{8,16},{16,24},{24,32},{32,40},{40,48},{48,56},{56,64},{64,7... | collective-permute-start | bytes 18440 | tf_op jit(solution)/shard_map/ppermute | solution.py:20
  14.9 0.7 exponential_negate_fusion
  15.5 1.0 broadcast_multiply_fusion
  16.6 2.3 reduce-window.6
  20.1 0.7 fusion.50
  20.8 0.9 fusion.49
  22.3 2.6 %copy.69 = bf16[1024,1024]{0,1:T(8,128)(2,1)} copy(bf16[1024,1024]{1,0:T(8,128)(2,1)S(1)} %copy-done.3) | data formatting | bytes 4194304 | tf_op args[0]
  24.9 0.7 multiply_convert_fusion.9
  25.7 0.7 copy-done.8
  26.4 5.2 %multiply_convert_fusion.5 = bf16[1024,1024]{0,1:T(8,128)(2,1)S(1)} fusion(bf16[1024,1024]{0,1:T(8,128)(2,1)S(1)} %copy-done, bf16[3,1024]{0,1:T(8,128)(2,1)} %copy-done.8, f32[1024]{0:T(1024)S(1)} %bitcast.102, f32[1024]{0:T(1024)S(1)} %bitcast.103, f32[1024]{0:T(1024)S(1)} %bitcast.101, f32[1024]{0:T(1024)S(1)} %bitcast.100), kind=kLoop, calls=%fused_computation.27 | loop fusion | flops 26214400 | bytes 4216832 | tf_op jit(solution)/shard_map/convert_element_type | solution.py:27
  31.7 2.8 %reshape.349 = bf16[4,256,16,64]{1,0,3,2:T(4,128)(2,1)} reshape(bf16[1024,1024]{0,1:T(8,128)(2,1)S(1)} %multiply_convert_fusion.5) | data formatting | bytes 4194304 | tf_op jit(solution)/shard_map/reshape.24
  34.5 4.6 %fusion.13 = f32[4,16,64,128]{3,2,1,0:T(8,128)S(1)} fusion(f32[4,256,128]{2,1,0:T(8,128)S(1)} %convert_element_type.110, f32[4,256,16]{1,2,0:T(8,128)S(1)} %copy.90, bf16[4,256,16,64]{1,0,3,2:T(4,128)(2,1)} %reshape.349), kind=kOutput, calls=%fused_computation.18 | convolution fusion | flops 272629760 | bytes 4784128 | tf_op jit(solution)/shard_map/csgjp,csgjn->cgjpn/dot_general | solution.py:78
  39.1 1.2 fusion.32
  42.1 56.2 %all-reduce = f32[512]{0:T(512)S(1)} all-reduce(f32[512]{0:T(512)S(1)} %dynamic-update-slice), channel_id=2, replica_groups=mesh['seq'=32,'chan'=8] {'seq'}, use_global_device_ids=true, to_apply=%add | all-reduce | flops 512 | bytes 4096
  98.7 3.9 %copy.94 = bf16[1024,1024]{0,1:T(8,128)(2,1)} copy(bf16[1024,1024]{1,0:T(8,128)(2,1)} %param.13) | data formatting | bytes 4194304 | tf_op args[2]
  102.7 1.3 fusion.51
  104.0 3.4 %reshape.364 = f32[4,256,1,16,64]{1,0,4,3,2:T(4,128)} reshape(bf16[1024,1024]{0,1:T(8,128)(2,1)S(1)} %multiply_convert_fusion.5) | data formatting | bytes 6291456 | tf_op jit(solution)/shard_map/convert_element_type | solution.py:111
  107.5 11.8 %fusion.1 = f32[16,1,64,128]{3,1,2,0:T(1,128)S(1)} fusion(f32[32,16,1,1]{0,2,3,1:T(1,128)S(1)} %copy.95, bf16[32,16,64,128]{3,2,1,0:T(8,128)(2,1)} %all-gather.4.cloned.1.call-done), kind=kOutput, calls=%fused_computation.2 | convolution fusion | flops 50331648 | bytes 8914944 | tf_op jit(solution)/shard_map/rgj,rgjpn->gjpn/dot_general | solution.py:101
  119.4 0.8 fusion.25
  120.1 1.4 copy-done.2
  121.5 0.7 copy-done.6
  122.2 5.4 %fusion.15 = f32[4,256,1,16,64]{1,4,3,0,2:T(8,128)S(1)} fusion(f32[4,16,64,256]{3,2,1,0:T(8,128)S(1)} %fusion.25, f32[4,256,1,16,64]{1,0,4,3,2:T(4,128)S(1)} %copy-done.2, f32[4,16,256]{2,1,0:T(8,128)S(1)} %copy.79, f32[4,16,256]{2,1,0:T(8,128)S(1)} %reduce_window_sum.55, f32[4,256,256]{2,1,0:T(8,128)S(1)} %copy-done.7, ...), kind=kOutput, calls=%fused_computation.21 | convolution fusion | flops 562036736 | bytes 15990848 | tf_op jit(solution)/shard_map/cgjts,csgjp->ctgjp/dot_general | solution.py:74
  127.5 2.8 %copy.93 = f32[4,256,1,16,64]{1,0,4,3,2:T(4,128)S(1)} copy(f32[4,256,1,16,64]{1,4,3,0,2:T(8,128)S(1)} %fusion.15) | data formatting | bytes 8388608 | tf_op jit(solution)/shard_map/add | solution.py:111
  130.4 1.0 copy.100
  131.9 1.3 multiply_reduce_fusion
  133.7 7.5 %convolution_bitcast_fusion = f32[2048,1024]{0,1:T(8,128)} fusion(bf16[1024,2048]{1,0:T(8,128)(2,1)S(1)} %copy-done.9, f32[1024]{0:T(1024)S(1)} %copy-done.10, f32[1024]{0:T(1024)S(1)} %add_rsqrt_fusion, f32[1024,1024]{0,1:T(8,128)S(1)} %bitcast.85, bf16[1024,1024]{0,1:T(8,128)(2,1)S(1)} %copy-done.1), kind=kOutput, calls=%fused_computation.13 | convolution fusion | flops 4304404480 | bytes 18882560 | tf_op jit(solution)/shard_map/dot_general | solution.py:123
  141.2 101.6 %reduce-scatter.2.cloned.1.call-done = f32[256,1024]{0,1:T(8,128)} async-done(((f32[2048,1024]{0,1:T(8,128)}), f32[256,1024]{0,1:T(8,128)}) %reduce-scatter.2.cloned.1.call-update) | async-done | bytes 1048592 | tf_op jit(solution)/shard_map/reduce_scatter | solution.py:122
  242.8 2.1 convert_bitcast_fusion
  (72 shorter events, 4.5 us)
Async XLA Ops:
  6.5 15.7 %copy-start.3 = (bf16[1024,1024]{1,0:T(8,128)(2,1)S(1)}, bf16[1024,1024]{1,0:T(8,128)(2,1)}, u32[]{:S(2)}) copy-start(bf16[1024,1024]{1,0:T(8,128)(2,1)} %param.11) | copy-start | bytes 6291460
  6.5 100.9 %all-gather.4.cloned.1.call-start = ((), (), s32[]{:S(2)}) async-start(), calls=%async_computation.2 | async-start | bytes 8650752 | tf_op jit(solution)/shard_map/all_gather | solution.py:95
  7.8 17.1 %collective-permute-start.1 = (bf16[3,2,1,128]{3,0,2,1:T(4,128)(2,1)S(1)}, bf16[3,2,1,128]{3,0,2,1:T(4,128)(2,1)S(1)}, u32[]{:S(2)}, u32[]{:S(2)}) collective-permute-start(bf16[3,2,1,128]{3,0,2,1:T(4,128)(2,1)S(1)} %slice.133), channel_id=1, source_target_pairs={{0,8},{8,16},{16,24},{24,32},{32,40},{40,48},{48,56},{56,64},{64,7... | collective-permute-start | bytes 4616 | tf_op jit(solution)/shard_map/ppermute | solution.py:20
  11.4 14.3 %collective-permute-start = (bf16[3,1024]{0,1:T(8,128)(2,1)}, bf16[3,1024]{0,1:T(8,128)(2,1)S(1)}, u32[]{:S(2)}, u32[]{:S(2)}) collective-permute-start(bf16[3,1024]{0,1:T(8,128)(2,1)} %copy.68), channel_id=1, source_target_pairs={{0,8},{8,16},{16,24},{24,32},{32,40},{40,48},{48,56},{56,64},{64,7... | collective-permute-start | bytes 18440 | tf_op jit(solution)/shard_map/ppermute | solution.py:20
  24.9 1.6 copy-start
  25.7 0.7 copy-start.8
  39.1 1.5 copy-start.12
  40.3 202.5 %reduce-scatter.2.cloned.1.call-start = ((), (), s32[]{:S(2)}) async-start(), calls=%async_computation.1 | async-start | bytes 9437184 | tf_op jit(solution)/shard_map/reduce_scatter | solution.py:122
  107.5 11.9 %copy-start.4 = (f32[1,16,64,128]{3,2,1,0:T(8,128)S(1)}, f32[1,16,64,128]{3,2,1,0:T(8,128)}, u32[]{:S(2)}) copy-start(f32[1,16,64,128]{3,2,1,0:T(8,128)} %get-tuple-element.13) | copy-start | bytes 1572868
  107.5 11.9 %copy-start.5 = (f32[1,16,64,128]{3,2,1,0:T(8,128)S(1)}, f32[1,16,64,128]{3,2,1,0:T(8,128)}, u32[]{:S(2)}) copy-start(f32[1,16,64,128]{3,2,1,0:T(8,128)} %get-tuple-element.14) | copy-start | bytes 1572868
  107.5 12.7 %copy-start.7 = (f32[4,256,256]{2,1,0:T(8,128)S(1)}, f32[4,256,256]{2,1,0:T(8,128)}, u32[]{:S(2)}) copy-start(f32[4,256,256]{2,1,0:T(8,128)} %fusion.51) | copy-start | bytes 3145732
  119.3 2.2 copy-start.2
  119.3 2.9 %copy-start.6 = (bf16[4,256,16,64]{1,0,3,2:T(4,128)(2,1)S(1)}, bf16[4,256,16,64]{1,0,3,2:T(4,128)(2,1)}, u32[]{:S(2)}) copy-start(bf16[4,256,16,64]{1,0,3,2:T(4,128)(2,1)} %reshape.349) | copy-start | bytes 6291460
  119.3 2.9 %copy-start.11 = (f32[16]{0:T(128)S(1)}, f32[16]{0:T(128)}, u32[]{:S(2)}) copy-start(f32[16]{0:T(128)} %param.17) | copy-start | bytes 196
  130.3 1.6 copy-start.1
  131.4 2.3 copy-start.9
  131.4 2.3 copy-start.10
Sparse Core Ops, SparseCore 0:
  40.5 60.3 all-gather.3
  141.4 101.4 reduce-scatter.1
where the time goes:
time: 254 us; the launch traced here: 252 us
  waiting for transfers between devices  102 us (40%)
  blocking collectives  56.2 us (22%)
  matrix products  31.3 us (12%)
  local copies, waits for them, and re-layouts  27 us (11%)
  other arithmetic  15.6 us (6%)
  between operations  14.5 us (6%)
  starting transfers between devices  5.45 us (2%)
    reduce_scatter x1, waiting for transfers between devices, local(): lax.psum_scatter(lax.dot_general(out_weight, normed, (((0,), (1,)), ((),...  102 us
    unnamed x1, blocking collectives  56.2 us
    unnamed x33, local copies, waits for them, and re-layouts  13.5 us
    dot_general x1, matrix products, local(): jnp.einsum('rgj,rgjpn->gjpn', factors, shard_piece, precision=lax.Precisi...  11.8 us
    dot_general x1, matrix products, local(): lax.dot_general(out_weight, normed, (((0,), (1,)), ((), ())), preferred_e...  7.5 us
    convert_element_type x2, other arithmetic, conv_silu(): return jax.nn.silu(acc).astype(jnp.bfloat16)  5.9 us
    ppermute x2, starting transfers between devices, passed_along(): return lax.ppermute(x, axis, pairs)  5.41 us
    dot_general x1, matrix products, local(): jnp.einsum('cgjts,csgjp->ctgjp', mixing, x_blocks, preferred_element_type...  5.35 us
  transfers between devices with their start and end apart: 4, of which 1 were waited for; matrix products, arithmetic and copies ran while one was open for 9% of the time, Pallas kernels for 0%

commit v1 on v0

--- a/solution.py
+++ b/solution.py
@@ -88,13 +88,27 @@
         )
     slab_decay = jnp.sum(block_decay, axis=0)
     device_index = lax.axis_index("seq")
-    decays = lax.all_gather(slab_decay[None], "seq", axis=0, tiled=True)
+    state_rows = groups * per_group * HEAD_DIM
+    decay_hi = slab_decay.reshape(-1).astype(jnp.bfloat16)
+    decay_rest = slab_decay.reshape(-1) - decay_hi.astype(jnp.float32)
+    decay_mid = decay_rest.astype(jnp.bfloat16)
+    decay_lo = (decay_rest - decay_mid.astype(jnp.float32)).astype(jnp.bfloat16)
+    decay_rows = jnp.zeros((8, STATE), jnp.bfloat16)
+    decay_rows = decay_rows.at[0:3, 0:head_count].set(jnp.stack((decay_hi, decay_mid, decay_lo)))
+    packed = jnp.concatenate(
+        (running.reshape(state_rows, STATE).astype(jnp.bfloat16), decay_rows), axis=0
+    )
+    gathered = lax.all_gather(packed, "seq", axis=0, tiled=False)
+    decays = (
+        jnp.sum(gathered[:, state_rows : state_rows + 3, 0:head_count].astype(jnp.float32), axis=1)
+        .reshape(-1, groups, per_group)
+    )
     before = jnp.cumsum(decays, axis=0) - decays
     through = before + decays
     mine = lax.dynamic_index_in_dim(before, device_index, 0, keepdims=False)
-    shard_piece = lax.all_gather(
-        running[None].astype(jnp.bfloat16), "seq", axis=0, tiled=True
-    ).astype(jnp.float32)
+    shard_piece = (
+        gathered[:, :state_rows].reshape((-1,) + running.shape).astype(jnp.float32)
+    )
     piece_rows = shard_piece.shape[0]
     owners = lax.broadcasted_iota(jnp.int32, (piece_rows, 1, 1), 0)
     factors = jnp.exp(jnp.where(owners < device_index, mine[None] - through, -jnp.inf))
@@ -122,12 +136,12 @@
     shares = lax.psum_scatter(
         lax.dot_general(
             out_weight, normed, (((0,), (1,)), ((), ())), preferred_element_type=jnp.float32
-        ),
+        ).astype(jnp.bfloat16),
         "chan",
         scatter_dimension=0,
         tiled=True,
     )
-    return shares.T.astype(jnp.bfloat16)
+    return shares.T
 
 
 def solution(mesh):

time: 254 us -> 207 us (0.81)
  blocking collectives: 56.2 us -> 0 us
  local copies, waits for them, and re-layouts: 27 us -> 33.5 us
  waiting for transfers between devices: 102 us -> 106 us
    unnamed x1 -> x0, blocking collectives: 56.2 us -> none
    all_gather x1, waiting for transfers between devices: 0.01 us -> 51.1 us  [local(): gathered = lax.all_gather(packed, 'seq', axis=0, tiled=False)]
    reduce_scatter x1, waiting for transfers between devices: 102 us -> 55.3 us  [local(): lax.psum_scatter(lax.dot_general(out_weight, normed, (((0,), (1,)), ((),...]
    slice x2 -> x1, local copies, waits for them, and re-layouts: 0.2 us -> 7.52 us  [local(): gathered[:, :state_rows].reshape((-1,) + running.shape).astype(jnp.float32)]
    unnamed x33 -> x28, local copies, waits for them, and re-layouts: 13.5 us -> 12.6 us
  transfers between devices with their start and end apart: 4 -> 4, of which waited for: 1 -> 2; matrix products, arithmetic and copies ran while one was open for 9% -> 10% of each run, Pallas kernels for 0% -> 0%
where the time goes in v1:
time: 207 us; the launch traced here: 205 us
  waiting for transfers between devices  106 us (51%)
  local copies, waits for them, and re-layouts  33.5 us (16%)
  matrix products  30.9 us (15%)
  other arithmetic  15.1 us (7%)
  between operations  13.8 us (7%)
  starting transfers between devices  5.64 us (3%)
    reduce_scatter x1, waiting for transfers between devices, local(): lax.psum_scatter(lax.dot_general(out_weight, normed, (((0,), (1,)), ((),...  55.3 us
    all_gather x1, waiting for transfers between devices, local(): gathered = lax.all_gather(packed, 'seq', axis=0, tiled=False)  51.1 us
    unnamed x28, local copies, waits for them, and re-layouts  12.6 us
    dot_general x1, matrix products, local(): jnp.einsum('rgj,rgjpn->gjpn', factors, shard_piece, precision=lax.Precisi...  11.8 us
    slice x1, local copies, waits for them, and re-layouts, local(): gathered[:, :state_rows].reshape((-1,) + running.shape).astype(jnp.float32)  7.52 us
    dot_general x1, matrix products, local(): lax.dot_general(out_weight, normed, (((0,), (1,)), ((), ())), preferred_e...  6.94 us
    convert_element_type x2, other arithmetic, conv_silu(): return jax.nn.silu(acc).astype(jnp.bfloat16)  5.9 us
    ppermute x2, starting transfers between devices, passed_along(): return lax.ppermute(x, axis, pairs)  5.41 us
  transfers between devices with their start and end apart: 4, of which 2 were waited for; matrix products, arithmetic and copies ran while one was open for 10% of the time, Pallas kernels for 0%

profile of v1, /device:TPU:24, one launch (start us, length us, event | category | flops | bytes accessed | tf_op | source)
XLA Modules:
  0.0 205.4 jit_solution(13733575640594806042)
XLA Ops:
  6.5 1.3 copy.45
  7.8 1.9 collective-permute-start.1
  9.7 0.7 slice.127
  10.5 0.9 copy.42
  11.4 3.5 %collective-permute-start = (bf16[3,1024]{0,1:T(8,128)(2,1)}, bf16[3,1024]{0,1:T(8,128)(2,1)S(1)}, u32[]{:S(2)}, u32[]{:S(2)}) collective-permute-start(bf16[3,1024]{0,1:T(8,128)(2,1)} %copy.42), channel_id=1, source_target_pairs={{0,8},{8,16},{16,24},{24,32},{32,40},{40,48},{48,56},{56,64},{64,7... | collective-permute-start | bytes 18440 | tf_op jit(solution)/shard_map/ppermute | solution.py:20
  15.5 1.0 broadcast_multiply_fusion
  16.6 2.3 %reduce-window.6 = f32[4,16,1,2,128]{4,1,2,3,0:T(8,128)S(1)} reduce-window(f32[4,16,1,2,128]{4,1,2,3,0:T(8,128)S(1)} %copy.49, f32[]{:T(128)} %constant.60.clone.1), window={size=1x1x1x1x128 pad=0_0x0_0x0_0x0_0x127_0}, to_apply=%region_0.1 | reduce-window | flops 2080768 | bytes 131076 | tf_op jit(solution)/shard_map/reduce-window
  20.6 0.7 fusion.64
  21.3 0.9 fusion.63
  22.3 2.6 %copy.43 = bf16[1024,1024]{0,1:T(8,128)(2,1)} copy(bf16[1024,1024]{1,0:T(8,128)(2,1)S(1)} %copy-done.3) | data formatting | bytes 4194304 | tf_op args[0]
  24.9 0.7 multiply_convert_fusion.9
  25.7 0.7 copy-done.8
  26.5 5.2 %multiply_convert_fusion.5 = bf16[1024,1024]{0,1:T(8,128)(2,1)S(1)} fusion(bf16[1024,1024]{0,1:T(8,128)(2,1)S(1)} %copy-done, bf16[3,1024]{0,1:T(8,128)(2,1)} %copy-done.8, f32[1024]{0:T(1024)S(1)} %bitcast.122, f32[1024]{0:T(1024)S(1)} %bitcast.123, f32[1024]{0:T(1024)S(1)} %bitcast.121, f32[1024]{0:T(1024)S(1)} %bitcast.120), kind=kLoop, calls=%fused_computation.27 | loop fusion | flops 26214400 | bytes 4216832 | tf_op jit(solution)/shard_map/convert_element_type | solution.py:27
  31.7 2.8 %reshape.433 = bf16[4,256,16,64]{1,0,3,2:T(4,128)(2,1)} reshape(bf16[1024,1024]{0,1:T(8,128)(2,1)S(1)} %multiply_convert_fusion.5) | data formatting | bytes 4194304 | tf_op jit(solution)/shard_map/reshape.53
  34.5 4.6 %fusion.13 = f32[4,16,64,128]{3,2,1,0:T(8,128)S(1)} fusion(f32[4,256,128]{2,1,0:T(8,128)S(1)} %convert_element_type.171, f32[4,256,16]{1,2,0:T(8,128)S(1)} %copy.61, bf16[4,256,16,64]{1,0,3,2:T(4,128)(2,1)} %reshape.433), kind=kOutput, calls=%fused_computation.17 | convolution fusion | flops 272629760 | bytes 4784128 | tf_op jit(solution)/shard_map/csgjp,csgjn->cgjpn/dot_general | solution.py:78
  39.1 1.1 fusion.32
  40.2 0.7 pad_maximum_fusion.2
  41.5 4.0 %copy.67 = bf16[1024,1024]{0,1:T(8,128)(2,1)} copy(bf16[1024,1024]{1,0:T(8,128)(2,1)} %param.15) | data formatting | bytes 4194304 | tf_op args[2]
  45.5 1.4 fusion.66
  46.9 3.4 %reshape.448 = f32[4,256,1,16,64]{1,0,4,3,2:T(4,128)} reshape(bf16[1024,1024]{0,1:T(8,128)(2,1)S(1)} %multiply_convert_fusion.5) | data formatting | bytes 6291456 | tf_op jit(solution)/shard_map/convert_element_type | solution.py:125
  50.3 51.1 %all-gather.3.cloned.1.call-done = bf16[33024,128]{1,0:T(8,128)(2,1)} async-done(((bf16[1032,128]{1,0:T(8,128)(2,1)}), bf16[33024,128]{1,0:T(8,128)(2,1)}) %all-gather.3.cloned.1.call-update) | async-done | bytes 8454160 | tf_op jit(solution)/shard_map/all_gather | solution.py:101
  101.4 0.9 convert_reduce_fusion
  102.3 7.5 %slice.180 = bf16[32,1024,128]{2,1,0:T(8,128)(2,1)} slice(bf16[32,1032,128]{2,1,0:T(8,128)(2,1)} %bitcast.104), slice={[0:32], [0:1024], [0:128]} | slice | bytes 16777216 | tf_op jit(solution)/shard_map/slice | solution.py:110
  110.0 11.8 %fusion.1 = f32[16,1,64,128]{3,1,2,0:T(1,128)S(1)} fusion(f32[32,16,1,1]{0,2,3,1:T(1,128)S(1)} %copy.68, bf16[32,16,64,128]{3,2,1,0:T(8,128)(2,1)} %bitcast.99), kind=kOutput, calls=%fused_computation.2 | convolution fusion | flops 50331648 | bytes 8914944 | tf_op jit(solution)/shard_map/rgj,rgjpn->gjpn/dot_general | solution.py:115
  121.9 0.8 fusion.25
  122.7 1.4 copy-done.2
  124.7 5.4 %fusion.15 = f32[4,256,1,16,64]{1,4,3,0,2:T(8,128)S(1)} fusion(f32[4,16,64,256]{3,2,1,0:T(8,128)S(1)} %fusion.25, f32[4,256,1,16,64]{1,0,4,3,2:T(4,128)S(1)} %copy-done.2, f32[4,16,256]{2,1,0:T(8,128)S(1)} %copy.53, f32[4,16,256]{2,1,0:T(8,128)S(1)} %reduce_window_sum.57, f32[4,256,256]{2,1,0:T(8,128)S(1)} %copy-done.7, ...), kind=kOutput, calls=%fused_computation.20 | convolution fusion | flops 562036736 | bytes 15990848 | tf_op jit(solution)/shard_map/cgjts,csgjp->ctgjp/dot_general | solution.py:74
  130.1 2.8 %copy.66 = f32[4,256,1,16,64]{1,0,4,3,2:T(4,128)S(1)} copy(f32[4,256,1,16,64]{1,4,3,0,2:T(8,128)S(1)} %fusion.15) | data formatting | bytes 8388608 | tf_op jit(solution)/shard_map/add | solution.py:125
  132.9 1.0 copy.73
  134.5 1.3 multiply_reduce_fusion
  136.3 6.9 %convert_bitcast_fusion = bf16[2048,1024]{0,1:T(8,128)(2,1)} fusion(bf16[1024,2048]{1,0:T(8,128)(2,1)S(1)} %copy-done.9, f32[1024]{0:T(1024)S(1)} %copy-done.10, f32[1024]{0:T(1024)S(1)} %add_rsqrt_fusion, f32[1024,1024]{0,1:T(8,128)S(1)} %bitcast.101, bf16[1024,1024]{0,1:T(8,128)(2,1)S(1)} %copy-done.1), kind=kOutput, calls=%fused_computation.22 | convolution fusion | flops 4306501632 | bytes 14688256 | tf_op jit(solution)/shard_map/dot_general | solution.py:137
  143.2 55.3 %reduce-scatter.2.cloned.1.call-done = bf16[256,1024]{0,1:T(8,128)(2,1)} async-done(((bf16[2048,1024]{0,1:T(8,128)(2,1)}), bf16[256,1024]{0,1:T(8,128)(2,1)}) %reduce-scatter.2.cloned.1.call-update) | async-done | bytes 524304 | tf_op jit(solution)/shard_map/reduce_scatter | solution.py:136
  (70 shorter events, 5.0 us)
Async XLA Ops:
  6.5 15.8 %copy-start.3 = (bf16[1024,1024]{1,0:T(8,128)(2,1)S(1)}, bf16[1024,1024]{1,0:T(8,128)(2,1)}, u32[]{:S(2)}) copy-start(bf16[1024,1024]{1,0:T(8,128)(2,1)} %param.13) | copy-start | bytes 6291460
  6.5 94.9 %all-gather.3.cloned.1.call-start = ((), (), s32[]{:S(2)}) async-start(), calls=%async_computation.2 | async-start | bytes 8718336 | tf_op jit(solution)/shard_map/all_gather | solution.py:101
  7.8 17.1 %collective-permute-start.1 = (bf16[3,2,1,128]{3,0,2,1:T(4,128)(2,1)S(1)}, bf16[3,2,1,128]{3,0,2,1:T(4,128)(2,1)S(1)}, u32[]{:S(2)}, u32[]{:S(2)}) collective-permute-start(bf16[3,2,1,128]{3,0,2,1:T(4,128)(2,1)S(1)} %slice.161), channel_id=1, source_target_pairs={{0,8},{8,16},{16,24},{24,32},{32,40},{40,48},{48,56},{56,64},{64,7... | collective-permute-start | bytes 4616 | tf_op jit(solution)/shard_map/ppermute | solution.py:20
  11.4 14.4 %collective-permute-start = (bf16[3,1024]{0,1:T(8,128)(2,1)}, bf16[3,1024]{0,1:T(8,128)(2,1)S(1)}, u32[]{:S(2)}, u32[]{:S(2)}) collective-permute-start(bf16[3,1024]{0,1:T(8,128)(2,1)} %copy.42), channel_id=1, source_target_pairs={{0,8},{8,16},{16,24},{24,32},{32,40},{40,48},{48,56},{56,64},{64,7... | collective-permute-start | bytes 18440 | tf_op jit(solution)/shard_map/ppermute | solution.py:20
  24.9 1.6 copy-start
  25.7 0.7 copy-start.8
  41.0 157.6 %reduce-scatter.2.cloned.1.call-start = ((), (), s32[]{:S(2)}) async-start(), calls=%async_computation.1 | async-start | bytes 4718592 | tf_op jit(solution)/shard_map/reduce_scatter | solution.py:136
  110.0 11.9 %copy-start.4 = (f32[1,16,64,128]{3,2,1,0:T(8,128)S(1)}, f32[1,16,64,128]{3,2,1,0:T(8,128)}, u32[]{:S(2)}) copy-start(f32[1,16,64,128]{3,2,1,0:T(8,128)} %get-tuple-element.25) | copy-start | bytes 1572868
  110.0 11.9 %copy-start.5 = (f32[1,16,64,128]{3,2,1,0:T(8,128)S(1)}, f32[1,16,64,128]{3,2,1,0:T(8,128)}, u32[]{:S(2)}) copy-start(f32[1,16,64,128]{3,2,1,0:T(8,128)} %get-tuple-element.26) | copy-start | bytes 1572868
  110.0 12.7 %copy-start.7 = (f32[4,256,256]{2,1,0:T(8,128)S(1)}, f32[4,256,256]{2,1,0:T(8,128)}, u32[]{:S(2)}) copy-start(f32[4,256,256]{2,1,0:T(8,128)} %fusion.66) | copy-start | bytes 3145732
  121.9 2.2 %copy-start.2 = (f32[4,256,1,16,64]{1,0,4,3,2:T(4,128)S(1)}, f32[4,256,1,16,64]{1,0,4,3,2:T(4,128)}, u32[]{:S(2)}) copy-start(f32[4,256,1,16,64]{1,0,4,3,2:T(4,128)} %reshape.448) | copy-start | bytes 12582916
  121.9 2.9 %copy-start.6 = (bf16[4,256,16,64]{1,0,3,2:T(4,128)(2,1)S(1)}, bf16[4,256,16,64]{1,0,3,2:T(4,128)(2,1)}, u32[]{:S(2)}) copy-start(bf16[4,256,16,64]{1,0,3,2:T(4,128)(2,1)} %reshape.433) | copy-start | bytes 6291460
  121.9 2.9 %copy-start.11 = (f32[16]{0:T(128)S(1)}, f32[16]{0:T(128)}, u32[]{:S(2)}) copy-start(f32[16]{0:T(128)} %param.19) | copy-start | bytes 196
  132.9 1.6 copy-start.1
  133.9 2.3 %copy-start.9 = (bf16[1024,2048]{1,0:T(8,128)(2,1)S(1)}, bf16[1024,2048]{1,0:T(8,128)(2,1)}, u32[]{:S(2)}) copy-start(bf16[1024,2048]{1,0:T(8,128)(2,1)} %param.23) | copy-start | bytes 12582916
  134.0 2.3 %copy-start.10 = (f32[1024]{0:T(1024)S(1)}, f32[1024]{0:T(1024)}, u32[]{:S(2)}) copy-start(f32[1024]{0:T(1024)} %param.22) | copy-start | bytes 12292
Sparse Core Ops, SparseCore 0:
  41.1 60.2 all-gather.2
  143.4 55.1 reduce-scatter.1

commit v2 on v1

--- a/solution.py
+++ b/solution.py
@@ -106,42 +106,56 @@
     before = jnp.cumsum(decays, axis=0) - decays
     through = before + decays
     mine = lax.dynamic_index_in_dim(before, device_index, 0, keepdims=False)
-    shard_piece = (
-        gathered[:, :state_rows].reshape((-1,) + running.shape).astype(jnp.float32)
-    )
-    piece_rows = shard_piece.shape[0]
+    piece_rows = gathered.shape[0]
     owners = lax.broadcasted_iota(jnp.int32, (piece_rows, 1, 1), 0)
     factors = jnp.exp(jnp.where(owners < device_index, mine[None] - through, -jnp.inf))
-    entering = jnp.zeros_like(running) + jnp.einsum(
-        "rgj,rgjpn->gjpn", factors, shard_piece, precision=lax.Precision.HIGHEST
+    factor_rows = jnp.concatenate(
+        (
+            jnp.repeat(factors.reshape(piece_rows, head_count), HEAD_DIM, axis=1),
+            jnp.zeros((piece_rows, gathered.shape[1] - state_rows), jnp.float32),
+        ),
+        axis=1,
     )
+    entering = jnp.sum(factor_rows[:, :, None] * gathered.astype(jnp.float32), axis=0)
+    entering = entering[:state_rows].reshape(running.shape)
     leading = jnp.cumsum(block_decay, axis=0) - block_decay
     state_in = (
         jnp.exp(leading)[..., None, None] * entering[None] + jnp.stack(local_in, axis=0)
     ).astype(jnp.bfloat16)
-    y_carry = jnp.exp(cumul)[..., None] * jnp.einsum(
-        "ctgn,cgjpn->ctgjp", c_blocks, state_in, preferred_element_type=jnp.float32
+    width = per_group * HEAD_DIM
+    y_pre = lax.optimization_barrier(
+        y_local + skip_gain.reshape(groups, per_group)[:, :, None] * x_blocks
     )
-    y_all = y_local + y_carry + skip_gain.reshape(groups, per_group)[:, :, None] * x_blocks
-    width = per_group * HEAD_DIM
-    gated = y_all.reshape(row_count, groups, width) * jax.nn.silu(
-        gate_input.reshape(row_count, groups, width).astype(jnp.float32)
-    )
-    square_mean = jnp.mean(gated * gated, axis=-1, keepdims=True)
-    normed = (
-        (gated * lax.rsqrt(square_mean + epsilon) * norm_gain.reshape(groups, width))
-        .astype(jnp.bfloat16)
-        .reshape(row_count, head_count * HEAD_DIM)
-    )
-    shares = lax.psum_scatter(
-        lax.dot_general(
-            out_weight, normed, (((0,), (1,)), ((), ())), preferred_element_type=jnp.float32
-        ).astype(jnp.bfloat16),
-        "chan",
-        scatter_dimension=0,
-        tiled=True,
-    )
-    return shares.T
+    chunk_count = 2
+    per_chunk = block_count // chunk_count
+    outs = []
+    for chunk in range(chunk_count):
+        part = slice(chunk * per_chunk, (chunk + 1) * per_chunk)
+        rows = per_chunk * BLOCK
+        y_carry = jnp.exp(cumul[part])[..., None] * jnp.einsum(
+            "ctgn,cgjpn->ctgjp", c_blocks[part], state_in[part], preferred_element_type=jnp.float32
+        )
+        y_all = y_pre[part] + y_carry
+        gate_rows = gate_input[chunk * rows : (chunk + 1) * rows]
+        gated = y_all.reshape(rows, groups, width) * jax.nn.silu(
+            gate_rows.reshape(rows, groups, width).astype(jnp.float32)
+        )
+        square_mean = jnp.mean(gated * gated, axis=-1, keepdims=True)
+        normed = (
+            (gated * lax.rsqrt(square_mean + epsilon) * norm_gain.reshape(groups, width))
+            .astype(jnp.bfloat16)
+            .reshape(rows, head_count * HEAD_DIM)
+        )
+        shares = lax.psum_scatter(
+            lax.dot_general(
+                out_weight, normed, (((0,), (1,)), ((), ())), preferred_element_type=jnp.float32
+            ).astype(jnp.bfloat16),
+            "chan",
+            scatter_dimension=0,
+            tiled=True,
+        )
+        outs.append(shares.T)
+    return jnp.concatenate(outs, axis=0)
 
 
 def solution(mesh):

time: 207 us -> 223 us (1.077)
  local copies, waits for them, and re-layouts: 33.5 us -> 52.5 us
  other arithmetic: 15.1 us -> 29.3 us
  waiting for transfers between devices: 106 us -> 93.4 us
  matrix products: 30.9 us -> 26.8 us
    all_gather x1, waiting for transfers between devices: 51.1 us -> 20.4 us  [local(): gathered = lax.all_gather(packed, 'seq', axis=0, tiled=False)]
    reduce_scatter x1 -> x2, waiting for transfers between devices: 55.3 us -> 73 us  [local(): lax.psum_scatter(lax.dot_general(out_weight, normed, (((0,), (1,)), ((),...]
    dot_general x2, matrix products: 12.6 us -> 2.46 us  [local(): jnp.einsum('ctgn,cgjpn->ctgjp', c_blocks[part], state_in[part], preferred...]
    another operation x12 -> x13, local copies, waits for them, and re-layouts: 3.45 us -> 13.5 us
    convert_element_type x1 -> x2, local copies, waits for them, and re-layouts: 3.4 us -> 12.3 us  [local(): skip_gain.reshape(groups, per_group)[:, :, None] * x_blocks]
    reduce_sum x0 -> x1, other arithmetic: none -> 6.47 us  [local(): jnp.sum(factor_rows[:, :, None] * gathered.astype(jnp.float32), axis=0)]
    dot_general x1, matrix products: 5.35 us -> 9.6 us  [local(): jnp.einsum('cgjts,csgjp->ctgjp', mixing, x_blocks, preferred_element_type...]
    slice x1 -> x3, local copies, waits for them, and re-layouts: 7.52 us -> 3.92 us  [the longest x1 3.22 us: local(): gate_rows = gate_input[chunk * rows:(chunk + 1) * rows]]
  transfers between devices with their start and end apart: 4 -> 5, of which waited for: 2 -> 3; matrix products, arithmetic and copies ran while one was open for 10% -> 27% of each run, Pallas kernels for 0% -> 0%
where the time goes in v2:
time: 223 us; the launch traced here: 222 us
  waiting for transfers between devices  93.4 us (42%)
  local copies, waits for them, and re-layouts  52.5 us (24%)
  other arithmetic  29.3 us (13%)
  matrix products  26.8 us (12%)
  between operations  13.6 us (6%)
  starting transfers between devices  5.9 us (3%)
    reduce_scatter x2, waiting for transfers between devices, local(): lax.psum_scatter(lax.dot_general(out_weight, normed, (((0,), (1,)), ((),...  73 us
    all_gather x1, waiting for transfers between devices, local(): gathered = lax.all_gather(packed, 'seq', axis=0, tiled=False)  20.4 us
    another operation x13, local copies, waits for them, and re-layouts  13.5 us
    unnamed x67, local copies, waits for them, and re-layouts  13 us
    convert_element_type x2, local copies, waits for them, and re-layouts, local(): skip_gain.reshape(groups, per_group)[:, :, None] * x_blocks  12.3 us
    dot_general x1, matrix products, local(): jnp.einsum('cgjts,csgjp->ctgjp', mixing, x_blocks, preferred_element_type...  9.6 us
    dot_general x2, matrix products, local(): lax.dot_general(out_weight, normed, (((0,), (1,)), ((), ())), preferred_e...  7.89 us
    convert_element_type x2, other arithmetic, conv_silu(): return jax.nn.silu(acc).astype(jnp.bfloat16)  7.48 us
  transfers between devices with their start and end apart: 5, of which 3 were waited for; matrix products, arithmetic and copies ran while one was open for 27% of the time, Pallas kernels for 0%

profile of v2, /device:TPU:24, one launch (start us, length us, event | category | flops | bytes accessed | tf_op | source)
XLA Modules:
  0.0 221.5 jit_solution(6085403516380943211)
XLA Ops:
  7.3 1.9 collective-permute-start
  9.2 1.1 copy.45
  10.3 3.5 %collective-permute-start.1 = (bf16[3,2,1,128]{3,0,2,1:T(4,128)(2,1)S(1)}, bf16[3,2,1,128]{3,0,2,1:T(4,128)(2,1)S(1)}, u32[]{:S(2)}, u32[]{:S(2)}) collective-permute-start(bf16[3,2,1,128]{3,0,2,1:T(4,128)(2,1)S(1)} %slice.205), channel_id=1, source_target_pairs={{0,8},{8,16},{16,24},{24,32},{32,40},{40,48},{48,56},{56,64},{64,7... | collective-permute-start | bytes 4616 | tf_op jit(solution)/shard_map/ppermute | solution.py:20
  15.6 2.3 %reduce-window.6 = f32[4,16,1,2,128]{4,1,2,3,0:T(8,128)S(1)} reduce-window(f32[4,16,1,2,128]{4,1,2,3,0:T(8,128)S(1)} %copy.49, f32[]{:T(128)} %constant.63.clone.1), window={size=1x1x1x1x128 pad=0_0x0_0x0_0x0_0x127_0}, to_apply=%region_0.1 | reduce-window | flops 2080768 | bytes 131076 | tf_op jit(solution)/shard_map/reduce-window
  18.8 1.0 fusion.40
  24.2 6.8 %multiply_convert_fusion.4 = bf16[1024,1024]{1,0:T(8,128)(2,1)S(1)} fusion(bf16[1024,1024]{1,0:T(8,128)(2,1)} %param.13, bf16[3,1024]{1,0:T(4,128)(2,1)} %copy-done.18, f32[1024]{0:T(1024)S(1)} %bitcast.153, f32[1024]{0:T(1024)S(1)} %bitcast.154, f32[1024]{0:T(1024)S(1)} %bitcast.152, f32[1024]{0:T(1024)S(1)} %bitcast.151), kind=kLoop, calls=%fused_computation.14 | loop fusion | flops 26214400 | bytes 4216832 | tf_op jit(solution)/shard_map/convert_element_type | solution.py:27
  31.0 4.0 %reshape.548 = bf16[4,256,16,64]{3,2,1,0:T(8,128)(2,1)} reshape(bf16[1024,1024]{1,0:T(8,128)(2,1)S(1)} %multiply_convert_fusion.4) | data formatting | bytes 4194304 | tf_op jit(solution)/shard_map/reshape.57
  35.0 5.9 %copy.54 = bf16[4,256,16,64]{1,3,2,0:T(8,128)(2,1)} copy(bf16[4,256,16,64]{3,2,1,0:T(8,128)(2,1)} %reshape.548) | data formatting | bytes 4194304 | tf_op jit(solution)/shard_map/reshape.57
  40.9 4.6 %fusion.7 = f32[4,16,64,128]{3,2,1,0:T(8,128)S(1)} fusion(bf16[4,256,16,64]{1,3,2,0:T(8,128)(2,1)} %copy.54, f32[4,256,128]{2,1,0:T(8,128)S(1)} %convert_element_type.194, f32[4,256,16]{1,2,0:T(8,128)} %copy.63), kind=kOutput, calls=%fused_computation.10 | convolution fusion | flops 272629760 | bytes 4784128 | tf_op jit(solution)/shard_map/csgjp,csgjn->cgjpn/dot_general | solution.py:78
  45.5 1.3 copy-done.4
  50.3 1.5 copy.53
  51.8 1.5 reshape.527
  54.5 3.2 %fusion.61 = (bf16[512,1024]{1,0:T(8,128)(2,1)}, bf16[512,1024]{1,0:T(8,128)(2,1)}) fusion(bf16[1024,1024]{1,0:T(8,128)(2,1)} %param.15), kind=kLoop, calls=%fused_computation.119 | loop fusion | bytes 4194304 | tf_op jit(solution)/shard_map/slice | solution.py:139
  57.8 2.3 %copy.80 = bf16[512,1024]{0,1:T(8,128)(2,1)} copy(bf16[512,1024]{1,0:T(8,128)(2,1)} %get-tuple-element.27) | data formatting | bytes 2097152
  63.1 2.3 %fusion.67 = f32[4,256,256]{2,1,0:T(8,128)} fusion(bf16[4,256,128]{2,1,0:T(8,128)(2,1)} %bitcast.137, bf16[4,256,128]{2,1,0:T(8,128)(2,1)S(1)} %bitcast.134), kind=kOutput, calls=%fused_computation.125 | convolution fusion | flops 67108864 | bytes 1572864 | tf_op jit(solution)/shard_map/ctgn,csgn->cgts/dot_general | solution.py:65
  65.3 4.4 %reshape.546 = f32[4,256,1,16,64]{4,3,1,0,2:T(8,128)} reshape(bf16[1024,1024]{1,0:T(8,128)(2,1)S(1)} %multiply_convert_fusion.4) | data formatting | bytes 6291456 | tf_op jit(solution)/shard_map/convert_element_type | solution.py:127
  69.7 7.9 %copy.56 = f32[4,256,1,16,64]{1,4,3,0,2:T(8,128)} copy(f32[4,256,1,16,64]{4,3,1,0,2:T(8,128)} %reshape.546) | data formatting | bytes 8388608 | tf_op jit(solution)/shard_map/convert_element_type | solution.py:127
  77.7 9.6 %bitcast_add_fusion = f32[4,256,1,16,64]{1,4,3,0,2:T(8,128)} fusion(f32[4,256,1,16,64]{1,4,3,0,2:T(8,128)} %copy.56, bf16[4,256,16,64]{1,3,2,0:T(8,128)(2,1)S(1)} %copy-done.5, f32[4,16,256]{2,1,0:T(8,128)S(1)} %copy-done.14, f32[4,16,256]{2,1,0:T(8,128)S(1)} %copy-done.13, f32[4,256,256]{2,1,0:T(8,128)} %fusion.67, pred[256,256]{1,0:T(8,128)(4,1)S(1)} %copy-done.15, ...), kind=kOutput, calls=%fused_computation.11 | convolution fusion | flops 559939584 | bytes 11731008 | tf_op jit(solution)/shard_map/cgjts,csgjp->ctgjp/dot_general | solution.py:74
  87.3 1.2 fusion.33
  88.5 20.4 %all-gather.3.cloned.1.call-done = bf16[33024,128]{1,0:T(8,128)(2,1)} async-done(((bf16[1032,128]{1,0:T(8,128)(2,1)}), bf16[33024,128]{1,0:T(8,128)(2,1)}) %all-gather.3.cloned.1.call-update) | async-done | bytes 8454160 | tf_op jit(solution)/shard_map/all_gather | solution.py:101
  110.3 6.5 %multiply_reduce_fusion = f32[1032,128]{1,0:T(8,128)S(1)} fusion(bf16[32,1032,128]{2,1,0:T(8,128)(2,1)} %bitcast.125, f32[32,1032]{1,0:T(8,128)S(1)} %concatenate.28), kind=kLoop, calls=%fused_computation | loop fusion | flops 12549120 | bytes 9114624 | tf_op jit(solution)/shard_map/reduce_sum | solution.py:119
  117.2 1.7 copy-done
  119.4 1.6 copy.70
  123.5 4.0 %fusion.11 = bf16[2048,512]{0,1:T(8,128)(2,1)} fusion(bf16[1024,2048]{1,0:T(8,128)(2,1)S(1)} %copy-done.27, f32[512]{0:T(512)S(1)} %add_rsqrt_fusion, f32[1024]{0:T(1024)S(1)} %copy-done.29, f32[512,1024]{0,1:T(8,128)S(1)} %bitcast.127, bf16[512,1024]{0,1:T(8,128)(2,1)S(1)} %copy-done.2), kind=kOutput, calls=%fused_computation.20 | convolution fusion | flops 2153250816 | bytes 9443328 | tf_op jit(solution)/shard_map/dot_general | solution.py:150
  128.7 1.3 copy.79
  130.1 2.0 slice_add_fusion.1
  132.1 1.6 copy.67
  133.9 1.0 copy-done.3
  136.3 3.9 %fusion.10 = bf16[2048,512]{0,1:T(8,128)(2,1)} fusion(bf16[1024,2048]{1,0:T(8,128)(2,1)S(1)} %copy-done.28, f32[1024]{0:T(1024)S(1)} %copy-done.29, f32[512]{0:T(512)S(1)} %add_rsqrt_fusion.1, f32[512,1024]{0,1:T(8,128)S(1)} %bitcast.129, bf16[512,1024]{0,1:T(8,128)(2,1)S(1)} %copy-done.3), kind=kOutput, calls=%fused_computation.19 | convolution fusion | flops 2153250816 | bytes 9443328 | tf_op jit(solution)/shard_map/dot_general | solution.py:150
  140.2 29.2 %reduce-scatter.5.cloned.1.call-done = bf16[256,512]{0,1:T(8,128)(2,1)} async-done(((bf16[2048,512]{0,1:T(8,128)(2,1)}), bf16[256,512]{0,1:T(8,128)(2,1)}) %reduce-scatter.5.cloned.1.call-update) | async-done | bytes 262160 | tf_op jit(solution)/shard_map/reduce_scatter | solution.py:149
  169.4 43.7 %reduce-scatter.3.cloned.1.call-done = bf16[256,512]{0,1:T(8,128)(2,1)} async-done(((bf16[2048,512]{0,1:T(8,128)(2,1)}), bf16[256,512]{0,1:T(8,128)(2,1)}) %reduce-scatter.3.cloned.1.call-update) | async-done | bytes 262160 | tf_op jit(solution)/shard_map/reduce_scatter | solution.py:149
  213.2 1.9 pad_maximum_fusion.2
  (127 shorter events, 22.7 us)
Async XLA Ops:
  6.5 13.4 %copy-start.16 = (f32[4,1024]{1,0:T(4,128)S(1)}, f32[4,1024]{1,0:T(4,128)}, u32[]{:S(2)}) copy-start(f32[4,1024]{1,0:T(4,128)} %param.20) | copy-start | bytes 49156
  6.5 14.0 %copy-start.21 = (f32[4,2,1,128]{3,2,1,0:T(1,128)S(1)}, f32[4,2,1,128]{3,2,1,0:T(1,128)}, u32[]{:S(2)}) copy-start(f32[4,2,1,128]{3,2,1,0:T(1,128)} %param.21) | copy-start | bytes 12292
  6.5 102.4 %all-gather.3.cloned.1.call-start = ((), (), s32[]{:S(2)}) async-start(), calls=%async_computation.4 | async-start | bytes 8718336 | tf_op jit(solution)/shard_map/all_gather | solution.py:101
  7.3 16.3 %collective-permute-start = (bf16[3,1024]{1,0:T(4,128)(2,1)S(1)}, bf16[3,1024]{1,0:T(4,128)(2,1)S(1)}, u32[]{:S(2)}, u32[]{:S(2)}) collective-permute-start(bf16[3,1024]{1,0:T(4,128)(2,1)S(1)} %slice.161), channel_id=1, source_target_pairs={{0,8},{8,16},{16,24},{24,32},{32,40},{40,48},{48,56},{56,64},{64,7... | collective-permute-start | bytes 18440 | tf_op jit(solution)/shard_map/ppermute | solution.py:20
  10.3 11.8 %collective-permute-start.1 = (bf16[3,2,1,128]{3,0,2,1:T(4,128)(2,1)S(1)}, bf16[3,2,1,128]{3,0,2,1:T(4,128)(2,1)S(1)}, u32[]{:S(2)}, u32[]{:S(2)}) collective-permute-start(bf16[3,2,1,128]{3,0,2,1:T(4,128)(2,1)S(1)} %slice.205), channel_id=1, source_target_pairs={{0,8},{8,16},{16,24},{24,32},{32,40},{40,48},{48,56},{56,64},{64,7... | collective-permute-start | bytes 4616 | tf_op jit(solution)/shard_map/ppermute | solution.py:20
  18.4 2.1 copy-start.8
  20.6 3.1 %copy-start.7 = (f32[4,256,1,16]{1,0,3,2:T(4,128)}, f32[4,256,1,16]{1,0,3,2:T(4,128)S(1)}, u32[]{:S(2)}) copy-start(f32[4,256,1,16]{1,0,3,2:T(4,128)S(1)} %reshape.531) | copy-start | bytes 196612
  20.8 3.4 %copy-start.17 = (f32[1,1024]{1,0:T(1,128)S(1)}, f32[1,1024]{1,0:T(1,128)}, u32[]{:S(2)}) copy-start(f32[1,1024]{1,0:T(1,128)} %get-tuple-element.39) | copy-start | bytes 12292
  40.9 5.9 %copy-start.20 = (f32[16]{0:T(128)S(1)}, f32[16]{0:T(128)}, u32[]{:S(2)}) copy-start(f32[16]{0:T(128)} %get-tuple-element.20) | copy-start | bytes 196
  40.9 5.9 %copy-start.22 = (f32[16]{0:T(128)S(1)}, f32[16]{0:T(128)}, u32[]{:S(2)}) copy-start(f32[16]{0:T(128)} %get-tuple-element.17) | copy-start | bytes 196
  40.9 5.9 %copy-start.23 = (f32[16]{0:T(128)S(1)}, f32[16]{0:T(128)}, u32[]{:S(2)}) copy-start(f32[16]{0:T(128)} %get-tuple-element.18) | copy-start | bytes 196
  40.9 5.9 %copy-start.24 = (f32[16]{0:T(128)S(1)}, f32[16]{0:T(128)}, u32[]{:S(2)}) copy-start(f32[16]{0:T(128)} %get-tuple-element.19) | copy-start | bytes 196
  45.4 1.3 copy-start.4
  45.5 2.3 %copy-start.19 = (bf16[8,128]{1,0:T(8,128)(2,1)S(1)}, bf16[8,128]{1,0:T(8,128)(2,1)}, u32[]{:S(2)}) copy-start(bf16[8,128]{1,0:T(8,128)(2,1)} %fusion.54) | copy-start | bytes 6148
  48.5 121.0 %reduce-scatter.5.cloned.1.call-start = ((), (), s32[]{:S(2)}) async-start(), calls=%async_computation.3 | async-start | bytes 2359296 | tf_op jit(solution)/shard_map/reduce_scatter | solution.py:149
  57.8 2.3 %copy-start.10 = (f32[4,16,256]{2,1,0:T(8,128)S(1)}, f32[4,16,256]{2,1,0:T(8,128)}, u32[]{:S(2)}) copy-start(f32[4,16,256]{2,1,0:T(8,128)} %reshape.527) | copy-start | bytes 196612
  69.7 7.9 %copy-start.5 = (bf16[4,256,16,64]{1,3,2,0:T(8,128)(2,1)S(1)}, bf16[4,256,16,64]{1,3,2,0:T(8,128)(2,1)}, u32[]{:S(2)}) copy-start(bf16[4,256,16,64]{1,3,2,0:T(8,128)(2,1)} %copy.54) | copy-start | bytes 6291460
  69.7 7.9 %copy-start.13 = (f32[4,16,256]{2,1,0:T(8,128)S(1)}, f32[4,16,256]{2,1,0:T(8,128)}, u32[]{:S(2)}) copy-start(f32[4,16,256]{2,1,0:T(8,128)} %reduce_window_sum.57) | copy-start | bytes 196612
  69.7 7.9 %copy-start.14 = (f32[4,16,256]{2,1,0:T(8,128)S(1)}, f32[4,16,256]{2,1,0:T(8,128)}, u32[]{:S(2)}) copy-start(f32[4,16,256]{2,1,0:T(8,128)} %copy.53) | copy-start | bytes 196612
  69.7 7.9 %copy-start.15 = (pred[256,256]{1,0:T(8,128)(4,1)S(1)}, pred[256,256]{1,0:T(8,128)(4,1)}, u32[]{:S(2)}) copy-start(pred[256,256]{1,0:T(8,128)(4,1)} %iota_compare_fusion) | copy-start | bytes 196612
  69.7 7.9 %copy-start.30 = (f32[16]{0:T(128)S(1)}, f32[16]{0:T(128)}, u32[]{:S(2)}) copy-start(f32[16]{0:T(128)} %param.19) | copy-start | bytes 196
  77.7 32.2 %copy-start.26 = (pred[32]{0:T(512)(128)(4,1)S(1)}, pred[32]{0:T(512)(128)(4,1)}, u32[]{:S(2)}) copy-start(pred[32]{0:T(512)(128)(4,1)} %iota_compare_fusion.3) | copy-start | bytes 100
  110.2 6.6 %copy-start.6 = (f32[1,1,16,64,128]{4,3,2,1,0:T(8,128)S(1)}, f32[1,1,16,64,128]{4,3,2,1,0:T(8,128)}, u32[]{:S(2)}) copy-start(f32[1,1,16,64,128]{4,3,2,1,0:T(8,128)} %get-tuple-element.25) | copy-start | bytes 1572868
  110.2 6.6 %copy-start.25 = (f32[4]{0:T(128)S(1)}, f32[4]{0:T(128)}, u32[]{:S(2)}) copy-start(f32[4]{0:T(128)} %pad.9.clone) | copy-start | bytes 52
  110.2 6.9 %copy-start.9 = (bf16[512,1,1,128]{3,0,2,1:T(8,128)(2,1)S(1)}, bf16[512,1,1,128]{3,0,2,1:T(8,128)(2,1)}, u32[]{:S(2)}) copy-start(bf16[512,1,1,128]{3,0,2,1:T(8,128)(2,1)} %get-tuple-element.29) | copy-start | bytes 393220
  110.3 6.9 %copy-start.11 = (f32[2,256,16]{1,2,0:T(8,128)S(1)}, f32[2,256,16]{1,2,0:T(8,128)}, u32[]{:S(2)}) copy-start(f32[2,256,16]{1,2,0:T(8,128)} %copy.69) | copy-start | bytes 98308
  116.7 2.2 copy-start
  121.0 2.5 %copy-start.27 = (bf16[1024,2048]{1,0:T(8,128)(2,1)S(1)}, bf16[1024,2048]{1,0:T(8,128)(2,1)}, u32[]{:S(2)}) copy-start(bf16[1024,2048]{1,0:T(8,128)(2,1)} %param.23) | copy-start | bytes 12582916
  121.2 2.3 %copy-start.29 = (f32[1024]{0:T(1024)S(1)}, f32[1024]{0:T(1024)}, u32[]{:S(2)}) copy-start(f32[1024]{0:T(1024)} %param.22) | copy-start | bytes 12292
  127.5 1.2 copy-start.1
  127.5 85.6 %reduce-scatter.3.cloned.1.call-start = ((), (), s32[]{:S(2)}) async-start(), calls=%async_computation.2 | async-start | bytes 2359296 | tf_op jit(solution)/shard_map/reduce_scatter | solution.py:149
  133.7 2.5 %copy-start.28 = (bf16[1024,2048]{1,0:T(8,128)(2,1)S(1)}, bf16[1024,2048]{1,0:T(8,128)(2,1)}, u32[]{:S(2)}) copy-start(bf16[1024,2048]{1,0:T(8,128)(2,1)} %param.23) | copy-start | bytes 12582916
  (4 other events, 3.8 us)
Sparse Core Ops, SparseCore 0:
  48.6 60.2 all-gather.2
  127.6 41.7 reduce-scatter.4
  172.0 41.1 reduce-scatter.2

commit v3 on v2

--- a/solution.py
+++ b/solution.py
@@ -126,7 +126,7 @@
     y_pre = lax.optimization_barrier(
         y_local + skip_gain.reshape(groups, per_group)[:, :, None] * x_blocks
     )
-    chunk_count = 2
+    chunk_count = 1
     per_chunk = block_count // chunk_count
     outs = []
     for chunk in range(chunk_count):

time: 223 us -> 188 us (0.84)
  local copies, waits for them, and re-layouts: 52.5 us -> 24.8 us
  other arithmetic: 29.3 us -> 22 us
  matrix products: 26.8 us -> 22.7 us
  waiting for transfers between devices: 93.4 us -> 96.9 us
    all_gather x1, waiting for transfers between devices: 20.4 us -> 41.5 us  [local(): gathered = lax.all_gather(packed, 'seq', axis=0, tiled=False)]
    reduce_scatter x2 -> x1, waiting for transfers between devices: 73 us -> 55.3 us  [local(): lax.psum_scatter(lax.dot_general(out_weight, normed, (((0,), (1,)), ((),...]
    another operation x13 -> x12, local copies, waits for them, and re-layouts: 13.5 us -> 3.46 us
    convert_element_type x2 -> x1, local copies, waits for them, and re-layouts: 12.3 us -> 3.41 us  [local(): skip_gain.reshape(groups, per_group)[:, :, None] * x_blocks]
    slice x2 -> x0, local copies, waits for them, and re-layouts: 3.88 us -> none  [the longest x1 3.22 us: local(): gate_rows = gate_input[chunk * rows:(chunk + 1) * rows]]
    unnamed x67 -> x26, local copies, waits for them, and re-layouts: 13 us -> 10.4 us
    dot_general x2 -> x1, matrix products: 7.89 us -> 6.94 us  [local(): lax.dot_general(out_weight, normed, (((0,), (1,)), ((), ())), preferred_e...]
  transfers between devices with their start and end apart: 5 -> 4, of which waited for: 3 -> 2; matrix products, arithmetic and copies ran while one was open for 27% -> 16% of each run, Pallas kernels for 0% -> 0%
where the time goes in v3:
time: 188 us; the launch traced here: 186 us
  waiting for transfers between devices  96.9 us (52%)
  local copies, waits for them, and re-layouts  24.8 us (13%)
  matrix products  22.7 us (12%)
  other arithmetic  22 us (12%)
  between operations  13.8 us (7%)
  starting transfers between devices  5.64 us (3%)
    reduce_scatter x1, waiting for transfers between devices, local(): lax.psum_scatter(lax.dot_general(out_weight, normed, (((0,), (1,)), ((),...  55.3 us
    all_gather x1, waiting for transfers between devices, local(): gathered = lax.all_gather(packed, 'seq', axis=0, tiled=False)  41.5 us
    unnamed x26, local copies, waits for them, and re-layouts  10.4 us
    dot_general x1, matrix products, local(): jnp.einsum('cgjts,csgjp->ctgjp', mixing, x_blocks, preferred_element_type...  9.06 us
    dot_general x1, matrix products, local(): lax.dot_general(out_weight, normed, (((0,), (1,)), ((), ())), preferred_e...  6.94 us
    reduce_sum x1, other arithmetic, local(): jnp.sum(factor_rows[:, :, None] * gathered.astype(jnp.float32), axis=0)  6.93 us
    convert_element_type x2, other arithmetic, conv_silu(): return jax.nn.silu(acc).astype(jnp.bfloat16)  5.9 us
    ppermute x2, starting transfers between devices, passed_along(): return lax.ppermute(x, axis, pairs)  5.41 us
  transfers between devices with their start and end apart: 4, of which 2 were waited for; matrix products, arithmetic and copies ran while one was open for 16% of the time, Pallas kernels for 0%

profile of v3, /device:TPU:24, one launch (start us, length us, event | category | flops | bytes accessed | tf_op | source)
XLA Modules:
  0.0 185.9 jit_solution(962432959057420575)
XLA Ops:
  6.5 0.9 slice.127
  7.4 0.9 copy.42
  8.3 1.9 %collective-permute-start = (bf16[3,1024]{0,1:T(8,128)(2,1)}, bf16[3,1024]{0,1:T(8,128)(2,1)S(1)}, u32[]{:S(2)}, u32[]{:S(2)}) collective-permute-start(bf16[3,1024]{0,1:T(8,128)(2,1)} %copy.42), channel_id=1, source_target_pairs={{0,8},{8,16},{16,24},{24,32},{32,40},{40,48},{48,56},{56,64},{64,7... | collective-permute-start | bytes 18440 | tf_op jit(solution)/shard_map/ppermute | solution.py:20
  10.2 1.1 copy.45
  11.3 3.5 %collective-permute-start.1 = (bf16[3,2,1,128]{3,0,2,1:T(4,128)(2,1)S(1)}, bf16[3,2,1,128]{3,0,2,1:T(4,128)(2,1)S(1)}, u32[]{:S(2)}, u32[]{:S(2)}) collective-permute-start(bf16[3,2,1,128]{3,0,2,1:T(4,128)(2,1)S(1)} %slice.161), channel_id=1, source_target_pairs={{0,8},{8,16},{16,24},{24,32},{32,40},{40,48},{48,56},{56,64},{64,7... | collective-permute-start | bytes 4616 | tf_op jit(solution)/shard_map/ppermute | solution.py:20
  14.9 0.7 exponential_negate_fusion
  15.5 1.0 broadcast_multiply_fusion
  16.6 2.3 %reduce-window.6 = f32[4,16,1,2,128]{4,1,2,3,0:T(8,128)S(1)} reduce-window(f32[4,16,1,2,128]{4,1,2,3,0:T(8,128)S(1)} %copy.49, f32[]{:T(128)} %constant.61.clone.1), window={size=1x1x1x1x128 pad=0_0x0_0x0_0x0_0x127_0}, to_apply=%region_0.1 | reduce-window | flops 2080768 | bytes 131076 | tf_op jit(solution)/shard_map/reduce-window
  20.3 0.9 fusion.58
  21.3 0.7 fusion.59
  22.3 2.6 %copy.43 = bf16[1024,1024]{0,1:T(8,128)(2,1)} copy(bf16[1024,1024]{1,0:T(8,128)(2,1)S(1)} %copy-done.3) | data formatting | bytes 4194304 | tf_op args[0]
  24.9 0.7 multiply_convert_fusion.9
  25.7 0.7 copy-done.6
  26.5 5.2 %multiply_convert_fusion.5 = bf16[1024,1024]{0,1:T(8,128)(2,1)S(1)} fusion(bf16[1024,1024]{0,1:T(8,128)(2,1)S(1)} %copy-done, bf16[3,1024]{0,1:T(8,128)(2,1)} %copy-done.6, f32[1024]{0:T(1024)S(1)} %bitcast.114, f32[1024]{0:T(1024)S(1)} %bitcast.115, f32[1024]{0:T(1024)S(1)} %bitcast.113, f32[1024]{0:T(1024)S(1)} %bitcast.112), kind=kLoop, calls=%fused_computation.26 | loop fusion | flops 26214400 | bytes 4216832 | tf_op jit(solution)/shard_map/convert_element_type | solution.py:27
  31.7 2.8 %reshape.430 = bf16[4,256,16,64]{1,0,3,2:T(4,128)(2,1)} reshape(bf16[1024,1024]{0,1:T(8,128)(2,1)S(1)} %multiply_convert_fusion.5) | data formatting | bytes 4194304 | tf_op jit(solution)/shard_map/reshape.54
  34.5 4.6 %fusion.11 = f32[4,16,64,128]{3,2,1,0:T(8,128)S(1)} fusion(f32[4,256,128]{2,1,0:T(8,128)S(1)} %convert_element_type.175, f32[4,256,16]{1,2,0:T(8,128)S(1)} %copy.62, bf16[4,256,16,64]{1,0,3,2:T(4,128)(2,1)} %reshape.430), kind=kOutput, calls=%fused_computation.16 | convolution fusion | flops 272629760 | bytes 4784128 | tf_op jit(solution)/shard_map/csgjp,csgjn->cgjpn/dot_general | solution.py:78
  39.1 1.1 fusion.28
  40.2 0.7 pad_maximum_fusion.2
  41.4 0.6 copy.53
  42.1 3.9 %copy.67 = bf16[1024,1024]{0,1:T(8,128)(2,1)} copy(bf16[1024,1024]{1,0:T(8,128)(2,1)} %param.15) | data formatting | bytes 4194304 | tf_op args[2]
  46.1 1.3 fusion.61
  47.4 3.4 %reshape.445 = f32[4,256,1,16,64]{1,0,4,3,2:T(4,128)} reshape(bf16[1024,1024]{0,1:T(8,128)(2,1)S(1)} %multiply_convert_fusion.5) | data formatting | bytes 6291456 | tf_op jit(solution)/shard_map/convert_element_type | solution.py:127
  50.8 9.1 %bitcast_add_fusion = f32[4,256,1,16,64]{1,4,3,0,2:T(8,128)} fusion(f32[4,256,1,16,64]{1,0,4,3,2:T(4,128)} %reshape.445, f32[4,16,256]{2,1,0:T(8,128)S(1)} %copy-done.7, f32[4,16,256]{2,1,0:T(8,128)S(1)} %reduce_window_sum.57, f32[4,256,256]{2,1,0:T(8,128)} %fusion.61, pred[256,256]{1,0:T(8,128)(4,1)S(1)} %iota_compare_fusion, f32[16]{0:T(128)S(1)} %copy-done.10, ...), kind=kOutput, calls=%fused_computation.19 | convolution fusion | flops 559939584 | bytes 11731008 | tf_op jit(solution)/shard_map/cgjts,csgjp->ctgjp/dot_general | solution.py:74
  59.9 41.5 %all-gather.3.cloned.1.call-done = bf16[33024,128]{1,0:T(8,128)(2,1)} async-done(((bf16[1032,128]{1,0:T(8,128)(2,1)}), bf16[33024,128]{1,0:T(8,128)(2,1)}) %all-gather.3.cloned.1.call-update) | async-done | bytes 8454160 | tf_op jit(solution)/shard_map/all_gather | solution.py:101
  101.4 0.9 convert_reduce_fusion
  102.7 6.9 %multiply_reduce_fusion = f32[1032,128]{1,0:T(8,128)S(1)} fusion(bf16[32,1032,128]{2,1,0:T(8,128)(2,1)} %bitcast.96, f32[32,1032]{1,0:T(8,128)S(1)} %concatenate.20), kind=kLoop, calls=%fused_computation | loop fusion | flops 12549120 | bytes 9114624 | tf_op jit(solution)/shard_map/reduce_sum | solution.py:119
  109.7 0.8 fusion.12
  110.6 2.8 %copy.66 = f32[4,256,1,16,64]{1,0,4,3,2:T(4,128)S(1)} copy(f32[4,256,1,16,64]{1,4,3,0,2:T(8,128)S(1)} %fusion.12) | data formatting | bytes 8388608 | tf_op jit(solution)/shard_map/add | solution.py:138
  113.4 1.0 copy.70
  115.0 1.3 multiply_reduce_fusion.1
  116.8 6.9 %convert_bitcast_fusion = bf16[2048,1024]{0,1:T(8,128)(2,1)} fusion(bf16[1024,2048]{1,0:T(8,128)(2,1)S(1)} %copy-done.8, f32[1024]{0:T(1024)S(1)} %copy-done.9, f32[1024]{0:T(1024)S(1)} %add_rsqrt_fusion, f32[1024,1024]{0,1:T(8,128)S(1)} %bitcast.93, bf16[1024,1024]{0,1:T(8,128)(2,1)S(1)} %copy-done.1), kind=kOutput, calls=%fused_computation.21 | convolution fusion | flops 4306501632 | bytes 14688256 | tf_op jit(solution)/shard_map/dot_general | solution.py:150
  123.7 55.3 %reduce-scatter.2.cloned.1.call-done = bf16[256,1024]{0,1:T(8,128)(2,1)} async-done(((bf16[2048,1024]{0,1:T(8,128)(2,1)}), bf16[256,1024]{0,1:T(8,128)(2,1)}) %reduce-scatter.2.cloned.1.call-update) | async-done | bytes 524304 | tf_op jit(solution)/shard_map/reduce_scatter | solution.py:149
  (70 shorter events, 3.9 us)
Async XLA Ops:
  6.5 15.8 %copy-start.3 = (bf16[1024,1024]{1,0:T(8,128)(2,1)S(1)}, bf16[1024,1024]{1,0:T(8,128)(2,1)}, u32[]{:S(2)}) copy-start(bf16[1024,1024]{1,0:T(8,128)(2,1)} %param.13) | copy-start | bytes 6291460
  6.5 94.9 %all-gather.3.cloned.1.call-start = ((), (), s32[]{:S(2)}) async-start(), calls=%async_computation.2 | async-start | bytes 8718336 | tf_op jit(solution)/shard_map/all_gather | solution.py:101
  8.3 17.4 %collective-permute-start = (bf16[3,1024]{0,1:T(8,128)(2,1)}, bf16[3,1024]{0,1:T(8,128)(2,1)S(1)}, u32[]{:S(2)}, u32[]{:S(2)}) collective-permute-start(bf16[3,1024]{0,1:T(8,128)(2,1)} %copy.42), channel_id=1, source_target_pairs={{0,8},{8,16},{16,24},{24,32},{32,40},{40,48},{48,56},{56,64},{64,7... | collective-permute-start | bytes 18440 | tf_op jit(solution)/shard_map/ppermute | solution.py:20
  11.3 13.6 %collective-permute-start.1 = (bf16[3,2,1,128]{3,0,2,1:T(4,128)(2,1)S(1)}, bf16[3,2,1,128]{3,0,2,1:T(4,128)(2,1)S(1)}, u32[]{:S(2)}, u32[]{:S(2)}) collective-permute-start(bf16[3,2,1,128]{3,0,2,1:T(4,128)(2,1)S(1)} %slice.161), channel_id=1, source_target_pairs={{0,8},{8,16},{16,24},{24,32},{32,40},{40,48},{48,56},{56,64},{64,7... | collective-permute-start | bytes 4616 | tf_op jit(solution)/shard_map/ppermute | solution.py:20
  24.9 1.6 copy-start
  25.7 0.7 copy-start.6
  41.0 138.1 %reduce-scatter.2.cloned.1.call-start = ((), (), s32[]{:S(2)}) async-start(), calls=%async_computation.1 | async-start | bytes 4718592 | tf_op jit(solution)/shard_map/reduce_scatter | solution.py:149
  46.0 4.8 %copy-start.7 = (f32[4,16,256]{2,1,0:T(8,128)S(1)}, f32[4,16,256]{2,1,0:T(8,128)}, u32[]{:S(2)}) copy-start(f32[4,16,256]{2,1,0:T(8,128)} %copy.53) | copy-start | bytes 196612
  46.0 4.8 %copy-start.10 = (f32[16]{0:T(128)S(1)}, f32[16]{0:T(128)}, u32[]{:S(2)}) copy-start(f32[16]{0:T(128)} %param.19) | copy-start | bytes 196
  102.7 7.0 %copy-start.2 = (f32[4,256,1,16,64]{1,4,3,0,2:T(8,128)S(1)}, f32[4,256,1,16,64]{1,4,3,0,2:T(8,128)}, u32[]{:S(2)}) copy-start(f32[4,256,1,16,64]{1,4,3,0,2:T(8,128)} %bitcast_add_fusion) | copy-start | bytes 12582916
  102.7 7.0 %copy-start.4 = (f32[1,16,64,128]{3,2,1,0:T(8,128)S(1)}, f32[1,16,64,128]{3,2,1,0:T(8,128)}, u32[]{:S(2)}) copy-start(f32[1,16,64,128]{3,2,1,0:T(8,128)} %get-tuple-element.23) | copy-start | bytes 1572868
  102.7 7.0 %copy-start.5 = (f32[1,16,64,128]{3,2,1,0:T(8,128)S(1)}, f32[1,16,64,128]{3,2,1,0:T(8,128)}, u32[]{:S(2)}) copy-start(f32[1,16,64,128]{3,2,1,0:T(8,128)} %get-tuple-element.24) | copy-start | bytes 1572868
  113.4 1.6 copy-start.1
  114.4 2.3 %copy-start.8 = (bf16[1024,2048]{1,0:T(8,128)(2,1)S(1)}, bf16[1024,2048]{1,0:T(8,128)(2,1)}, u32[]{:S(2)}) copy-start(bf16[1024,2048]{1,0:T(8,128)(2,1)} %param.23) | copy-start | bytes 12582916
  114.4 2.3 %copy-start.9 = (f32[1024]{0:T(1024)S(1)}, f32[1024]{0:T(1024)}, u32[]{:S(2)}) copy-start(f32[1024]{0:T(1024)} %param.22) | copy-start | bytes 12292
Sparse Core Ops, SparseCore 0:
  41.1 60.2 all-gather.2
  123.8 55.1 reduce-scatter.1

commit v4 on v3

--- a/solution.py
+++ b/solution.py
@@ -87,37 +87,20 @@
             jnp.exp(block_decay[block_index])[..., None, None] * running + block_states[block_index]
         )
     slab_decay = jnp.sum(block_decay, axis=0)
-    device_index = lax.axis_index("seq")
-    state_rows = groups * per_group * HEAD_DIM
-    decay_hi = slab_decay.reshape(-1).astype(jnp.bfloat16)
-    decay_rest = slab_decay.reshape(-1) - decay_hi.astype(jnp.float32)
-    decay_mid = decay_rest.astype(jnp.bfloat16)
-    decay_lo = (decay_rest - decay_mid.astype(jnp.float32)).astype(jnp.bfloat16)
-    decay_rows = jnp.zeros((8, STATE), jnp.bfloat16)
-    decay_rows = decay_rows.at[0:3, 0:head_count].set(jnp.stack((decay_hi, decay_mid, decay_lo)))
-    packed = jnp.concatenate(
-        (running.reshape(state_rows, STATE).astype(jnp.bfloat16), decay_rows), axis=0
-    )
-    gathered = lax.all_gather(packed, "seq", axis=0, tiled=False)
-    decays = (
-        jnp.sum(gathered[:, state_rows : state_rows + 3, 0:head_count].astype(jnp.float32), axis=1)
-        .reshape(-1, groups, per_group)
-    )
-    before = jnp.cumsum(decays, axis=0) - decays
-    through = before + decays
-    mine = lax.dynamic_index_in_dim(before, device_index, 0, keepdims=False)
-    piece_rows = gathered.shape[0]
-    owners = lax.broadcasted_iota(jnp.int32, (piece_rows, 1, 1), 0)
-    factors = jnp.exp(jnp.where(owners < device_index, mine[None] - through, -jnp.inf))
-    factor_rows = jnp.concatenate(
-        (
-            jnp.repeat(factors.reshape(piece_rows, head_count), HEAD_DIM, axis=1),
-            jnp.zeros((piece_rows, gathered.shape[1] - state_rows), jnp.float32),
-        ),
-        axis=1,
-    )
-    entering = jnp.sum(factor_rows[:, :, None] * gathered.astype(jnp.float32), axis=0)
-    entering = entering[:state_rows].reshape(running.shape)
+    seq_count = lax.axis_size("seq")
+    carried_decay = passed_along(slab_decay, "seq", 1)
+    carried_state = passed_along(running.astype(jnp.bfloat16), "seq", 1).astype(jnp.float32)
+    distance = 1
+    while distance < seq_count:
+        earlier_decay = passed_along(carried_decay, "seq", distance)
+        earlier_state = passed_along(carried_state.astype(jnp.bfloat16), "seq", distance)
+        carried_state = (
+            jnp.exp(carried_decay)[..., None, None] * earlier_state.astype(jnp.float32)
+            + carried_state
+        )
+        carried_decay = earlier_decay + carried_decay
+        distance *= 2
+    entering = carried_state
     leading = jnp.cumsum(block_decay, axis=0) - block_decay
     state_in = (
         jnp.exp(leading)[..., None, None] * entering[None] + jnp.stack(local_in, axis=0)

time: 188 us -> 202 us (1.074)
  starting transfers between devices: 5.64 us -> 26.5 us
  waiting for transfers between devices: 96.9 us -> 84.3 us
  local copies, waits for them, and re-layouts: 24.8 us -> 30.8 us
    all_gather x1 -> x0, waiting for transfers between devices: 41.5 us -> none  [local(): gathered = lax.all_gather(packed, 'seq', axis=0, tiled=False)]
    ppermute x2 -> x13, waiting for transfers between devices: 0.01 us -> 26.5 us  [passed_along(): return lax.ppermute(x, axis, pairs)]
    ppermute x2 -> x13, starting transfers between devices: 5.41 us -> 26.5 us  [passed_along(): return lax.ppermute(x, axis, pairs)]
    reduce_sum x2 -> x0, other arithmetic: 7.82 us -> none  [the longest x1 6.93 us: local(): jnp.sum(factor_rows[:, :, None] * gathered.astype(jnp.float32), axis=0)]
    convert_element_type x3 -> x5, other arithmetic: 1.14 us -> 4.81 us  [the longest x4 3.51 us: local(): carried_state.astype(jnp.bfloat16)]
    another operation x12 -> x9, local copies, waits for them, and re-layouts: 3.46 us -> 6.84 us
    mul x0 -> x5, other arithmetic: none -> 3.11 us  [the longest x4 1.81 us: local(): jnp.exp(carried_decay)[..., None, None] * earlier_state.astype(jnp.float32)]
    reduce_scatter x1, waiting for transfers between devices: 55.3 us -> 57.8 us  [local(): lax.psum_scatter(lax.dot_general(out_weight, normed, (((0,), (1,)), ((),...]
  transfers between devices with their start and end apart: 4 -> 14, of which waited for: 2 -> 9; matrix products, arithmetic and copies ran while one was open for 16% -> 20% of each run, Pallas kernels for 0% -> 0%
where the time goes in v4:
time: 202 us; the launch traced here: 200 us
  waiting for transfers between devices  84.3 us (42%)
  local copies, waits for them, and re-layouts  30.8 us (15%)
  starting transfers between devices  26.5 us (13%)
  other arithmetic  22.9 us (11%)
  matrix products  21.7 us (11%)
  between operations  13.9 us (7%)
    reduce_scatter x1, waiting for transfers between devices, local(): lax.psum_scatter(lax.dot_general(out_weight, normed, (((0,), (1,)), ((),...  57.8 us
    ppermute x13, waiting for transfers between devices, passed_along(): return lax.ppermute(x, axis, pairs)  26.5 us
    ppermute x13, starting transfers between devices, passed_along(): return lax.ppermute(x, axis, pairs)  26.5 us
    unnamed x38, local copies, waits for them, and re-layouts  11.8 us
    dot_general x1, matrix products, local(): jnp.einsum('cgjts,csgjp->ctgjp', mixing, x_blocks, preferred_element_type...  7.96 us
    dot_general x1, matrix products, local(): lax.dot_general(out_weight, normed, (((0,), (1,)), ((), ())), preferred_e...  6.98 us
    another operation x9, local copies, waits for them, and re-layouts  6.84 us
    convert_element_type x2, other arithmetic, conv_silu(): return jax.nn.silu(acc).astype(jnp.bfloat16)  5.97 us
  transfers between devices with their start and end apart: 14, of which 9 were waited for; matrix products, arithmetic and copies ran while one was open for 20% of the time, Pallas kernels for 0%

profile of v4, /device:TPU:24, one launch (start us, length us, event | category | flops | bytes accessed | tf_op | source)
XLA Modules:
  0.0 200.1 jit_solution(7101594682582366939)
XLA Ops:
  8.3 1.9 collective-permute-start
  11.3 3.5 %collective-permute-start.1 = (bf16[3,2,1,128]{3,0,2,1:T(4,128)(2,1)S(1)}, bf16[3,2,1,128]{3,0,2,1:T(4,128)(2,1)S(1)}, u32[]{:S(2)}, u32[]{:S(2)}) collective-permute-start(bf16[3,2,1,128]{3,0,2,1:T(4,128)(2,1)S(1)} %slice.133), channel_id=1, source_target_pairs={{0,8},{8,16},{16,24},{24,32},{32,40},{40,48},{48,56},{56,64},{64,7... | collective-permute-start | bytes 4616 | tf_op jit(solution)/shard_map/ppermute | solution.py:20
  16.6 2.3 %reduce-window.6 = f32[4,16,1,2,128]{4,1,2,3,0:T(8,128)S(1)} reduce-window(f32[4,16,1,2,128]{4,1,2,3,0:T(8,128)S(1)} %copy.45, f32[]{:T(128)} %constant.13.clone.1), window={size=1x1x1x1x128 pad=0_0x0_0x0_0x0_0x127_0}, to_apply=%region_0.1 | reduce-window | flops 2080768 | bytes 131076 | tf_op jit(solution)/shard_map/reduce-window
  23.5 2.6 %copy.39 = bf16[1024,1024]{0,1:T(8,128)(2,1)} copy(bf16[1024,1024]{1,0:T(8,128)(2,1)S(1)} %copy-done.4) | data formatting | bytes 4194304 | tf_op args[0]
  27.7 5.3 %multiply_convert_fusion.5 = bf16[1024,1024]{0,1:T(8,128)(2,1)S(1)} fusion(bf16[1024,1024]{0,1:T(8,128)(2,1)S(1)} %copy-done, bf16[3,1024]{0,1:T(8,128)(2,1)} %collective-permute-done, f32[1024]{0:T(1024)S(1)} %bitcast.95, f32[1024]{0:T(1024)S(1)} %bitcast.96, f32[1024]{0:T(1024)S(1)} %bitcast.94, f32[1024]{0:T(1024)S(1)} %bitcast.93), kind=kLoop, calls=%fused_computation.25 | loop fusion | flops 26214400 | bytes 4216832 | tf_op jit(solution)/shard_map/convert_element_type | solution.py:27
  33.0 2.8 %reshape.334 = bf16[4,256,16,64]{1,0,3,2:T(4,128)(2,1)} reshape(bf16[1024,1024]{0,1:T(8,128)(2,1)S(1)} %multiply_convert_fusion.5) | data formatting | bytes 4194304 | tf_op jit(solution)/shard_map/reshape.24
  35.7 4.6 %fusion.11 = f32[4,16,64,128]{3,2,1,0:T(8,128)S(1)} fusion(f32[4,256,128]{2,1,0:T(8,128)S(1)} %convert_element_type.133, f32[4,256,16]{1,2,0:T(8,128)S(1)} %copy.58, bf16[4,256,16,64]{1,0,3,2:T(4,128)(2,1)} %reshape.334), kind=kOutput, calls=%fused_computation.15 | convolution fusion | flops 272629760 | bytes 4784128 | tf_op jit(solution)/shard_map/csgjp,csgjn->cgjpn/dot_general | solution.py:78
  41.7 1.9 collective-permute-start.7
  43.6 3.5 %collective-permute-start.2 = (f32[1,16]{1,0:T(1,128)S(1)}, f32[1,16]{1,0:T(1,128)S(1)}, u32[]{:S(2)}, u32[]{:S(2)}) collective-permute-start(f32[1,16]{1,0:T(1,128)S(1)} %bitcast.101), channel_id=1, source_target_pairs={{0,8},{8,16},{16,24},{24,32},{32,40},{40,48},{48,56},{56,64},{64,7... | collective-permute-start | bytes 200 | tf_op jit(solution)/shard_map/ppermute | solution.py:20
  47.1 4.4 %collective-permute-done.2 = f32[1,16]{1,0:T(1,128)S(1)} collective-permute-done((f32[1,16]{1,0:T(1,128)S(1)}, f32[1,16]{1,0:T(1,128)S(1)}, u32[]{:S(2)}, u32[]{:S(2)}) %collective-permute-start.2) | collective-permute-done | bytes 96 | tf_op jit(solution)/shard_map/ppermute | solution.py:20
  51.5 1.9 collective-permute-start.3
  53.4 1.9 collective-permute-start.8
  55.4 3.1 %collective-permute-done.3 = f32[1,16]{1,0:T(1,128)S(1)} collective-permute-done((f32[1,16]{1,0:T(1,128)S(1)}, f32[1,16]{1,0:T(1,128)S(1)}, u32[]{:S(2)}, u32[]{:S(2)}) %collective-permute-start.3) | collective-permute-done | bytes 96 | tf_op jit(solution)/shard_map/ppermute | solution.py:20
  58.5 4.8 %collective-permute-done.8 = bf16[1,16,64,128]{3,2,1,0:T(8,128)(2,1)S(1)} collective-permute-done((bf16[1,16,64,128]{3,2,1,0:T(8,128)(2,1)S(1)}, bf16[1,16,64,128]{3,2,1,0:T(8,128)(2,1)S(1)}, u32[]{:S(2)}, u32[]{:S(2)}) %collective-permute-start.8) | collective-permute-done | bytes 262176 | tf_op jit(solution)/shard_map/ppermute | solution.py:20
  64.1 1.9 collective-permute-start.9
  67.3 1.5 reshape.342
  69.5 1.5 reshape.339
  71.9 4.0 %copy.61 = bf16[1024,1024]{0,1:T(8,128)(2,1)} copy(bf16[1024,1024]{1,0:T(8,128)(2,1)} %param.13) | data formatting | bytes 4194304 | tf_op args[2]
  75.9 1.9 collective-permute-start.4
  77.8 1.5 reduce_window_sum.44
  79.3 4.1 %collective-permute-done.4 = f32[1,16]{1,0:T(1,128)S(1)} collective-permute-done((f32[1,16]{1,0:T(1,128)S(1)}, f32[1,16]{1,0:T(1,128)S(1)}, u32[]{:S(2)}, u32[]{:S(2)}) %collective-permute-start.4) | collective-permute-done | bytes 96 | tf_op jit(solution)/shard_map/ppermute | solution.py:20
  84.0 1.9 collective-permute-start.5
  86.2 1.9 collective-permute-start.10
  88.2 3.7 %collective-permute-done.5 = f32[1,16]{1,0:T(1,128)S(1)} collective-permute-done((f32[1,16]{1,0:T(1,128)S(1)}, f32[1,16]{1,0:T(1,128)S(1)}, u32[]{:S(2)}, u32[]{:S(2)}) %collective-permute-start.5) | collective-permute-done | bytes 96 | tf_op jit(solution)/shard_map/ppermute | solution.py:20
  94.3 3.6 %collective-permute-done.6 = f32[1,16]{1,0:T(1,128)S(1)} collective-permute-done((f32[1,16]{1,0:T(1,128)S(1)}, f32[1,16]{1,0:T(1,128)S(1)}, u32[]{:S(2)}, u32[]{:S(2)}) %collective-permute-start.6) | collective-permute-done | bytes 96 | tf_op jit(solution)/shard_map/ppermute | solution.py:20
  102.9 3.4 %reshape.347 = f32[4,256,1,16,64]{1,0,4,3,2:T(4,128)} reshape(bf16[1024,1024]{0,1:T(8,128)(2,1)S(1)} %multiply_convert_fusion.5) | data formatting | bytes 6291456 | tf_op jit(solution)/shard_map/convert_element_type | solution.py:110
  106.3 2.5 %collective-permute-done.11 = bf16[1,16,64,128]{3,2,1,0:T(8,128)(2,1)} collective-permute-done((bf16[1,16,64,128]{3,2,1,0:T(8,128)(2,1)}, bf16[1,16,64,128]{3,2,1,0:T(8,128)(2,1)}, u32[]{:S(2)}, u32[]{:S(2)}) %collective-permute-start.11) | collective-permute-done | bytes 262176 | tf_op jit(solution)/shard_map/ppermute | solution.py:20
  110.2 1.6 collective-permute-start.12
  111.8 8.0 %bitcast_add_fusion = f32[4,256,1,16,64]{1,4,3,0,2:T(8,128)S(1)} fusion(f32[4,256,1,16,64]{1,0,4,3,2:T(4,128)} %reshape.347, f32[4,16,256]{2,1,0:T(8,128)} %copy.49, f32[4,16,256]{2,1,0:T(8,128)S(1)} %copy-done.10, f32[4,256,256]{2,1,0:T(8,128)} %fusion.50, pred[256,256]{1,0:T(8,128)(4,1)} %iota_compare_fusion, f32[16]{0:T(128)} %param.17, ...), kind=kOutput, calls=%fused_computation.18 | convolution fusion | flops 559939584 | bytes 11731008 | tf_op jit(solution)/shard_map/cgjts,csgjp->ctgjp/dot_general | solution.py:74
  122.3 2.8 %copy.60 = f32[4,256,1,16,64]{1,0,4,3,2:T(4,128)S(1)} copy(f32[4,256,1,16,64]{1,4,3,0,2:T(8,128)S(1)} %fusion.12) | data formatting | bytes 8388608 | tf_op jit(solution)/shard_map/add | solution.py:121
  128.5 7.0 %convert_bitcast_fusion = bf16[2048,1024]{0,1:T(8,128)(2,1)} fusion(bf16[1024,2048]{1,0:T(8,128)(2,1)S(1)} %copy-done.15, f32[1024]{0:T(1024)S(1)} %copy-done.16, f32[1024]{0:T(1024)S(1)} %add_rsqrt_fusion, f32[1024,1024]{0,1:T(8,128)S(1)} %bitcast.82, bf16[1024,1024]{0,1:T(8,128)(2,1)S(1)} %copy-done.1), kind=kOutput, calls=%fused_computation.20 | convolution fusion | flops 4306501632 | bytes 14688256 | tf_op jit(solution)/shard_map/dot_general | solution.py:133
  135.5 57.8 %reduce-scatter.2.cloned.1.call-done = bf16[256,1024]{0,1:T(8,128)(2,1)} async-done(((bf16[2048,1024]{0,1:T(8,128)(2,1)}), bf16[256,1024]{0,1:T(8,128)(2,1)}) %reduce-scatter.2.cloned.1.call-update) | async-done | bytes 524304 | tf_op jit(solution)/shard_map/reduce_scatter | solution.py:132
  (96 shorter events, 31.2 us)
Async XLA Ops:
  6.5 16.9 %copy-start.4 = (bf16[1024,1024]{1,0:T(8,128)(2,1)S(1)}, bf16[1024,1024]{1,0:T(8,128)(2,1)}, u32[]{:S(2)}) copy-start(bf16[1024,1024]{1,0:T(8,128)(2,1)} %param.11) | copy-start | bytes 6291460
  6.5 186.7 %reduce-scatter.2.cloned.1.call-start = ((), (), s32[]{:S(2)}) async-start(), calls=%async_computation.1 | async-start | bytes 4718592 | tf_op jit(solution)/shard_map/reduce_scatter | solution.py:132
  8.3 18.6 %collective-permute-start = (bf16[3,1024]{0,1:T(8,128)(2,1)}, bf16[3,1024]{0,1:T(8,128)(2,1)}, u32[]{:S(2)}, u32[]{:S(2)}) collective-permute-start(bf16[3,1024]{0,1:T(8,128)(2,1)} %copy.38), channel_id=1, source_target_pairs={{0,8},{8,16},{16,24},{24,32},{32,40},{40,48},{48,56},{56,64},{64,7... | collective-permute-start | bytes 18440 | tf_op jit(solution)/shard_map/ppermute | solution.py:20
  11.3 14.8 %collective-permute-start.1 = (bf16[3,2,1,128]{3,0,2,1:T(4,128)(2,1)S(1)}, bf16[3,2,1,128]{3,0,2,1:T(4,128)(2,1)S(1)}, u32[]{:S(2)}, u32[]{:S(2)}) collective-permute-start(bf16[3,2,1,128]{3,0,2,1:T(4,128)(2,1)S(1)} %slice.133), channel_id=1, source_target_pairs={{0,8},{8,16},{16,24},{24,32},{32,40},{40,48},{48,56},{56,64},{64,7... | collective-permute-start | bytes 4616 | tf_op jit(solution)/shard_map/ppermute | solution.py:20
  21.1 0.6 copy-start.8
  26.1 1.6 copy-start
  41.7 11.8 %collective-permute-start.7 = (bf16[1,16,64,128]{3,2,1,0:T(8,128)(2,1)S(1)}, bf16[1,16,64,128]{3,2,1,0:T(8,128)(2,1)S(1)}, u32[]{:S(2)}, u32[]{:S(2)}) collective-permute-start(bf16[1,16,64,128]{3,2,1,0:T(8,128)(2,1)S(1)} %get-tuple-element.15), channel_id=1, source_target_pairs={{0,8},{8,16},{16,24},{24,32},{32,40},{40,48},{48,56},{56,64},{64,7... | collective-permute-start | bytes 786440 | tf_op jit(solution)/shard_map/ppermute | solution.py:20
  43.6 7.9 %collective-permute-start.2 = (f32[1,16]{1,0:T(1,128)S(1)}, f32[1,16]{1,0:T(1,128)S(1)}, u32[]{:S(2)}, u32[]{:S(2)}) collective-permute-start(f32[1,16]{1,0:T(1,128)S(1)} %bitcast.101), channel_id=1, source_target_pairs={{0,8},{8,16},{16,24},{24,32},{32,40},{40,48},{48,56},{56,64},{64,7... | collective-permute-start | bytes 200 | tf_op jit(solution)/shard_map/ppermute | solution.py:20
  51.5 7.0 %collective-permute-start.3 = (f32[1,16]{1,0:T(1,128)S(1)}, f32[1,16]{1,0:T(1,128)S(1)}, u32[]{:S(2)}, u32[]{:S(2)}) collective-permute-start(f32[1,16]{1,0:T(1,128)S(1)} %collective-permute-done.2), channel_id=1, source_target_pairs={{0,8},{8,16},{16,24},{24,32},{32,40},{40,48},{48,56},{56,64},{64,7... | collective-permute-start | bytes 200 | tf_op jit(solution)/shard_map/ppermute | solution.py:20
  53.4 9.8 %collective-permute-start.8 = (bf16[1,16,64,128]{3,2,1,0:T(8,128)(2,1)S(1)}, bf16[1,16,64,128]{3,2,1,0:T(8,128)(2,1)S(1)}, u32[]{:S(2)}, u32[]{:S(2)}) collective-permute-start(bf16[1,16,64,128]{3,2,1,0:T(8,128)(2,1)S(1)} %collective-permute-done.7), channel_id=1, source_target_pairs={{0,8},{8,16},{16,24},{24,32},{32,40},{40,48},{48,56},{56,64},{64,7... | collective-permute-start | bytes 786440 | tf_op jit(solution)/shard_map/ppermute | solution.py:20
  58.5 20.8 %copy-start.12 = (f32[1,16]{1,0:T(1,128)}, f32[1,16]{1,0:T(1,128)S(1)}, u32[]{:S(2)}) copy-start(f32[1,16]{1,0:T(1,128)S(1)} %get-tuple-element.14) | copy-start | bytes 196
  64.1 21.8 %collective-permute-start.9 = (bf16[1,16,64,128]{3,2,1,0:T(8,128)(2,1)}, bf16[1,16,64,128]{3,2,1,0:T(8,128)(2,1)S(1)}, u32[]{:S(2)}, u32[]{:S(2)}) collective-permute-start(bf16[1,16,64,128]{3,2,1,0:T(8,128)(2,1)} %fusion.29), channel_id=1, source_target_pairs={{0,16},{8,24},{16,32},{24,40},{32,48},{40,56},{48,64},{56,72},{64,... | collective-permute-start | bytes 786440 | tf_op jit(solution)/shard_map/ppermute | solution.py:20
  69.5 8.3 %copy-start.9 = (f32[4,16,256]{2,1,0:T(8,128)S(1)}, f32[4,16,256]{2,1,0:T(8,128)}, u32[]{:S(2)}) copy-start(f32[4,16,256]{2,1,0:T(8,128)} %reshape.342) | copy-start | bytes 196612
  75.9 7.5 %collective-permute-start.4 = (f32[1,16]{1,0:T(1,128)S(1)}, f32[1,16]{1,0:T(1,128)S(1)}, u32[]{:S(2)}, u32[]{:S(2)}) collective-permute-start(f32[1,16]{1,0:T(1,128)S(1)} %get-tuple-element.14), channel_id=1, source_target_pairs={{0,16},{8,24},{16,32},{24,40},{32,48},{40,56},{48,64},{56,72},{64,... | collective-permute-start | bytes 200 | tf_op jit(solution)/shard_map/ppermute | solution.py:20
  84.0 7.8 %collective-permute-start.5 = (f32[1,16]{1,0:T(1,128)S(1)}, f32[1,16]{1,0:T(1,128)S(1)}, u32[]{:S(2)}, u32[]{:S(2)}) collective-permute-start(f32[1,16]{1,0:T(1,128)S(1)} %get-tuple-element.12), channel_id=1, source_target_pairs={{0,32},{8,40},{16,48},{24,56},{32,64},{40,72},{48,80},{56,88},{64,... | collective-permute-start | bytes 200 | tf_op jit(solution)/shard_map/ppermute | solution.py:20
  86.2 12.2 %collective-permute-start.10 = (bf16[1,16,64,128]{3,2,1,0:T(8,128)(2,1)S(1)}, bf16[1,16,64,128]{3,2,1,0:T(8,128)(2,1)S(1)}, u32[]{:S(2)}, u32[]{:S(2)}) collective-permute-start(bf16[1,16,64,128]{3,2,1,0:T(8,128)(2,1)S(1)} %fusion.44), channel_id=1, source_target_pairs={{0,32},{8,40},{16,48},{24,56},{32,64},{40,72},{48,80},{56,88},{64,... | collective-permute-start | bytes 786440 | tf_op jit(solution)/shard_map/ppermute | solution.py:20
  92.5 5.4 %collective-permute-start.6 = (f32[1,16]{1,0:T(1,128)S(1)}, f32[1,16]{1,0:T(1,128)S(1)}, u32[]{:S(2)}, u32[]{:S(2)}) collective-permute-start(f32[1,16]{1,0:T(1,128)S(1)} %get-tuple-element.10), channel_id=1, source_target_pairs={{0,64},{8,72},{16,80},{24,88},{32,96},{40,104},{48,112},{56,120},{... | collective-permute-start | bytes 200 | tf_op jit(solution)/shard_map/ppermute | solution.py:20
  98.5 0.7 copy-start.2
  100.2 8.6 %collective-permute-start.11 = (bf16[1,16,64,128]{3,2,1,0:T(8,128)(2,1)}, bf16[1,16,64,128]{3,2,1,0:T(8,128)(2,1)}, u32[]{:S(2)}, u32[]{:S(2)}) collective-permute-start(bf16[1,16,64,128]{3,2,1,0:T(8,128)(2,1)} %fusion.30), channel_id=1, source_target_pairs={{0,64},{8,72},{16,80},{24,88},{32,96},{40,104},{48,112},{56,120},{... | collective-permute-start | bytes 786440 | tf_op jit(solution)/shard_map/ppermute | solution.py:20
  102.9 5.9 %copy-start.3 = (bf16[1,16,64,128]{3,2,1,0:T(8,128)(2,1)S(1)}, bf16[1,16,64,128]{3,2,1,0:T(8,128)(2,1)}, u32[]{:S(2)}) copy-start(bf16[1,16,64,128]{3,2,1,0:T(8,128)(2,1)} %copy-done.2) | copy-start | bytes 786436
  102.9 8.9 %copy-start.10 = (f32[4,16,256]{2,1,0:T(8,128)S(1)}, f32[4,16,256]{2,1,0:T(8,128)}, u32[]{:S(2)}) copy-start(f32[4,16,256]{2,1,0:T(8,128)} %reduce_window_sum.44) | copy-start | bytes 196612
  110.1 10.0 %copy-start.11 = (f32[16]{0:T(128)S(1)}, f32[16]{0:T(128)}, u32[]{:S(2)}) copy-start(f32[16]{0:T(128)} %get-tuple-element.9) | copy-start | bytes 196
  110.1 10.0 %copy-start.14 = (f32[16]{0:T(128)S(1)}, f32[16]{0:T(128)}, u32[]{:S(2)}) copy-start(f32[16]{0:T(128)} %exponential_bitcast_fusion.5) | copy-start | bytes 196
  110.1 11.3 %copy-start.5 = (f32[1,16,64,128]{3,2,1,0:T(8,128)S(1)}, f32[1,16,64,128]{3,2,1,0:T(8,128)}, u32[]{:S(2)}) copy-start(f32[1,16,64,128]{3,2,1,0:T(8,128)} %get-tuple-element.16) | copy-start | bytes 1572868
  110.2 11.3 %copy-start.6 = (f32[1,16,64,128]{3,2,1,0:T(8,128)S(1)}, f32[1,16,64,128]{3,2,1,0:T(8,128)}, u32[]{:S(2)}) copy-start(f32[1,16,64,128]{3,2,1,0:T(8,128)} %get-tuple-element.17) | copy-start | bytes 1572868
  110.2 11.3 %copy-start.7 = (f32[1,16,64,128]{3,2,1,0:T(8,128)S(1)}, f32[1,16,64,128]{3,2,1,0:T(8,128)}, u32[]{:S(2)}) copy-start(f32[1,16,64,128]{3,2,1,0:T(8,128)} %get-tuple-element.18) | copy-start | bytes 1572868
  110.2 11.3 %copy-start.13 = (f32[4]{0:T(128)S(1)}, f32[4]{0:T(128)}, u32[]{:S(2)}) copy-start(f32[4]{0:T(128)} %pad.clone) | copy-start | bytes 52
  110.2 9.9 %collective-permute-start.12 = (bf16[1,16,64,128]{3,2,1,0:T(8,128)(2,1)S(1)}, bf16[1,16,64,128]{3,2,1,0:T(8,128)(2,1)S(1)}, u32[]{:S(2)}, u32[]{:S(2)}) collective-permute-start(bf16[1,16,64,128]{3,2,1,0:T(8,128)(2,1)S(1)} %fusion.42), channel_id=1, source_target_pairs={{0,128},{8,136},{16,144},{24,152},{32,160},{40,168},{48,176},{56,1... | collective-permute-start | bytes 786440 | tf_op jit(solution)/shard_map/ppermute | solution.py:20
  125.1 1.6 copy-start.1
  126.1 2.3 %copy-start.15 = (bf16[1024,2048]{1,0:T(8,128)(2,1)S(1)}, bf16[1024,2048]{1,0:T(8,128)(2,1)}, u32[]{:S(2)}) copy-start(bf16[1024,2048]{1,0:T(8,128)(2,1)} %param.21) | copy-start | bytes 12582916
  126.1 2.3 %copy-start.16 = (f32[1024]{0:T(1024)S(1)}, f32[1024]{0:T(1024)}, u32[]{:S(2)}) copy-start(f32[1024]{0:T(1024)} %param.20) | copy-start | bytes 12292
Sparse Core Ops, SparseCore 0:
  135.6 57.6 reduce-scatter.1

commit v5 on v4

--- a/solution.py
+++ b/solution.py
@@ -1,6 +1,10 @@
+import functools
+
 import jax
 import jax.numpy as jnp
 from jax import lax
+from jax.experimental import pallas as pl
+from jax.experimental.pallas import tpu as pltpu
 from jax.sharding import PartitionSpec as P
 
 HEADS = 128
@@ -25,6 +29,116 @@
     for offset in range(kernel.shape[0]):
         acc = acc + kernel[offset] * padded[offset : offset + length].astype(jnp.float32)
     return jax.nn.silu(acc).astype(jnp.bfloat16)
+
+
+MESH = pl.DeviceIdType.MESH
+
+
+def scan_distances(count):
+    distances = []
+    distance = 1
+    while distance < count:
+        distances.append(distance)
+        distance *= 2
+    return distances
+
+
+def state_scan_kernel(count, state_ref, decay_ref, out_ref, cur_d, send_s, send_d, recv_s, recv_d, ssem, rsem):
+    me = lax.axis_index("seq")
+    chan = lax.axis_index("chan")
+    distances = scan_distances(count)
+    rounds = [1] + distances
+    barrier = pltpu.get_barrier_semaphore()
+    peers = jnp.int32(0)
+    for distance in distances:
+        for target in (me + distance, me - distance):
+            valid = jnp.logical_and(target >= 0, target < count)
+
+            @pl.when(valid)
+            def _():
+                pl.semaphore_signal(barrier, 1, device_id=(target, chan), device_id_type=MESH)
+
+            peers = peers + valid.astype(jnp.int32)
+    pl.semaphore_wait(barrier, peers)
+
+    outgoing = []
+    for index, distance in enumerate(rounds):
+        if index == 0:
+            send_s[index] = state_ref[...].astype(jnp.bfloat16)
+            send_d[index] = decay_ref[...]
+        else:
+            send_s[index] = out_ref[...].astype(jnp.bfloat16)
+            send_d[index] = cur_d[...]
+        pair = []
+        for part, (src, dst) in enumerate(((send_s, recv_s), (send_d, recv_d))):
+            pair.append(
+                lambda target, src=src, dst=dst, part=part, index=index: pltpu.make_async_remote_copy(
+                    src_ref=src.at[index],
+                    dst_ref=dst.at[index],
+                    send_sem=ssem.at[index, part],
+                    recv_sem=rsem.at[index, part],
+                    device_id=(target, chan),
+                    device_id_type=MESH,
+                )
+            )
+        sends = me + distance < count
+        receives = me - distance >= 0
+
+        @pl.when(sends)
+        def _():
+            for make in pair:
+                make(me + distance).start()
+
+        outgoing.append((sends, pair, distance))
+
+        @pl.when(receives)
+        def _():
+            for make in pair:
+                make(me - distance).wait_recv()
+            if index == 0:
+                out_ref[...] = recv_s[index].astype(jnp.float32)
+                cur_d[...] = recv_d[index]
+            else:
+                scale = jnp.exp(cur_d[:, 0:1, :])
+                out_ref[...] = scale * recv_s[index].astype(jnp.float32) + out_ref[...]
+                cur_d[...] = recv_d[index] + cur_d[...]
+
+        if index == 0:
+
+            @pl.when(jnp.logical_not(receives))
+            def _():
+                out_ref[...] = jnp.zeros_like(out_ref)
+                cur_d[...] = jnp.zeros_like(cur_d)
+
+    for sends, pair, distance in outgoing:
+
+        @pl.when(sends)
+        def _():
+            for make in pair:
+                make(me + distance).wait_send()
+
+
+def state_scan(state, decay):
+    count = lax.axis_size("seq")
+    rounds = 1 + len(scan_distances(count))
+    heads, rows, width = state.shape
+    return pl.pallas_call(
+        functools.partial(state_scan_kernel, count),
+        out_shape=jax.ShapeDtypeStruct(state.shape, jnp.float32),
+        in_specs=[pl.BlockSpec(memory_space=pltpu.VMEM)] * 2,
+        out_specs=pl.BlockSpec(memory_space=pltpu.VMEM),
+        scratch_shapes=[
+            pltpu.VMEM(decay.shape, jnp.float32),
+            pltpu.VMEM((rounds,) + state.shape, jnp.bfloat16),
+            pltpu.VMEM((rounds,) + decay.shape, jnp.float32),
+            pltpu.VMEM((rounds,) + state.shape, jnp.bfloat16),
+            pltpu.VMEM((rounds,) + decay.shape, jnp.float32),
+            pltpu.SemaphoreType.DMA((rounds, 2)),
+            pltpu.SemaphoreType.DMA((rounds, 2)),
+        ],
+        compiler_params=pltpu.CompilerParams(collective_id=0, has_side_effects=True),
+        name="state_scan",
+    )(state, decay)
 
 
 def local(
@@ -87,20 +201,11 @@
             jnp.exp(block_decay[block_index])[..., None, None] * running + block_states[block_index]
         )
     slab_decay = jnp.sum(block_decay, axis=0)
-    seq_count = lax.axis_size("seq")
-    carried_decay = passed_along(slab_decay, "seq", 1)
-    carried_state = passed_along(running.astype(jnp.bfloat16), "seq", 1).astype(jnp.float32)
-    distance = 1
-    while distance < seq_count:
-        earlier_decay = passed_along(carried_decay, "seq", distance)
-        earlier_state = passed_along(carried_state.astype(jnp.bfloat16), "seq", distance)
-        carried_state = (
-            jnp.exp(carried_decay)[..., None, None] * earlier_state.astype(jnp.float32)
-            + carried_state
-        )
-        carried_decay = earlier_decay + carried_decay
-        distance *= 2
-    entering = carried_state
+    state_shape = (groups * per_group, HEAD_DIM, STATE)
+    decay_tile = jnp.broadcast_to(
+        slab_decay.reshape(groups * per_group, 1, 1), (groups * per_group, 8, STATE)
+    )
+    entering = state_scan(running.reshape(state_shape), decay_tile).reshape(running.shape)
     leading = jnp.cumsum(block_decay, axis=0) - block_decay
     state_in = (
         jnp.exp(leading)[..., None, None] * entering[None] + jnp.stack(local_in, axis=0)

time: 202 us -> 188 us (0.931)
  Pallas kernels: 0 us -> 43.9 us
  waiting for transfers between devices: 84.3 us -> 59 us
  starting transfers between devices: 26.5 us -> 5.41 us
  other arithmetic: 22.9 us -> 16.4 us
  local copies, waits for them, and re-layouts: 30.8 us -> 25.6 us
    pallas_call x0 -> x1, Pallas kernels: none -> 43.9 us  [state_scan(): pl.pallas_call(functools.partial(state_scan_kernel, count), out_shape=jax...]
    ppermute x13 -> x2, waiting for transfers between devices: 26.5 us -> 0.01 us  [passed_along(): return lax.ppermute(x, axis, pairs)]
    ppermute x13 -> x2, starting transfers between devices: 26.5 us -> 5.41 us  [passed_along(): return lax.ppermute(x, axis, pairs)]
    convert_element_type x5 -> x0, other arithmetic: 4.81 us -> none  [the longest x4 3.51 us: local(): carried_state.astype(jnp.bfloat16)]
    another operation x9, local copies, waits for them, and re-layouts: 6.84 us -> 3.27 us
    mul x5 -> x0, other arithmetic: 3.11 us -> none  [the longest x4 1.81 us: local(): jnp.exp(carried_decay)[..., None, None] * earlier_state.astype(jnp.float32)]
    dot_general x1, matrix products: 0.81 us -> 3.13 us  [local(): jnp.einsum('ctgn,cgjpn->ctgjp', c_blocks[part], state_in[part], preferred...]
    unnamed x38 -> x36, local copies, waits for them, and re-layouts: 11.8 us -> 9.65 us
  transfers between devices with their start and end apart: 14 -> 3, of which waited for: 9 -> 1; matrix products, arithmetic and copies ran while one was open for 20% -> 11% of each run, Pallas kernels for 0% -> 0%
where the time goes in v5:
time: 188 us; the launch traced here: 187 us
  waiting for transfers between devices  59 us (31%)
  Pallas kernels  43.9 us (23%)
  local copies, waits for them, and re-layouts  25.6 us (14%)
  matrix products  22.6 us (12%)
  other arithmetic  16.4 us (9%)
  between operations  13.7 us (7%)
  starting transfers between devices  5.41 us (3%)
    reduce_scatter x1, waiting for transfers between devices, local(): lax.psum_scatter(lax.dot_general(out_weight, normed, (((0,), (1,)), ((),...  59 us
    pallas_call x1, Pallas kernels, state_scan(): pl.pallas_call(functools.partial(state_scan_kernel, count), out_shape=jax...  43.9 us
    unnamed x36, local copies, waits for them, and re-layouts  9.65 us
    dot_general x1, matrix products, local(): jnp.einsum('cgjts,csgjp->ctgjp', mixing, x_blocks, preferred_element_type...  8.92 us
    dot_general x1, matrix products, local(): lax.dot_general(out_weight, normed, (((0,), (1,)), ((), ())), preferred_e...  6.94 us
    convert_element_type x2, other arithmetic, conv_silu(): return jax.nn.silu(acc).astype(jnp.bfloat16)  5.9 us
    ppermute x2, starting transfers between devices, passed_along(): return lax.ppermute(x, axis, pairs)  5.41 us
  transfers between devices with their start and end apart: 3, of which 1 were waited for; matrix products, arithmetic and copies ran while one was open for 11% of the time, Pallas kernels for 0%

profile of v5, /device:TPU:24, one launch (start us, length us, event | category | flops | bytes accessed | tf_op | source)
XLA Modules:
  0.0 186.6 jit_solution(3505827021793439657)
XLA Ops:
  6.5 0.9 slice.101
  7.4 0.9 copy.38
  8.3 1.9 %collective-permute-start = (bf16[3,1024]{0,1:T(8,128)(2,1)}, bf16[3,1024]{0,1:T(8,128)(2,1)}, u32[]{:S(2)}, u32[]{:S(2)}) collective-permute-start(bf16[3,1024]{0,1:T(8,128)(2,1)} %copy.38), channel_id=1, source_target_pairs={{0,8},{8,16},{16,24},{24,32},{32,40},{40,48},{48,56},{56,64},{64,7... | collective-permute-start | bytes 18440 | tf_op jit(solution)/shard_map/ppermute | solution.py:24
  10.2 1.1 copy.41
  11.3 3.5 %collective-permute-start.1 = (bf16[3,2,1,128]{3,0,2,1:T(4,128)(2,1)S(1)}, bf16[3,2,1,128]{3,0,2,1:T(4,128)(2,1)S(1)}, u32[]{:S(2)}, u32[]{:S(2)}) collective-permute-start(bf16[3,2,1,128]{3,0,2,1:T(4,128)(2,1)S(1)} %slice.133), channel_id=1, source_target_pairs={{0,8},{8,16},{16,24},{24,32},{32,40},{40,48},{48,56},{56,64},{64,7... | collective-permute-start | bytes 4616 | tf_op jit(solution)/shard_map/ppermute | solution.py:24
  14.9 0.7 exponential_negate_fusion
  15.5 1.0 broadcast_multiply_fusion
  16.6 2.3 %reduce-window.6 = f32[4,16,1,2,128]{4,1,2,3,0:T(8,128)S(1)} reduce-window(f32[4,16,1,2,128]{4,1,2,3,0:T(8,128)S(1)} %copy.45, f32[]{:T(128)} %constant.13.clone.1), window={size=1x1x1x1x128 pad=0_0x0_0x0_0x0_0x127_0}, to_apply=%region_0.1 | reduce-window | flops 2080768 | bytes 131076 | tf_op jit(solution)/shard_map/reduce-window
  19.6 0.8 slice_reduce_fusion
  20.4 1.1 fusion.32
  21.7 0.9 fusion.44
  22.6 0.7 fusion.45
  24.0 0.6 iota_compare_fusion
  24.6 2.6 %copy.39 = bf16[1024,1024]{0,1:T(8,128)(2,1)} copy(bf16[1024,1024]{1,0:T(8,128)(2,1)S(1)} %copy-done.2) | data formatting | bytes 4194304 | tf_op args[0]
  28.0 0.6 copy.58
  28.6 3.9 %copy.61 = bf16[1024,1024]{0,1:T(8,128)(2,1)} copy(bf16[1024,1024]{1,0:T(8,128)(2,1)} %param.13) | data formatting | bytes 4194304 | tf_op args[2]
  33.2 0.7 multiply_convert_fusion.9
  34.2 0.8 convert_element_type.97
  35.0 5.2 %multiply_convert_fusion.5 = bf16[1024,1024]{0,1:T(8,128)(2,1)S(1)} fusion(bf16[1024,1024]{0,1:T(8,128)(2,1)S(1)} %copy-done, bf16[3,1024]{0,1:T(8,128)(2,1)} %collective-permute-done, f32[1024]{0:T(1024)S(1)} %bitcast.84, f32[1024]{0:T(1024)S(1)} %bitcast.85, f32[1024]{0:T(1024)S(1)} %bitcast.83, f32[1024]{0:T(1024)S(1)} %bitcast.82), kind=kLoop, calls=%fused_computation.25 | loop fusion | flops 26214400 | bytes 4216832 | tf_op jit(solution)/shard_map/convert_element_type | solution.py:31
  40.3 3.4 %reshape.338 = f32[4,256,1,16,64]{1,0,4,3,2:T(4,128)} reshape(bf16[1024,1024]{0,1:T(8,128)(2,1)S(1)} %multiply_convert_fusion.5) | data formatting | bytes 6291456 | tf_op jit(solution)/shard_map/convert_element_type | solution.py:215
  43.7 2.8 %reshape.324 = bf16[4,256,16,64]{1,0,3,2:T(4,128)(2,1)} reshape(bf16[1024,1024]{0,1:T(8,128)(2,1)S(1)} %multiply_convert_fusion.5) | data formatting | bytes 4194304 | tf_op jit(solution)/shard_map/reshape.26
  46.5 8.9 %bitcast_add_fusion = f32[4,256,1,16,64]{1,4,3,0,2:T(8,128)} fusion(f32[4,256,1,16,64]{1,0,4,3,2:T(4,128)} %reshape.338, f32[4,16,256]{2,1,0:T(8,128)} %copy.49, f32[4,16,256]{2,1,0:T(8,128)S(1)} %reduce_window_sum.44, f32[4,256,256]{2,1,0:T(8,128)S(1)} %fusion.46, pred[256,256]{1,0:T(8,128)(4,1)} %iota_compare_fusion, f32[16]{0:T(128)S(1)} %copy-done.15, ...), kind=kOutput, calls=%fused_computation.18 | convolution fusion | flops 559939584 | bytes 11731008 | tf_op jit(solution)/shard_map/cgjts,csgjp->ctgjp/dot_general | solution.py:188
  55.5 3.3 %fusion.11 = f32[4,16,64,128]{3,2,1,0:T(8,128)S(1)} fusion(f32[4,256,128]{2,1,0:T(8,128)S(1)} %copy-done.4, f32[4,256,16]{1,2,0:T(8,128)S(1)} %copy-done.5, bf16[4,256,16,64]{1,0,3,2:T(4,128)(2,1)S(1)} %copy-done.3), kind=kOutput, calls=%fused_computation.15 | convolution fusion | flops 272629760 | bytes 4784128 | tf_op jit(solution)/shard_map/csgjp,csgjn->cgjpn/dot_general | solution.py:192
  58.8 1.1 fusion.28
  59.9 0.7 broadcast_in_dim.15.decay_ref
  60.6 43.9 %state_scan.1 = f32[16,64,128]{2,1,0:T(8,128)} custom-call(f32[16,64,128]{2,1,0:T(8,128)} %get-tuple-element.9.state_ref, f32[16,8,128]{2,1,0:T(8,128)} %broadcast_in_dim.15.decay_ref), custom_call_target="tpu_custom_call" | custom-call | tf_op jit(solution)/shard_map/state_scan/pallas_call | solution.py:125
  104.6 3.1 %fusion.12 = f32[4,256,1,16,64]{1,4,3,0,2:T(8,128)S(1)} fusion(f32[4,256,1,16,64]{1,4,3,0,2:T(8,128)} %bitcast_add_fusion, bf16[4,256,128,1]{2,1,3,0:T(8,128)(2,1)S(1)} %bitcast.74, f32[4,256,16]{1,2,0:T(8,128)S(1)} %copy.55, f32[1,16,64,128]{3,2,1,0:T(8,128)S(1)} %get-tuple-element.10, f32[1,16,64,128]{3,2,1,0:T(8,128)S(1)} %get-tuple-element.11, ...), kind=kOutput, calls=%fused_computation.17 | convolution fusion | flops 273678336 | bytes 10813712 | tf_op jit(solution)/shard_map/ctgn,cgjpn->ctgjp/dot_general | solution.py:223
  107.7 2.8 %copy.60 = f32[4,256,1,16,64]{1,0,4,3,2:T(4,128)S(1)} copy(f32[4,256,1,16,64]{1,4,3,0,2:T(8,128)S(1)} %fusion.12) | data formatting | bytes 8388608 | tf_op jit(solution)/shard_map/add | solution.py:226
  110.5 1.0 copy.64
  112.1 1.3 multiply_reduce_fusion
  113.9 6.9 %convert_bitcast_fusion = bf16[2048,1024]{0,1:T(8,128)(2,1)} fusion(bf16[1024,2048]{1,0:T(8,128)(2,1)S(1)} %copy-done.13, f32[1024]{0:T(1024)S(1)} %copy-done.14, f32[1024]{0:T(1024)S(1)} %add_rsqrt_fusion, f32[1024,1024]{0,1:T(8,128)S(1)} %bitcast.71, bf16[1024,1024]{0,1:T(8,128)(2,1)S(1)} %copy-done.1), kind=kOutput, calls=%fused_computation.20 | convolution fusion | flops 4306501632 | bytes 14688256 | tf_op jit(solution)/shard_map/dot_general | solution.py:238
  120.8 59.0 %reduce-scatter.2.cloned.1.call-done = bf16[256,1024]{0,1:T(8,128)(2,1)} async-done(((bf16[2048,1024]{0,1:T(8,128)(2,1)}), bf16[256,1024]{0,1:T(8,128)(2,1)}) %reduce-scatter.2.cloned.1.call-update) | async-done | bytes 524304 | tf_op jit(solution)/shard_map/reduce_scatter | solution.py:237
  (65 shorter events, 4.4 us)
Async XLA Ops:
  6.5 18.1 %copy-start.2 = (bf16[1024,1024]{1,0:T(8,128)(2,1)S(1)}, bf16[1024,1024]{1,0:T(8,128)(2,1)}, u32[]{:S(2)}) copy-start(bf16[1024,1024]{1,0:T(8,128)(2,1)} %param.11) | copy-start | bytes 6291460
  6.5 173.3 %reduce-scatter.2.cloned.1.call-start = ((), (), s32[]{:S(2)}) async-start(), calls=%async_computation.1 | async-start | bytes 4718592 | tf_op jit(solution)/shard_map/reduce_scatter | solution.py:237
  8.3 26.7 %collective-permute-start = (bf16[3,1024]{0,1:T(8,128)(2,1)}, bf16[3,1024]{0,1:T(8,128)(2,1)}, u32[]{:S(2)}, u32[]{:S(2)}) collective-permute-start(bf16[3,1024]{0,1:T(8,128)(2,1)} %copy.38), channel_id=1, source_target_pairs={{0,8},{8,16},{16,24},{24,32},{32,40},{40,48},{48,56},{56,64},{64,7... | collective-permute-start | bytes 18440 | tf_op jit(solution)/shard_map/ppermute | solution.py:24
  11.3 21.8 %collective-permute-start.1 = (bf16[3,2,1,128]{3,0,2,1:T(4,128)(2,1)S(1)}, bf16[3,2,1,128]{3,0,2,1:T(4,128)(2,1)S(1)}, u32[]{:S(2)}, u32[]{:S(2)}) collective-permute-start(bf16[3,2,1,128]{3,0,2,1:T(4,128)(2,1)S(1)} %slice.133), channel_id=1, source_target_pairs={{0,8},{8,16},{16,24},{24,32},{32,40},{40,48},{48,56},{56,64},{64,7... | collective-permute-start | bytes 4616 | tf_op jit(solution)/shard_map/ppermute | solution.py:24
  32.6 2.5 %copy-start = (bf16[1024,1024]{0,1:T(8,128)(2,1)S(1)}, bf16[1024,1024]{0,1:T(8,128)(2,1)}, u32[]{:S(2)}) copy-start(bf16[1024,1024]{0,1:T(8,128)(2,1)} %copy.39) | copy-start | bytes 6291460
  40.3 6.2 %copy-start.15 = (f32[16]{0:T(128)S(1)}, f32[16]{0:T(128)}, u32[]{:S(2)}) copy-start(f32[16]{0:T(128)} %param.17) | copy-start | bytes 196
  46.5 8.9 %copy-start.3 = (bf16[4,256,16,64]{1,0,3,2:T(4,128)(2,1)S(1)}, bf16[4,256,16,64]{1,0,3,2:T(4,128)(2,1)}, u32[]{:S(2)}) copy-start(bf16[4,256,16,64]{1,0,3,2:T(4,128)(2,1)} %reshape.324) | copy-start | bytes 6291460
  46.5 8.9 %copy-start.4 = (f32[4,256,128]{2,1,0:T(8,128)S(1)}, f32[4,256,128]{2,1,0:T(8,128)}, u32[]{:S(2)}) copy-start(f32[4,256,128]{2,1,0:T(8,128)} %convert_element_type.97) | copy-start | bytes 1572868
  46.5 8.9 %copy-start.5 = (f32[4,256,16]{1,2,0:T(8,128)S(1)}, f32[4,256,16]{1,2,0:T(8,128)}, u32[]{:S(2)}) copy-start(f32[4,256,16]{1,2,0:T(8,128)} %copy.58) | copy-start | bytes 196612
  55.4 3.4 %copy-start.8 = (f32[16]{0:T(128)S(1)}, f32[16]{0:T(128)}, u32[]{:S(2)}) copy-start(f32[16]{0:T(128)} %get-tuple-element.5) | copy-start | bytes 196
  55.4 3.4 %copy-start.9 = (f32[16]{0:T(128)S(1)}, f32[16]{0:T(128)}, u32[]{:S(2)}) copy-start(f32[16]{0:T(128)} %get-tuple-element.6) | copy-start | bytes 196
  55.4 3.4 %copy-start.10 = (f32[16]{0:T(128)S(1)}, f32[16]{0:T(128)}, u32[]{:S(2)}) copy-start(f32[16]{0:T(128)} %get-tuple-element.7) | copy-start | bytes 196
  55.4 3.4 %copy-start.11 = (f32[16]{0:T(128)S(1)}, f32[16]{0:T(128)}, u32[]{:S(2)}) copy-start(f32[16]{0:T(128)} %get-tuple-element.8) | copy-start | bytes 196
  58.8 1.1 copy-start.7
  58.8 45.8 %copy-start.6 = (f32[4,16]{1,0:T(4,128)S(1)}, f32[4,16]{1,0:T(4,128)}, u32[]{:S(2)}) copy-start(f32[4,16]{1,0:T(4,128)} %subtract_exponential_fusion) | copy-start | bytes 772
  58.8 45.8 %copy-start.12 = (f32[4]{0:T(128)S(1)}, f32[4]{0:T(128)}, u32[]{:S(2)}) copy-start(f32[4]{0:T(128)} %pad.clone) | copy-start | bytes 52
  110.5 1.6 copy-start.1
  111.5 2.3 %copy-start.13 = (bf16[1024,2048]{1,0:T(8,128)(2,1)S(1)}, bf16[1024,2048]{1,0:T(8,128)(2,1)}, u32[]{:S(2)}) copy-start(bf16[1024,2048]{1,0:T(8,128)(2,1)} %param.21) | copy-start | bytes 12582916
  111.6 2.3 %copy-start.14 = (f32[1024]{0:T(1024)S(1)}, f32[1024]{0:T(1024)}, u32[]{:S(2)}) copy-start(f32[1024]{0:T(1024)} %param.20) | copy-start | bytes 12292
Sparse Core Ops, SparseCore 0:
  121.0 58.7 reduce-scatter.1

commit v6 on v5

--- a/solution.py
+++ b/solution.py
@@ -47,7 +47,6 @@
     me = lax.axis_index("seq")
     chan = lax.axis_index("chan")
     distances = scan_distances(count)
-    rounds = [1] + distances
     barrier = pltpu.get_barrier_semaphore()
     peers = jnp.int32(0)
     for distance in distances:
@@ -61,56 +60,65 @@
             peers = peers + valid.astype(jnp.int32)
     pl.semaphore_wait(barrier, peers)
 
+    rounds = [[1, 2]] + [[distance] for distance in distances[1:]]
     outgoing = []
-    for index, distance in enumerate(rounds):
+    slot = 0
+    for index, round_distances in enumerate(rounds):
         if index == 0:
             send_s[index] = state_ref[...].astype(jnp.bfloat16)
             send_d[index] = decay_ref[...]
         else:
             send_s[index] = out_ref[...].astype(jnp.bfloat16)
             send_d[index] = cur_d[...]
-        pair = []
-        for part, (src, dst) in enumerate(((send_s, recv_s), (send_d, recv_d))):
-            pair.append(
-                lambda target, src=src, dst=dst, part=part, index=index: pltpu.make_async_remote_copy(
-                    src_ref=src.at[index],
-                    dst_ref=dst.at[index],
-                    send_sem=ssem.at[index, part],
-                    recv_sem=rsem.at[index, part],
-                    device_id=(target, chan),
-                    device_id_type=MESH,
+        for distance in round_distances:
+            pair = []
+            for part, (src, dst) in enumerate(((send_s, recv_s), (send_d, recv_d))):
+                pair.append(
+                    lambda target, src=src, dst=dst, part=part, index=index, slot=slot: (
+                        pltpu.make_async_remote_copy(
+                            src_ref=src.at[index],
+                            dst_ref=dst.at[slot],
+                            send_sem=ssem.at[slot, part],
+                            recv_sem=rsem.at[slot, part],
+                            device_id=(target, chan),
+                            device_id_type=MESH,
+                        )
+                    )
                 )
-            )
-        sends = me + distance < count
-        receives = me - distance >= 0
-
-        @pl.when(sends)
-        def _():
-            for make in pair:
-                make(me + distance).start()
-
-        outgoing.append((sends, pair, distance))
-
-        @pl.when(receives)
-        def _():
-            for make in pair:
-                make(me - distance).wait_recv()
-            if index == 0:
-                out_ref[...] = recv_s[index].astype(jnp.float32)
-                cur_d[...] = recv_d[index]
-            else:
-                scale = jnp.exp(cur_d[:, 0:1, :])
-                out_ref[...] = scale * recv_s[index].astype(jnp.float32) + out_ref[...]
-                cur_d[...] = recv_d[index] + cur_d[...]
-
-        if index == 0:
-
-            @pl.when(jnp.logical_not(receives))
+            sends = me + distance < count
+
+            @pl.when(sends)
             def _():
-                out_ref[...] = jnp.zeros_like(out_ref)
-                cur_d[...] = jnp.zeros_like(cur_d)
-
-    for sends, pair, distance in outgoing:
+                for make in pair:
+                    make(me + distance).start()
+
+            outgoing.append((sends, pair, distance, slot))
+            slot += 1
+
+        for sends, pair, distance, at in outgoing[-len(round_distances):]:
+            receives = me - distance >= 0
+            first = index == 0 and distance == 1
+
+            @pl.when(receives)
+            def _():
+                for make in pair:
+                    make(me - distance).wait_recv()
+                if first:
+                    out_ref[...] = recv_s[at].astype(jnp.float32)
+                    cur_d[...] = recv_d[at]
+                else:
+                    scale = jnp.exp(cur_d[:, 0:1, :])
+                    out_ref[...] = scale * recv_s[at].astype(jnp.float32) + out_ref[...]
+                    cur_d[...] = recv_d[at] + cur_d[...]
+
+            if first:
+
+                @pl.when(jnp.logical_not(receives))
+                def _():
+                    out_ref[...] = jnp.zeros_like(out_ref)
+                    cur_d[...] = jnp.zeros_like(cur_d)
+
+    for sends, pair, distance, at in outgoing:
 
         @pl.when(sends)
         def _():
@@ -120,8 +128,8 @@
 
 def state_scan(state, decay):
     count = lax.axis_size("seq")
-    rounds = 1 + len(scan_distances(count))
-    heads, rows, width = state.shape
+    rounds = len(scan_distances(count))
+    slots = rounds + 1
     return pl.pallas_call(
         functools.partial(state_scan_kernel, count),
         out_shape=jax.ShapeDtypeStruct(state.shape, jnp.float32),
@@ -131,10 +139,10 @@
             pltpu.VMEM(decay.shape, jnp.float32),
             pltpu.VMEM((rounds,) + state.shape, jnp.bfloat16),
             pltpu.VMEM((rounds,) + decay.shape, jnp.float32),
-            pltpu.VMEM((rounds,) + state.shape, jnp.bfloat16),
-            pltpu.VMEM((rounds,) + decay.shape, jnp.float32),
-            pltpu.SemaphoreType.DMA((rounds, 2)),
-            pltpu.SemaphoreType.DMA((rounds, 2)),
+            pltpu.VMEM((slots,) + state.shape, jnp.bfloat16),
+            pltpu.VMEM((slots,) + decay.shape, jnp.float32),
+            pltpu.SemaphoreType.DMA((slots, 2)),
+            pltpu.SemaphoreType.DMA((slots, 2)),
         ],
         compiler_params=pltpu.CompilerParams(collective_id=0, has_side_effects=True),
         name="state_scan",

time: 188 us -> 191 us (1.016)
  waiting for transfers between devices: 59 us -> 64 us
  Pallas kernels: 43.9 us -> 41.8 us
    reduce_scatter x1, waiting for transfers between devices: 59 us -> 63.9 us  [local(): lax.psum_scatter(lax.dot_general(out_weight, normed, (((0,), (1,)), ((),...]
    pallas_call x1, Pallas kernels: 43.9 us -> 41.8 us  [state_scan(): pl.pallas_call(functools.partial(state_scan_kernel, count), out_shape=jax...]
where the time goes in v6:
time: 191 us; the launch traced here: 189 us
  waiting for transfers between devices  64 us (34%)
  Pallas kernels  41.8 us (22%)
  local copies, waits for them, and re-layouts  25.6 us (13%)
  matrix products  22.6 us (12%)
  other arithmetic  16.3 us (9%)
  between operations  13.7 us (7%)
  starting transfers between devices  5.41 us (3%)
    reduce_scatter x1, waiting for transfers between devices, local(): lax.psum_scatter(lax.dot_general(out_weight, normed, (((0,), (1,)), ((),...  63.9 us
    pallas_call x1, Pallas kernels, state_scan(): pl.pallas_call(functools.partial(state_scan_kernel, count), out_shape=jax...  41.8 us
    unnamed x36, local copies, waits for them, and re-layouts  9.65 us
    dot_general x1, matrix products, local(): jnp.einsum('cgjts,csgjp->ctgjp', mixing, x_blocks, preferred_element_type...  8.92 us
    dot_general x1, matrix products, local(): lax.dot_general(out_weight, normed, (((0,), (1,)), ((), ())), preferred_e...  6.94 us
    convert_element_type x2, other arithmetic, conv_silu(): return jax.nn.silu(acc).astype(jnp.bfloat16)  5.9 us
    ppermute x2, starting transfers between devices, passed_along(): return lax.ppermute(x, axis, pairs)  5.41 us
  transfers between devices with their start and end apart: 3, of which 1 were waited for; matrix products, arithmetic and copies ran while one was open for 11% of the time, Pallas kernels for 0%

profile of v6, /device:TPU:24, one launch (start us, length us, event | category | flops | bytes accessed | tf_op | source)
XLA Modules:
  0.0 189.5 jit_solution(12282186789637394478)
XLA Ops:
  6.5 0.9 slice.101
  7.4 0.9 copy.38
  8.3 1.9 %collective-permute-start = (bf16[3,1024]{0,1:T(8,128)(2,1)}, bf16[3,1024]{0,1:T(8,128)(2,1)}, u32[]{:S(2)}, u32[]{:S(2)}) collective-permute-start(bf16[3,1024]{0,1:T(8,128)(2,1)} %copy.38), channel_id=1, source_target_pairs={{0,8},{8,16},{16,24},{24,32},{32,40},{40,48},{48,56},{56,64},{64,7... | collective-permute-start | bytes 18440 | tf_op jit(solution)/shard_map/ppermute | solution.py:24
  10.2 1.1 copy.41
  11.3 3.5 %collective-permute-start.1 = (bf16[3,2,1,128]{3,0,2,1:T(4,128)(2,1)S(1)}, bf16[3,2,1,128]{3,0,2,1:T(4,128)(2,1)S(1)}, u32[]{:S(2)}, u32[]{:S(2)}) collective-permute-start(bf16[3,2,1,128]{3,0,2,1:T(4,128)(2,1)S(1)} %slice.133), channel_id=1, source_target_pairs={{0,8},{8,16},{16,24},{24,32},{32,40},{40,48},{48,56},{56,64},{64,7... | collective-permute-start | bytes 4616 | tf_op jit(solution)/shard_map/ppermute | solution.py:24
  14.9 0.7 exponential_negate_fusion
  15.5 1.0 broadcast_multiply_fusion
  16.6 2.3 %reduce-window.6 = f32[4,16,1,2,128]{4,1,2,3,0:T(8,128)S(1)} reduce-window(f32[4,16,1,2,128]{4,1,2,3,0:T(8,128)S(1)} %copy.45, f32[]{:T(128)} %constant.13.clone.1), window={size=1x1x1x1x128 pad=0_0x0_0x0_0x0_0x127_0}, to_apply=%region_0.1 | reduce-window | flops 2080768 | bytes 131076 | tf_op jit(solution)/shard_map/reduce-window
  19.6 0.8 slice_reduce_fusion
  20.4 1.1 fusion.32
  21.7 0.9 fusion.44
  22.6 0.7 fusion.45
  24.0 0.6 iota_compare_fusion
  24.6 2.6 %copy.39 = bf16[1024,1024]{0,1:T(8,128)(2,1)} copy(bf16[1024,1024]{1,0:T(8,128)(2,1)S(1)} %copy-done.2) | data formatting | bytes 4194304 | tf_op args[0]
  28.0 0.6 copy.58
  28.6 3.9 %copy.61 = bf16[1024,1024]{0,1:T(8,128)(2,1)} copy(bf16[1024,1024]{1,0:T(8,128)(2,1)} %param.13) | data formatting | bytes 4194304 | tf_op args[2]
  33.2 0.7 multiply_convert_fusion.9
  34.2 0.8 convert_element_type.97
  35.0 5.2 %multiply_convert_fusion.5 = bf16[1024,1024]{0,1:T(8,128)(2,1)S(1)} fusion(bf16[1024,1024]{0,1:T(8,128)(2,1)S(1)} %copy-done, bf16[3,1024]{0,1:T(8,128)(2,1)} %collective-permute-done, f32[1024]{0:T(1024)S(1)} %bitcast.84, f32[1024]{0:T(1024)S(1)} %bitcast.85, f32[1024]{0:T(1024)S(1)} %bitcast.83, f32[1024]{0:T(1024)S(1)} %bitcast.82), kind=kLoop, calls=%fused_computation.25 | loop fusion | flops 26214400 | bytes 4216832 | tf_op jit(solution)/shard_map/convert_element_type | solution.py:31
  40.3 3.4 %reshape.338 = f32[4,256,1,16,64]{1,0,4,3,2:T(4,128)} reshape(bf16[1024,1024]{0,1:T(8,128)(2,1)S(1)} %multiply_convert_fusion.5) | data formatting | bytes 6291456 | tf_op jit(solution)/shard_map/convert_element_type | solution.py:223
  43.7 2.8 %reshape.324 = bf16[4,256,16,64]{1,0,3,2:T(4,128)(2,1)} reshape(bf16[1024,1024]{0,1:T(8,128)(2,1)S(1)} %multiply_convert_fusion.5) | data formatting | bytes 4194304 | tf_op jit(solution)/shard_map/reshape.26
  46.5 8.9 %bitcast_add_fusion = f32[4,256,1,16,64]{1,4,3,0,2:T(8,128)} fusion(f32[4,256,1,16,64]{1,0,4,3,2:T(4,128)} %reshape.338, f32[4,16,256]{2,1,0:T(8,128)} %copy.49, f32[4,16,256]{2,1,0:T(8,128)S(1)} %reduce_window_sum.44, f32[4,256,256]{2,1,0:T(8,128)S(1)} %fusion.46, pred[256,256]{1,0:T(8,128)(4,1)} %iota_compare_fusion, f32[16]{0:T(128)S(1)} %copy-done.15, ...), kind=kOutput, calls=%fused_computation.18 | convolution fusion | flops 559939584 | bytes 11731008 | tf_op jit(solution)/shard_map/cgjts,csgjp->ctgjp/dot_general | solution.py:196
  55.5 3.3 %fusion.11 = f32[4,16,64,128]{3,2,1,0:T(8,128)S(1)} fusion(f32[4,256,128]{2,1,0:T(8,128)S(1)} %copy-done.4, f32[4,256,16]{1,2,0:T(8,128)S(1)} %copy-done.5, bf16[4,256,16,64]{1,0,3,2:T(4,128)(2,1)S(1)} %copy-done.3), kind=kOutput, calls=%fused_computation.15 | convolution fusion | flops 272629760 | bytes 4784128 | tf_op jit(solution)/shard_map/csgjp,csgjn->cgjpn/dot_general | solution.py:200
  58.8 1.1 fusion.28
  59.9 0.7 broadcast_in_dim.15.decay_ref
  60.6 41.8 %state_scan.1 = f32[16,64,128]{2,1,0:T(8,128)} custom-call(f32[16,64,128]{2,1,0:T(8,128)} %get-tuple-element.9.state_ref, f32[16,8,128]{2,1,0:T(8,128)} %broadcast_in_dim.15.decay_ref), custom_call_target="tpu_custom_call" | custom-call | tf_op jit(solution)/shard_map/state_scan/pallas_call | solution.py:133
  102.4 3.1 %fusion.12 = f32[4,256,1,16,64]{1,4,3,0,2:T(8,128)S(1)} fusion(f32[4,256,1,16,64]{1,4,3,0,2:T(8,128)} %bitcast_add_fusion, bf16[4,256,128,1]{2,1,3,0:T(8,128)(2,1)S(1)} %bitcast.74, f32[4,256,16]{1,2,0:T(8,128)S(1)} %copy.55, f32[1,16,64,128]{3,2,1,0:T(8,128)S(1)} %get-tuple-element.10, f32[1,16,64,128]{3,2,1,0:T(8,128)S(1)} %get-tuple-element.11, ...), kind=kOutput, calls=%fused_computation.17 | convolution fusion | flops 273678336 | bytes 10813712 | tf_op jit(solution)/shard_map/ctgn,cgjpn->ctgjp/dot_general | solution.py:231
  105.5 2.8 %copy.60 = f32[4,256,1,16,64]{1,0,4,3,2:T(4,128)S(1)} copy(f32[4,256,1,16,64]{1,4,3,0,2:T(8,128)S(1)} %fusion.12) | data formatting | bytes 8388608 | tf_op jit(solution)/shard_map/add | solution.py:234
  108.4 1.0 copy.64
  109.9 1.3 multiply_reduce_fusion
  111.7 6.9 %convert_bitcast_fusion = bf16[2048,1024]{0,1:T(8,128)(2,1)} fusion(bf16[1024,2048]{1,0:T(8,128)(2,1)S(1)} %copy-done.13, f32[1024]{0:T(1024)S(1)} %copy-done.14, f32[1024]{0:T(1024)S(1)} %add_rsqrt_fusion, f32[1024,1024]{0,1:T(8,128)S(1)} %bitcast.71, bf16[1024,1024]{0,1:T(8,128)(2,1)S(1)} %copy-done.1), kind=kOutput, calls=%fused_computation.20 | convolution fusion | flops 4306501632 | bytes 14688256 | tf_op jit(solution)/shard_map/dot_general | solution.py:246
  118.7 63.9 %reduce-scatter.2.cloned.1.call-done = bf16[256,1024]{0,1:T(8,128)(2,1)} async-done(((bf16[2048,1024]{0,1:T(8,128)(2,1)}), bf16[256,1024]{0,1:T(8,128)(2,1)}) %reduce-scatter.2.cloned.1.call-update) | async-done | bytes 524304 | tf_op jit(solution)/shard_map/reduce_scatter | solution.py:245
  (65 shorter events, 4.4 us)
Async XLA Ops:
  6.5 18.1 %copy-start.2 = (bf16[1024,1024]{1,0:T(8,128)(2,1)S(1)}, bf16[1024,1024]{1,0:T(8,128)(2,1)}, u32[]{:S(2)}) copy-start(bf16[1024,1024]{1,0:T(8,128)(2,1)} %param.11) | copy-start | bytes 6291460
  6.5 176.1 %reduce-scatter.2.cloned.1.call-start = ((), (), s32[]{:S(2)}) async-start(), calls=%async_computation.1 | async-start | bytes 4718592 | tf_op jit(solution)/shard_map/reduce_scatter | solution.py:245
  8.3 26.7 %collective-permute-start = (bf16[3,1024]{0,1:T(8,128)(2,1)}, bf16[3,1024]{0,1:T(8,128)(2,1)}, u32[]{:S(2)}, u32[]{:S(2)}) collective-permute-start(bf16[3,1024]{0,1:T(8,128)(2,1)} %copy.38), channel_id=1, source_target_pairs={{0,8},{8,16},{16,24},{24,32},{32,40},{40,48},{48,56},{56,64},{64,7... | collective-permute-start | bytes 18440 | tf_op jit(solution)/shard_map/ppermute | solution.py:24
  11.3 21.8 %collective-permute-start.1 = (bf16[3,2,1,128]{3,0,2,1:T(4,128)(2,1)S(1)}, bf16[3,2,1,128]{3,0,2,1:T(4,128)(2,1)S(1)}, u32[]{:S(2)}, u32[]{:S(2)}) collective-permute-start(bf16[3,2,1,128]{3,0,2,1:T(4,128)(2,1)S(1)} %slice.133), channel_id=1, source_target_pairs={{0,8},{8,16},{16,24},{24,32},{32,40},{40,48},{48,56},{56,64},{64,7... | collective-permute-start | bytes 4616 | tf_op jit(solution)/shard_map/ppermute | solution.py:24
  32.6 2.5 %copy-start = (bf16[1024,1024]{0,1:T(8,128)(2,1)S(1)}, bf16[1024,1024]{0,1:T(8,128)(2,1)}, u32[]{:S(2)}) copy-start(bf16[1024,1024]{0,1:T(8,128)(2,1)} %copy.39) | copy-start | bytes 6291460
  40.3 6.2 %copy-start.15 = (f32[16]{0:T(128)S(1)}, f32[16]{0:T(128)}, u32[]{:S(2)}) copy-start(f32[16]{0:T(128)} %param.17) | copy-start | bytes 196
  46.5 8.9 %copy-start.3 = (bf16[4,256,16,64]{1,0,3,2:T(4,128)(2,1)S(1)}, bf16[4,256,16,64]{1,0,3,2:T(4,128)(2,1)}, u32[]{:S(2)}) copy-start(bf16[4,256,16,64]{1,0,3,2:T(4,128)(2,1)} %reshape.324) | copy-start | bytes 6291460
  46.5 8.9 %copy-start.4 = (f32[4,256,128]{2,1,0:T(8,128)S(1)}, f32[4,256,128]{2,1,0:T(8,128)}, u32[]{:S(2)}) copy-start(f32[4,256,128]{2,1,0:T(8,128)} %convert_element_type.97) | copy-start | bytes 1572868
  46.5 8.9 %copy-start.5 = (f32[4,256,16]{1,2,0:T(8,128)S(1)}, f32[4,256,16]{1,2,0:T(8,128)}, u32[]{:S(2)}) copy-start(f32[4,256,16]{1,2,0:T(8,128)} %copy.58) | copy-start | bytes 196612
  55.4 3.4 %copy-start.8 = (f32[16]{0:T(128)S(1)}, f32[16]{0:T(128)}, u32[]{:S(2)}) copy-start(f32[16]{0:T(128)} %get-tuple-element.5) | copy-start | bytes 196
  55.4 3.4 %copy-start.9 = (f32[16]{0:T(128)S(1)}, f32[16]{0:T(128)}, u32[]{:S(2)}) copy-start(f32[16]{0:T(128)} %get-tuple-element.6) | copy-start | bytes 196
  55.4 3.4 %copy-start.10 = (f32[16]{0:T(128)S(1)}, f32[16]{0:T(128)}, u32[]{:S(2)}) copy-start(f32[16]{0:T(128)} %get-tuple-element.7) | copy-start | bytes 196
  55.4 3.4 %copy-start.11 = (f32[16]{0:T(128)S(1)}, f32[16]{0:T(128)}, u32[]{:S(2)}) copy-start(f32[16]{0:T(128)} %get-tuple-element.8) | copy-start | bytes 196
  58.8 1.1 copy-start.7
  58.8 43.6 %copy-start.6 = (f32[4,16]{1,0:T(4,128)S(1)}, f32[4,16]{1,0:T(4,128)}, u32[]{:S(2)}) copy-start(f32[4,16]{1,0:T(4,128)} %subtract_exponential_fusion) | copy-start | bytes 772
  58.8 43.6 %copy-start.12 = (f32[4]{0:T(128)S(1)}, f32[4]{0:T(128)}, u32[]{:S(2)}) copy-start(f32[4]{0:T(128)} %pad.clone) | copy-start | bytes 52
  108.3 1.6 copy-start.1
  109.4 2.3 %copy-start.13 = (bf16[1024,2048]{1,0:T(8,128)(2,1)S(1)}, bf16[1024,2048]{1,0:T(8,128)(2,1)}, u32[]{:S(2)}) copy-start(bf16[1024,2048]{1,0:T(8,128)(2,1)} %param.21) | copy-start | bytes 12582916
  109.4 2.3 %copy-start.14 = (f32[1024]{0:T(1024)S(1)}, f32[1024]{0:T(1024)}, u32[]{:S(2)}) copy-start(f32[1024]{0:T(1024)} %param.20) | copy-start | bytes 12292
Sparse Core Ops, SparseCore 0:
  118.8 63.7 reduce-scatter.1

commit v7 on v6

--- a/solution.py
+++ b/solution.py
@@ -43,111 +43,185 @@
     return distances
 
 
-def state_scan_kernel(count, state_ref, decay_ref, out_ref, cur_d, send_s, send_d, recv_s, recv_d, ssem, rsem):
+def scale_add(out, decay, incoming, base):
+    for head in range(out.shape[0]):
+        out[head] = jnp.exp(decay[head : head + 1, :]) * incoming[head] + base[head]
+
+
+def state_scan_kernel(
+    count, state_ref, decay_ref, out_ref,
+    own_s, own_d, pair_s, pair_d, cur_s, cur_d, send_s, send_d, recv_s, recv_d, back_s, ssem, rsem,
+):
     me = lax.axis_index("seq")
     chan = lax.axis_index("chan")
-    distances = scan_distances(count)
+    core = me % 2
+    chip = me // 2
+    chips = count // 2
+    half = state_ref.shape[0] // 2
+    partner = me + 1 - 2 * core
+    distances = scan_distances(chips)
+
     barrier = pltpu.get_barrier_semaphore()
-    peers = jnp.int32(0)
+    pl.semaphore_signal(barrier, 1, device_id=(partner, chan), device_id_type=MESH)
+    peers = jnp.int32(1)
     for distance in distances:
-        for target in (me + distance, me - distance):
-            valid = jnp.logical_and(target >= 0, target < count)
+        for target in (chip + distance, chip - distance):
+            valid = jnp.logical_and(target >= 0, target < chips)
 
             @pl.when(valid)
-            def _():
-                pl.semaphore_signal(barrier, 1, device_id=(target, chan), device_id_type=MESH)
+            def _(target=target):
+                pl.semaphore_signal(
+                    barrier, 1, device_id=(2 * target + core, chan), device_id_type=MESH
+                )
 
             peers = peers + valid.astype(jnp.int32)
     pl.semaphore_wait(barrier, peers)
+
+    def remote(src, dst, slot, part, target):
+        return pltpu.make_async_remote_copy(
+            src_ref=src, dst_ref=dst, send_sem=ssem.at[slot, part], recv_sem=rsem.at[slot, part],
+            device_id=(target, chan), device_id_type=MESH,
+        )
+
+    own_s[...] = state_ref[...].astype(jnp.bfloat16)
+    own_d[...] = decay_ref[...]
+    first = [
+        lambda t: remote(own_s, pair_s, 0, 0, t),
+        lambda t: remote(own_s.at[0:half], pair_s.at[0:half], 0, 0, t),
+    ]
+    first_d = lambda t: remote(own_d, pair_d, 0, 1, t)
+
+    @pl.when(core == 0)
+    def _():
+        first[0](partner).start()
+        first_d(partner).start()
+        first[1](partner).wait_recv()
+        first_d(partner).wait_recv()
+        cur_d[...] = own_d[0:half] + pair_d[0:half]
+        scale_add(cur_s, pair_d[0:half], state_ref.at[0:half], pair_s[0:half].astype(jnp.float32))
+
+    @pl.when(core == 1)
+    def _():
+        first[1](partner).start()
+        first_d(partner).start()
+        first[0](partner).wait_recv()
+        first_d(partner).wait_recv()
+        cur_d[...] = own_d[half:] + pair_d[half:]
+        scale_add(
+            cur_s, own_d[half:], pair_s[half:].astype(jnp.float32), state_ref.at[half:]
+        )
 
     rounds = [[1, 2]] + [[distance] for distance in distances[1:]]
     outgoing = []
     slot = 0
     for index, round_distances in enumerate(rounds):
-        if index == 0:
-            send_s[index] = state_ref[...].astype(jnp.bfloat16)
-            send_d[index] = decay_ref[...]
-        else:
-            send_s[index] = out_ref[...].astype(jnp.bfloat16)
-            send_d[index] = cur_d[...]
+        send_s[index] = cur_s[...].astype(jnp.bfloat16)
+        send_d[index] = cur_d[...]
+        start = slot
         for distance in round_distances:
-            pair = []
-            for part, (src, dst) in enumerate(((send_s, recv_s), (send_d, recv_d))):
-                pair.append(
-                    lambda target, src=src, dst=dst, part=part, index=index, slot=slot: (
-                        pltpu.make_async_remote_copy(
-                            src_ref=src.at[index],
-                            dst_ref=dst.at[slot],
-                            send_sem=ssem.at[slot, part],
-                            recv_sem=rsem.at[slot, part],
-                            device_id=(target, chan),
-                            device_id_type=MESH,
-                        )
-                    )
-                )
-            sends = me + distance < count
+            makers = (
+                lambda t, index=index, slot=slot: remote(send_s.at[index], recv_s.at[slot], slot + 1, 0, t),
+                lambda t, index=index, slot=slot: remote(send_d.at[index], recv_d.at[slot], slot + 1, 1, t),
+            )
+            sends = chip + distance < chips
 
             @pl.when(sends)
-            def _():
-                for make in pair:
-                    make(me + distance).start()
-
-            outgoing.append((sends, pair, distance, slot))
+            def _(makers=makers, distance=distance):
+                for make in makers:
+                    make(2 * (chip + distance) + core).start()
+
+            outgoing.append((sends, makers, distance))
             slot += 1
-
-        for sends, pair, distance, at in outgoing[-len(round_distances):]:
-            receives = me - distance >= 0
-            first = index == 0 and distance == 1
+        for at in range(start, slot):
+            sends, makers, distance = outgoing[at]
+            receives = chip - distance >= 0
+            opening = index == 0 and distance == 1
 
             @pl.when(receives)
-            def _():
-                for make in pair:
-                    make(me - distance).wait_recv()
-                if first:
-                    out_ref[...] = recv_s[at].astype(jnp.float32)
+            def _(makers=makers, distance=distance, at=at, opening=opening):
+                for make in makers:
+                    make(2 * (chip - distance) + core).wait_recv()
+                if opening:
+                    cur_s[...] = recv_s[at].astype(jnp.float32)
                     cur_d[...] = recv_d[at]
                 else:
-                    scale = jnp.exp(cur_d[:, 0:1, :])
-                    out_ref[...] = scale * recv_s[at].astype(jnp.float32) + out_ref[...]
+                    scale_add(cur_s, cur_d[...], recv_s.at[at], cur_s)
                     cur_d[...] = recv_d[at] + cur_d[...]
 
-            if first:
+            if opening:
 
                 @pl.when(jnp.logical_not(receives))
                 def _():
-                    out_ref[...] = jnp.zeros_like(out_ref)
+                    cur_s[...] = jnp.zeros_like(cur_s)
                     cur_d[...] = jnp.zeros_like(cur_d)
 
-    for sends, pair, distance, at in outgoing:
+    last = len(outgoing) + 1
+    own_half = send_s.at[len(rounds)]
+    own_half[...] = cur_s[...].astype(jnp.bfloat16)
+    final = remote(own_half, back_s, last, 0, partner)
+    final.start()
+    final.wait_recv()
+
+    @pl.when(core == 0)
+    def _():
+        out_ref[0:half] = cur_s[...]
+        out_ref[half:] = back_s[...].astype(jnp.float32)
+
+    @pl.when(core == 1)
+    def _():
+        out_ref[0:half] = back_s[...].astype(jnp.float32)
+        out_ref[half:] = cur_s[...]
+        scale_add(out_ref, pair_d[...], out_ref, pair_s)
+
+    final.wait_send()
+
+    @pl.when(core == 0)
+    def _():
+        first[0](partner).wait_send()
+        first_d(partner).wait_send()
+
+    @pl.when(core == 1)
+    def _():
+        first[1](partner).wait_send()
+        first_d(partner).wait_send()
+
+    for sends, makers, distance in outgoing:
 
         @pl.when(sends)
-        def _():
-            for make in pair:
-                make(me + distance).wait_send()
+        def _(makers=makers, distance=distance):
+            for make in makers:
+                make(2 * (chip + distance) + core).wait_send()
 
 
 def state_scan(state, decay):
     count = lax.axis_size("seq")
-    rounds = len(scan_distances(count))
-    slots = rounds + 1
+    rounds = len(scan_distances(count // 2))
+    heads = state.shape[0]
+    half_shape = (heads // 2,) + state.shape[1:]
+    half_decay = (heads // 2,) + decay.shape[1:]
     return pl.pallas_call(
         functools.partial(state_scan_kernel, count),
         out_shape=jax.ShapeDtypeStruct(state.shape, jnp.float32),
         in_specs=[pl.BlockSpec(memory_space=pltpu.VMEM)] * 2,
         out_specs=pl.BlockSpec(memory_space=pltpu.VMEM),
         scratch_shapes=[
+            pltpu.VMEM(state.shape, jnp.bfloat16),
             pltpu.VMEM(decay.shape, jnp.float32),
-            pltpu.VMEM((rounds,) + state.shape, jnp.bfloat16),
-            pltpu.VMEM((rounds,) + decay.shape, jnp.float32),
-            pltpu.VMEM((slots,) + state.shape, jnp.bfloat16),
-            pltpu.VMEM((slots,) + decay.shape, jnp.float32),
-            pltpu.SemaphoreType.DMA((slots, 2)),
-            pltpu.SemaphoreType.DMA((slots, 2)),
+            pltpu.VMEM(state.shape, jnp.bfloat16),
+            pltpu.VMEM(decay.shape, jnp.float32),
+            pltpu.VMEM(half_shape, jnp.float32),
+            pltpu.VMEM(half_decay, jnp.float32),
+            pltpu.VMEM((rounds + 1,) + half_shape, jnp.bfloat16),
+            pltpu.VMEM((rounds,) + half_decay, jnp.float32),
+            pltpu.VMEM((rounds + 1,) + half_shape, jnp.bfloat16),
+            pltpu.VMEM((rounds + 1,) + half_decay, jnp.float32),
+            pltpu.VMEM(half_shape, jnp.bfloat16),
+            pltpu.SemaphoreType.DMA((rounds + 3, 2)),
+            pltpu.SemaphoreType.DMA((rounds + 3, 2)),
         ],
         compiler_params=pltpu.CompilerParams(collective_id=0, has_side_effects=True),
         name="state_scan",
     )(state, decay)
-
 
 def local(
     inner_input,
@@ -210,9 +284,7 @@
         )
     slab_decay = jnp.sum(block_decay, axis=0)
     state_shape = (groups * per_group, HEAD_DIM, STATE)
-    decay_tile = jnp.broadcast_to(
-        slab_decay.reshape(groups * per_group, 1, 1), (groups * per_group, 8, STATE)
-    )
+    decay_tile = jnp.broadcast_to(slab_decay.reshape(groups * per_group, 1), (groups * per_group, STATE))
     entering = state_scan(running.reshape(state_shape), decay_tile).reshape(running.shape)
     leading = jnp.cumsum(block_decay, axis=0) - block_decay
     state_in = (

time: 191 us -> 171 us (0.90)
  Pallas kernels: 41.8 us -> 27 us
  waiting for transfers between devices: 64 us -> 58.9 us
    pallas_call x1, Pallas kernels: 41.8 us -> 27 us  [state_scan(): pl.pallas_call(functools.partial(state_scan_kernel, count), out_shape=jax...]
    reduce_scatter x1, waiting for transfers between devices: 63.9 us -> 58.8 us  [local(): lax.psum_scatter(lax.dot_general(out_weight, normed, (((0,), (1,)), ((),...]
  transfers between devices with their start and end apart: 3 -> 3, of which waited for: 1 -> 1; matrix products, arithmetic and copies ran while one was open for 11% -> 12% of each run, Pallas kernels for 0% -> 0%
where the time goes in v7:
time: 171 us; the launch traced here: 170 us
  waiting for transfers between devices  58.9 us (34%)
  Pallas kernels  27 us (16%)
  local copies, waits for them, and re-layouts  25.6 us (15%)
  matrix products  22.6 us (13%)
  other arithmetic  16.4 us (10%)
  between operations  13.7 us (8%)
  starting transfers between devices  5.41 us (3%)
    reduce_scatter x1, waiting for transfers between devices, local(): lax.psum_scatter(lax.dot_general(out_weight, normed, (((0,), (1,)), ((),...  58.8 us
    pallas_call x1, Pallas kernels, state_scan(): pl.pallas_call(functools.partial(state_scan_kernel, count), out_shape=jax...  27 us
    unnamed x36, local copies, waits for them, and re-layouts  9.65 us
    dot_general x1, matrix products, local(): jnp.einsum('cgjts,csgjp->ctgjp', mixing, x_blocks, preferred_element_type...  8.92 us
    dot_general x1, matrix products, local(): lax.dot_general(out_weight, normed, (((0,), (1,)), ((), ())), preferred_e...  6.94 us
    convert_element_type x2, other arithmetic, conv_silu(): return jax.nn.silu(acc).astype(jnp.bfloat16)  5.9 us
    ppermute x2, starting transfers between devices, passed_along(): return lax.ppermute(x, axis, pairs)  5.41 us
  transfers between devices with their start and end apart: 3, of which 1 were waited for; matrix products, arithmetic and copies ran while one was open for 12% of the time, Pallas kernels for 0%

profile of v7, /device:TPU:24, one launch (start us, length us, event | category | flops | bytes accessed | tf_op | source)
XLA Modules:
  0.0 169.6 jit_solution(10004737426398591365)
XLA Ops:
  6.5 0.9 slice.101
  7.4 0.9 copy.38
  8.3 1.9 %collective-permute-start = (bf16[3,1024]{0,1:T(8,128)(2,1)}, bf16[3,1024]{0,1:T(8,128)(2,1)}, u32[]{:S(2)}, u32[]{:S(2)}) collective-permute-start(bf16[3,1024]{0,1:T(8,128)(2,1)} %copy.38), channel_id=1, source_target_pairs={{0,8},{8,16},{16,24},{24,32},{32,40},{40,48},{48,56},{56,64},{64,7... | collective-permute-start | bytes 18440 | tf_op jit(solution)/shard_map/ppermute | solution.py:24
  10.2 1.1 copy.41
  11.3 3.5 %collective-permute-start.1 = (bf16[3,2,1,128]{3,0,2,1:T(4,128)(2,1)S(1)}, bf16[3,2,1,128]{3,0,2,1:T(4,128)(2,1)S(1)}, u32[]{:S(2)}, u32[]{:S(2)}) collective-permute-start(bf16[3,2,1,128]{3,0,2,1:T(4,128)(2,1)S(1)} %slice.133), channel_id=1, source_target_pairs={{0,8},{8,16},{16,24},{24,32},{32,40},{40,48},{48,56},{56,64},{64,7... | collective-permute-start | bytes 4616 | tf_op jit(solution)/shard_map/ppermute | solution.py:24
  14.9 0.7 exponential_negate_fusion
  15.5 1.0 broadcast_multiply_fusion
  16.6 2.3 %reduce-window.6 = f32[4,16,1,2,128]{4,1,2,3,0:T(8,128)S(1)} reduce-window(f32[4,16,1,2,128]{4,1,2,3,0:T(8,128)S(1)} %copy.45, f32[]{:T(128)} %constant.13.clone.1), window={size=1x1x1x1x128 pad=0_0x0_0x0_0x0_0x127_0}, to_apply=%region_0.1 | reduce-window | flops 2080768 | bytes 131076 | tf_op jit(solution)/shard_map/reduce-window
  19.6 0.8 slice_reduce_fusion
  20.4 1.1 fusion.32
  21.7 0.9 fusion.44
  22.6 0.7 fusion.45
  24.0 0.6 iota_compare_fusion
  24.6 2.6 %copy.39 = bf16[1024,1024]{0,1:T(8,128)(2,1)} copy(bf16[1024,1024]{1,0:T(8,128)(2,1)S(1)} %copy-done.2) | data formatting | bytes 4194304 | tf_op args[0]
  28.0 0.6 copy.58
  28.6 3.9 %copy.61 = bf16[1024,1024]{0,1:T(8,128)(2,1)} copy(bf16[1024,1024]{1,0:T(8,128)(2,1)} %param.13) | data formatting | bytes 4194304 | tf_op args[2]
  33.2 0.7 multiply_convert_fusion.9
  34.2 0.8 convert_element_type.97
  35.0 5.2 %multiply_convert_fusion.5 = bf16[1024,1024]{0,1:T(8,128)(2,1)S(1)} fusion(bf16[1024,1024]{0,1:T(8,128)(2,1)S(1)} %copy-done, bf16[3,1024]{0,1:T(8,128)(2,1)} %collective-permute-done, f32[1024]{0:T(1024)S(1)} %bitcast.84, f32[1024]{0:T(1024)S(1)} %bitcast.85, f32[1024]{0:T(1024)S(1)} %bitcast.83, f32[1024]{0:T(1024)S(1)} %bitcast.82), kind=kLoop, calls=%fused_computation.25 | loop fusion | flops 26214400 | bytes 4216832 | tf_op jit(solution)/shard_map/convert_element_type | solution.py:31
  40.3 3.4 %reshape.338 = f32[4,256,1,16,64]{1,0,4,3,2:T(4,128)} reshape(bf16[1024,1024]{0,1:T(8,128)(2,1)S(1)} %multiply_convert_fusion.5) | data formatting | bytes 6291456 | tf_op jit(solution)/shard_map/convert_element_type | solution.py:295
  43.7 2.8 %reshape.324 = bf16[4,256,16,64]{1,0,3,2:T(4,128)(2,1)} reshape(bf16[1024,1024]{0,1:T(8,128)(2,1)S(1)} %multiply_convert_fusion.5) | data formatting | bytes 4194304 | tf_op jit(solution)/shard_map/reshape.26
  46.5 8.9 %bitcast_add_fusion = f32[4,256,1,16,64]{1,4,3,0,2:T(8,128)} fusion(f32[4,256,1,16,64]{1,0,4,3,2:T(4,128)} %reshape.338, f32[4,16,256]{2,1,0:T(8,128)} %copy.49, f32[4,16,256]{2,1,0:T(8,128)S(1)} %reduce_window_sum.44, f32[4,256,256]{2,1,0:T(8,128)S(1)} %fusion.46, pred[256,256]{1,0:T(8,128)(4,1)} %iota_compare_fusion, f32[16]{0:T(128)S(1)} %copy-done.15, ...), kind=kOutput, calls=%fused_computation.18 | convolution fusion | flops 559939584 | bytes 11731008 | tf_op jit(solution)/shard_map/cgjts,csgjp->ctgjp/dot_general | solution.py:270
  55.5 3.3 %fusion.11 = f32[4,16,64,128]{3,2,1,0:T(8,128)S(1)} fusion(f32[4,256,128]{2,1,0:T(8,128)S(1)} %copy-done.4, f32[4,256,16]{1,2,0:T(8,128)S(1)} %copy-done.5, bf16[4,256,16,64]{1,0,3,2:T(4,128)(2,1)S(1)} %copy-done.3), kind=kOutput, calls=%fused_computation.15 | convolution fusion | flops 272629760 | bytes 4784128 | tf_op jit(solution)/shard_map/csgjp,csgjn->cgjpn/dot_general | solution.py:274
  58.8 1.1 fusion.28
  59.9 0.7 broadcast_in_dim.15.decay_ref
  60.6 27.0 %state_scan.1 = f32[16,64,128]{2,1,0:T(8,128)} custom-call(f32[16,64,128]{2,1,0:T(8,128)} %get-tuple-element.9.state_ref, f32[16,128]{1,0:T(8,128)} %broadcast_in_dim.15.decay_ref), custom_call_target="tpu_custom_call" | custom-call | tf_op jit(solution)/shard_map/state_scan/pallas_call | solution.py:202
  87.6 3.1 %fusion.12 = f32[4,256,1,16,64]{1,4,3,0,2:T(8,128)S(1)} fusion(f32[4,256,1,16,64]{1,4,3,0,2:T(8,128)} %bitcast_add_fusion, bf16[4,256,128,1]{2,1,3,0:T(8,128)(2,1)S(1)} %bitcast.74, f32[4,256,16]{1,2,0:T(8,128)S(1)} %copy.55, f32[1,16,64,128]{3,2,1,0:T(8,128)S(1)} %get-tuple-element.10, f32[1,16,64,128]{3,2,1,0:T(8,128)S(1)} %get-tuple-element.11, ...), kind=kOutput, calls=%fused_computation.17 | convolution fusion | flops 273678336 | bytes 10813712 | tf_op jit(solution)/shard_map/ctgn,cgjpn->ctgjp/dot_general | solution.py:303
  90.8 2.8 %copy.60 = f32[4,256,1,16,64]{1,0,4,3,2:T(4,128)S(1)} copy(f32[4,256,1,16,64]{1,4,3,0,2:T(8,128)S(1)} %fusion.12) | data formatting | bytes 8388608 | tf_op jit(solution)/shard_map/add | solution.py:306
  93.6 1.0 copy.64
  95.2 1.3 multiply_reduce_fusion
  97.0 6.9 %convert_bitcast_fusion = bf16[2048,1024]{0,1:T(8,128)(2,1)} fusion(bf16[1024,2048]{1,0:T(8,128)(2,1)S(1)} %copy-done.13, f32[1024]{0:T(1024)S(1)} %copy-done.14, f32[1024]{0:T(1024)S(1)} %add_rsqrt_fusion, f32[1024,1024]{0,1:T(8,128)S(1)} %bitcast.71, bf16[1024,1024]{0,1:T(8,128)(2,1)S(1)} %copy-done.1), kind=kOutput, calls=%fused_computation.20 | convolution fusion | flops 4306501632 | bytes 14688256 | tf_op jit(solution)/shard_map/dot_general | solution.py:318
  103.9 58.8 %reduce-scatter.2.cloned.1.call-done = bf16[256,1024]{0,1:T(8,128)(2,1)} async-done(((bf16[2048,1024]{0,1:T(8,128)(2,1)}), bf16[256,1024]{0,1:T(8,128)(2,1)}) %reduce-scatter.2.cloned.1.call-update) | async-done | bytes 524304 | tf_op jit(solution)/shard_map/reduce_scatter | solution.py:317
  (65 shorter events, 4.4 us)
Async XLA Ops:
  6.5 18.1 %copy-start.2 = (bf16[1024,1024]{1,0:T(8,128)(2,1)S(1)}, bf16[1024,1024]{1,0:T(8,128)(2,1)}, u32[]{:S(2)}) copy-start(bf16[1024,1024]{1,0:T(8,128)(2,1)} %param.11) | copy-start | bytes 6291460
  6.5 156.2 %reduce-scatter.2.cloned.1.call-start = ((), (), s32[]{:S(2)}) async-start(), calls=%async_computation.1 | async-start | bytes 4718592 | tf_op jit(solution)/shard_map/reduce_scatter | solution.py:317
  8.3 26.7 %collective-permute-start = (bf16[3,1024]{0,1:T(8,128)(2,1)}, bf16[3,1024]{0,1:T(8,128)(2,1)}, u32[]{:S(2)}, u32[]{:S(2)}) collective-permute-start(bf16[3,1024]{0,1:T(8,128)(2,1)} %copy.38), channel_id=1, source_target_pairs={{0,8},{8,16},{16,24},{24,32},{32,40},{40,48},{48,56},{56,64},{64,7... | collective-permute-start | bytes 18440 | tf_op jit(solution)/shard_map/ppermute | solution.py:24
  11.3 21.8 %collective-permute-start.1 = (bf16[3,2,1,128]{3,0,2,1:T(4,128)(2,1)S(1)}, bf16[3,2,1,128]{3,0,2,1:T(4,128)(2,1)S(1)}, u32[]{:S(2)}, u32[]{:S(2)}) collective-permute-start(bf16[3,2,1,128]{3,0,2,1:T(4,128)(2,1)S(1)} %slice.133), channel_id=1, source_target_pairs={{0,8},{8,16},{16,24},{24,32},{32,40},{40,48},{48,56},{56,64},{64,7... | collective-permute-start | bytes 4616 | tf_op jit(solution)/shard_map/ppermute | solution.py:24
  32.6 2.5 %copy-start = (bf16[1024,1024]{0,1:T(8,128)(2,1)S(1)}, bf16[1024,1024]{0,1:T(8,128)(2,1)}, u32[]{:S(2)}) copy-start(bf16[1024,1024]{0,1:T(8,128)(2,1)} %copy.39) | copy-start | bytes 6291460
  40.3 6.2 %copy-start.15 = (f32[16]{0:T(128)S(1)}, f32[16]{0:T(128)}, u32[]{:S(2)}) copy-start(f32[16]{0:T(128)} %param.17) | copy-start | bytes 196
  46.5 8.9 %copy-start.3 = (bf16[4,256,16,64]{1,0,3,2:T(4,128)(2,1)S(1)}, bf16[4,256,16,64]{1,0,3,2:T(4,128)(2,1)}, u32[]{:S(2)}) copy-start(bf16[4,256,16,64]{1,0,3,2:T(4,128)(2,1)} %reshape.324) | copy-start | bytes 6291460
  46.5 8.9 %copy-start.4 = (f32[4,256,128]{2,1,0:T(8,128)S(1)}, f32[4,256,128]{2,1,0:T(8,128)}, u32[]{:S(2)}) copy-start(f32[4,256,128]{2,1,0:T(8,128)} %convert_element_type.97) | copy-start | bytes 1572868
  46.5 8.9 %copy-start.5 = (f32[4,256,16]{1,2,0:T(8,128)S(1)}, f32[4,256,16]{1,2,0:T(8,128)}, u32[]{:S(2)}) copy-start(f32[4,256,16]{1,2,0:T(8,128)} %copy.58) | copy-start | bytes 196612
  55.4 3.4 %copy-start.8 = (f32[16]{0:T(128)S(1)}, f32[16]{0:T(128)}, u32[]{:S(2)}) copy-start(f32[16]{0:T(128)} %get-tuple-element.5) | copy-start | bytes 196
  55.4 3.4 %copy-start.9 = (f32[16]{0:T(128)S(1)}, f32[16]{0:T(128)}, u32[]{:S(2)}) copy-start(f32[16]{0:T(128)} %get-tuple-element.6) | copy-start | bytes 196
  55.4 3.4 %copy-start.10 = (f32[16]{0:T(128)S(1)}, f32[16]{0:T(128)}, u32[]{:S(2)}) copy-start(f32[16]{0:T(128)} %get-tuple-element.7) | copy-start | bytes 196
  55.4 3.4 %copy-start.11 = (f32[16]{0:T(128)S(1)}, f32[16]{0:T(128)}, u32[]{:S(2)}) copy-start(f32[16]{0:T(128)} %get-tuple-element.8) | copy-start | bytes 196
  58.8 1.1 copy-start.7
  58.8 28.9 %copy-start.6 = (f32[4,16]{1,0:T(4,128)S(1)}, f32[4,16]{1,0:T(4,128)}, u32[]{:S(2)}) copy-start(f32[4,16]{1,0:T(4,128)} %subtract_exponential_fusion) | copy-start | bytes 772
  58.8 28.9 %copy-start.12 = (f32[4]{0:T(128)S(1)}, f32[4]{0:T(128)}, u32[]{:S(2)}) copy-start(f32[4]{0:T(128)} %pad.clone) | copy-start | bytes 52
  93.6 1.6 copy-start.1
  94.6 2.3 %copy-start.13 = (bf16[1024,2048]{1,0:T(8,128)(2,1)S(1)}, bf16[1024,2048]{1,0:T(8,128)(2,1)}, u32[]{:S(2)}) copy-start(bf16[1024,2048]{1,0:T(8,128)(2,1)} %param.21) | copy-start | bytes 12582916
  94.6 2.3 %copy-start.14 = (f32[1024]{0:T(1024)S(1)}, f32[1024]{0:T(1024)}, u32[]{:S(2)}) copy-start(f32[1024]{0:T(1024)} %param.20) | copy-start | bytes 12292
Sparse Core Ops, SparseCore 0:
  104.0 58.6 reduce-scatter.1

commit v8 on v7

--- a/solution.py
+++ b/solution.py
@@ -223,6 +223,96 @@
         name="state_scan",
     )(state, decay)
 
+def ring_kernel(count, pieces, normed_ref, weight_ref, out_ref, send_buf, recv_buf, ssem, rsem):
+    me = lax.axis_index("chan")
+    seq = lax.axis_index("seq")
+    width = out_ref.shape[1]
+    rows = normed_ref.shape[0] // (2 * pieces)
+    targets = (lax.rem(me + 1, count), lax.rem(me + count - 1, count))
+
+    barrier = pltpu.get_barrier_semaphore()
+    for target in targets:
+        pl.semaphore_signal(barrier, 1, device_id=(seq, target), device_id_type=MESH)
+    pl.semaphore_wait(barrier, 2)
+
+    def copy(direction, step, piece):
+        return pltpu.make_async_remote_copy(
+            src_ref=send_buf.at[direction, step, piece],
+            dst_ref=recv_buf.at[direction, step, piece],
+            send_sem=ssem.at[direction, step, piece],
+            recv_sem=rsem.at[direction, step, piece],
+            device_id=(seq, targets[direction]),
+            device_id_type=MESH,
+        )
+
+    def block(direction, step):
+        if direction == 0:
+            return lax.rem(me + 2 * count - 1 - step, count)
+        return lax.rem(me + 1 + step, count)
+
+    def partial(direction, step, piece):
+        start = (direction * pieces + piece) * rows
+        column = pl.multiple_of(block(direction, step) * width, width)
+        return jnp.dot(
+            normed_ref[pl.ds(start, rows), :],
+            weight_ref[:, pl.ds(column, width)],
+            preferred_element_type=jnp.float32,
+        )
+
+    def run_step(step, first, last):
+        for piece in range(pieces):
+            for direction in range(2):
+                value = partial(direction, step, piece)
+                if not first:
+                    copy(direction, step - 1, piece).wait_recv()
+                    value = value + recv_buf[direction, step - 1, piece].astype(jnp.float32)
+                if last:
+                    start = (direction * pieces + piece) * rows
+                    out_ref[pl.ds(start, rows), :] = value.astype(out_ref.dtype)
+                else:
+                    send_buf[direction, step, piece] = value.astype(send_buf.dtype)
+                    copy(direction, step, piece).start()
+
+    run_step(0, True, False)
+
+    def middle(step, carry):
+        run_step(step, False, False)
+        return carry
+
+    lax.fori_loop(1, count - 1, middle, 0)
+    run_step(count - 1, False, True)
+
+    def drain(step, carry):
+        for piece in range(pieces):
+            for direction in range(2):
+                copy(direction, step, piece).wait_send()
+        return carry
+
+    lax.fori_loop(0, count - 1, drain, 0)
+
+
+def ring_projection(normed, weight):
+    count = lax.axis_size("chan")
+    pieces = 4
+    tokens = normed.shape[0]
+    width = weight.shape[1] // count
+    rows = tokens // (2 * pieces)
+    buffers = (2, count - 1, pieces, rows, width)
+    return pl.pallas_call(
+        functools.partial(ring_kernel, count, pieces),
+        out_shape=jax.ShapeDtypeStruct((tokens, width), jnp.bfloat16),
+        in_specs=[pl.BlockSpec(memory_space=pltpu.VMEM)] * 2,
+        out_specs=pl.BlockSpec(memory_space=pltpu.VMEM),
+        scratch_shapes=[
+            pltpu.VMEM(buffers, jnp.bfloat16),
+            pltpu.VMEM(buffers, jnp.bfloat16),
+            pltpu.SemaphoreType.DMA(buffers[:3]),
+            pltpu.SemaphoreType.DMA(buffers[:3]),
+        ],
+        compiler_params=pltpu.CompilerParams(collective_id=1, has_side_effects=True),
+        name="ring_projection",
+    )(normed, weight)
+
 def local(
     inner_input,
     state_maps,
@@ -314,15 +404,7 @@
             .astype(jnp.bfloat16)
             .reshape(rows, head_count * HEAD_DIM)
         )
-        shares = lax.psum_scatter(
-            lax.dot_general(
-                out_weight, normed, (((0,), (1,)), ((), ())), preferred_element_type=jnp.float32
-            ).astype(jnp.bfloat16),
-            "chan",
-            scatter_dimension=0,
-            tiled=True,
-        )
-        outs.append(shares.T)
+        outs.append(ring_projection(normed, out_weight))
     return jnp.concatenate(outs, axis=0)
 
 

time: 171 us -> 175 us (1.023)
  waiting for transfers between devices: 58.9 us -> 0.01 us
  Pallas kernels: 27 us -> 80 us
  local copies, waits for them, and re-layouts: 25.6 us -> 46.4 us
  between operations: 13.7 us -> 0.36 us
  other arithmetic: 16.4 us -> 23.4 us
  matrix products: 22.6 us -> 18.2 us
    reduce_scatter x1 -> x0, waiting for transfers between devices: 58.8 us -> none  [local(): lax.psum_scatter(lax.dot_general(out_weight, normed, (((0,), (1,)), ((),...]
    pallas_call x0 -> x1, Pallas kernels: none -> 53 us  [ring_projection(): pl.pallas_call(functools.partial(ring_kernel, count, pieces), out_shape=j...]
    reshape x1 -> x3, local copies, waits for them, and re-layouts: 0.01 us -> 15.9 us  [the longest x2 15.9 us: local(): y_all.reshape(rows, groups, width)]
    convert_element_type x1 -> x2, local copies, waits for them, and re-layouts: 3.41 us -> 12.1 us  [local(): skip_gain.reshape(groups, per_group)[:, :, None] * x_blocks]
    dot_general x1 -> x0, matrix products: 6.94 us -> none  [local(): lax.dot_general(out_weight, normed, (((0,), (1,)), ((), ())), preferred_e...]
    another operation x9 -> x10, local copies, waits for them, and re-layouts: 3.27 us -> 9.37 us
    unnamed x36 -> x30, local copies, waits for them, and re-layouts: 9.65 us -> 3.63 us
    convert_element_type x0 -> x1, other arithmetic: none -> 2.91 us  [local(): normed = (gated * lax.rsqrt(square_mean + epsilon) * norm_gain.reshape(gr...]
  transfers between devices with their start and end apart: 3 -> 2, of which waited for: 1 -> 0; matrix products, arithmetic and copies ran while one was open for 12% -> 8% of each run, Pallas kernels for 0% -> 0%
where the time goes in v8:
time: 175 us; the launch traced here: 174 us
  Pallas kernels  80 us (46%)
  local copies, waits for them, and re-layouts  46.4 us (27%)
  other arithmetic  23.4 us (13%)
  matrix products  18.2 us (10%)
  starting transfers between devices  5.41 us (3%)
    pallas_call x1, Pallas kernels, ring_projection(): pl.pallas_call(functools.partial(ring_kernel, count, pieces), out_shape=j...  53 us
    pallas_call x1, Pallas kernels, state_scan(): pl.pallas_call(functools.partial(state_scan_kernel, count), out_shape=jax...  27 us
    reshape x2, local copies, waits for them, and re-layouts, local(): y_all.reshape(rows, groups, width)  15.9 us
    convert_element_type x2, local copies, waits for them, and re-layouts, local(): skip_gain.reshape(groups, per_group)[:, :, None] * x_blocks  12.1 us
    dot_general x1, matrix products, local(): jnp.einsum('cgjts,csgjp->ctgjp', mixing, x_blocks, preferred_element_type...  9.57 us
    another operation x10, local copies, waits for them, and re-layouts  9.37 us
    convert_element_type x2, other arithmetic, conv_silu(): return jax.nn.silu(acc).astype(jnp.bfloat16)  7.63 us
    ppermute x2, starting transfers between devices, passed_along(): return lax.ppermute(x, axis, pairs)  5.41 us
  transfers between devices with their start and end apart: 2, of which 0 were waited for; matrix products, arithmetic and copies ran while one was open for 8% of the time, Pallas kernels for 0%

profile of v8, /device:TPU:24, one launch (start us, length us, event | category | flops | bytes accessed | tf_op | source)
XLA Modules:
  0.0 173.8 jit_solution(2803715015796861601)
XLA Ops:
  0.0 0.7 slice.101
  0.7 1.9 %collective-permute-start = (bf16[3,1024]{1,0:T(4,128)(2,1)S(1)}, bf16[3,1024]{1,0:T(4,128)(2,1)S(1)}, u32[]{:S(2)}, u32[]{:S(2)}) collective-permute-start(bf16[3,1024]{1,0:T(4,128)(2,1)S(1)} %slice.101), channel_id=1, source_target_pairs={{0,8},{8,16},{16,24},{24,32},{32,40},{40,48},{48,56},{56,64},{64,7... | collective-permute-start | bytes 18440 | tf_op jit(solution)/shard_map/ppermute | solution.py:24
  2.6 1.1 copy.40
  3.8 3.5 %collective-permute-start.1 = (bf16[3,2,1,128]{3,0,2,1:T(4,128)(2,1)S(1)}, bf16[3,2,1,128]{3,0,2,1:T(4,128)(2,1)S(1)}, u32[]{:S(2)}, u32[]{:S(2)}) collective-permute-start(bf16[3,2,1,128]{3,0,2,1:T(4,128)(2,1)S(1)} %slice.133), channel_id=1, source_target_pairs={{0,8},{8,16},{16,24},{24,32},{32,40},{40,48},{48,56},{56,64},{64,7... | collective-permute-start | bytes 4616 | tf_op jit(solution)/shard_map/ppermute | solution.py:24
  7.3 0.7 exponential_negate_fusion
  7.9 1.0 broadcast_multiply_fusion
  9.0 2.3 %reduce-window.6 = f32[4,16,1,2,128]{4,1,2,3,0:T(8,128)S(1)} reduce-window(f32[4,16,1,2,128]{4,1,2,3,0:T(8,128)S(1)} %copy.44, f32[]{:T(128)} %constant.13.clone.1), window={size=1x1x1x1x128 pad=0_0x0_0x0_0x0_0x127_0}, to_apply=%region_0.1 | reduce-window | flops 2080768 | bytes 131076 | tf_op jit(solution)/shard_map/reduce-window
  12.0 0.9 slice_reduce_fusion
  12.9 1.0 fusion.28
  14.1 0.9 fusion.39
  15.1 0.7 fusion.40
  16.5 0.6 iota_compare_fusion
  17.9 0.6 copy.58
  19.2 0.7 multiply_convert_fusion.8
  20.2 0.8 convert_element_type.91
  21.6 6.9 %multiply_convert_fusion.5 = bf16[1024,1024]{1,0:T(8,128)(2,1)S(1)} fusion(bf16[1024,1024]{1,0:T(8,128)(2,1)} %param.11, bf16[3,1024]{1,0:T(4,128)(2,1)} %copy-done.4, f32[1024]{0:T(1024)S(1)} %bitcast.74, f32[1024]{0:T(1024)S(1)} %bitcast.75, f32[1024]{0:T(1024)S(1)} %bitcast.73, f32[1024]{0:T(1024)S(1)} %bitcast.72), kind=kLoop, calls=%fused_computation.23 | loop fusion | flops 26214400 | bytes 4216832 | tf_op jit(solution)/shard_map/convert_element_type | solution.py:31
  28.6 4.5 %reshape.340 = f32[4,256,1,16,64]{4,3,1,0,2:T(8,128)} reshape(bf16[1024,1024]{1,0:T(8,128)(2,1)S(1)} %multiply_convert_fusion.5) | data formatting | bytes 6291456 | tf_op jit(solution)/shard_map/convert_element_type | solution.py:385
  33.0 4.0 %reshape.343 = bf16[4,256,16,64]{3,2,1,0:T(8,128)(2,1)} reshape(bf16[1024,1024]{1,0:T(8,128)(2,1)S(1)} %multiply_convert_fusion.5) | data formatting | bytes 4194304 | tf_op jit(solution)/shard_map/reshape.26
  37.1 7.7 %copy.51 = f32[4,256,1,16,64]{1,4,3,0,2:T(8,128)} copy(f32[4,256,1,16,64]{4,3,1,0,2:T(8,128)} %reshape.340) | data formatting | bytes 8388608 | tf_op jit(solution)/shard_map/convert_element_type | solution.py:385
  44.7 4.9 %copy.49 = bf16[4,256,16,64]{1,3,2,0:T(8,128)(2,1)S(1)} copy(bf16[4,256,16,64]{3,2,1,0:T(8,128)(2,1)} %reshape.343) | data formatting | bytes 4194304 | tf_op jit(solution)/shard_map/reshape.26
  49.6 9.6 %bitcast_add_fusion = f32[4,256,1,16,64]{1,4,3,0,2:T(8,128)} fusion(f32[4,256,1,16,64]{1,4,3,0,2:T(8,128)} %copy.51, bf16[4,256,16,64]{1,3,2,0:T(8,128)(2,1)S(1)} %copy.49, f32[4,16,256]{2,1,0:T(8,128)} %copy.48, f32[4,16,256]{2,1,0:T(8,128)S(1)} %reduce_window_sum.44, f32[4,256,256]{2,1,0:T(8,128)S(1)} %fusion.41, pred[256,256]{1,0:T(8,128)(4,1)} %iota_compare_fusion, ...), kind=kOutput, calls=%fused_computation.18 | convolution fusion | flops 559939584 | bytes 11731008 | tf_op jit(solution)/shard_map/cgjts,csgjp->ctgjp/dot_general | solution.py:360
  59.3 3.3 %fusion.11 = f32[4,16,64,128]{3,2,1,0:T(8,128)S(1)} fusion(bf16[4,256,16,64]{1,3,2,0:T(8,128)(2,1)S(1)} %copy.49, f32[4,256,128]{2,1,0:T(8,128)S(1)} %copy-done.2, f32[4,256,16]{1,2,0:T(8,128)S(1)} %copy-done.3), kind=kOutput, calls=%fused_computation.15 | convolution fusion | flops 272629760 | bytes 4784128 | tf_op jit(solution)/shard_map/csgjp,csgjn->cgjpn/dot_general | solution.py:364
  62.6 1.1 fusion.24
  63.6 0.7 broadcast_in_dim.15.decay_ref
  64.3 27.0 %state_scan.1 = f32[16,64,128]{2,1,0:T(8,128)} custom-call(f32[16,64,128]{2,1,0:T(8,128)} %get-tuple-element.9.state_ref, f32[16,128]{1,0:T(8,128)} %broadcast_in_dim.15.decay_ref), custom_call_target="tpu_custom_call" | custom-call | tf_op jit(solution)/shard_map/state_scan/pallas_call | solution.py:202
  91.4 5.1 %fusion.12 = f32[4,256,1,16,64]{1,4,3,0,2:T(8,128)} fusion(f32[4,256,1,16,64]{1,4,3,0,2:T(8,128)} %bitcast_add_fusion, bf16[4,256,128,1]{2,1,3,0:T(8,128)(2,1)S(1)} %bitcast.64, f32[4,256,16]{1,2,0:T(8,128)S(1)} %copy.55, f32[1,16,64,128]{3,2,1,0:T(8,128)S(1)} %get-tuple-element.10, f32[1,16,64,128]{3,2,1,0:T(8,128)S(1)} %get-tuple-element.11, ...), kind=kOutput, calls=%fused_computation.17 | convolution fusion | flops 273678336 | bytes 10813712 | tf_op jit(solution)/shard_map/ctgn,cgjpn->ctgjp/dot_general | solution.py:393
  96.5 8.1 %copy.66 = f32[4,256,1,16,64]{4,3,1,0,2:T(8,128)} copy(f32[4,256,1,16,64]{1,4,3,0,2:T(8,128)} %fusion.12) | data formatting | bytes 8388608 | tf_op jit(solution)/shard_map/reshape | solution.py:398
  104.6 7.8 %reshape.342 = f32[1024,1024]{1,0:T(8,128)} reshape(f32[4,256,1,16,64]{4,3,1,0,2:T(8,128)} %copy.66) | data formatting | bytes 8388608 | tf_op jit(solution)/shard_map/reshape | solution.py:398
  112.4 3.7 %multiply_reduce_fusion = f32[1024]{0:T(1024)S(1)} fusion(f32[1024,1024]{1,0:T(8,128)} %reshape.342, bf16[1024,1024]{1,0:T(8,128)(2,1)S(1)} %copy-done.1), kind=kLoop, calls=%fused_computation.20 | loop fusion | flops 8387584 | bytes 6295552 | tf_op jit(solution)/shard_map/reduce_sum | solution.py:401
  116.1 2.9 %multiply_convert_fusion.4.normed_ref = bf16[1024,1024]{1,0:T(8,128)(2,1)} fusion(f32[1024]{0:T(1024)S(1)} %copy-done.6, f32[1024]{0:T(1024)S(1)} %add_rsqrt_fusion, f32[1024,1024]{1,0:T(8,128)S(1)} %copy-done, bf16[1024,1024]{1,0:T(8,128)(2,1)S(1)} %copy-done.1), kind=kLoop, calls=%fused_computation.19 | loop fusion | flops 9437184 | bytes 8396800 | tf_op jit(solution)/shard_map/convert_element_type | solution.py:404
  119.0 53.0 %ring_projection.1 = bf16[1024,256]{1,0:T(8,128)(2,1)} custom-call(bf16[1024,1024]{1,0:T(8,128)(2,1)} %multiply_convert_fusion.4.normed_ref, bf16[1024,2048]{1,0:T(8,128)(2,1)} %weight_ref.1), custom_call_target="tpu_custom_call" | custom-call | tf_op jit(solution)/shard_map/ring_projection/pallas_call | solution.py:301
  172.0 1.9 %copy.77 = bf16[1024,256]{1,0:T(8,128)(2,1)} copy(bf16[1024,256]{1,0:T(8,128)(2,1)} %ring_projection.1) | data formatting | bytes 1048576
  (59 shorter events, 4.1 us)
Async XLA Ops:
  0.7 20.3 %collective-permute-start = (bf16[3,1024]{1,0:T(4,128)(2,1)S(1)}, bf16[3,1024]{1,0:T(4,128)(2,1)S(1)}, u32[]{:S(2)}, u32[]{:S(2)}) collective-permute-start(bf16[3,1024]{1,0:T(4,128)(2,1)S(1)} %slice.101), channel_id=1, source_target_pairs={{0,8},{8,16},{16,24},{24,32},{32,40},{40,48},{48,56},{56,64},{64,7... | collective-permute-start | bytes 18440 | tf_op jit(solution)/shard_map/ppermute | solution.py:24
  3.8 15.4 %collective-permute-start.1 = (bf16[3,2,1,128]{3,0,2,1:T(4,128)(2,1)S(1)}, bf16[3,2,1,128]{3,0,2,1:T(4,128)(2,1)S(1)}, u32[]{:S(2)}, u32[]{:S(2)}) collective-permute-start(bf16[3,2,1,128]{3,0,2,1:T(4,128)(2,1)S(1)} %slice.133), channel_id=1, source_target_pairs={{0,8},{8,16},{16,24},{24,32},{32,40},{40,48},{48,56},{56,64},{64,7... | collective-permute-start | bytes 4616 | tf_op jit(solution)/shard_map/ppermute | solution.py:24
  21.0 0.6 copy-start.4
  44.7 4.9 %copy-start.13 = (f32[16]{0:T(128)S(1)}, f32[16]{0:T(128)}, u32[]{:S(2)}) copy-start(f32[16]{0:T(128)} %param.17) | copy-start | bytes 196
  49.6 9.6 %copy-start.2 = (f32[4,256,128]{2,1,0:T(8,128)S(1)}, f32[4,256,128]{2,1,0:T(8,128)}, u32[]{:S(2)}) copy-start(f32[4,256,128]{2,1,0:T(8,128)} %convert_element_type.91) | copy-start | bytes 1572868
  49.6 9.6 %copy-start.3 = (f32[4,256,16]{1,2,0:T(8,128)S(1)}, f32[4,256,16]{1,2,0:T(8,128)}, u32[]{:S(2)}) copy-start(f32[4,256,16]{1,2,0:T(8,128)} %copy.58) | copy-start | bytes 196612
  59.2 3.3 %copy-start.8 = (f32[16]{0:T(128)S(1)}, f32[16]{0:T(128)}, u32[]{:S(2)}) copy-start(f32[16]{0:T(128)} %get-tuple-element.5) | copy-start | bytes 196
  59.2 3.3 %copy-start.9 = (f32[16]{0:T(128)S(1)}, f32[16]{0:T(128)}, u32[]{:S(2)}) copy-start(f32[16]{0:T(128)} %get-tuple-element.6) | copy-start | bytes 196
  59.2 3.3 %copy-start.10 = (f32[16]{0:T(128)S(1)}, f32[16]{0:T(128)}, u32[]{:S(2)}) copy-start(f32[16]{0:T(128)} %get-tuple-element.7) | copy-start | bytes 196
  59.2 3.3 %copy-start.11 = (f32[16]{0:T(128)S(1)}, f32[16]{0:T(128)}, u32[]{:S(2)}) copy-start(f32[16]{0:T(128)} %get-tuple-element.8) | copy-start | bytes 196
  59.2 4.4 %copy-start.7 = (f32[16]{0:T(128)S(1)}, f32[16]{0:T(128)}, u32[]{:S(2)}) copy-start(f32[16]{0:T(128)} %get-tuple-element.19) | copy-start | bytes 196
  62.5 28.8 %copy-start.5 = (f32[4,16]{1,0:T(4,128)S(1)}, f32[4,16]{1,0:T(4,128)}, u32[]{:S(2)}) copy-start(f32[4,16]{1,0:T(4,128)} %subtract_exponential_fusion) | copy-start | bytes 772
  62.5 28.8 %copy-start.12 = (f32[4]{0:T(128)S(1)}, f32[4]{0:T(128)}, u32[]{:S(2)}) copy-start(f32[4]{0:T(128)} %pad.clone) | copy-start | bytes 52
  104.6 7.8 %copy-start.1 = (bf16[1024,1024]{1,0:T(8,128)(2,1)S(1)}, bf16[1024,1024]{1,0:T(8,128)(2,1)}, u32[]{:S(2)}) copy-start(bf16[1024,1024]{1,0:T(8,128)(2,1)} %param.13) | copy-start | bytes 6291460
  112.3 3.7 %copy-start = (f32[1024,1024]{1,0:T(8,128)S(1)}, f32[1024,1024]{1,0:T(8,128)}, u32[]{:S(2)}) copy-start(f32[1024,1024]{1,0:T(8,128)} %reshape.342) | copy-start | bytes 12582916
  112.3 3.7 %copy-start.6 = (f32[1024]{0:T(1024)S(1)}, f32[1024]{0:T(1024)}, u32[]{:S(2)}) copy-start(f32[1024]{0:T(1024)} %param.20) | copy-start | bytes 12292

commit v9 on v8

--- a/solution.py
+++ b/solution.py
@@ -227,7 +227,7 @@
     me = lax.axis_index("chan")
     seq = lax.axis_index("seq")
     width = out_ref.shape[1]
-    rows = normed_ref.shape[0] // (2 * pieces)
+    rows = normed_ref.shape[1] // (2 * pieces)
     targets = (lax.rem(me + 1, count), lax.rem(me + count - 1, count))
 
     barrier = pltpu.get_barrier_semaphore()
@@ -253,9 +253,10 @@
     def partial(direction, step, piece):
         start = (direction * pieces + piece) * rows
         column = pl.multiple_of(block(direction, step) * width, width)
-        return jnp.dot(
-            normed_ref[pl.ds(start, rows), :],
+        return lax.dot_general(
+            normed_ref[:, pl.ds(start, rows)],
             weight_ref[:, pl.ds(column, width)],
+            (((0,), (0,)), ((), ())),
             preferred_element_type=jnp.float32,
         )
 
@@ -294,7 +295,7 @@
 def ring_projection(normed, weight):
     count = lax.axis_size("chan")
     pieces = 4
-    tokens = normed.shape[0]
+    tokens = normed.shape[1]
     width = weight.shape[1] // count
     rows = tokens // (2 * pieces)
     buffers = (2, count - 1, pieces, rows, width)
@@ -404,7 +405,7 @@
             .astype(jnp.bfloat16)
             .reshape(rows, head_count * HEAD_DIM)
         )
-        outs.append(ring_projection(normed, out_weight))
+        outs.append(ring_projection(normed.T, out_weight))
     return jnp.concatenate(outs, axis=0)
 
 

time: 175 us -> 149 us (0.85)
  local copies, waits for them, and re-layouts: 46.4 us -> 27 us
  other arithmetic: 23.4 us -> 19.5 us
  matrix products: 18.2 us -> 15.6 us
    reshape x3 -> x1, local copies, waits for them, and re-layouts: 15.9 us -> 0.01 us  [the longest x2 15.9 us: local(): y_all.reshape(rows, groups, width)]
    convert_element_type x2 -> x1, local copies, waits for them, and re-layouts: 12.1 us -> 3.41 us  [local(): skip_gain.reshape(groups, per_group)[:, :, None] * x_blocks]
    unnamed x30 -> x35, local copies, waits for them, and re-layouts: 3.63 us -> 11.1 us
    another operation x10 -> x9, local copies, waits for them, and re-layouts: 9.37 us -> 3.27 us
    transpose x0 -> x1, other arithmetic: none -> 3.14 us  [local(): outs.append(ring_projection(normed.T, out_weight))]
    convert_element_type x1 -> x0, other arithmetic: 2.91 us -> none  [local(): normed = (gated * lax.rsqrt(square_mean + epsilon) * norm_gain.reshape(gr...]
    add x0 -> x1, local copies, waits for them, and re-layouts: none -> 2.79 us  [local(): y_all = y_pre[part] + y_carry]
    reduce_sum x1, other arithmetic: 3.68 us -> 1.34 us  [local(): square_mean = jnp.mean(gated * gated, axis=-1, keepdims=True)]
  transfers between devices with their start and end apart: 2 -> 2, of which waited for: 0 -> 0; matrix products, arithmetic and copies ran while one was open for 8% -> 14% of each run, Pallas kernels for 0% -> 0%
where the time goes in v9:
time: 149 us; the launch traced here: 148 us
  Pallas kernels  80.1 us (54%)
  local copies, waits for them, and re-layouts  27 us (18%)
  other arithmetic  19.5 us (13%)
  matrix products  15.6 us (10%)
  starting transfers between devices  5.41 us (4%)
    pallas_call x1, Pallas kernels, ring_projection(): pl.pallas_call(functools.partial(ring_kernel, count, pieces), out_shape=j...  53.1 us
    pallas_call x1, Pallas kernels, state_scan(): pl.pallas_call(functools.partial(state_scan_kernel, count), out_shape=jax...  27 us
    unnamed x35, local copies, waits for them, and re-layouts  11.1 us
    dot_general x1, matrix products, local(): jnp.einsum('cgjts,csgjp->ctgjp', mixing, x_blocks, preferred_element_type...  8.92 us
    convert_element_type x2, other arithmetic, conv_silu(): return jax.nn.silu(acc).astype(jnp.bfloat16)  5.9 us
    ppermute x2, starting transfers between devices, passed_along(): return lax.ppermute(x, axis, pairs)  5.41 us
    convert_element_type x1, local copies, waits for them, and re-layouts, local(): skip_gain.reshape(groups, per_group)[:, :, None] * x_blocks  3.41 us
    dot_general x1, matrix products, local(): jnp.einsum('csgjp,csgjn->cgjpn', x_blocks, weighted, preferred_element_ty...  3.29 us
  transfers between devices with their start and end apart: 2, of which 0 were waited for; matrix products, arithmetic and copies ran while one was open for 14% of the time, Pallas kernels for 0%

profile of v9, /device:TPU:24, one launch (start us, length us, event | category | flops | bytes accessed | tf_op | source)
XLA Modules:
  0.0 148.1 jit_solution(968649561720013993)
XLA Ops:
  0.0 0.9 slice.101
  0.9 0.9 copy.44
  1.8 1.9 %collective-permute-start = (bf16[3,1024]{0,1:T(8,128)(2,1)}, bf16[3,1024]{0,1:T(8,128)(2,1)}, u32[]{:S(2)}, u32[]{:S(2)}) collective-permute-start(bf16[3,1024]{0,1:T(8,128)(2,1)} %copy.44), channel_id=1, source_target_pairs={{0,8},{8,16},{16,24},{24,32},{32,40},{40,48},{48,56},{56,64},{64,7... | collective-permute-start | bytes 18440 | tf_op jit(solution)/shard_map/ppermute | solution.py:24
  3.7 1.1 copy.47
  4.8 3.5 %collective-permute-start.1 = (bf16[3,2,1,128]{3,0,2,1:T(4,128)(2,1)S(1)}, bf16[3,2,1,128]{3,0,2,1:T(4,128)(2,1)S(1)}, u32[]{:S(2)}, u32[]{:S(2)}) collective-permute-start(bf16[3,2,1,128]{3,0,2,1:T(4,128)(2,1)S(1)} %slice.133), channel_id=1, source_target_pairs={{0,8},{8,16},{16,24},{24,32},{32,40},{40,48},{48,56},{56,64},{64,7... | collective-permute-start | bytes 4616 | tf_op jit(solution)/shard_map/ppermute | solution.py:24
  8.3 0.7 exponential_negate_fusion
  9.0 1.0 broadcast_multiply_fusion
  10.1 2.3 %reduce-window.6 = f32[4,16,1,2,128]{4,1,2,3,0:T(8,128)S(1)} reduce-window(f32[4,16,1,2,128]{4,1,2,3,0:T(8,128)S(1)} %copy.51, f32[]{:T(128)} %constant.13.clone.1), window={size=1x1x1x1x128 pad=0_0x0_0x0_0x0_0x127_0}, to_apply=%region_0.1 | reduce-window | flops 2080768 | bytes 131076 | tf_op jit(solution)/shard_map/reduce-window
  13.0 0.8 slice_reduce_fusion
  13.9 1.1 fusion.31
  15.1 0.9 fusion.42
  16.1 0.7 fusion.43
  17.4 0.6 iota_compare_fusion
  18.1 2.6 %copy.45 = bf16[1024,1024]{0,1:T(8,128)(2,1)} copy(bf16[1024,1024]{1,0:T(8,128)(2,1)S(1)} %copy-done.2) | data formatting | bytes 4194304 | tf_op args[0]
  22.1 3.9 %copy.67 = bf16[1024,1024]{0,1:T(8,128)(2,1)} copy(bf16[1024,1024]{1,0:T(8,128)(2,1)} %param.13) | data formatting | bytes 4194304 | tf_op args[2]
  26.6 0.7 multiply_convert_fusion.8
  27.7 0.8 convert_element_type.91
  28.5 5.2 %multiply_convert_fusion.5 = bf16[1024,1024]{0,1:T(8,128)(2,1)S(1)} fusion(bf16[1024,1024]{0,1:T(8,128)(2,1)S(1)} %copy-done.1, bf16[3,1024]{0,1:T(8,128)(2,1)} %collective-permute-done, f32[1024]{0:T(1024)S(1)} %bitcast.82, f32[1024]{0:T(1024)S(1)} %bitcast.83, f32[1024]{0:T(1024)S(1)} %bitcast.81, f32[1024]{0:T(1024)S(1)} %bitcast.80), kind=kLoop, calls=%fused_computation.24 | loop fusion | flops 26214400 | bytes 4216832 | tf_op jit(solution)/shard_map/convert_element_type | solution.py:31
  33.7 3.4 %reshape.338 = f32[4,256,1,16,64]{1,0,4,3,2:T(4,128)} reshape(bf16[1024,1024]{0,1:T(8,128)(2,1)S(1)} %multiply_convert_fusion.5) | data formatting | bytes 6291456 | tf_op jit(solution)/shard_map/convert_element_type | solution.py:386
  37.1 2.8 %reshape.324 = bf16[4,256,16,64]{1,0,3,2:T(4,128)(2,1)} reshape(bf16[1024,1024]{0,1:T(8,128)(2,1)S(1)} %multiply_convert_fusion.5) | data formatting | bytes 4194304 | tf_op jit(solution)/shard_map/reshape.26
  39.9 8.9 %bitcast_add_fusion = f32[4,256,1,16,64]{1,4,3,0,2:T(8,128)} fusion(f32[4,256,1,16,64]{1,0,4,3,2:T(4,128)} %reshape.338, f32[4,16,256]{2,1,0:T(8,128)} %copy.55, f32[4,16,256]{2,1,0:T(8,128)S(1)} %reduce_window_sum.44, f32[4,256,256]{2,1,0:T(8,128)S(1)} %fusion.44, pred[256,256]{1,0:T(8,128)(4,1)} %iota_compare_fusion, f32[16]{0:T(128)S(1)} %copy-done.14, ...), kind=kOutput, calls=%fused_computation.18 | convolution fusion | flops 559939584 | bytes 11731008 | tf_op jit(solution)/shard_map/cgjts,csgjp->ctgjp/dot_general | solution.py:361
  48.9 3.3 %fusion.11 = f32[4,16,64,128]{3,2,1,0:T(8,128)S(1)} fusion(f32[4,256,128]{2,1,0:T(8,128)S(1)} %copy-done.4, f32[4,256,16]{1,2,0:T(8,128)S(1)} %copy-done.5, bf16[4,256,16,64]{1,0,3,2:T(4,128)(2,1)S(1)} %copy-done.3), kind=kOutput, calls=%fused_computation.15 | convolution fusion | flops 272629760 | bytes 4784128 | tf_op jit(solution)/shard_map/csgjp,csgjn->cgjpn/dot_general | solution.py:365
  52.3 1.1 fusion.27
  53.4 0.7 broadcast_in_dim.15.decay_ref
  54.0 27.0 %state_scan.1 = f32[16,64,128]{2,1,0:T(8,128)} custom-call(f32[16,64,128]{2,1,0:T(8,128)} %get-tuple-element.9.state_ref, f32[16,128]{1,0:T(8,128)} %broadcast_in_dim.15.decay_ref), custom_call_target="tpu_custom_call" | custom-call | tf_op jit(solution)/shard_map/state_scan/pallas_call | solution.py:202
  81.1 3.1 %fusion.12 = f32[4,256,1,16,64]{1,4,3,0,2:T(8,128)S(1)} fusion(f32[4,256,1,16,64]{1,4,3,0,2:T(8,128)} %bitcast_add_fusion, bf16[4,256,128,1]{2,1,3,0:T(8,128)(2,1)S(1)} %bitcast.72, f32[4,256,16]{1,2,0:T(8,128)S(1)} %copy.61, f32[1,16,64,128]{3,2,1,0:T(8,128)S(1)} %get-tuple-element.10, f32[1,16,64,128]{3,2,1,0:T(8,128)S(1)} %get-tuple-element.11, ...), kind=kOutput, calls=%fused_computation.17 | convolution fusion | flops 273678336 | bytes 10813712 | tf_op jit(solution)/shard_map/ctgn,cgjpn->ctgjp/dot_general | solution.py:394
  84.2 2.8 %copy.66 = f32[4,256,1,16,64]{1,0,4,3,2:T(4,128)S(1)} copy(f32[4,256,1,16,64]{1,4,3,0,2:T(8,128)S(1)} %fusion.12) | data formatting | bytes 8388608 | tf_op jit(solution)/shard_map/add | solution.py:397
  87.0 1.0 copy.70
  88.6 1.3 multiply_reduce_fusion
  90.0 3.1 %fusion.17.normed_ref = bf16[1024,1024]{1,0:T(8,128)(2,1)} fusion(f32[1024]{0:T(1024)S(1)} %copy-done.7, f32[1024]{0:T(1024)S(1)} %add_rsqrt_fusion, f32[1024,1024]{0,1:T(8,128)S(1)} %bitcast.69, bf16[1024,1024]{0,1:T(8,128)(2,1)S(1)} %copy-done), kind=kLoop, calls=%fused_computation.31 | loop fusion | flops 9437184 | bytes 8396800 | tf_op jit(solution)/shard_map/transpose | solution.py:408
  93.1 53.1 %ring_projection.1 = bf16[1024,256]{1,0:T(8,128)(2,1)} custom-call(bf16[1024,1024]{1,0:T(8,128)(2,1)} %fusion.17.normed_ref, bf16[1024,2048]{1,0:T(8,128)(2,1)} %weight_ref.1), custom_call_target="tpu_custom_call" | custom-call | tf_op jit(solution)/shard_map/ring_projection/pallas_call | solution.py:302
  146.2 1.9 %copy.85 = bf16[1024,256]{1,0:T(8,128)(2,1)} copy(bf16[1024,256]{1,0:T(8,128)(2,1)} %ring_projection.1) | data formatting | bytes 1048576
  (62 shorter events, 4.6 us)
Async XLA Ops:
  0.0 18.1 %copy-start.2 = (bf16[1024,1024]{1,0:T(8,128)(2,1)S(1)}, bf16[1024,1024]{1,0:T(8,128)(2,1)}, u32[]{:S(2)}) copy-start(bf16[1024,1024]{1,0:T(8,128)(2,1)} %param.11) | copy-start | bytes 6291460
  1.8 26.7 %collective-permute-start = (bf16[3,1024]{0,1:T(8,128)(2,1)}, bf16[3,1024]{0,1:T(8,128)(2,1)}, u32[]{:S(2)}, u32[]{:S(2)}) collective-permute-start(bf16[3,1024]{0,1:T(8,128)(2,1)} %copy.44), channel_id=1, source_target_pairs={{0,8},{8,16},{16,24},{24,32},{32,40},{40,48},{48,56},{56,64},{64,7... | collective-permute-start | bytes 18440 | tf_op jit(solution)/shard_map/ppermute | solution.py:24
  4.8 21.8 %collective-permute-start.1 = (bf16[3,2,1,128]{3,0,2,1:T(4,128)(2,1)S(1)}, bf16[3,2,1,128]{3,0,2,1:T(4,128)(2,1)S(1)}, u32[]{:S(2)}, u32[]{:S(2)}) collective-permute-start(bf16[3,2,1,128]{3,0,2,1:T(4,128)(2,1)S(1)} %slice.133), channel_id=1, source_target_pairs={{0,8},{8,16},{16,24},{24,32},{32,40},{40,48},{48,56},{56,64},{64,7... | collective-permute-start | bytes 4616 | tf_op jit(solution)/shard_map/ppermute | solution.py:24
  26.0 2.5 %copy-start.1 = (bf16[1024,1024]{0,1:T(8,128)(2,1)S(1)}, bf16[1024,1024]{0,1:T(8,128)(2,1)}, u32[]{:S(2)}) copy-start(bf16[1024,1024]{0,1:T(8,128)(2,1)} %copy.45) | copy-start | bytes 6291460
  33.7 6.2 %copy-start.14 = (f32[16]{0:T(128)S(1)}, f32[16]{0:T(128)}, u32[]{:S(2)}) copy-start(f32[16]{0:T(128)} %param.17) | copy-start | bytes 196
  39.9 8.9 %copy-start.3 = (bf16[4,256,16,64]{1,0,3,2:T(4,128)(2,1)S(1)}, bf16[4,256,16,64]{1,0,3,2:T(4,128)(2,1)}, u32[]{:S(2)}) copy-start(bf16[4,256,16,64]{1,0,3,2:T(4,128)(2,1)} %reshape.324) | copy-start | bytes 6291460
  39.9 8.9 %copy-start.4 = (f32[4,256,128]{2,1,0:T(8,128)S(1)}, f32[4,256,128]{2,1,0:T(8,128)}, u32[]{:S(2)}) copy-start(f32[4,256,128]{2,1,0:T(8,128)} %convert_element_type.91) | copy-start | bytes 1572868
  39.9 8.9 %copy-start.5 = (f32[4,256,16]{1,2,0:T(8,128)S(1)}, f32[4,256,16]{1,2,0:T(8,128)}, u32[]{:S(2)}) copy-start(f32[4,256,16]{1,2,0:T(8,128)} %copy.64) | copy-start | bytes 196612
  48.9 3.4 %copy-start.9 = (f32[16]{0:T(128)S(1)}, f32[16]{0:T(128)}, u32[]{:S(2)}) copy-start(f32[16]{0:T(128)} %get-tuple-element.5) | copy-start | bytes 196
  48.9 3.4 %copy-start.10 = (f32[16]{0:T(128)S(1)}, f32[16]{0:T(128)}, u32[]{:S(2)}) copy-start(f32[16]{0:T(128)} %get-tuple-element.6) | copy-start | bytes 196
  48.9 3.4 %copy-start.11 = (f32[16]{0:T(128)S(1)}, f32[16]{0:T(128)}, u32[]{:S(2)}) copy-start(f32[16]{0:T(128)} %get-tuple-element.7) | copy-start | bytes 196
  48.9 3.4 %copy-start.12 = (f32[16]{0:T(128)S(1)}, f32[16]{0:T(128)}, u32[]{:S(2)}) copy-start(f32[16]{0:T(128)} %get-tuple-element.8) | copy-start | bytes 196
  52.2 1.1 copy-start.8
  52.2 28.8 %copy-start.6 = (f32[4,16]{1,0:T(4,128)S(1)}, f32[4,16]{1,0:T(4,128)}, u32[]{:S(2)}) copy-start(f32[4,16]{1,0:T(4,128)} %subtract_exponential_fusion) | copy-start | bytes 772
  52.2 28.8 %copy-start.13 = (f32[4]{0:T(128)S(1)}, f32[4]{0:T(128)}, u32[]{:S(2)}) copy-start(f32[4]{0:T(128)} %pad.clone) | copy-start | bytes 52
  87.0 1.6 %copy-start = (bf16[1024,1024]{0,1:T(8,128)(2,1)S(1)}, bf16[1024,1024]{0,1:T(8,128)(2,1)}, u32[]{:S(2)}) copy-start(bf16[1024,1024]{0,1:T(8,128)(2,1)} %copy.67) | copy-start | bytes 6291460
  88.1 1.9 %copy-start.7 = (f32[1024]{0:T(1024)S(1)}, f32[1024]{0:T(1024)}, u32[]{:S(2)}) copy-start(f32[1024]{0:T(1024)} %param.20) | copy-start | bytes 12292

commit v10 on v9

--- a/solution.py
+++ b/solution.py
@@ -294,7 +294,7 @@
 
 def ring_projection(normed, weight):
     count = lax.axis_size("chan")
-    pieces = 4
+    pieces = 8
     tokens = normed.shape[1]
     width = weight.shape[1] // count
     rows = tokens // (2 * pieces)

time: 149 us -> 166 us (1.11)
  Pallas kernels: 80.1 us -> 96.7 us
    pallas_call x1, Pallas kernels: 53.1 us -> 69.7 us  [ring_projection(): pl.pallas_call(functools.partial(ring_kernel, count, pieces), out_shape=j...]
  transfers between devices with their start and end apart: 2 -> 2, of which waited for: 0 -> 0; matrix products, arithmetic and copies ran while one was open for 14% -> 13% of each run, Pallas kernels for 0% -> 0%
where the time goes in v10:
time: 166 us; the launch traced here: 165 us
  Pallas kernels  96.7 us (58%)
  local copies, waits for them, and re-layouts  27 us (16%)
  other arithmetic  19.5 us (12%)
  matrix products  15.6 us (9%)
  starting transfers between devices  5.41 us (3%)
    pallas_call x1, Pallas kernels, ring_projection(): pl.pallas_call(functools.partial(ring_kernel, count, pieces), out_shape=j...  69.7 us
    pallas_call x1, Pallas kernels, state_scan(): pl.pallas_call(functools.partial(state_scan_kernel, count), out_shape=jax...  27 us
    unnamed x35, local copies, waits for them, and re-layouts  11.1 us
    dot_general x1, matrix products, local(): jnp.einsum('cgjts,csgjp->ctgjp', mixing, x_blocks, preferred_element_type...  8.92 us
    convert_element_type x2, other arithmetic, conv_silu(): return jax.nn.silu(acc).astype(jnp.bfloat16)  5.9 us
    ppermute x2, starting transfers between devices, passed_along(): return lax.ppermute(x, axis, pairs)  5.41 us
    convert_element_type x1, local copies, waits for them, and re-layouts, local(): skip_gain.reshape(groups, per_group)[:, :, None] * x_blocks  3.41 us
  transfers between devices with their start and end apart: 2, of which 0 were waited for; matrix products, arithmetic and copies ran while one was open for 13% of the time, Pallas kernels for 0%

profile of v10, /device:TPU:24, one launch (start us, length us, event | category | flops | bytes accessed | tf_op | source)
XLA Modules:
  0.0 164.7 jit_solution(17615280382448631918)
XLA Ops:
  0.0 0.9 slice.101
  0.9 0.9 copy.44
  1.8 1.9 %collective-permute-start = (bf16[3,1024]{0,1:T(8,128)(2,1)}, bf16[3,1024]{0,1:T(8,128)(2,1)}, u32[]{:S(2)}, u32[]{:S(2)}) collective-permute-start(bf16[3,1024]{0,1:T(8,128)(2,1)} %copy.44), channel_id=1, source_target_pairs={{0,8},{8,16},{16,24},{24,32},{32,40},{40,48},{48,56},{56,64},{64,7... | collective-permute-start | bytes 18440 | tf_op jit(solution)/shard_map/ppermute | solution.py:24
  3.7 1.1 copy.47
  4.8 3.5 %collective-permute-start.1 = (bf16[3,2,1,128]{3,0,2,1:T(4,128)(2,1)S(1)}, bf16[3,2,1,128]{3,0,2,1:T(4,128)(2,1)S(1)}, u32[]{:S(2)}, u32[]{:S(2)}) collective-permute-start(bf16[3,2,1,128]{3,0,2,1:T(4,128)(2,1)S(1)} %slice.133), channel_id=1, source_target_pairs={{0,8},{8,16},{16,24},{24,32},{32,40},{40,48},{48,56},{56,64},{64,7... | collective-permute-start | bytes 4616 | tf_op jit(solution)/shard_map/ppermute | solution.py:24
  8.3 0.7 exponential_negate_fusion
  9.0 1.0 broadcast_multiply_fusion
  10.1 2.3 %reduce-window.6 = f32[4,16,1,2,128]{4,1,2,3,0:T(8,128)S(1)} reduce-window(f32[4,16,1,2,128]{4,1,2,3,0:T(8,128)S(1)} %copy.51, f32[]{:T(128)} %constant.13.clone.1), window={size=1x1x1x1x128 pad=0_0x0_0x0_0x0_0x127_0}, to_apply=%region_0.1 | reduce-window | flops 2080768 | bytes 131076 | tf_op jit(solution)/shard_map/reduce-window
  13.0 0.8 slice_reduce_fusion
  13.9 1.1 fusion.31
  15.1 0.9 fusion.42
  16.1 0.7 fusion.43
  17.4 0.6 iota_compare_fusion
  18.1 2.6 %copy.45 = bf16[1024,1024]{0,1:T(8,128)(2,1)} copy(bf16[1024,1024]{1,0:T(8,128)(2,1)S(1)} %copy-done.2) | data formatting | bytes 4194304 | tf_op args[0]
  22.1 3.9 %copy.67 = bf16[1024,1024]{0,1:T(8,128)(2,1)} copy(bf16[1024,1024]{1,0:T(8,128)(2,1)} %param.13) | data formatting | bytes 4194304 | tf_op args[2]
  26.6 0.7 multiply_convert_fusion.8
  27.7 0.8 convert_element_type.91
  28.5 5.2 %multiply_convert_fusion.5 = bf16[1024,1024]{0,1:T(8,128)(2,1)S(1)} fusion(bf16[1024,1024]{0,1:T(8,128)(2,1)S(1)} %copy-done.1, bf16[3,1024]{0,1:T(8,128)(2,1)} %collective-permute-done, f32[1024]{0:T(1024)S(1)} %bitcast.82, f32[1024]{0:T(1024)S(1)} %bitcast.83, f32[1024]{0:T(1024)S(1)} %bitcast.81, f32[1024]{0:T(1024)S(1)} %bitcast.80), kind=kLoop, calls=%fused_computation.24 | loop fusion | flops 26214400 | bytes 4216832 | tf_op jit(solution)/shard_map/convert_element_type | solution.py:31
  33.7 3.4 %reshape.338 = f32[4,256,1,16,64]{1,0,4,3,2:T(4,128)} reshape(bf16[1024,1024]{0,1:T(8,128)(2,1)S(1)} %multiply_convert_fusion.5) | data formatting | bytes 6291456 | tf_op jit(solution)/shard_map/convert_element_type | solution.py:386
  37.1 2.8 %reshape.324 = bf16[4,256,16,64]{1,0,3,2:T(4,128)(2,1)} reshape(bf16[1024,1024]{0,1:T(8,128)(2,1)S(1)} %multiply_convert_fusion.5) | data formatting | bytes 4194304 | tf_op jit(solution)/shard_map/reshape.26
  39.9 8.9 %bitcast_add_fusion = f32[4,256,1,16,64]{1,4,3,0,2:T(8,128)} fusion(f32[4,256,1,16,64]{1,0,4,3,2:T(4,128)} %reshape.338, f32[4,16,256]{2,1,0:T(8,128)} %copy.55, f32[4,16,256]{2,1,0:T(8,128)S(1)} %reduce_window_sum.44, f32[4,256,256]{2,1,0:T(8,128)S(1)} %fusion.44, pred[256,256]{1,0:T(8,128)(4,1)} %iota_compare_fusion, f32[16]{0:T(128)S(1)} %copy-done.14, ...), kind=kOutput, calls=%fused_computation.18 | convolution fusion | flops 559939584 | bytes 11731008 | tf_op jit(solution)/shard_map/cgjts,csgjp->ctgjp/dot_general | solution.py:361
  48.9 3.3 %fusion.11 = f32[4,16,64,128]{3,2,1,0:T(8,128)S(1)} fusion(f32[4,256,128]{2,1,0:T(8,128)S(1)} %copy-done.4, f32[4,256,16]{1,2,0:T(8,128)S(1)} %copy-done.5, bf16[4,256,16,64]{1,0,3,2:T(4,128)(2,1)S(1)} %copy-done.3), kind=kOutput, calls=%fused_computation.15 | convolution fusion | flops 272629760 | bytes 4784128 | tf_op jit(solution)/shard_map/csgjp,csgjn->cgjpn/dot_general | solution.py:365
  52.3 1.1 fusion.27
  53.4 0.7 broadcast_in_dim.15.decay_ref
  54.0 27.0 %state_scan.1 = f32[16,64,128]{2,1,0:T(8,128)} custom-call(f32[16,64,128]{2,1,0:T(8,128)} %get-tuple-element.9.state_ref, f32[16,128]{1,0:T(8,128)} %broadcast_in_dim.15.decay_ref), custom_call_target="tpu_custom_call" | custom-call | tf_op jit(solution)/shard_map/state_scan/pallas_call | solution.py:202
  81.1 3.1 %fusion.12 = f32[4,256,1,16,64]{1,4,3,0,2:T(8,128)S(1)} fusion(f32[4,256,1,16,64]{1,4,3,0,2:T(8,128)} %bitcast_add_fusion, bf16[4,256,128,1]{2,1,3,0:T(8,128)(2,1)S(1)} %bitcast.72, f32[4,256,16]{1,2,0:T(8,128)S(1)} %copy.61, f32[1,16,64,128]{3,2,1,0:T(8,128)S(1)} %get-tuple-element.10, f32[1,16,64,128]{3,2,1,0:T(8,128)S(1)} %get-tuple-element.11, ...), kind=kOutput, calls=%fused_computation.17 | convolution fusion | flops 273678336 | bytes 10813712 | tf_op jit(solution)/shard_map/ctgn,cgjpn->ctgjp/dot_general | solution.py:394
  84.2 2.8 %copy.66 = f32[4,256,1,16,64]{1,0,4,3,2:T(4,128)S(1)} copy(f32[4,256,1,16,64]{1,4,3,0,2:T(8,128)S(1)} %fusion.12) | data formatting | bytes 8388608 | tf_op jit(solution)/shard_map/add | solution.py:397
  87.0 1.0 copy.70
  88.6 1.3 multiply_reduce_fusion
  90.0 3.1 %fusion.17.normed_ref = bf16[1024,1024]{1,0:T(8,128)(2,1)} fusion(f32[1024]{0:T(1024)S(1)} %copy-done.7, f32[1024]{0:T(1024)S(1)} %add_rsqrt_fusion, f32[1024,1024]{0,1:T(8,128)S(1)} %bitcast.69, bf16[1024,1024]{0,1:T(8,128)(2,1)S(1)} %copy-done), kind=kLoop, calls=%fused_computation.31 | loop fusion | flops 9437184 | bytes 8396800 | tf_op jit(solution)/shard_map/transpose | solution.py:408
  93.1 69.7 %ring_projection.1 = bf16[1024,256]{1,0:T(8,128)(2,1)} custom-call(bf16[1024,1024]{1,0:T(8,128)(2,1)} %fusion.17.normed_ref, bf16[1024,2048]{1,0:T(8,128)(2,1)} %weight_ref.1), custom_call_target="tpu_custom_call" | custom-call | tf_op jit(solution)/shard_map/ring_projection/pallas_call | solution.py:302
  162.8 1.9 %copy.85 = bf16[1024,256]{1,0:T(8,128)(2,1)} copy(bf16[1024,256]{1,0:T(8,128)(2,1)} %ring_projection.1) | data formatting | bytes 1048576
  (62 shorter events, 4.6 us)
Async XLA Ops:
  0.0 18.1 %copy-start.2 = (bf16[1024,1024]{1,0:T(8,128)(2,1)S(1)}, bf16[1024,1024]{1,0:T(8,128)(2,1)}, u32[]{:S(2)}) copy-start(bf16[1024,1024]{1,0:T(8,128)(2,1)} %param.11) | copy-start | bytes 6291460
  1.8 26.7 %collective-permute-start = (bf16[3,1024]{0,1:T(8,128)(2,1)}, bf16[3,1024]{0,1:T(8,128)(2,1)}, u32[]{:S(2)}, u32[]{:S(2)}) collective-permute-start(bf16[3,1024]{0,1:T(8,128)(2,1)} %copy.44), channel_id=1, source_target_pairs={{0,8},{8,16},{16,24},{24,32},{32,40},{40,48},{48,56},{56,64},{64,7... | collective-permute-start | bytes 18440 | tf_op jit(solution)/shard_map/ppermute | solution.py:24
  4.8 21.8 %collective-permute-start.1 = (bf16[3,2,1,128]{3,0,2,1:T(4,128)(2,1)S(1)}, bf16[3,2,1,128]{3,0,2,1:T(4,128)(2,1)S(1)}, u32[]{:S(2)}, u32[]{:S(2)}) collective-permute-start(bf16[3,2,1,128]{3,0,2,1:T(4,128)(2,1)S(1)} %slice.133), channel_id=1, source_target_pairs={{0,8},{8,16},{16,24},{24,32},{32,40},{40,48},{48,56},{56,64},{64,7... | collective-permute-start | bytes 4616 | tf_op jit(solution)/shard_map/ppermute | solution.py:24
  26.0 2.5 %copy-start.1 = (bf16[1024,1024]{0,1:T(8,128)(2,1)S(1)}, bf16[1024,1024]{0,1:T(8,128)(2,1)}, u32[]{:S(2)}) copy-start(bf16[1024,1024]{0,1:T(8,128)(2,1)} %copy.45) | copy-start | bytes 6291460
  33.7 6.2 %copy-start.14 = (f32[16]{0:T(128)S(1)}, f32[16]{0:T(128)}, u32[]{:S(2)}) copy-start(f32[16]{0:T(128)} %param.17) | copy-start | bytes 196
  39.9 8.9 %copy-start.3 = (bf16[4,256,16,64]{1,0,3,2:T(4,128)(2,1)S(1)}, bf16[4,256,16,64]{1,0,3,2:T(4,128)(2,1)}, u32[]{:S(2)}) copy-start(bf16[4,256,16,64]{1,0,3,2:T(4,128)(2,1)} %reshape.324) | copy-start | bytes 6291460
  39.9 8.9 %copy-start.4 = (f32[4,256,128]{2,1,0:T(8,128)S(1)}, f32[4,256,128]{2,1,0:T(8,128)}, u32[]{:S(2)}) copy-start(f32[4,256,128]{2,1,0:T(8,128)} %convert_element_type.91) | copy-start | bytes 1572868
  39.9 8.9 %copy-start.5 = (f32[4,256,16]{1,2,0:T(8,128)S(1)}, f32[4,256,16]{1,2,0:T(8,128)}, u32[]{:S(2)}) copy-start(f32[4,256,16]{1,2,0:T(8,128)} %copy.64) | copy-start | bytes 196612
  48.9 3.4 %copy-start.9 = (f32[16]{0:T(128)S(1)}, f32[16]{0:T(128)}, u32[]{:S(2)}) copy-start(f32[16]{0:T(128)} %get-tuple-element.5) | copy-start | bytes 196
  48.9 3.4 %copy-start.10 = (f32[16]{0:T(128)S(1)}, f32[16]{0:T(128)}, u32[]{:S(2)}) copy-start(f32[16]{0:T(128)} %get-tuple-element.6) | copy-start | bytes 196
  48.9 3.4 %copy-start.11 = (f32[16]{0:T(128)S(1)}, f32[16]{0:T(128)}, u32[]{:S(2)}) copy-start(f32[16]{0:T(128)} %get-tuple-element.7) | copy-start | bytes 196
  48.9 3.4 %copy-start.12 = (f32[16]{0:T(128)S(1)}, f32[16]{0:T(128)}, u32[]{:S(2)}) copy-start(f32[16]{0:T(128)} %get-tuple-element.8) | copy-start | bytes 196
  52.2 1.1 copy-start.8
  52.2 28.8 %copy-start.6 = (f32[4,16]{1,0:T(4,128)S(1)}, f32[4,16]{1,0:T(4,128)}, u32[]{:S(2)}) copy-start(f32[4,16]{1,0:T(4,128)} %subtract_exponential_fusion) | copy-start | bytes 772
  52.2 28.8 %copy-start.13 = (f32[4]{0:T(128)S(1)}, f32[4]{0:T(128)}, u32[]{:S(2)}) copy-start(f32[4]{0:T(128)} %pad.clone) | copy-start | bytes 52
  87.0 1.6 copy-start
  88.1 1.9 %copy-start.7 = (f32[1024]{0:T(1024)S(1)}, f32[1024]{0:T(1024)}, u32[]{:S(2)}) copy-start(f32[1024]{0:T(1024)} %param.20) | copy-start | bytes 12292

commit v11 on v10

--- a/solution.py
+++ b/solution.py
@@ -294,7 +294,7 @@
 
 def ring_projection(normed, weight):
     count = lax.axis_size("chan")
-    pieces = 8
+    pieces = 2
     tokens = normed.shape[1]
     width = weight.shape[1] // count
     rows = tokens // (2 * pieces)

time: 166 us -> 149 us (0.90)
  Pallas kernels: 96.7 us -> 80.3 us
    pallas_call x1, Pallas kernels: 69.7 us -> 53.2 us  [ring_projection(): pl.pallas_call(functools.partial(ring_kernel, count, pieces), out_shape=j...]
  transfers between devices with their start and end apart: 2 -> 2, of which waited for: 0 -> 0; matrix products, arithmetic and copies ran while one was open for 13% -> 14% of each run, Pallas kernels for 0% -> 0%
where the time goes in v11:
time: 149 us; the launch traced here: 148 us
  Pallas kernels  80.3 us (54%)
  local copies, waits for them, and re-layouts  27 us (18%)
  other arithmetic  19.3 us (13%)
  matrix products  15.6 us (10%)
  starting transfers between devices  5.41 us (4%)
    pallas_call x1, Pallas kernels, ring_projection(): pl.pallas_call(functools.partial(ring_kernel, count, pieces), out_shape=j...  53.2 us
    pallas_call x1, Pallas kernels, state_scan(): pl.pallas_call(functools.partial(state_scan_kernel, count), out_shape=jax...  27 us
    unnamed x35, local copies, waits for them, and re-layouts  11.1 us
    dot_general x1, matrix products, local(): jnp.einsum('cgjts,csgjp->ctgjp', mixing, x_blocks, preferred_element_type...  8.92 us
    convert_element_type x2, other arithmetic, conv_silu(): return jax.nn.silu(acc).astype(jnp.bfloat16)  5.9 us
    ppermute x2, starting transfers between devices, passed_along(): return lax.ppermute(x, axis, pairs)  5.41 us
    convert_element_type x1, local copies, waits for them, and re-layouts, local(): skip_gain.reshape(groups, per_group)[:, :, None] * x_blocks  3.41 us
    dot_general x1, matrix products, local(): jnp.einsum('csgjp,csgjn->cgjpn', x_blocks, weighted, preferred_element_ty...  3.29 us
  transfers between devices with their start and end apart: 2, of which 0 were waited for; matrix products, arithmetic and copies ran while one was open for 14% of the time, Pallas kernels for 0%

profile of v11, /device:TPU:24, one launch (start us, length us, event | category | flops | bytes accessed | tf_op | source)
XLA Modules:
  0.0 148.0 jit_solution(2103588974693098912)
XLA Ops:
  0.0 0.9 slice.101
  0.9 0.9 copy.44
  1.8 1.9 %collective-permute-start = (bf16[3,1024]{0,1:T(8,128)(2,1)}, bf16[3,1024]{0,1:T(8,128)(2,1)}, u32[]{:S(2)}, u32[]{:S(2)}) collective-permute-start(bf16[3,1024]{0,1:T(8,128)(2,1)} %copy.44), channel_id=1, source_target_pairs={{0,8},{8,16},{16,24},{24,32},{32,40},{40,48},{48,56},{56,64},{64,7... | collective-permute-start | bytes 18440 | tf_op jit(solution)/shard_map/ppermute | solution.py:24
  3.7 1.1 copy.47
  4.8 3.5 %collective-permute-start.1 = (bf16[3,2,1,128]{3,0,2,1:T(4,128)(2,1)S(1)}, bf16[3,2,1,128]{3,0,2,1:T(4,128)(2,1)S(1)}, u32[]{:S(2)}, u32[]{:S(2)}) collective-permute-start(bf16[3,2,1,128]{3,0,2,1:T(4,128)(2,1)S(1)} %slice.133), channel_id=1, source_target_pairs={{0,8},{8,16},{16,24},{24,32},{32,40},{40,48},{48,56},{56,64},{64,7... | collective-permute-start | bytes 4616 | tf_op jit(solution)/shard_map/ppermute | solution.py:24
  8.3 0.7 exponential_negate_fusion
  9.0 1.0 broadcast_multiply_fusion
  10.1 2.3 %reduce-window.6 = f32[4,16,1,2,128]{4,1,2,3,0:T(8,128)S(1)} reduce-window(f32[4,16,1,2,128]{4,1,2,3,0:T(8,128)S(1)} %copy.51, f32[]{:T(128)} %constant.13.clone.1), window={size=1x1x1x1x128 pad=0_0x0_0x0_0x0_0x127_0}, to_apply=%region_0.1 | reduce-window | flops 2080768 | bytes 131076 | tf_op jit(solution)/shard_map/reduce-window
  13.0 0.8 slice_reduce_fusion
  13.9 1.1 fusion.31
  15.1 0.9 fusion.42
  16.1 0.7 fusion.43
  17.4 0.6 iota_compare_fusion
  18.1 2.6 %copy.45 = bf16[1024,1024]{0,1:T(8,128)(2,1)} copy(bf16[1024,1024]{1,0:T(8,128)(2,1)S(1)} %copy-done.2) | data formatting | bytes 4194304 | tf_op args[0]
  22.1 3.9 %copy.67 = bf16[1024,1024]{0,1:T(8,128)(2,1)} copy(bf16[1024,1024]{1,0:T(8,128)(2,1)} %param.13) | data formatting | bytes 4194304 | tf_op args[2]
  26.6 0.7 multiply_convert_fusion.8
  27.7 0.8 convert_element_type.91
  28.5 5.2 %multiply_convert_fusion.5 = bf16[1024,1024]{0,1:T(8,128)(2,1)S(1)} fusion(bf16[1024,1024]{0,1:T(8,128)(2,1)S(1)} %copy-done.1, bf16[3,1024]{0,1:T(8,128)(2,1)} %collective-permute-done, f32[1024]{0:T(1024)S(1)} %bitcast.82, f32[1024]{0:T(1024)S(1)} %bitcast.83, f32[1024]{0:T(1024)S(1)} %bitcast.81, f32[1024]{0:T(1024)S(1)} %bitcast.80), kind=kLoop, calls=%fused_computation.24 | loop fusion | flops 26214400 | bytes 4216832 | tf_op jit(solution)/shard_map/convert_element_type | solution.py:31
  33.7 3.4 %reshape.338 = f32[4,256,1,16,64]{1,0,4,3,2:T(4,128)} reshape(bf16[1024,1024]{0,1:T(8,128)(2,1)S(1)} %multiply_convert_fusion.5) | data formatting | bytes 6291456 | tf_op jit(solution)/shard_map/convert_element_type | solution.py:386
  37.1 2.8 %reshape.324 = bf16[4,256,16,64]{1,0,3,2:T(4,128)(2,1)} reshape(bf16[1024,1024]{0,1:T(8,128)(2,1)S(1)} %multiply_convert_fusion.5) | data formatting | bytes 4194304 | tf_op jit(solution)/shard_map/reshape.26
  39.9 8.9 %bitcast_add_fusion = f32[4,256,1,16,64]{1,4,3,0,2:T(8,128)} fusion(f32[4,256,1,16,64]{1,0,4,3,2:T(4,128)} %reshape.338, f32[4,16,256]{2,1,0:T(8,128)} %copy.55, f32[4,16,256]{2,1,0:T(8,128)S(1)} %reduce_window_sum.44, f32[4,256,256]{2,1,0:T(8,128)S(1)} %fusion.44, pred[256,256]{1,0:T(8,128)(4,1)} %iota_compare_fusion, f32[16]{0:T(128)S(1)} %copy-done.14, ...), kind=kOutput, calls=%fused_computation.18 | convolution fusion | flops 559939584 | bytes 11731008 | tf_op jit(solution)/shard_map/cgjts,csgjp->ctgjp/dot_general | solution.py:361
  48.9 3.3 %fusion.11 = f32[4,16,64,128]{3,2,1,0:T(8,128)S(1)} fusion(f32[4,256,128]{2,1,0:T(8,128)S(1)} %copy-done.4, f32[4,256,16]{1,2,0:T(8,128)S(1)} %copy-done.5, bf16[4,256,16,64]{1,0,3,2:T(4,128)(2,1)S(1)} %copy-done.3), kind=kOutput, calls=%fused_computation.15 | convolution fusion | flops 272629760 | bytes 4784128 | tf_op jit(solution)/shard_map/csgjp,csgjn->cgjpn/dot_general | solution.py:365
  52.3 1.1 fusion.27
  53.4 0.7 broadcast_in_dim.15.decay_ref
  54.0 27.0 %state_scan.1 = f32[16,64,128]{2,1,0:T(8,128)} custom-call(f32[16,64,128]{2,1,0:T(8,128)} %get-tuple-element.9.state_ref, f32[16,128]{1,0:T(8,128)} %broadcast_in_dim.15.decay_ref), custom_call_target="tpu_custom_call" | custom-call | tf_op jit(solution)/shard_map/state_scan/pallas_call | solution.py:202
  81.1 3.1 %fusion.12 = f32[4,256,1,16,64]{1,4,3,0,2:T(8,128)S(1)} fusion(f32[4,256,1,16,64]{1,4,3,0,2:T(8,128)} %bitcast_add_fusion, bf16[4,256,128,1]{2,1,3,0:T(8,128)(2,1)S(1)} %bitcast.72, f32[4,256,16]{1,2,0:T(8,128)S(1)} %copy.61, f32[1,16,64,128]{3,2,1,0:T(8,128)S(1)} %get-tuple-element.10, f32[1,16,64,128]{3,2,1,0:T(8,128)S(1)} %get-tuple-element.11, ...), kind=kOutput, calls=%fused_computation.17 | convolution fusion | flops 273678336 | bytes 10813712 | tf_op jit(solution)/shard_map/ctgn,cgjpn->ctgjp/dot_general | solution.py:394
  84.2 2.8 %copy.66 = f32[4,256,1,16,64]{1,0,4,3,2:T(4,128)S(1)} copy(f32[4,256,1,16,64]{1,4,3,0,2:T(8,128)S(1)} %fusion.12) | data formatting | bytes 8388608 | tf_op jit(solution)/shard_map/add | solution.py:397
  87.0 1.0 copy.70
  88.6 1.3 multiply_reduce_fusion
  90.0 2.9 %fusion.17.normed_ref = bf16[1024,1024]{1,0:T(8,128)(2,1)} fusion(f32[1024]{0:T(1024)S(1)} %copy-done.7, f32[1024]{0:T(1024)S(1)} %add_rsqrt_fusion, f32[1024,1024]{0,1:T(8,128)S(1)} %bitcast.69, bf16[1024,1024]{0,1:T(8,128)(2,1)S(1)} %copy-done), kind=kLoop, calls=%fused_computation.31 | loop fusion | flops 9437184 | bytes 8396800 | tf_op jit(solution)/shard_map/transpose | solution.py:408
  92.9 53.2 %ring_projection.1 = bf16[1024,256]{1,0:T(8,128)(2,1)} custom-call(bf16[1024,1024]{1,0:T(8,128)(2,1)} %fusion.17.normed_ref, bf16[1024,2048]{1,0:T(8,128)(2,1)} %weight_ref.1), custom_call_target="tpu_custom_call" | custom-call | tf_op jit(solution)/shard_map/ring_projection/pallas_call | solution.py:302
  146.1 1.9 %copy.85 = bf16[1024,256]{1,0:T(8,128)(2,1)} copy(bf16[1024,256]{1,0:T(8,128)(2,1)} %ring_projection.1) | data formatting | bytes 1048576
  (62 shorter events, 4.6 us)
Async XLA Ops:
  0.0 18.1 %copy-start.2 = (bf16[1024,1024]{1,0:T(8,128)(2,1)S(1)}, bf16[1024,1024]{1,0:T(8,128)(2,1)}, u32[]{:S(2)}) copy-start(bf16[1024,1024]{1,0:T(8,128)(2,1)} %param.11) | copy-start | bytes 6291460
  1.8 26.7 %collective-permute-start = (bf16[3,1024]{0,1:T(8,128)(2,1)}, bf16[3,1024]{0,1:T(8,128)(2,1)}, u32[]{:S(2)}, u32[]{:S(2)}) collective-permute-start(bf16[3,1024]{0,1:T(8,128)(2,1)} %copy.44), channel_id=1, source_target_pairs={{0,8},{8,16},{16,24},{24,32},{32,40},{40,48},{48,56},{56,64},{64,7... | collective-permute-start | bytes 18440 | tf_op jit(solution)/shard_map/ppermute | solution.py:24
  4.8 21.8 %collective-permute-start.1 = (bf16[3,2,1,128]{3,0,2,1:T(4,128)(2,1)S(1)}, bf16[3,2,1,128]{3,0,2,1:T(4,128)(2,1)S(1)}, u32[]{:S(2)}, u32[]{:S(2)}) collective-permute-start(bf16[3,2,1,128]{3,0,2,1:T(4,128)(2,1)S(1)} %slice.133), channel_id=1, source_target_pairs={{0,8},{8,16},{16,24},{24,32},{32,40},{40,48},{48,56},{56,64},{64,7... | collective-permute-start | bytes 4616 | tf_op jit(solution)/shard_map/ppermute | solution.py:24
  26.0 2.5 %copy-start.1 = (bf16[1024,1024]{0,1:T(8,128)(2,1)S(1)}, bf16[1024,1024]{0,1:T(8,128)(2,1)}, u32[]{:S(2)}) copy-start(bf16[1024,1024]{0,1:T(8,128)(2,1)} %copy.45) | copy-start | bytes 6291460
  33.7 6.2 %copy-start.14 = (f32[16]{0:T(128)S(1)}, f32[16]{0:T(128)}, u32[]{:S(2)}) copy-start(f32[16]{0:T(128)} %param.17) | copy-start | bytes 196
  39.9 8.9 %copy-start.3 = (bf16[4,256,16,64]{1,0,3,2:T(4,128)(2,1)S(1)}, bf16[4,256,16,64]{1,0,3,2:T(4,128)(2,1)}, u32[]{:S(2)}) copy-start(bf16[4,256,16,64]{1,0,3,2:T(4,128)(2,1)} %reshape.324) | copy-start | bytes 6291460
  39.9 8.9 %copy-start.4 = (f32[4,256,128]{2,1,0:T(8,128)S(1)}, f32[4,256,128]{2,1,0:T(8,128)}, u32[]{:S(2)}) copy-start(f32[4,256,128]{2,1,0:T(8,128)} %convert_element_type.91) | copy-start | bytes 1572868
  39.9 8.9 %copy-start.5 = (f32[4,256,16]{1,2,0:T(8,128)S(1)}, f32[4,256,16]{1,2,0:T(8,128)}, u32[]{:S(2)}) copy-start(f32[4,256,16]{1,2,0:T(8,128)} %copy.64) | copy-start | bytes 196612
  48.9 3.4 %copy-start.9 = (f32[16]{0:T(128)S(1)}, f32[16]{0:T(128)}, u32[]{:S(2)}) copy-start(f32[16]{0:T(128)} %get-tuple-element.5) | copy-start | bytes 196
  48.9 3.4 %copy-start.10 = (f32[16]{0:T(128)S(1)}, f32[16]{0:T(128)}, u32[]{:S(2)}) copy-start(f32[16]{0:T(128)} %get-tuple-element.6) | copy-start | bytes 196
  48.9 3.4 %copy-start.11 = (f32[16]{0:T(128)S(1)}, f32[16]{0:T(128)}, u32[]{:S(2)}) copy-start(f32[16]{0:T(128)} %get-tuple-element.7) | copy-start | bytes 196
  48.9 3.4 %copy-start.12 = (f32[16]{0:T(128)S(1)}, f32[16]{0:T(128)}, u32[]{:S(2)}) copy-start(f32[16]{0:T(128)} %get-tuple-element.8) | copy-start | bytes 196
  52.2 1.1 copy-start.8
  52.2 28.8 %copy-start.6 = (f32[4,16]{1,0:T(4,128)S(1)}, f32[4,16]{1,0:T(4,128)}, u32[]{:S(2)}) copy-start(f32[4,16]{1,0:T(4,128)} %subtract_exponential_fusion) | copy-start | bytes 772
  52.2 28.8 %copy-start.13 = (f32[4]{0:T(128)S(1)}, f32[4]{0:T(128)}, u32[]{:S(2)}) copy-start(f32[4]{0:T(128)} %pad.clone) | copy-start | bytes 52
  87.0 1.6 %copy-start = (bf16[1024,1024]{0,1:T(8,128)(2,1)S(1)}, bf16[1024,1024]{0,1:T(8,128)(2,1)}, u32[]{:S(2)}) copy-start(bf16[1024,1024]{0,1:T(8,128)(2,1)} %copy.67) | copy-start | bytes 6291460
  88.1 1.9 %copy-start.7 = (f32[1024]{0:T(1024)S(1)}, f32[1024]{0:T(1024)}, u32[]{:S(2)}) copy-start(f32[1024]{0:T(1024)} %param.20) | copy-start | bytes 12292

commit v12 on v11

--- a/solution.py
+++ b/solution.py
@@ -382,9 +382,7 @@
         jnp.exp(leading)[..., None, None] * entering[None] + jnp.stack(local_in, axis=0)
     ).astype(jnp.bfloat16)
     width = per_group * HEAD_DIM
-    y_pre = lax.optimization_barrier(
-        y_local + skip_gain.reshape(groups, per_group)[:, :, None] * x_blocks
-    )
+    y_pre = y_local + skip_gain.reshape(groups, per_group)[:, :, None] * x_blocks
     chunk_count = 1
     per_chunk = block_count // chunk_count
     outs = []

time: 149 us -> 151 us (1.013)
  local copies, waits for them, and re-layouts: 27 us -> 30 us
  matrix products: 15.6 us -> 13.4 us
    dot_general x1, matrix products: 8.92 us -> 5.29 us  [local(): jnp.einsum('cgjts,csgjp->ctgjp', mixing, x_blocks, preferred_element_type...]
    unnamed x35 -> x57, local copies, waits for them, and re-layouts: 11.1 us -> 11.9 us
  transfers between devices with their start and end apart: 2 -> 2, of which waited for: 0 -> 0; matrix products, arithmetic and copies ran while one was open for 14% -> 18% of each run, Pallas kernels for 0% -> 0%
where the time goes in v12:
time: 151 us; the launch traced here: 150 us
  Pallas kernels  80.3 us (53%)
  local copies, waits for them, and re-layouts  30 us (20%)
  other arithmetic  20.7 us (14%)
  matrix products  13.4 us (9%)
  starting transfers between devices  5.41 us (4%)
    pallas_call x1, Pallas kernels, ring_projection(): pl.pallas_call(functools.partial(ring_kernel, count, pieces), out_shape=j...  53.2 us
    pallas_call x1, Pallas kernels, state_scan(): pl.pallas_call(functools.partial(state_scan_kernel, count), out_shape=jax...  27 us
    unnamed x57, local copies, waits for them, and re-layouts  11.9 us
    convert_element_type x2, other arithmetic, conv_silu(): return jax.nn.silu(acc).astype(jnp.bfloat16)  5.74 us
    ppermute x2, starting transfers between devices, passed_along(): return lax.ppermute(x, axis, pairs)  5.41 us
    dot_general x1, matrix products, local(): jnp.einsum('cgjts,csgjp->ctgjp', mixing, x_blocks, preferred_element_type...  5.29 us
    dot_general x1, matrix products, local(): jnp.einsum('csgjp,csgjn->cgjpn', x_blocks, weighted, preferred_element_ty...  4.64 us
    another operation x9, local copies, waits for them, and re-layouts  3.95 us
  transfers between devices with their start and end apart: 2, of which 0 were waited for; matrix products, arithmetic and copies ran while one was open for 18% of the time, Pallas kernels for 0%

profile of v12, /device:TPU:24, one launch (start us, length us, event | category | flops | bytes accessed | tf_op | source)
XLA Modules:
  0.0 150.2 jit_solution(1221551614546139557)
XLA Ops:
  0.0 1.3 copy.47
  1.9 1.9 %collective-permute-start.1 = (bf16[3,2,1,128]{3,0,2,1:T(4,128)(2,1)}, bf16[3,2,1,128]{3,0,2,1:T(4,128)(2,1)}, u32[]{:S(2)}, u32[]{:S(2)}) collective-permute-start(bf16[3,2,1,128]{3,0,2,1:T(4,128)(2,1)} %slice.133), channel_id=1, source_target_pairs={{0,8},{8,16},{16,24},{24,32},{32,40},{40,48},{48,56},{56,64},{64,7... | collective-permute-start | bytes 4616 | tf_op jit(solution)/shard_map/ppermute | solution.py:24
  3.8 0.7 slice.101
  4.7 3.5 %collective-permute-start = (bf16[3,1024]{0,1:T(8,128)(2,1)S(1)}, bf16[3,1024]{0,1:T(8,128)(2,1)S(1)}, u32[]{:S(2)}, u32[]{:S(2)}) collective-permute-start(bf16[3,1024]{0,1:T(8,128)(2,1)S(1)} %copy.44), channel_id=1, source_target_pairs={{0,8},{8,16},{16,24},{24,32},{32,40},{40,48},{48,56},{56,64},{64,7... | collective-permute-start | bytes 18440 | tf_op jit(solution)/shard_map/ppermute | solution.py:24
  8.2 0.7 exponential_negate_fusion
  8.9 1.0 broadcast_multiply_fusion
  10.0 2.3 %reduce-window.6 = f32[4,16,1,2,128]{4,1,2,3,0:T(8,128)S(1)} reduce-window(f32[4,16,1,2,128]{4,1,2,3,0:T(8,128)S(1)} %copy.51, f32[]{:T(128)} %constant.13.clone.1), window={size=1x1x1x1x128 pad=0_0x0_0x0_0x0_0x127_0}, to_apply=%region_0.1 | reduce-window | flops 2080768 | bytes 131076 | tf_op jit(solution)/shard_map/reduce-window
  12.8 0.7 reshape.340
  13.5 0.9 exponential_bitcast_fusion
  14.4 0.8 slice_reduce_fusion
  15.2 1.0 fusion.32
  17.1 1.3 fusion.44
  18.4 1.5 fusion.43
  19.9 1.3 subtract_exponential_fusion
  22.0 2.5 %copy.45 = bf16[1024,1024]{0,1:T(8,128)(2,1)} copy(bf16[1024,1024]{1,0:T(8,128)(2,1)S(1)} %copy-done.3) | data formatting | bytes 4194304 | tf_op args[0]
  26.6 3.9 %copy.67 = bf16[1024,1024]{0,1:T(8,128)(2,1)} copy(bf16[1024,1024]{1,0:T(8,128)(2,1)} %param.13) | data formatting | bytes 4194304 | tf_op args[2]
  31.1 1.5 multiply_convert_fusion.8
  32.6 1.4 fusion.45
  34.1 4.3 %multiply_convert_fusion.5 = bf16[1024,1024]{0,1:T(8,128)(2,1)S(1)} fusion(bf16[1024,1024]{0,1:T(8,128)(2,1)S(1)} %copy-done.1, bf16[3,1024]{0,1:T(8,128)(2,1)S(1)} %collective-permute-done, f32[1024]{0:T(1024)S(1)} %bitcast.84, f32[1024]{0:T(1024)S(1)} %bitcast.85, f32[1024]{0:T(1024)S(1)} %bitcast.83, f32[1024]{0:T(1024)S(1)} %bitcast.82), kind=kLoop, calls=%fused_computation.24 | loop fusion | flops 26214400 | bytes 4216832 | tf_op jit(solution)/shard_map/convert_element_type | solution.py:31
  38.3 2.8 %reshape.324 = bf16[4,256,16,64]{1,0,3,2:T(4,128)(2,1)} reshape(bf16[1024,1024]{0,1:T(8,128)(2,1)S(1)} %multiply_convert_fusion.5) | data formatting | bytes 4194304 | tf_op jit(solution)/shard_map/reshape.26
  41.2 3.4 %reshape.338 = f32[4,256,1,16,64]{1,0,4,3,2:T(4,128)} reshape(bf16[1024,1024]{0,1:T(8,128)(2,1)S(1)} %multiply_convert_fusion.5) | data formatting | bytes 6291456 | tf_op jit(solution)/shard_map/convert_element_type | solution.py:385
  44.6 4.6 %fusion.11 = f32[4,16,64,128]{3,2,1,0:T(8,128)S(1)} fusion(f32[4,256,128]{2,1,0:T(8,128)S(1)} %convert_element_type.91, f32[4,256,16]{1,2,0:T(8,128)S(1)} %copy-done.9, bf16[4,256,16,64]{1,0,3,2:T(4,128)(2,1)} %reshape.324), kind=kOutput, calls=%fused_computation.15 | convolution fusion | flops 272629760 | bytes 4784128 | tf_op jit(solution)/shard_map/csgjp,csgjn->cgjpn/dot_general | solution.py:365
  49.3 1.1 fusion.28
  51.1 27.0 %state_scan.1 = f32[16,64,128]{2,1,0:T(8,128)} custom-call(f32[16,64,128]{2,1,0:T(8,128)} %get-tuple-element.11.state_ref, f32[16,128]{1,0:T(8,128)} %broadcast_in_dim.15.decay_ref), custom_call_target="tpu_custom_call" | custom-call | tf_op jit(solution)/shard_map/state_scan/pallas_call | solution.py:202
  78.2 2.1 %fusion.21 = f32[4,16,64,256]{3,2,1,0:T(8,128)S(1)} fusion(bf16[4,256,128,1]{2,1,3,0:T(8,128)(2,1)S(1)} %bitcast.74, f32[1,16,64,128]{3,2,1,0:T(8,128)S(1)} %get-tuple-element.12, f32[1,16,64,128]{3,2,1,0:T(8,128)S(1)} %get-tuple-element.13, f32[1,16,64,128]{3,2,1,0:T(8,128)} %get-tuple-element.14, f32[4]{0:T(128)S(1)} %copy-done.24, ...), kind=kOutput, calls=%fused_computation.37 | convolution fusion | flops 271581184 | bytes 6553872 | tf_op jit(solution)/shard_map/ctgn,cgjpn->ctgjp/dot_general | solution.py:392
  80.9 5.3 %fusion.12 = f32[4,256,1,16,64]{1,4,3,0,2:T(8,128)S(1)} fusion(f32[4,16,64,256]{3,2,1,0:T(8,128)S(1)} %fusion.21, f32[4,256,1,16,64]{1,0,4,3,2:T(4,128)S(1)} %copy-done.2, f32[4,16,256]{2,1,0:T(8,128)S(1)} %copy-done.7, f32[4,16,256]{2,1,0:T(8,128)S(1)} %reduce_window_sum.44, f32[4,256,256]{2,1,0:T(8,128)S(1)} %copy-done.5, ...), kind=kOutput, calls=%fused_computation.17 | convolution fusion | flops 562036736 | bytes 15990848 | tf_op jit(solution)/shard_map/cgjts,csgjp->ctgjp/dot_general | solution.py:361
  86.2 2.8 %copy.66 = f32[4,256,1,16,64]{1,0,4,3,2:T(4,128)S(1)} copy(f32[4,256,1,16,64]{1,4,3,0,2:T(8,128)S(1)} %fusion.12) | data formatting | bytes 8388608 | tf_op jit(solution)/shard_map/add | solution.py:395
  89.0 1.0 copy.70
  90.6 1.3 multiply_reduce_fusion
  92.0 3.1 %fusion.17.normed_ref = bf16[1024,1024]{1,0:T(8,128)(2,1)} fusion(f32[1024]{0:T(1024)S(1)} %copy-done.14, f32[1024]{0:T(1024)S(1)} %add_rsqrt_fusion, f32[1024,1024]{0,1:T(8,128)S(1)} %bitcast.71, bf16[1024,1024]{0,1:T(8,128)(2,1)S(1)} %copy-done), kind=kLoop, calls=%fused_computation.31 | loop fusion | flops 9437184 | bytes 8396800 | tf_op jit(solution)/shard_map/transpose | solution.py:406
  95.1 53.2 %ring_projection.1 = bf16[1024,256]{1,0:T(8,128)(2,1)} custom-call(bf16[1024,1024]{1,0:T(8,128)(2,1)} %fusion.17.normed_ref, bf16[1024,2048]{1,0:T(8,128)(2,1)} %weight_ref.1), custom_call_target="tpu_custom_call" | custom-call | tf_op jit(solution)/shard_map/ring_projection/pallas_call | solution.py:302
  148.4 1.9 %copy.85 = bf16[1024,256]{1,0:T(8,128)(2,1)} copy(bf16[1024,256]{1,0:T(8,128)(2,1)} %ring_projection.1) | data formatting | bytes 1048576
  (84 shorter events, 7.5 us)
Async XLA Ops:
  0.0 22.0 %copy-start.3 = (bf16[1024,1024]{1,0:T(8,128)(2,1)S(1)}, bf16[1024,1024]{1,0:T(8,128)(2,1)}, u32[]{:S(2)}) copy-start(bf16[1024,1024]{1,0:T(8,128)(2,1)} %param.11) | copy-start | bytes 6291460
  1.9 29.2 %collective-permute-start.1 = (bf16[3,2,1,128]{3,0,2,1:T(4,128)(2,1)}, bf16[3,2,1,128]{3,0,2,1:T(4,128)(2,1)}, u32[]{:S(2)}, u32[]{:S(2)}) collective-permute-start(bf16[3,2,1,128]{3,0,2,1:T(4,128)(2,1)} %slice.133), channel_id=1, source_target_pairs={{0,8},{8,16},{16,24},{24,32},{32,40},{40,48},{48,56},{56,64},{64,7... | collective-permute-start | bytes 4616 | tf_op jit(solution)/shard_map/ppermute | solution.py:24
  4.7 29.3 %collective-permute-start = (bf16[3,1024]{0,1:T(8,128)(2,1)S(1)}, bf16[3,1024]{0,1:T(8,128)(2,1)S(1)}, u32[]{:S(2)}, u32[]{:S(2)}) collective-permute-start(bf16[3,1024]{0,1:T(8,128)(2,1)S(1)} %copy.44), channel_id=1, source_target_pairs={{0,8},{8,16},{16,24},{24,32},{32,40},{40,48},{48,56},{56,64},{64,7... | collective-permute-start | bytes 18440 | tf_op jit(solution)/shard_map/ppermute | solution.py:24
  24.5 6.5 %copy-start.15 = (f32[1,2,1,128]{3,2,1,0:T(1,128)S(1)}, f32[1,2,1,128]{3,2,1,0:T(1,128)}, u32[]{:S(2)}) copy-start(f32[1,2,1,128]{3,2,1,0:T(1,128)} %get-tuple-element.25) | copy-start | bytes 3076
  24.5 6.6 %copy-start.16 = (f32[1,2,1,128]{3,2,1,0:T(1,128)S(1)}, f32[1,2,1,128]{3,2,1,0:T(1,128)}, u32[]{:S(2)}) copy-start(f32[1,2,1,128]{3,2,1,0:T(1,128)} %get-tuple-element.26) | copy-start | bytes 3076
  24.5 6.6 %copy-start.17 = (f32[1,2,1,128]{3,2,1,0:T(1,128)S(1)}, f32[1,2,1,128]{3,2,1,0:T(1,128)}, u32[]{:S(2)}) copy-start(f32[1,2,1,128]{3,2,1,0:T(1,128)} %get-tuple-element.27) | copy-start | bytes 3076
  24.5 6.6 %copy-start.18 = (f32[1,2,1,128]{3,2,1,0:T(1,128)S(1)}, f32[1,2,1,128]{3,2,1,0:T(1,128)}, u32[]{:S(2)}) copy-start(f32[1,2,1,128]{3,2,1,0:T(1,128)} %get-tuple-element.28) | copy-start | bytes 3076
  26.6 7.5 %copy-start.10 = (f32[1,1024]{1,0:T(1,128)S(1)}, f32[1,1024]{1,0:T(1,128)}, u32[]{:S(2)}) copy-start(f32[1,1024]{1,0:T(1,128)} %get-tuple-element.22) | copy-start | bytes 12292
  26.6 7.5 %copy-start.11 = (f32[1,1024]{1,0:T(1,128)S(1)}, f32[1,1024]{1,0:T(1,128)}, u32[]{:S(2)}) copy-start(f32[1,1024]{1,0:T(1,128)} %get-tuple-element.23) | copy-start | bytes 12292
  26.6 7.5 %copy-start.12 = (f32[1,1024]{1,0:T(1,128)S(1)}, f32[1,1024]{1,0:T(1,128)}, u32[]{:S(2)}) copy-start(f32[1,1024]{1,0:T(1,128)} %get-tuple-element.24) | copy-start | bytes 12292
  30.5 3.6 %copy-start.1 = (bf16[1024,1024]{0,1:T(8,128)(2,1)S(1)}, bf16[1024,1024]{0,1:T(8,128)(2,1)}, u32[]{:S(2)}) copy-start(bf16[1024,1024]{0,1:T(8,128)(2,1)} %copy.45) | copy-start | bytes 6291460
  38.3 6.3 %copy-start.9 = (f32[4,256,16]{1,2,0:T(8,128)S(1)}, f32[4,256,16]{1,2,0:T(8,128)}, u32[]{:S(2)}) copy-start(f32[4,256,16]{1,2,0:T(8,128)} %copy.64) | copy-start | bytes 196612
  44.6 4.7 %copy-start.20 = (f32[16]{0:T(128)S(1)}, f32[16]{0:T(128)}, u32[]{:S(2)}) copy-start(f32[16]{0:T(128)} %get-tuple-element.5) | copy-start | bytes 196
  44.6 4.7 %copy-start.21 = (f32[16]{0:T(128)S(1)}, f32[16]{0:T(128)}, u32[]{:S(2)}) copy-start(f32[16]{0:T(128)} %get-tuple-element.6) | copy-start | bytes 196
  44.6 4.7 %copy-start.22 = (f32[16]{0:T(128)S(1)}, f32[16]{0:T(128)}, u32[]{:S(2)}) copy-start(f32[16]{0:T(128)} %get-tuple-element.7) | copy-start | bytes 196
  44.6 4.7 %copy-start.23 = (f32[16]{0:T(128)S(1)}, f32[16]{0:T(128)}, u32[]{:S(2)}) copy-start(f32[16]{0:T(128)} %get-tuple-element.8) | copy-start | bytes 196
  49.2 1.2 copy-start.19
  49.2 28.9 %copy-start.13 = (f32[4,16]{1,0:T(4,128)S(1)}, f32[4,16]{1,0:T(4,128)}, u32[]{:S(2)}) copy-start(f32[4,16]{1,0:T(4,128)} %subtract_exponential_fusion) | copy-start | bytes 772
  49.3 28.9 %copy-start.24 = (f32[4]{0:T(128)S(1)}, f32[4]{0:T(128)}, u32[]{:S(2)}) copy-start(f32[4]{0:T(128)} %pad.clone) | copy-start | bytes 52
  50.4 29.9 %copy-start.4 = (bf16[4,256,16,64]{1,0,3,2:T(4,128)(2,1)S(1)}, bf16[4,256,16,64]{1,0,3,2:T(4,128)(2,1)}, u32[]{:S(2)}) copy-start(bf16[4,256,16,64]{1,0,3,2:T(4,128)(2,1)} %reshape.324) | copy-start | bytes 6291460
  50.4 29.9 %copy-start.6 = (pred[256,256]{1,0:T(8,128)(4,1)S(1)}, pred[256,256]{1,0:T(8,128)(4,1)}, u32[]{:S(2)}) copy-start(pred[256,256]{1,0:T(8,128)(4,1)} %iota_compare_fusion) | copy-start | bytes 196612
  50.4 29.9 %copy-start.25 = (f32[16]{0:T(128)S(1)}, f32[16]{0:T(128)}, u32[]{:S(2)}) copy-start(f32[16]{0:T(128)} %param.17) | copy-start | bytes 196
  78.1 2.5 %copy-start.2 = (f32[4,256,1,16,64]{1,0,4,3,2:T(4,128)S(1)}, f32[4,256,1,16,64]{1,0,4,3,2:T(4,128)}, u32[]{:S(2)}) copy-start(f32[4,256,1,16,64]{1,0,4,3,2:T(4,128)} %reshape.338) | copy-start | bytes 12582916
  78.2 2.8 %copy-start.5 = (f32[4,256,256]{2,1,0:T(8,128)S(1)}, f32[4,256,256]{2,1,0:T(8,128)}, u32[]{:S(2)}) copy-start(f32[4,256,256]{2,1,0:T(8,128)} %fusion.45) | copy-start | bytes 3145732
  78.2 2.8 %copy-start.7 = (f32[4,16,256]{2,1,0:T(8,128)S(1)}, f32[4,16,256]{2,1,0:T(8,128)}, u32[]{:S(2)}) copy-start(f32[4,16,256]{2,1,0:T(8,128)} %copy.55) | copy-start | bytes 196612
  78.2 2.8 %copy-start.8 = (f32[4,256,16]{1,2,0:T(8,128)S(1)}, f32[4,256,16]{1,2,0:T(8,128)}, u32[]{:S(2)}) copy-start(f32[4,256,16]{1,2,0:T(8,128)} %copy.61) | copy-start | bytes 196612
  89.0 1.6 %copy-start = (bf16[1024,1024]{0,1:T(8,128)(2,1)S(1)}, bf16[1024,1024]{0,1:T(8,128)(2,1)}, u32[]{:S(2)}) copy-start(bf16[1024,1024]{0,1:T(8,128)(2,1)} %copy.67) | copy-start | bytes 6291460
  90.1 1.9 %copy-start.14 = (f32[1024]{0:T(1024)S(1)}, f32[1024]{0:T(1024)}, u32[]{:S(2)}) copy-start(f32[1024]{0:T(1024)} %param.20) | copy-start | bytes 12292

commit v13 on v11

--- a/solution.py
+++ b/solution.py
@@ -301,7 +301,7 @@
     buffers = (2, count - 1, pieces, rows, width)
     return pl.pallas_call(
         functools.partial(ring_kernel, count, pieces),
-        out_shape=jax.ShapeDtypeStruct((tokens, width), jnp.bfloat16),
+        out_shape=jax.ShapeDtypeStruct((tokens, width), jnp.float32),
         in_specs=[pl.BlockSpec(memory_space=pltpu.VMEM)] * 2,
         out_specs=pl.BlockSpec(memory_space=pltpu.VMEM),
         scratch_shapes=[
@@ -333,11 +333,20 @@
     per_group = HEADS // NGROUPS
     head_count = groups * per_group
     block_count = row_count // BLOCK
-    tail_inner, tail_maps = passed_along(
-        (inner_input[row_count - kernel_remainder :], state_maps[row_count - kernel_remainder :]),
+    map_width = state_maps.shape[1] * state_maps.shape[2] * state_maps.shape[3]
+    tails = passed_along(
+        jnp.concatenate(
+            (
+                inner_input[row_count - kernel_remainder :],
+                state_maps[row_count - kernel_remainder :].reshape(kernel_remainder, map_width),
+            ),
+            axis=1,
+        ),
         "seq",
         1,
     )
+    tail_inner = tails[:, : inner_input.shape[1]]
+    tail_maps = tails[:, inner_input.shape[1] :].reshape((kernel_remainder,) + state_maps.shape[1:])
     inner_conv = conv_silu(
         jnp.concatenate((tail_inner, inner_input), axis=0), conv_kernel, row_count
     )
@@ -405,7 +414,7 @@
             .astype(jnp.bfloat16)
             .reshape(rows, head_count * HEAD_DIM)
         )
-        outs.append(ring_projection(normed.T, out_weight))
+        outs.append(ring_projection(normed.T, out_weight).astype(jnp.bfloat16))
     return jnp.concatenate(outs, axis=0)
 
 

time: 149 us -> 152 us (1.020)
  other arithmetic: 19.3 us -> 25.5 us
  starting transfers between devices: 5.41 us -> 2.04 us
    convert_element_type x2, other arithmetic: 5.9 us -> 9.48 us  [conv_silu(): return jax.nn.silu(acc).astype(jnp.bfloat16)]
    ppermute x2 -> x1, starting transfers between devices: 5.41 us -> 2.04 us  [passed_along(): return lax.ppermute(x, axis, pairs)]
    another operation x9, local copies, waits for them, and re-layouts: 3.27 us -> 5.35 us
    convert_element_type x0 -> x1, other arithmetic: none -> 2.07 us  [local(): outs.append(ring_projection(normed.T, out_weight).astype(jnp.bfloat16))]
    unnamed x35 -> x44, local copies, waits for them, and re-layouts: 11.1 us -> 10 us
  transfers between devices with their start and end apart: 2 -> 1, of which waited for: 0 -> 0; matrix products, arithmetic and copies ran while one was open for 14% -> 15% of each run, Pallas kernels for 0% -> 0%
where the time goes in v13:
time: 152 us
  Pallas kernels  80.2 us (53%)
  local copies, waits for them, and re-layouts  28.5 us (19%)
  other arithmetic  25.5 us (17%)
  matrix products  14.9 us (10%)
  starting transfers between devices  2.04 us (1%)
    pallas_call x1, Pallas kernels, ring_projection(): pl.pallas_call(functools.partial(ring_kernel, count, pieces), out_shape=j...  53.4 us
    pallas_call x1, Pallas kernels, state_scan(): pl.pallas_call(functools.partial(state_scan_kernel, count), out_shape=jax...  26.9 us
    unnamed x44, local copies, waits for them, and re-layouts  10 us
    convert_element_type x2, other arithmetic, conv_silu(): return jax.nn.silu(acc).astype(jnp.bfloat16)  9.48 us
    dot_general x1, matrix products, local(): jnp.einsum('cgjts,csgjp->ctgjp', mixing, x_blocks, preferred_element_type...  8.23 us
    another operation x9, local copies, waits for them, and re-layouts  5.35 us
    convert_element_type x1, local copies, waits for them, and re-layouts, local(): skip_gain.reshape(groups, per_group)[:, :, None] * x_blocks  3.42 us
    dot_general x1, matrix products, local(): jnp.einsum('csgjp,csgjn->cgjpn', x_blocks, weighted, preferred_element_ty...  3.29 us
  transfers between devices with their start and end apart: 1, of which 0 were waited for; matrix products, arithmetic and copies ran while one was open for 15% of the time, Pallas kernels for 0%

profile of v13, /device:TPU:24, one launch (start us, length us, event | category | flops | bytes accessed | tf_op | source)
XLA Modules:
  0.0 151.6 jit_solution(17625871288389647384)
XLA Ops:
  0.0 0.8 slice_bitcast_fusion.1
  0.8 0.7 slice.107
  1.5 0.9 copy.72
  2.4 2.0 %collective-permute-start = (bf16[3,1280]{0,1:T(8,128)(2,1)}, bf16[3,1280]{0,1:T(8,128)(2,1)S(1)}, u32[]{:S(2)}, u32[]{:S(2)}) collective-permute-start(bf16[3,1280]{0,1:T(8,128)(2,1)} %copy.72), channel_id=1, source_target_pairs={{0,8},{8,16},{16,24},{24,32},{32,40},{40,48},{48,56},{56,64},{64,7... | collective-permute-start | bytes 23048 | tf_op jit(solution)/shard_map/ppermute | solution.py:24
  5.1 1.0 broadcast_multiply_fusion
  6.2 2.3 %reduce-window.6 = f32[4,16,1,2,128]{4,1,2,3,0:T(8,128)S(1)} reduce-window(f32[4,16,1,2,128]{4,1,2,3,0:T(8,128)S(1)} %copy.79, f32[]{:T(128)} %constant.13.clone.1), window={size=1x1x1x1x128 pad=0_0x0_0x0_0x0_0x127_0}, to_apply=%region_0.1 | reduce-window | flops 2080768 | bytes 131076 | tf_op jit(solution)/shard_map/reduce-window
  9.1 0.7 exponential_bitcast_fusion
  9.8 0.9 slice_reduce_fusion
  10.7 1.0 fusion.31
  11.9 0.9 fusion.42
  12.9 1.3 fusion.43
  14.8 0.7 multiply_bitcast_fusion
  16.2 3.9 %copy.73 = bf16[1024,1024]{0,1:T(8,128)(2,1)} copy(bf16[1024,1024]{1,0:T(8,128)(2,1)} %param.11) | data formatting | bytes 4194304 | tf_op args[0]
  21.6 0.9 reshape.337
  22.5 0.9 copy.89
  23.3 0.9 copy.92
  24.2 2.6 %copy.95 = bf16[1024,1024]{0,1:T(8,128)(2,1)} copy(bf16[1024,1024]{1,0:T(8,128)(2,1)S(1)} %copy-done.2) | data formatting | bytes 4194304 | tf_op args[2]
  26.8 8.8 %multiply_convert_fusion.5 = bf16[1024,1024]{0,1:T(8,128)(2,1)S(1)} fusion(bf16[1024,1024]{0,1:T(8,128)(2,1)} %copy.73, bf16[3,1024]{0,1:T(8,128)(2,1)S(1)} %slice.137, f32[1024]{0:T(1024)S(1)} %bitcast.91, f32[1024]{0:T(1024)S(1)} %bitcast.92, f32[1024]{0:T(1024)S(1)} %bitcast.90, f32[1024]{0:T(1024)S(1)} %bitcast.89), kind=kLoop, calls=%fused_computation.24 | loop fusion | flops 26214400 | bytes 4216832 | tf_op jit(solution)/shard_map/convert_element_type | solution.py:31
  35.7 3.4 %reshape.346 = f32[4,256,1,16,64]{1,0,4,3,2:T(4,128)} reshape(bf16[1024,1024]{0,1:T(8,128)(2,1)S(1)} %multiply_convert_fusion.5) | data formatting | bytes 6291456 | tf_op jit(solution)/shard_map/convert_element_type | solution.py:395
  39.1 2.8 %reshape.331 = bf16[4,256,16,64]{1,0,3,2:T(4,128)(2,1)} reshape(bf16[1024,1024]{0,1:T(8,128)(2,1)S(1)} %multiply_convert_fusion.5) | data formatting | bytes 4194304 | tf_op jit(solution)/shard_map/reshape.28
  43.1 1.0 copy-done.1
  44.2 8.2 %bitcast_add_fusion = f32[4,256,1,16,64]{1,4,3,0,2:T(8,128)} fusion(f32[4,256,1,16,64]{1,0,4,3,2:T(4,128)S(1)} %copy-done.1, f32[4,16,256]{2,1,0:T(8,128)S(1)} %copy.83, f32[4,16,256]{2,1,0:T(8,128)S(1)} %reduce_window_sum.44, f32[4,256,256]{2,1,0:T(8,128)S(1)} %fusion.44, pred[256,256]{1,0:T(8,128)(4,1)S(1)} %copy-done.6, f32[16]{0:T(128)S(1)} %copy-done.18, ...), kind=kOutput, calls=%fused_computation.18 | convolution fusion | flops 559939584 | bytes 11731008 | tf_op jit(solution)/shard_map/cgjts,csgjp->ctgjp/dot_general | solution.py:370
  52.4 3.3 %fusion.11 = f32[4,16,64,128]{3,2,1,0:T(8,128)S(1)} fusion(f32[4,256,128]{2,1,0:T(8,128)S(1)} %convert_element_type.94, f32[4,256,16]{1,2,0:T(8,128)S(1)} %copy.92, bf16[4,256,16,64]{1,0,3,2:T(4,128)(2,1)S(1)} %copy-done.3), kind=kOutput, calls=%fused_computation.15 | convolution fusion | flops 272629760 | bytes 4784128 | tf_op jit(solution)/shard_map/csgjp,csgjn->cgjpn/dot_general | solution.py:374
  55.8 1.1 fusion.27
  57.5 26.9 %state_scan.1 = f32[16,64,128]{2,1,0:T(8,128)} custom-call(f32[16,64,128]{2,1,0:T(8,128)} %get-tuple-element.9.state_ref, f32[16,128]{1,0:T(8,128)} %broadcast_in_dim.15.decay_ref), custom_call_target="tpu_custom_call" | custom-call | tf_op jit(solution)/shard_map/state_scan/pallas_call | solution.py:202
  84.4 3.1 %fusion.12 = f32[4,256,1,16,64]{1,4,3,0,2:T(8,128)S(1)} fusion(f32[4,256,1,16,64]{1,4,3,0,2:T(8,128)} %bitcast_add_fusion, bf16[4,256,128,1]{2,1,3,0:T(8,128)(2,1)S(1)} %bitcast.80, f32[4,256,16]{1,2,0:T(8,128)S(1)} %copy.89, f32[1,16,64,128]{3,2,1,0:T(8,128)S(1)} %get-tuple-element.10, f32[1,16,64,128]{3,2,1,0:T(8,128)S(1)} %get-tuple-element.11, ...), kind=kOutput, calls=%fused_computation.17 | convolution fusion | flops 273678336 | bytes 10813712 | tf_op jit(solution)/shard_map/ctgn,cgjpn->ctgjp/dot_general | solution.py:403
  87.5 2.8 %copy.94 = f32[4,256,1,16,64]{1,0,4,3,2:T(4,128)S(1)} copy(f32[4,256,1,16,64]{1,4,3,0,2:T(8,128)S(1)} %fusion.12) | data formatting | bytes 8388608 | tf_op jit(solution)/shard_map/add | solution.py:406
  90.3 1.0 copy.99
  91.9 1.3 multiply_reduce_fusion
  93.3 2.9 %fusion.17.normed_ref = bf16[1024,1024]{1,0:T(8,128)(2,1)} fusion(f32[1024]{0:T(1024)S(1)} %copy-done.8, f32[1024]{0:T(1024)S(1)} %add_rsqrt_fusion, f32[1024,1024]{0,1:T(8,128)S(1)} %bitcast.77, bf16[1024,1024]{0,1:T(8,128)(2,1)S(1)} %copy-done), kind=kLoop, calls=%fused_computation.31 | loop fusion | flops 9437184 | bytes 8396800 | tf_op jit(solution)/shard_map/transpose | solution.py:417
  96.2 53.4 %ring_projection.1 = f32[1024,256]{1,0:T(8,128)} custom-call(bf16[1024,1024]{1,0:T(8,128)(2,1)} %fusion.17.normed_ref, bf16[1024,2048]{1,0:T(8,128)(2,1)} %weight_ref.1), custom_call_target="tpu_custom_call" | custom-call | tf_op jit(solution)/shard_map/ring_projection/pallas_call | solution.py:302
  149.6 2.1 %convert_element_type.99 = bf16[1024,256]{1,0:T(8,128)(2,1)} convert(f32[1024,256]{1,0:T(8,128)} %ring_projection.1) | non-fusion elementwise | flops 262144 | bytes 1572864 | tf_op jit(solution)/shard_map/convert_element_type | solution.py:417
  (73 shorter events, 6.7 us)
Async XLA Ops:
  0.0 21.4 %copy-start.4 = (bf16[1024,2,1,128]{3,1,2,0:T(2,128)(2,1)S(1)}, bf16[1024,2,1,128]{3,1,2,0:T(2,128)(2,1)}, u32[]{:S(2)}) copy-start(bf16[1024,2,1,128]{3,1,2,0:T(2,128)(2,1)} %param.12) | copy-start | bytes 1572868
  2.4 21.7 %copy-start.2 = (bf16[1024,1024]{1,0:T(8,128)(2,1)S(1)}, bf16[1024,1024]{1,0:T(8,128)(2,1)}, u32[]{:S(2)}) copy-start(bf16[1024,1024]{1,0:T(8,128)(2,1)} %param.13) | copy-start | bytes 6291460
  2.4 24.4 %collective-permute-start = (bf16[3,1280]{0,1:T(8,128)(2,1)}, bf16[3,1280]{0,1:T(8,128)(2,1)S(1)}, u32[]{:S(2)}, u32[]{:S(2)}) collective-permute-start(bf16[3,1280]{0,1:T(8,128)(2,1)} %copy.72), channel_id=1, source_target_pairs={{0,8},{8,16},{16,24},{24,32},{32,40},{40,48},{48,56},{56,64},{64,7... | collective-permute-start | bytes 23048 | tf_op jit(solution)/shard_map/ppermute | solution.py:24
  21.5 5.2 %copy-start.5 = (f32[4,16,256]{2,1,0:T(8,128)S(1)}, f32[4,16,256]{2,1,0:T(8,128)}, u32[]{:S(2)}) copy-start(f32[4,16,256]{2,1,0:T(8,128)} %reshape.340) | copy-start | bytes 196612
  35.6 6.3 %copy-start.9 = (f32[1,2,1,128]{3,2,1,0:T(1,128)S(1)}, f32[1,2,1,128]{3,2,1,0:T(1,128)}, u32[]{:S(2)}) copy-start(f32[1,2,1,128]{3,2,1,0:T(1,128)} %get-tuple-element.25) | copy-start | bytes 3076
  35.6 6.3 %copy-start.10 = (f32[1,2,1,128]{3,2,1,0:T(1,128)S(1)}, f32[1,2,1,128]{3,2,1,0:T(1,128)}, u32[]{:S(2)}) copy-start(f32[1,2,1,128]{3,2,1,0:T(1,128)} %get-tuple-element.26) | copy-start | bytes 3076
  35.6 6.3 %copy-start.11 = (f32[1,2,1,128]{3,2,1,0:T(1,128)S(1)}, f32[1,2,1,128]{3,2,1,0:T(1,128)}, u32[]{:S(2)}) copy-start(f32[1,2,1,128]{3,2,1,0:T(1,128)} %get-tuple-element.27) | copy-start | bytes 3076
  35.6 6.3 %copy-start.12 = (f32[1,2,1,128]{3,2,1,0:T(1,128)S(1)}, f32[1,2,1,128]{3,2,1,0:T(1,128)}, u32[]{:S(2)}) copy-start(f32[1,2,1,128]{3,2,1,0:T(1,128)} %get-tuple-element.28) | copy-start | bytes 3076
  39.1 4.0 %copy-start.6 = (pred[256,256]{1,0:T(8,128)(4,1)S(1)}, pred[256,256]{1,0:T(8,128)(4,1)}, u32[]{:S(2)}) copy-start(pred[256,256]{1,0:T(8,128)(4,1)} %iota_compare_fusion) | copy-start | bytes 196612
  39.1 4.0 %copy-start.18 = (f32[16]{0:T(128)S(1)}, f32[16]{0:T(128)}, u32[]{:S(2)}) copy-start(f32[16]{0:T(128)} %param.17) | copy-start | bytes 196
  41.9 2.2 %copy-start.1 = (f32[4,256,1,16,64]{1,0,4,3,2:T(4,128)S(1)}, f32[4,256,1,16,64]{1,0,4,3,2:T(4,128)}, u32[]{:S(2)}) copy-start(f32[4,256,1,16,64]{1,0,4,3,2:T(4,128)} %reshape.346) | copy-start | bytes 12582916
  44.2 8.2 %copy-start.3 = (bf16[4,256,16,64]{1,0,3,2:T(4,128)(2,1)S(1)}, bf16[4,256,16,64]{1,0,3,2:T(4,128)(2,1)}, u32[]{:S(2)}) copy-start(bf16[4,256,16,64]{1,0,3,2:T(4,128)(2,1)} %reshape.331) | copy-start | bytes 6291460
  52.4 3.3 %copy-start.14 = (f32[16]{0:T(128)S(1)}, f32[16]{0:T(128)}, u32[]{:S(2)}) copy-start(f32[16]{0:T(128)} %get-tuple-element.5) | copy-start | bytes 196
  52.4 3.4 %copy-start.15 = (f32[16]{0:T(128)S(1)}, f32[16]{0:T(128)}, u32[]{:S(2)}) copy-start(f32[16]{0:T(128)} %get-tuple-element.6) | copy-start | bytes 196
  52.4 3.4 %copy-start.16 = (f32[16]{0:T(128)S(1)}, f32[16]{0:T(128)}, u32[]{:S(2)}) copy-start(f32[16]{0:T(128)} %get-tuple-element.7) | copy-start | bytes 196
  52.4 3.4 %copy-start.17 = (f32[16]{0:T(128)S(1)}, f32[16]{0:T(128)}, u32[]{:S(2)}) copy-start(f32[16]{0:T(128)} %get-tuple-element.8) | copy-start | bytes 196
  55.7 1.1 copy-start.13
  55.7 28.6 %copy-start.7 = (f32[4,16]{1,0:T(4,128)S(1)}, f32[4,16]{1,0:T(4,128)}, u32[]{:S(2)}) copy-start(f32[4,16]{1,0:T(4,128)} %subtract_exponential_fusion) | copy-start | bytes 772
  90.3 1.6 %copy-start = (bf16[1024,1024]{0,1:T(8,128)(2,1)S(1)}, bf16[1024,1024]{0,1:T(8,128)(2,1)}, u32[]{:S(2)}) copy-start(bf16[1024,1024]{0,1:T(8,128)(2,1)} %copy.95) | copy-start | bytes 6291460
  91.4 1.9 %copy-start.8 = (f32[1024]{0:T(1024)S(1)}, f32[1024]{0:T(1024)}, u32[]{:S(2)}) copy-start(f32[1024]{0:T(1024)} %param.20) | copy-start | bytes 12292

commit v14 on v11

--- a/solution.py
+++ b/solution.py
@@ -294,7 +294,7 @@
 
 def ring_projection(normed, weight):
     count = lax.axis_size("chan")
-    pieces = 2
+    pieces = 1
     tokens = normed.shape[1]
     width = weight.shape[1] // count
     rows = tokens // (2 * pieces)

time: 149 us -> 159 us (1.067)
  Pallas kernels: 80.3 us -> 90.2 us
    pallas_call x1, Pallas kernels: 53.2 us -> 63.1 us  [ring_projection(): pl.pallas_call(functools.partial(ring_kernel, count, pieces), out_shape=j...]
  transfers between devices with their start and end apart: 2 -> 2, of which waited for: 0 -> 0; matrix products, arithmetic and copies ran while one was open for 14% -> 13% of each run, Pallas kernels for 0% -> 0%
where the time goes in v14:
time: 159 us; the launch traced here: 158 us
  Pallas kernels  90.2 us (57%)
  local copies, waits for them, and re-layouts  27 us (17%)
  other arithmetic  19.3 us (12%)
  matrix products  15.6 us (10%)
  starting transfers between devices  5.41 us (3%)
    pallas_call x1, Pallas kernels, ring_projection(): pl.pallas_call(functools.partial(ring_kernel, count, pieces), out_shape=j...  63.1 us
    pallas_call x1, Pallas kernels, state_scan(): pl.pallas_call(functools.partial(state_scan_kernel, count), out_shape=jax...  27 us
    unnamed x35, local copies, waits for them, and re-layouts  11.1 us
    dot_general x1, matrix products, local(): jnp.einsum('cgjts,csgjp->ctgjp', mixing, x_blocks, preferred_element_type...  8.92 us
    convert_element_type x2, other arithmetic, conv_silu(): return jax.nn.silu(acc).astype(jnp.bfloat16)  5.9 us
    ppermute x2, starting transfers between devices, passed_along(): return lax.ppermute(x, axis, pairs)  5.41 us
    convert_element_type x1, local copies, waits for them, and re-layouts, local(): skip_gain.reshape(groups, per_group)[:, :, None] * x_blocks  3.41 us
    dot_general x1, matrix products, local(): jnp.einsum('csgjp,csgjn->cgjpn', x_blocks, weighted, preferred_element_ty...  3.29 us
  transfers between devices with their start and end apart: 2, of which 0 were waited for; matrix products, arithmetic and copies ran while one was open for 13% of the time, Pallas kernels for 0%

profile of v14, /device:TPU:24, one launch (start us, length us, event | category | flops | bytes accessed | tf_op | source)
XLA Modules:
  0.0 157.9 jit_solution(7607616557073652518)
XLA Ops:
  0.0 0.9 slice.101
  0.9 0.9 copy.44
  1.8 1.9 %collective-permute-start = (bf16[3,1024]{0,1:T(8,128)(2,1)}, bf16[3,1024]{0,1:T(8,128)(2,1)}, u32[]{:S(2)}, u32[]{:S(2)}) collective-permute-start(bf16[3,1024]{0,1:T(8,128)(2,1)} %copy.44), channel_id=1, source_target_pairs={{0,8},{8,16},{16,24},{24,32},{32,40},{40,48},{48,56},{56,64},{64,7... | collective-permute-start | bytes 18440 | tf_op jit(solution)/shard_map/ppermute | solution.py:24
  3.7 1.1 copy.47
  4.8 3.5 %collective-permute-start.1 = (bf16[3,2,1,128]{3,0,2,1:T(4,128)(2,1)S(1)}, bf16[3,2,1,128]{3,0,2,1:T(4,128)(2,1)S(1)}, u32[]{:S(2)}, u32[]{:S(2)}) collective-permute-start(bf16[3,2,1,128]{3,0,2,1:T(4,128)(2,1)S(1)} %slice.133), channel_id=1, source_target_pairs={{0,8},{8,16},{16,24},{24,32},{32,40},{40,48},{48,56},{56,64},{64,7... | collective-permute-start | bytes 4616 | tf_op jit(solution)/shard_map/ppermute | solution.py:24
  8.3 0.7 exponential_negate_fusion
  9.0 1.0 broadcast_multiply_fusion
  10.1 2.3 %reduce-window.6 = f32[4,16,1,2,128]{4,1,2,3,0:T(8,128)S(1)} reduce-window(f32[4,16,1,2,128]{4,1,2,3,0:T(8,128)S(1)} %copy.51, f32[]{:T(128)} %constant.13.clone.1), window={size=1x1x1x1x128 pad=0_0x0_0x0_0x0_0x127_0}, to_apply=%region_0.1 | reduce-window | flops 2080768 | bytes 131076 | tf_op jit(solution)/shard_map/reduce-window
  13.0 0.8 slice_reduce_fusion
  13.9 1.1 fusion.31
  15.1 0.9 fusion.42
  16.1 0.7 fusion.43
  17.4 0.6 iota_compare_fusion
  18.1 2.6 %copy.45 = bf16[1024,1024]{0,1:T(8,128)(2,1)} copy(bf16[1024,1024]{1,0:T(8,128)(2,1)S(1)} %copy-done.2) | data formatting | bytes 4194304 | tf_op args[0]
  22.1 3.9 %copy.67 = bf16[1024,1024]{0,1:T(8,128)(2,1)} copy(bf16[1024,1024]{1,0:T(8,128)(2,1)} %param.13) | data formatting | bytes 4194304 | tf_op args[2]
  26.6 0.7 multiply_convert_fusion.8
  27.7 0.8 convert_element_type.91
  28.5 5.2 %multiply_convert_fusion.5 = bf16[1024,1024]{0,1:T(8,128)(2,1)S(1)} fusion(bf16[1024,1024]{0,1:T(8,128)(2,1)S(1)} %copy-done.1, bf16[3,1024]{0,1:T(8,128)(2,1)} %collective-permute-done, f32[1024]{0:T(1024)S(1)} %bitcast.82, f32[1024]{0:T(1024)S(1)} %bitcast.83, f32[1024]{0:T(1024)S(1)} %bitcast.81, f32[1024]{0:T(1024)S(1)} %bitcast.80), kind=kLoop, calls=%fused_computation.24 | loop fusion | flops 26214400 | bytes 4216832 | tf_op jit(solution)/shard_map/convert_element_type | solution.py:31
  33.7 3.4 %reshape.338 = f32[4,256,1,16,64]{1,0,4,3,2:T(4,128)} reshape(bf16[1024,1024]{0,1:T(8,128)(2,1)S(1)} %multiply_convert_fusion.5) | data formatting | bytes 6291456 | tf_op jit(solution)/shard_map/convert_element_type | solution.py:386
  37.1 2.8 %reshape.324 = bf16[4,256,16,64]{1,0,3,2:T(4,128)(2,1)} reshape(bf16[1024,1024]{0,1:T(8,128)(2,1)S(1)} %multiply_convert_fusion.5) | data formatting | bytes 4194304 | tf_op jit(solution)/shard_map/reshape.26
  39.9 8.9 %bitcast_add_fusion = f32[4,256,1,16,64]{1,4,3,0,2:T(8,128)} fusion(f32[4,256,1,16,64]{1,0,4,3,2:T(4,128)} %reshape.338, f32[4,16,256]{2,1,0:T(8,128)} %copy.55, f32[4,16,256]{2,1,0:T(8,128)S(1)} %reduce_window_sum.44, f32[4,256,256]{2,1,0:T(8,128)S(1)} %fusion.44, pred[256,256]{1,0:T(8,128)(4,1)} %iota_compare_fusion, f32[16]{0:T(128)S(1)} %copy-done.14, ...), kind=kOutput, calls=%fused_computation.18 | convolution fusion | flops 559939584 | bytes 11731008 | tf_op jit(solution)/shard_map/cgjts,csgjp->ctgjp/dot_general | solution.py:361
  48.9 3.3 %fusion.11 = f32[4,16,64,128]{3,2,1,0:T(8,128)S(1)} fusion(f32[4,256,128]{2,1,0:T(8,128)S(1)} %copy-done.4, f32[4,256,16]{1,2,0:T(8,128)S(1)} %copy-done.5, bf16[4,256,16,64]{1,0,3,2:T(4,128)(2,1)S(1)} %copy-done.3), kind=kOutput, calls=%fused_computation.15 | convolution fusion | flops 272629760 | bytes 4784128 | tf_op jit(solution)/shard_map/csgjp,csgjn->cgjpn/dot_general | solution.py:365
  52.3 1.1 fusion.27
  53.4 0.7 broadcast_in_dim.15.decay_ref
  54.0 27.0 %state_scan.1 = f32[16,64,128]{2,1,0:T(8,128)} custom-call(f32[16,64,128]{2,1,0:T(8,128)} %get-tuple-element.9.state_ref, f32[16,128]{1,0:T(8,128)} %broadcast_in_dim.15.decay_ref), custom_call_target="tpu_custom_call" | custom-call | tf_op jit(solution)/shard_map/state_scan/pallas_call | solution.py:202
  81.1 3.1 %fusion.12 = f32[4,256,1,16,64]{1,4,3,0,2:T(8,128)S(1)} fusion(f32[4,256,1,16,64]{1,4,3,0,2:T(8,128)} %bitcast_add_fusion, bf16[4,256,128,1]{2,1,3,0:T(8,128)(2,1)S(1)} %bitcast.72, f32[4,256,16]{1,2,0:T(8,128)S(1)} %copy.61, f32[1,16,64,128]{3,2,1,0:T(8,128)S(1)} %get-tuple-element.10, f32[1,16,64,128]{3,2,1,0:T(8,128)S(1)} %get-tuple-element.11, ...), kind=kOutput, calls=%fused_computation.17 | convolution fusion | flops 273678336 | bytes 10813712 | tf_op jit(solution)/shard_map/ctgn,cgjpn->ctgjp/dot_general | solution.py:394
  84.2 2.8 %copy.66 = f32[4,256,1,16,64]{1,0,4,3,2:T(4,128)S(1)} copy(f32[4,256,1,16,64]{1,4,3,0,2:T(8,128)S(1)} %fusion.12) | data formatting | bytes 8388608 | tf_op jit(solution)/shard_map/add | solution.py:397
  87.0 1.0 copy.70
  88.6 1.3 multiply_reduce_fusion
  90.0 2.9 %fusion.17.normed_ref = bf16[1024,1024]{1,0:T(8,128)(2,1)} fusion(f32[1024]{0:T(1024)S(1)} %copy-done.7, f32[1024]{0:T(1024)S(1)} %add_rsqrt_fusion, f32[1024,1024]{0,1:T(8,128)S(1)} %bitcast.69, bf16[1024,1024]{0,1:T(8,128)(2,1)S(1)} %copy-done), kind=kLoop, calls=%fused_computation.31 | loop fusion | flops 9437184 | bytes 8396800 | tf_op jit(solution)/shard_map/transpose | solution.py:408
  92.9 63.1 %ring_projection.1 = bf16[1024,256]{1,0:T(8,128)(2,1)} custom-call(bf16[1024,1024]{1,0:T(8,128)(2,1)} %fusion.17.normed_ref, bf16[1024,2048]{1,0:T(8,128)(2,1)} %weight_ref.1), custom_call_target="tpu_custom_call" | custom-call | tf_op jit(solution)/shard_map/ring_projection/pallas_call | solution.py:302
  156.0 1.9 %copy.85 = bf16[1024,256]{1,0:T(8,128)(2,1)} copy(bf16[1024,256]{1,0:T(8,128)(2,1)} %ring_projection.1) | data formatting | bytes 1048576
  (62 shorter events, 4.6 us)
Async XLA Ops:
  0.0 18.1 %copy-start.2 = (bf16[1024,1024]{1,0:T(8,128)(2,1)S(1)}, bf16[1024,1024]{1,0:T(8,128)(2,1)}, u32[]{:S(2)}) copy-start(bf16[1024,1024]{1,0:T(8,128)(2,1)} %param.11) | copy-start | bytes 6291460
  1.8 26.7 %collective-permute-start = (bf16[3,1024]{0,1:T(8,128)(2,1)}, bf16[3,1024]{0,1:T(8,128)(2,1)}, u32[]{:S(2)}, u32[]{:S(2)}) collective-permute-start(bf16[3,1024]{0,1:T(8,128)(2,1)} %copy.44), channel_id=1, source_target_pairs={{0,8},{8,16},{16,24},{24,32},{32,40},{40,48},{48,56},{56,64},{64,7... | collective-permute-start | bytes 18440 | tf_op jit(solution)/shard_map/ppermute | solution.py:24
  4.8 21.8 %collective-permute-start.1 = (bf16[3,2,1,128]{3,0,2,1:T(4,128)(2,1)S(1)}, bf16[3,2,1,128]{3,0,2,1:T(4,128)(2,1)S(1)}, u32[]{:S(2)}, u32[]{:S(2)}) collective-permute-start(bf16[3,2,1,128]{3,0,2,1:T(4,128)(2,1)S(1)} %slice.133), channel_id=1, source_target_pairs={{0,8},{8,16},{16,24},{24,32},{32,40},{40,48},{48,56},{56,64},{64,7... | collective-permute-start | bytes 4616 | tf_op jit(solution)/shard_map/ppermute | solution.py:24
  26.0 2.5 %copy-start.1 = (bf16[1024,1024]{0,1:T(8,128)(2,1)S(1)}, bf16[1024,1024]{0,1:T(8,128)(2,1)}, u32[]{:S(2)}) copy-start(bf16[1024,1024]{0,1:T(8,128)(2,1)} %copy.45) | copy-start | bytes 6291460
  33.7 6.2 %copy-start.14 = (f32[16]{0:T(128)S(1)}, f32[16]{0:T(128)}, u32[]{:S(2)}) copy-start(f32[16]{0:T(128)} %param.17) | copy-start | bytes 196
  39.9 8.9 %copy-start.3 = (bf16[4,256,16,64]{1,0,3,2:T(4,128)(2,1)S(1)}, bf16[4,256,16,64]{1,0,3,2:T(4,128)(2,1)}, u32[]{:S(2)}) copy-start(bf16[4,256,16,64]{1,0,3,2:T(4,128)(2,1)} %reshape.324) | copy-start | bytes 6291460
  39.9 8.9 %copy-start.4 = (f32[4,256,128]{2,1,0:T(8,128)S(1)}, f32[4,256,128]{2,1,0:T(8,128)}, u32[]{:S(2)}) copy-start(f32[4,256,128]{2,1,0:T(8,128)} %convert_element_type.91) | copy-start | bytes 1572868
  39.9 8.9 %copy-start.5 = (f32[4,256,16]{1,2,0:T(8,128)S(1)}, f32[4,256,16]{1,2,0:T(8,128)}, u32[]{:S(2)}) copy-start(f32[4,256,16]{1,2,0:T(8,128)} %copy.64) | copy-start | bytes 196612
  48.9 3.4 %copy-start.9 = (f32[16]{0:T(128)S(1)}, f32[16]{0:T(128)}, u32[]{:S(2)}) copy-start(f32[16]{0:T(128)} %get-tuple-element.5) | copy-start | bytes 196
  48.9 3.4 %copy-start.10 = (f32[16]{0:T(128)S(1)}, f32[16]{0:T(128)}, u32[]{:S(2)}) copy-start(f32[16]{0:T(128)} %get-tuple-element.6) | copy-start | bytes 196
  48.9 3.4 %copy-start.11 = (f32[16]{0:T(128)S(1)}, f32[16]{0:T(128)}, u32[]{:S(2)}) copy-start(f32[16]{0:T(128)} %get-tuple-element.7) | copy-start | bytes 196
  48.9 3.4 %copy-start.12 = (f32[16]{0:T(128)S(1)}, f32[16]{0:T(128)}, u32[]{:S(2)}) copy-start(f32[16]{0:T(128)} %get-tuple-element.8) | copy-start | bytes 196
  52.2 1.1 copy-start.8
  52.2 28.8 %copy-start.6 = (f32[4,16]{1,0:T(4,128)S(1)}, f32[4,16]{1,0:T(4,128)}, u32[]{:S(2)}) copy-start(f32[4,16]{1,0:T(4,128)} %subtract_exponential_fusion) | copy-start | bytes 772
  52.2 28.8 %copy-start.13 = (f32[4]{0:T(128)S(1)}, f32[4]{0:T(128)}, u32[]{:S(2)}) copy-start(f32[4]{0:T(128)} %pad.clone) | copy-start | bytes 52
  87.0 1.6 %copy-start = (bf16[1024,1024]{0,1:T(8,128)(2,1)S(1)}, bf16[1024,1024]{0,1:T(8,128)(2,1)}, u32[]{:S(2)}) copy-start(bf16[1024,1024]{0,1:T(8,128)(2,1)} %copy.67) | copy-start | bytes 6291460
  88.1 1.9 %copy-start.7 = (f32[1024]{0:T(1024)S(1)}, f32[1024]{0:T(1024)}, u32[]{:S(2)}) copy-start(f32[1024]{0:T(1024)} %param.20) | copy-start | bytes 12292

commit v15 on v11

--- a/solution.py
+++ b/solution.py
@@ -77,9 +77,9 @@
             peers = peers + valid.astype(jnp.int32)
     pl.semaphore_wait(barrier, peers)
 
-    def remote(src, dst, slot, part, target):
+    def remote(src, dst, slot, part, target, piece=0):
         return pltpu.make_async_remote_copy(
-            src_ref=src, dst_ref=dst, send_sem=ssem.at[slot, part], recv_sem=rsem.at[slot, part],
+            src_ref=src, dst_ref=dst, send_sem=ssem.at[slot, part, piece], recv_sem=rsem.at[slot, part, piece],
             device_id=(target, chan), device_id_type=MESH,
         )
 
@@ -97,7 +97,9 @@
         first_d(partner).start()
         first[1](partner).wait_recv()
         first_d(partner).wait_recv()
-        cur_d[...] = own_d[0:half] + pair_d[0:half]
+        for piece in range(cur_d.shape[0]):
+            rows = slice(piece * cur_d.shape[1], (piece + 1) * cur_d.shape[1])
+            cur_d[piece] = own_d[rows] + pair_d[rows]
         scale_add(cur_s, pair_d[0:half], state_ref.at[0:half], pair_s[0:half].astype(jnp.float32))
 
     @pl.when(core == 1)
@@ -106,56 +108,79 @@
         first_d(partner).start()
         first[0](partner).wait_recv()
         first_d(partner).wait_recv()
-        cur_d[...] = own_d[half:] + pair_d[half:]
+        for piece in range(cur_d.shape[0]):
+            rows = slice(half + piece * cur_d.shape[1], half + (piece + 1) * cur_d.shape[1])
+            cur_d[piece] = own_d[rows] + pair_d[rows]
         scale_add(
             cur_s, own_d[half:], pair_s[half:].astype(jnp.float32), state_ref.at[half:]
         )
 
     rounds = [[1, 2]] + [[distance] for distance in distances[1:]]
-    outgoing = []
+    pieces = cur_d.shape[0]
+    per_piece = half // pieces
+    plan = []
     slot = 0
     for index, round_distances in enumerate(rounds):
-        send_s[index] = cur_s[...].astype(jnp.bfloat16)
-        send_d[index] = cur_d[...]
-        start = slot
-        for distance in round_distances:
-            makers = (
-                lambda t, index=index, slot=slot: remote(send_s.at[index], recv_s.at[slot], slot + 1, 0, t),
-                lambda t, index=index, slot=slot: remote(send_d.at[index], recv_d.at[slot], slot + 1, 1, t),
-            )
+        plan.append([(distance, slot + offset) for offset, distance in enumerate(round_distances)])
+        slot += len(round_distances)
+    outgoing = []
+
+    def makers(index, at, piece):
+        heads = slice(piece * per_piece, (piece + 1) * per_piece)
+        return (
+            lambda t: remote(send_s.at[index, heads], recv_s.at[at, heads], at + 1, 0, t, piece),
+            lambda t: remote(send_d.at[index, piece], recv_d.at[at, piece], at + 1, 1, t, piece),
+        )
+
+    def send(index, piece):
+        heads = slice(piece * per_piece, (piece + 1) * per_piece)
+        send_s[index, heads] = cur_s[heads].astype(jnp.bfloat16)
+        send_d[index, piece] = cur_d[piece]
+        for distance, at in plan[index]:
+            pair = makers(index, at, piece)
             sends = chip + distance < chips
 
             @pl.when(sends)
-            def _(makers=makers, distance=distance):
-                for make in makers:
+            def _(pair=pair, distance=distance):
+                for make in pair:
                     make(2 * (chip + distance) + core).start()
 
-            outgoing.append((sends, makers, distance))
-            slot += 1
-        for at in range(start, slot):
-            sends, makers, distance = outgoing[at]
+            outgoing.append((sends, pair, distance))
+
+    def receive(index, piece):
+        heads = slice(piece * per_piece, (piece + 1) * per_piece)
+        for distance, at in plan[index]:
+            pair = makers(index, at, piece)
             receives = chip - distance >= 0
             opening = index == 0 and distance == 1
 
             @pl.when(receives)
-            def _(makers=makers, distance=distance, at=at, opening=opening):
-                for make in makers:
+            def _(pair=pair, distance=distance, at=at, opening=opening):
+                for make in pair:
                     make(2 * (chip - distance) + core).wait_recv()
                 if opening:
-                    cur_s[...] = recv_s[at].astype(jnp.float32)
-                    cur_d[...] = recv_d[at]
+                    cur_s[heads] = recv_s[at, heads].astype(jnp.float32)
+                    cur_d[piece] = recv_d[at, piece]
                 else:
-                    scale_add(cur_s, cur_d[...], recv_s.at[at], cur_s)
-                    cur_d[...] = recv_d[at] + cur_d[...]
+                    scale_add(cur_s.at[heads], cur_d[piece], recv_s.at[at, heads], cur_s.at[heads])
+                    cur_d[piece] = recv_d[at, piece] + cur_d[piece]
 
             if opening:
 
                 @pl.when(jnp.logical_not(receives))
                 def _():
-                    cur_s[...] = jnp.zeros_like(cur_s)
-                    cur_d[...] = jnp.zeros_like(cur_d)
-
-    last = len(outgoing) + 1
+                    cur_s[heads] = jnp.zeros((per_piece,) + cur_s.shape[1:], jnp.float32)
+                    cur_d[piece] = jnp.zeros(cur_d.shape[1:], jnp.float32)
+
+    for piece in range(pieces):
+        send(0, piece)
+    for index in range(len(rounds)):
+        for piece in range(pieces):
+            receive(index, piece)
+            if index + 1 < len(rounds):
+                send(index + 1, piece)
+
+    last = slot + 1
     own_half = send_s.at[len(rounds)]
     own_half[...] = cur_s[...].astype(jnp.bfloat16)
     final = remote(own_half, back_s, last, 0, partner)
@@ -198,7 +223,7 @@
     rounds = len(scan_distances(count // 2))
     heads = state.shape[0]
     half_shape = (heads // 2,) + state.shape[1:]
-    half_decay = (heads // 2,) + decay.shape[1:]
+    half_decay = (2, heads // 4) + decay.shape[1:]
     return pl.pallas_call(
         functools.partial(state_scan_kernel, count),
         out_shape=jax.ShapeDtypeStruct(state.shape, jnp.float32),
@@ -216,8 +241,8 @@
             pltpu.VMEM((rounds + 1,) + half_shape, jnp.bfloat16),
             pltpu.VMEM((rounds + 1,) + half_decay, jnp.float32),
             pltpu.VMEM(half_shape, jnp.bfloat16),
-            pltpu.SemaphoreType.DMA((rounds + 3, 2)),
-            pltpu.SemaphoreType.DMA((rounds + 3, 2)),
+            pltpu.SemaphoreType.DMA((rounds + 3, 2, 2)),
+            pltpu.SemaphoreType.DMA((rounds + 3, 2, 2)),
         ],
         compiler_params=pltpu.CompilerParams(collective_id=0, has_side_effects=True),
         name="state_scan",

time: 149 us -> 147 us (0.987)
  no operation moved by 1% of the time
where the time goes in v15:
time: 147 us
  Pallas kernels  79 us (54%)
  local copies, waits for them, and re-layouts  27 us (18%)
  other arithmetic  19.3 us (13%)
  matrix products  15.6 us (11%)
  starting transfers between devices  5.41 us (4%)
    pallas_call x1, Pallas kernels, ring_projection(): pl.pallas_call(functools.partial(ring_kernel, count, pieces), out_shape=j...  53.2 us
    pallas_call x1, Pallas kernels, state_scan(): pl.pallas_call(functools.partial(state_scan_kernel, count), out_shape=jax...  25.8 us
    unnamed x35, local copies, waits for them, and re-layouts  11.1 us
    dot_general x1, matrix products, local(): jnp.einsum('cgjts,csgjp->ctgjp', mixing, x_blocks, preferred_element_type...  8.92 us
    convert_element_type x2, other arithmetic, conv_silu(): return jax.nn.silu(acc).astype(jnp.bfloat16)  5.9 us
    ppermute x2, starting transfers between devices, passed_along(): return lax.ppermute(x, axis, pairs)  5.41 us
    convert_element_type x1, local copies, waits for them, and re-layouts, local(): skip_gain.reshape(groups, per_group)[:, :, None] * x_blocks  3.41 us
    dot_general x1, matrix products, local(): jnp.einsum('csgjp,csgjn->cgjpn', x_blocks, weighted, preferred_element_ty...  3.29 us
  transfers between devices with their start and end apart: 2, of which 0 were waited for; matrix products, arithmetic and copies ran while one was open for 14% of the time, Pallas kernels for 0%

profile of v15, /device:TPU:24, one launch (start us, length us, event | category | flops | bytes accessed | tf_op | source)
XLA Modules:
  0.0 146.7 jit_solution(14664419489210453288)
XLA Ops:
  0.0 0.9 slice.101
  0.9 0.9 copy.44
  1.8 1.9 %collective-permute-start = (bf16[3,1024]{0,1:T(8,128)(2,1)}, bf16[3,1024]{0,1:T(8,128)(2,1)}, u32[]{:S(2)}, u32[]{:S(2)}) collective-permute-start(bf16[3,1024]{0,1:T(8,128)(2,1)} %copy.44), channel_id=1, source_target_pairs={{0,8},{8,16},{16,24},{24,32},{32,40},{40,48},{48,56},{56,64},{64,7... | collective-permute-start | bytes 18440 | tf_op jit(solution)/shard_map/ppermute | solution.py:24
  3.7 1.1 copy.47
  4.8 3.5 %collective-permute-start.1 = (bf16[3,2,1,128]{3,0,2,1:T(4,128)(2,1)S(1)}, bf16[3,2,1,128]{3,0,2,1:T(4,128)(2,1)S(1)}, u32[]{:S(2)}, u32[]{:S(2)}) collective-permute-start(bf16[3,2,1,128]{3,0,2,1:T(4,128)(2,1)S(1)} %slice.133), channel_id=1, source_target_pairs={{0,8},{8,16},{16,24},{24,32},{32,40},{40,48},{48,56},{56,64},{64,7... | collective-permute-start | bytes 4616 | tf_op jit(solution)/shard_map/ppermute | solution.py:24
  8.3 0.7 exponential_negate_fusion
  9.0 1.0 broadcast_multiply_fusion
  10.1 2.3 %reduce-window.6 = f32[4,16,1,2,128]{4,1,2,3,0:T(8,128)S(1)} reduce-window(f32[4,16,1,2,128]{4,1,2,3,0:T(8,128)S(1)} %copy.51, f32[]{:T(128)} %constant.13.clone.1), window={size=1x1x1x1x128 pad=0_0x0_0x0_0x0_0x127_0}, to_apply=%region_0.1 | reduce-window | flops 2080768 | bytes 131076 | tf_op jit(solution)/shard_map/reduce-window
  13.0 0.8 slice_reduce_fusion
  13.9 1.1 fusion.31
  15.1 0.9 fusion.42
  16.1 0.7 fusion.43
  17.4 0.6 iota_compare_fusion
  18.1 2.6 %copy.45 = bf16[1024,1024]{0,1:T(8,128)(2,1)} copy(bf16[1024,1024]{1,0:T(8,128)(2,1)S(1)} %copy-done.2) | data formatting | bytes 4194304 | tf_op args[0]
  22.1 3.9 %copy.67 = bf16[1024,1024]{0,1:T(8,128)(2,1)} copy(bf16[1024,1024]{1,0:T(8,128)(2,1)} %param.13) | data formatting | bytes 4194304 | tf_op args[2]
  26.6 0.7 multiply_convert_fusion.8
  27.7 0.8 convert_element_type.91
  28.5 5.2 %multiply_convert_fusion.5 = bf16[1024,1024]{0,1:T(8,128)(2,1)S(1)} fusion(bf16[1024,1024]{0,1:T(8,128)(2,1)S(1)} %copy-done.1, bf16[3,1024]{0,1:T(8,128)(2,1)} %collective-permute-done, f32[1024]{0:T(1024)S(1)} %bitcast.82, f32[1024]{0:T(1024)S(1)} %bitcast.83, f32[1024]{0:T(1024)S(1)} %bitcast.81, f32[1024]{0:T(1024)S(1)} %bitcast.80), kind=kLoop, calls=%fused_computation.24 | loop fusion | flops 26214400 | bytes 4216832 | tf_op jit(solution)/shard_map/convert_element_type | solution.py:31
  33.7 3.4 %reshape.338 = f32[4,256,1,16,64]{1,0,4,3,2:T(4,128)} reshape(bf16[1024,1024]{0,1:T(8,128)(2,1)S(1)} %multiply_convert_fusion.5) | data formatting | bytes 6291456 | tf_op jit(solution)/shard_map/convert_element_type | solution.py:411
  37.1 2.8 %reshape.324 = bf16[4,256,16,64]{1,0,3,2:T(4,128)(2,1)} reshape(bf16[1024,1024]{0,1:T(8,128)(2,1)S(1)} %multiply_convert_fusion.5) | data formatting | bytes 4194304 | tf_op jit(solution)/shard_map/reshape.26
  39.9 8.9 %bitcast_add_fusion = f32[4,256,1,16,64]{1,4,3,0,2:T(8,128)} fusion(f32[4,256,1,16,64]{1,0,4,3,2:T(4,128)} %reshape.338, f32[4,16,256]{2,1,0:T(8,128)} %copy.55, f32[4,16,256]{2,1,0:T(8,128)S(1)} %reduce_window_sum.44, f32[4,256,256]{2,1,0:T(8,128)S(1)} %fusion.44, pred[256,256]{1,0:T(8,128)(4,1)} %iota_compare_fusion, f32[16]{0:T(128)S(1)} %copy-done.14, ...), kind=kOutput, calls=%fused_computation.18 | convolution fusion | flops 559939584 | bytes 11731008 | tf_op jit(solution)/shard_map/cgjts,csgjp->ctgjp/dot_general | solution.py:386
  48.9 3.3 %fusion.11 = f32[4,16,64,128]{3,2,1,0:T(8,128)S(1)} fusion(f32[4,256,128]{2,1,0:T(8,128)S(1)} %copy-done.4, f32[4,256,16]{1,2,0:T(8,128)S(1)} %copy-done.5, bf16[4,256,16,64]{1,0,3,2:T(4,128)(2,1)S(1)} %copy-done.3), kind=kOutput, calls=%fused_computation.15 | convolution fusion | flops 272629760 | bytes 4784128 | tf_op jit(solution)/shard_map/csgjp,csgjn->cgjpn/dot_general | solution.py:390
  52.3 1.1 fusion.27
  53.4 0.7 broadcast_in_dim.15.decay_ref
  54.0 25.8 %state_scan.1 = f32[16,64,128]{2,1,0:T(8,128)} custom-call(f32[16,64,128]{2,1,0:T(8,128)} %get-tuple-element.9.state_ref, f32[16,128]{1,0:T(8,128)} %broadcast_in_dim.15.decay_ref), custom_call_target="tpu_custom_call" | custom-call | tf_op jit(solution)/shard_map/state_scan/pallas_call | solution.py:227
  79.8 3.1 %fusion.12 = f32[4,256,1,16,64]{1,4,3,0,2:T(8,128)S(1)} fusion(f32[4,256,1,16,64]{1,4,3,0,2:T(8,128)} %bitcast_add_fusion, bf16[4,256,128,1]{2,1,3,0:T(8,128)(2,1)S(1)} %bitcast.72, f32[4,256,16]{1,2,0:T(8,128)S(1)} %copy.61, f32[1,16,64,128]{3,2,1,0:T(8,128)S(1)} %get-tuple-element.10, f32[1,16,64,128]{3,2,1,0:T(8,128)S(1)} %get-tuple-element.11, ...), kind=kOutput, calls=%fused_computation.17 | convolution fusion | flops 273678336 | bytes 10813712 | tf_op jit(solution)/shard_map/ctgn,cgjpn->ctgjp/dot_general | solution.py:419
  82.9 2.8 %copy.66 = f32[4,256,1,16,64]{1,0,4,3,2:T(4,128)S(1)} copy(f32[4,256,1,16,64]{1,4,3,0,2:T(8,128)S(1)} %fusion.12) | data formatting | bytes 8388608 | tf_op jit(solution)/shard_map/add | solution.py:422
  85.7 1.0 copy.70
  87.3 1.3 multiply_reduce_fusion
  88.7 2.9 %fusion.17.normed_ref = bf16[1024,1024]{1,0:T(8,128)(2,1)} fusion(f32[1024]{0:T(1024)S(1)} %copy-done.7, f32[1024]{0:T(1024)S(1)} %add_rsqrt_fusion, f32[1024,1024]{0,1:T(8,128)S(1)} %bitcast.69, bf16[1024,1024]{0,1:T(8,128)(2,1)S(1)} %copy-done), kind=kLoop, calls=%fused_computation.31 | loop fusion | flops 9437184 | bytes 8396800 | tf_op jit(solution)/shard_map/transpose | solution.py:433
  91.6 53.2 %ring_projection.1 = bf16[1024,256]{1,0:T(8,128)(2,1)} custom-call(bf16[1024,1024]{1,0:T(8,128)(2,1)} %fusion.17.normed_ref, bf16[1024,2048]{1,0:T(8,128)(2,1)} %weight_ref.1), custom_call_target="tpu_custom_call" | custom-call | tf_op jit(solution)/shard_map/ring_projection/pallas_call | solution.py:327
  144.8 1.9 %copy.85 = bf16[1024,256]{1,0:T(8,128)(2,1)} copy(bf16[1024,256]{1,0:T(8,128)(2,1)} %ring_projection.1) | data formatting | bytes 1048576
  (62 shorter events, 4.6 us)
Async XLA Ops:
  0.0 18.1 %copy-start.2 = (bf16[1024,1024]{1,0:T(8,128)(2,1)S(1)}, bf16[1024,1024]{1,0:T(8,128)(2,1)}, u32[]{:S(2)}) copy-start(bf16[1024,1024]{1,0:T(8,128)(2,1)} %param.11) | copy-start | bytes 6291460
  1.8 26.7 %collective-permute-start = (bf16[3,1024]{0,1:T(8,128)(2,1)}, bf16[3,1024]{0,1:T(8,128)(2,1)}, u32[]{:S(2)}, u32[]{:S(2)}) collective-permute-start(bf16[3,1024]{0,1:T(8,128)(2,1)} %copy.44), channel_id=1, source_target_pairs={{0,8},{8,16},{16,24},{24,32},{32,40},{40,48},{48,56},{56,64},{64,7... | collective-permute-start | bytes 18440 | tf_op jit(solution)/shard_map/ppermute | solution.py:24
  4.8 21.8 %collective-permute-start.1 = (bf16[3,2,1,128]{3,0,2,1:T(4,128)(2,1)S(1)}, bf16[3,2,1,128]{3,0,2,1:T(4,128)(2,1)S(1)}, u32[]{:S(2)}, u32[]{:S(2)}) collective-permute-start(bf16[3,2,1,128]{3,0,2,1:T(4,128)(2,1)S(1)} %slice.133), channel_id=1, source_target_pairs={{0,8},{8,16},{16,24},{24,32},{32,40},{40,48},{48,56},{56,64},{64,7... | collective-permute-start | bytes 4616 | tf_op jit(solution)/shard_map/ppermute | solution.py:24
  26.0 2.5 %copy-start.1 = (bf16[1024,1024]{0,1:T(8,128)(2,1)S(1)}, bf16[1024,1024]{0,1:T(8,128)(2,1)}, u32[]{:S(2)}) copy-start(bf16[1024,1024]{0,1:T(8,128)(2,1)} %copy.45) | copy-start | bytes 6291460
  33.7 6.2 %copy-start.14 = (f32[16]{0:T(128)S(1)}, f32[16]{0:T(128)}, u32[]{:S(2)}) copy-start(f32[16]{0:T(128)} %param.17) | copy-start | bytes 196
  39.9 8.9 %copy-start.3 = (bf16[4,256,16,64]{1,0,3,2:T(4,128)(2,1)S(1)}, bf16[4,256,16,64]{1,0,3,2:T(4,128)(2,1)}, u32[]{:S(2)}) copy-start(bf16[4,256,16,64]{1,0,3,2:T(4,128)(2,1)} %reshape.324) | copy-start | bytes 6291460
  39.9 8.9 %copy-start.4 = (f32[4,256,128]{2,1,0:T(8,128)S(1)}, f32[4,256,128]{2,1,0:T(8,128)}, u32[]{:S(2)}) copy-start(f32[4,256,128]{2,1,0:T(8,128)} %convert_element_type.91) | copy-start | bytes 1572868
  39.9 8.9 %copy-start.5 = (f32[4,256,16]{1,2,0:T(8,128)S(1)}, f32[4,256,16]{1,2,0:T(8,128)}, u32[]{:S(2)}) copy-start(f32[4,256,16]{1,2,0:T(8,128)} %copy.64) | copy-start | bytes 196612
  48.9 3.4 %copy-start.9 = (f32[16]{0:T(128)S(1)}, f32[16]{0:T(128)}, u32[]{:S(2)}) copy-start(f32[16]{0:T(128)} %get-tuple-element.5) | copy-start | bytes 196
  48.9 3.4 %copy-start.10 = (f32[16]{0:T(128)S(1)}, f32[16]{0:T(128)}, u32[]{:S(2)}) copy-start(f32[16]{0:T(128)} %get-tuple-element.6) | copy-start | bytes 196
  48.9 3.4 %copy-start.11 = (f32[16]{0:T(128)S(1)}, f32[16]{0:T(128)}, u32[]{:S(2)}) copy-start(f32[16]{0:T(128)} %get-tuple-element.7) | copy-start | bytes 196
  48.9 3.4 %copy-start.12 = (f32[16]{0:T(128)S(1)}, f32[16]{0:T(128)}, u32[]{:S(2)}) copy-start(f32[16]{0:T(128)} %get-tuple-element.8) | copy-start | bytes 196
  52.2 1.1 copy-start.8
  52.2 27.6 %copy-start.6 = (f32[4,16]{1,0:T(4,128)S(1)}, f32[4,16]{1,0:T(4,128)}, u32[]{:S(2)}) copy-start(f32[4,16]{1,0:T(4,128)} %subtract_exponential_fusion) | copy-start | bytes 772
  52.2 27.6 %copy-start.13 = (f32[4]{0:T(128)S(1)}, f32[4]{0:T(128)}, u32[]{:S(2)}) copy-start(f32[4]{0:T(128)} %pad.clone) | copy-start | bytes 52
  85.7 1.6 %copy-start = (bf16[1024,1024]{0,1:T(8,128)(2,1)S(1)}, bf16[1024,1024]{0,1:T(8,128)(2,1)}, u32[]{:S(2)}) copy-start(bf16[1024,1024]{0,1:T(8,128)(2,1)} %copy.67) | copy-start | bytes 6291460
  86.8 1.9 %copy-start.7 = (f32[1024]{0:T(1024)S(1)}, f32[1024]{0:T(1024)}, u32[]{:S(2)}) copy-start(f32[1024]{0:T(1024)} %param.20) | copy-start | bytes 12292

commit v16 on v15

--- a/solution.py
+++ b/solution.py
@@ -252,7 +252,7 @@
     me = lax.axis_index("chan")
     seq = lax.axis_index("seq")
     width = out_ref.shape[1]
-    rows = normed_ref.shape[1] // (2 * pieces)
+    rows = normed_ref.shape[2]
     targets = (lax.rem(me + 1, count), lax.rem(me + count - 1, count))
 
     barrier = pltpu.get_barrier_semaphore()
@@ -279,7 +279,7 @@
         start = (direction * pieces + piece) * rows
         column = pl.multiple_of(block(direction, step) * width, width)
         return lax.dot_general(
-            normed_ref[:, pl.ds(start, rows)],
+            normed_ref[direction * pieces + piece],
             weight_ref[:, pl.ds(column, width)],
             (((0,), (0,)), ((), ())),
             preferred_element_type=jnp.float32,
@@ -319,8 +319,8 @@
 
 def ring_projection(normed, weight):
     count = lax.axis_size("chan")
-    pieces = 2
-    tokens = normed.shape[1]
+    pieces = normed.shape[0] // 2
+    tokens = normed.shape[0] * normed.shape[2]
     width = weight.shape[1] // count
     rows = tokens // (2 * pieces)
     buffers = (2, count - 1, pieces, rows, width)
@@ -421,16 +421,17 @@
         )
         y_all = y_pre[part] + y_carry
         gate_rows = gate_input[chunk * rows : (chunk + 1) * rows]
-        gated = y_all.reshape(rows, groups, width) * jax.nn.silu(
-            gate_rows.reshape(rows, groups, width).astype(jnp.float32)
-        )
-        square_mean = jnp.mean(gated * gated, axis=-1, keepdims=True)
-        normed = (
-            (gated * lax.rsqrt(square_mean + epsilon) * norm_gain.reshape(groups, width))
+        blocks_here = rows // BLOCK
+        y_cols = y_all.reshape(blocks_here, BLOCK, groups, width).transpose(0, 2, 3, 1)
+        gate_cols = gate_rows.reshape(blocks_here, BLOCK, groups, width).transpose(0, 2, 3, 1)
+        gated = y_cols * jax.nn.silu(gate_cols.astype(jnp.float32))
+        square_mean = jnp.mean(gated * gated, axis=2, keepdims=True)
+        normed_blocks = (
+            (gated * lax.rsqrt(square_mean + epsilon) * norm_gain.reshape(groups, width, 1))
             .astype(jnp.bfloat16)
-            .reshape(rows, head_count * HEAD_DIM)
-        )
-        outs.append(ring_projection(normed.T, out_weight))
+            .reshape(blocks_here, head_count * HEAD_DIM, BLOCK)
+        )
+        outs.append(ring_projection(normed_blocks, out_weight))
     return jnp.concatenate(outs, axis=0)
 
 

time: 147 us -> 153 us (1.041)
  local copies, waits for them, and re-layouts: 27 us -> 34.1 us
  other arithmetic: 19.3 us -> 17.1 us
    convert_element_type x1 -> x2, local copies, waits for them, and re-layouts: 3.41 us -> 12.1 us  [local(): skip_gain.reshape(groups, per_group)[:, :, None] * x_blocks]
    unnamed x35 -> x30, local copies, waits for them, and re-layouts: 11.1 us -> 3.51 us
    another operation x9 -> x10, local copies, waits for them, and re-layouts: 3.27 us -> 9.38 us
    convert_element_type x0 -> x1, local copies, waits for them, and re-layouts: none -> 3.01 us  [local(): gated = y_cols * jax.nn.silu(gate_cols.astype(jnp.float32))]
    transpose x1 -> x0, other arithmetic: 2.92 us -> none  [local(): outs.append(ring_projection(normed.T, out_weight))]
    add x1 -> x0, local copies, waits for them, and re-layouts: 2.79 us -> none  [local(): y_all = y_pre[part] + y_carry]
    reshape x0 -> x1, other arithmetic: none -> 1.79 us  [local(): normed_blocks = (gated * lax.rsqrt(square_mean + epsilon) * norm_gain.res...]
  transfers between devices with their start and end apart: 2 -> 2, of which waited for: 0 -> 0; matrix products, arithmetic and copies ran while one was open for 14% -> 12% of each run, Pallas kernels for 0% -> 0%
where the time goes in v16:
time: 153 us; the launch traced here: 152 us
  Pallas kernels  79 us (52%)
  local copies, waits for them, and re-layouts  34.1 us (22%)
  other arithmetic  17.1 us (11%)
  matrix products  16.4 us (11%)
  starting transfers between devices  5.41 us (4%)
    pallas_call x1, Pallas kernels, ring_projection(): pl.pallas_call(functools.partial(ring_kernel, count, pieces), out_shape=j...  53.2 us
    pallas_call x1, Pallas kernels, state_scan(): pl.pallas_call(functools.partial(state_scan_kernel, count), out_shape=jax...  25.8 us
    convert_element_type x2, local copies, waits for them, and re-layouts, local(): skip_gain.reshape(groups, per_group)[:, :, None] * x_blocks  12.1 us
    dot_general x1, matrix products, local(): jnp.einsum('cgjts,csgjp->ctgjp', mixing, x_blocks, preferred_element_type...  9.57 us
    another operation x10, local copies, waits for them, and re-layouts  9.38 us
    ppermute x2, starting transfers between devices, passed_along(): return lax.ppermute(x, axis, pairs)  5.41 us
    convert_element_type x2, other arithmetic, conv_silu(): return jax.nn.silu(acc).astype(jnp.bfloat16)  4.47 us
    unnamed x30, local copies, waits for them, and re-layouts  3.51 us
  transfers between devices with their start and end apart: 2, of which 0 were waited for; matrix products, arithmetic and copies ran while one was open for 12% of the time, Pallas kernels for 0%

profile of v16, /device:TPU:24, one launch (start us, length us, event | category | flops | bytes accessed | tf_op | source)
XLA Modules:
  0.0 152.3 jit_solution(12738883914433264623)
XLA Ops:
  0.0 1.3 copy.37
  1.3 1.9 %collective-permute-start.1 = (bf16[3,2,1,128]{3,0,2,1:T(4,128)(2,1)S(1)}, bf16[3,2,1,128]{3,0,2,1:T(4,128)(2,1)S(1)}, u32[]{:S(2)}, u32[]{:S(2)}) collective-permute-start(bf16[3,2,1,128]{3,0,2,1:T(4,128)(2,1)S(1)} %slice.133), channel_id=1, source_target_pairs={{0,8},{8,16},{16,24},{24,32},{32,40},{40,48},{48,56},{56,64},{64,7... | collective-permute-start | bytes 4616 | tf_op jit(solution)/shard_map/ppermute | solution.py:24
  3.2 1.3 slice.101
  4.5 3.5 %collective-permute-start = (bf16[3,1024]{1,0:T(4,128)(2,1)}, bf16[3,1024]{1,0:T(4,128)(2,1)}, u32[]{:S(2)}, u32[]{:S(2)}) collective-permute-start(bf16[3,1024]{1,0:T(4,128)(2,1)} %slice.101), channel_id=1, source_target_pairs={{0,8},{8,16},{16,24},{24,32},{32,40},{40,48},{48,56},{56,64},{64,7... | collective-permute-start | bytes 18440 | tf_op jit(solution)/shard_map/ppermute | solution.py:24
  8.0 0.7 exponential_negate_fusion
  8.7 1.0 broadcast_multiply_fusion
  9.8 2.3 %reduce-window.6 = f32[4,16,1,2,128]{4,1,2,3,0:T(8,128)S(1)} reduce-window(f32[4,16,1,2,128]{4,1,2,3,0:T(8,128)S(1)} %copy.41, f32[]{:T(128)} %constant.13.clone.1), window={size=1x1x1x1x128 pad=0_0x0_0x0_0x0_0x127_0}, to_apply=%region_0.1 | reduce-window | flops 2080768 | bytes 131076 | tf_op jit(solution)/shard_map/reduce-window
  12.7 0.9 slice_reduce_fusion
  13.6 1.0 fusion.28
  14.9 0.7 fusion.40
  15.6 0.9 fusion.39
  17.2 0.6 iota_compare_fusion
  18.0 0.6 copy.55
  18.6 0.6 copy.45
  19.3 3.0 %copy.57 = f32[4,256,1,1024]{1,3,0,2:T(8,128)} copy(bf16[4,256,1,1024]{3,1,0,2:T(8,128)(2,1)S(1)} %bitcast.86) | data formatting | bytes 6291456 | tf_op jit(solution)/shard_map/convert_element_type | solution.py:427
  22.9 0.7 multiply_convert_fusion.8
  24.0 0.8 convert_element_type.95
  24.8 3.8 %multiply_convert_fusion.5 = bf16[1024,1024]{1,0:T(8,128)(2,1)S(1)} fusion(bf16[1024,1024]{1,0:T(8,128)(2,1)S(1)} %copy-done.1, bf16[3,1024]{1,0:T(4,128)(2,1)} %collective-permute-done, f32[1024]{0:T(1024)S(1)} %bitcast.94, f32[1024]{0:T(1024)S(1)} %bitcast.95, f32[1024]{0:T(1024)S(1)} %bitcast.93, f32[1024]{0:T(1024)S(1)} %bitcast.92), kind=kLoop, calls=%fused_computation.23 | loop fusion | flops 26214400 | bytes 4216832 | tf_op jit(solution)/shard_map/convert_element_type | solution.py:31
  28.6 4.0 %reshape.335 = bf16[4,256,16,64]{3,2,1,0:T(8,128)(2,1)} reshape(bf16[1024,1024]{1,0:T(8,128)(2,1)S(1)} %multiply_convert_fusion.5) | data formatting | bytes 4194304 | tf_op jit(solution)/shard_map/reshape.26
  32.6 4.4 %reshape.333 = f32[4,256,1,16,64]{4,3,1,0,2:T(8,128)} reshape(bf16[1024,1024]{1,0:T(8,128)(2,1)S(1)} %multiply_convert_fusion.5) | data formatting | bytes 6291456 | tf_op jit(solution)/shard_map/convert_element_type | solution.py:411
  37.1 4.8 %copy.46 = bf16[4,256,16,64]{1,3,2,0:T(8,128)(2,1)S(1)} copy(bf16[4,256,16,64]{3,2,1,0:T(8,128)(2,1)} %reshape.335) | data formatting | bytes 4194304 | tf_op jit(solution)/shard_map/reshape.26
  41.9 7.7 %copy.48 = f32[4,256,1,16,64]{1,4,3,0,2:T(8,128)} copy(f32[4,256,1,16,64]{4,3,1,0,2:T(8,128)} %reshape.333) | data formatting | bytes 8388608 | tf_op jit(solution)/shard_map/convert_element_type | solution.py:411
  49.6 9.6 %bitcast_add_fusion = f32[4,256,1,16,64]{1,4,3,0,2:T(8,128)} fusion(f32[4,256,1,16,64]{1,4,3,0,2:T(8,128)} %copy.48, bf16[4,256,16,64]{1,3,2,0:T(8,128)(2,1)S(1)} %copy.46, f32[4,16,256]{2,1,0:T(8,128)} %copy.45, f32[4,16,256]{2,1,0:T(8,128)S(1)} %reduce_window_sum.44, f32[4,256,256]{2,1,0:T(8,128)S(1)} %fusion.41, pred[256,256]{1,0:T(8,128)(4,1)} %iota_compare_fusion, ...), kind=kOutput, calls=%fused_computation.13 | convolution fusion | flops 559939584 | bytes 11731008 | tf_op jit(solution)/shard_map/cgjts,csgjp->ctgjp/dot_general | solution.py:386
  59.3 3.3 %fusion.7 = f32[4,16,64,128]{3,2,1,0:T(8,128)S(1)} fusion(bf16[4,256,16,64]{1,3,2,0:T(8,128)(2,1)S(1)} %copy.46, f32[4,256,128]{2,1,0:T(8,128)S(1)} %copy-done.3, f32[4,256,16]{1,2,0:T(8,128)S(1)} %copy-done.4), kind=kOutput, calls=%fused_computation.9 | convolution fusion | flops 272629760 | bytes 4784128 | tf_op jit(solution)/shard_map/csgjp,csgjn->cgjpn/dot_general | solution.py:390
  62.6 1.1 fusion.24
  63.7 0.7 broadcast_in_dim.15.decay_ref
  64.3 25.8 %state_scan.1 = f32[16,64,128]{2,1,0:T(8,128)} custom-call(f32[16,64,128]{2,1,0:T(8,128)} %get-tuple-element.11.state_ref, f32[16,128]{1,0:T(8,128)} %broadcast_in_dim.15.decay_ref), custom_call_target="tpu_custom_call" | custom-call | tf_op jit(solution)/shard_map/state_scan/pallas_call | solution.py:227
  90.1 3.3 %fusion.8 = f32[4,256,1,16,64]{1,4,3,0,2:T(8,128)S(1)} fusion(f32[4,256,1,16,64]{1,4,3,0,2:T(8,128)} %bitcast_add_fusion, bf16[4,256,128,1]{2,1,3,0:T(8,128)(2,1)S(1)} %bitcast.83, f32[4,256,16]{1,2,0:T(8,128)S(1)} %copy.52, f32[1,16,64,128]{3,2,1,0:T(8,128)S(1)} %get-tuple-element.12, f32[1,16,64,128]{3,2,1,0:T(8,128)S(1)} %get-tuple-element.13, ...), kind=kOutput, calls=%fused_computation.12 | convolution fusion | flops 273678336 | bytes 10813712 | tf_op jit(solution)/shard_map/ctgn,cgjpn->ctgjp/dot_general | solution.py:419
  93.7 1.7 %multiply_reduce_fusion = (f32[4,256]{1,0:T(4,128)S(1)}, f32[4,1,1024,256]{3,2,0,1:T(8,128)S(1)}) fusion(f32[4,256,1,1024]{1,3,0,2:T(8,128)S(1)} %copy-done, f32[4,256,1,16,64]{1,4,3,0,2:T(8,128)S(1)} %fusion.8), kind=kLoop, calls=%fused_computation.20 | loop fusion | flops 7339008 | bytes 12587008 | tf_op jit(solution)/shard_map/reduce_sum | solution.py:428
  95.5 1.8 %fusion.16.normed_ref = bf16[4,1024,256]{2,1,0:T(8,128)(2,1)} fusion(f32[4,1,1024,256]{3,2,0,1:T(8,128)S(1)} %get-tuple-element.10, f32[1024]{0:T(1024)S(1)} %copy-done.6, f32[4,256]{1,0:T(4,128)S(1)} %add_rsqrt_fusion), kind=kLoop, calls=%fused_computation.28 | loop fusion | flops 3145728 | bytes 6299648 | tf_op jit(solution)/shard_map/reshape | solution.py:432
  97.2 53.2 %ring_projection.1 = bf16[1024,256]{1,0:T(8,128)(2,1)} custom-call(bf16[4,1024,256]{2,1,0:T(8,128)(2,1)} %fusion.16.normed_ref, bf16[1024,2048]{1,0:T(8,128)(2,1)} %weight_ref.1), custom_call_target="tpu_custom_call" | custom-call | tf_op jit(solution)/shard_map/ring_projection/pallas_call | solution.py:327
  150.5 1.9 %copy.71 = bf16[1024,256]{1,0:T(8,128)(2,1)} copy(bf16[1024,256]{1,0:T(8,128)(2,1)} %ring_projection.1) | data formatting | bytes 1048576
  (58 shorter events, 3.2 us)
Async XLA Ops:
  0.0 19.3 %copy-start.2 = (bf16[1024,1024]{1,0:T(8,128)(2,1)S(1)}, bf16[1024,1024]{1,0:T(8,128)(2,1)}, u32[]{:S(2)}) copy-start(bf16[1024,1024]{1,0:T(8,128)(2,1)} %param.13) | copy-start | bytes 6291460
  1.3 21.6 %collective-permute-start.1 = (bf16[3,2,1,128]{3,0,2,1:T(4,128)(2,1)S(1)}, bf16[3,2,1,128]{3,0,2,1:T(4,128)(2,1)S(1)}, u32[]{:S(2)}, u32[]{:S(2)}) collective-permute-start(bf16[3,2,1,128]{3,0,2,1:T(4,128)(2,1)S(1)} %slice.133), channel_id=1, source_target_pairs={{0,8},{8,16},{16,24},{24,32},{32,40},{40,48},{48,56},{56,64},{64,7... | collective-permute-start | bytes 4616 | tf_op jit(solution)/shard_map/ppermute | solution.py:24
  4.5 20.3 %collective-permute-start = (bf16[3,1024]{1,0:T(4,128)(2,1)}, bf16[3,1024]{1,0:T(4,128)(2,1)}, u32[]{:S(2)}, u32[]{:S(2)}) collective-permute-start(bf16[3,1024]{1,0:T(4,128)(2,1)} %slice.101), channel_id=1, source_target_pairs={{0,8},{8,16},{16,24},{24,32},{32,40},{40,48},{48,56},{56,64},{64,7... | collective-permute-start | bytes 18440 | tf_op jit(solution)/shard_map/ppermute | solution.py:24
  22.3 2.5 %copy-start.1 = (bf16[1024,1024]{1,0:T(8,128)(2,1)S(1)}, bf16[1024,1024]{1,0:T(8,128)(2,1)}, u32[]{:S(2)}) copy-start(bf16[1024,1024]{1,0:T(8,128)(2,1)} %param.11) | copy-start | bytes 6291460
  41.9 7.7 %copy-start.13 = (f32[16]{0:T(128)S(1)}, f32[16]{0:T(128)}, u32[]{:S(2)}) copy-start(f32[16]{0:T(128)} %param.17) | copy-start | bytes 196
  49.6 9.6 %copy-start.3 = (f32[4,256,128]{2,1,0:T(8,128)S(1)}, f32[4,256,128]{2,1,0:T(8,128)}, u32[]{:S(2)}) copy-start(f32[4,256,128]{2,1,0:T(8,128)} %convert_element_type.95) | copy-start | bytes 1572868
  49.6 9.6 %copy-start.4 = (f32[4,256,16]{1,2,0:T(8,128)S(1)}, f32[4,256,16]{1,2,0:T(8,128)}, u32[]{:S(2)}) copy-start(f32[4,256,16]{1,2,0:T(8,128)} %copy.55) | copy-start | bytes 196612
  59.2 3.3 %copy-start.8 = (f32[16]{0:T(128)S(1)}, f32[16]{0:T(128)}, u32[]{:S(2)}) copy-start(f32[16]{0:T(128)} %get-tuple-element.5) | copy-start | bytes 196
  59.2 3.3 %copy-start.9 = (f32[16]{0:T(128)S(1)}, f32[16]{0:T(128)}, u32[]{:S(2)}) copy-start(f32[16]{0:T(128)} %get-tuple-element.6) | copy-start | bytes 196
  59.2 3.3 %copy-start.10 = (f32[16]{0:T(128)S(1)}, f32[16]{0:T(128)}, u32[]{:S(2)}) copy-start(f32[16]{0:T(128)} %get-tuple-element.7) | copy-start | bytes 196
  59.3 3.3 %copy-start.11 = (f32[16]{0:T(128)S(1)}, f32[16]{0:T(128)}, u32[]{:S(2)}) copy-start(f32[16]{0:T(128)} %get-tuple-element.8) | copy-start | bytes 196
  59.3 4.4 %copy-start.7 = (f32[16]{0:T(128)S(1)}, f32[16]{0:T(128)}, u32[]{:S(2)}) copy-start(f32[16]{0:T(128)} %get-tuple-element.21) | copy-start | bytes 196
  62.5 27.6 %copy-start.5 = (f32[4,16]{1,0:T(4,128)S(1)}, f32[4,16]{1,0:T(4,128)}, u32[]{:S(2)}) copy-start(f32[4,16]{1,0:T(4,128)} %subtract_exponential_fusion) | copy-start | bytes 772
  62.6 27.6 %copy-start.12 = (f32[4]{0:T(128)S(1)}, f32[4]{0:T(128)}, u32[]{:S(2)}) copy-start(f32[4]{0:T(128)} %pad.clone) | copy-start | bytes 52
  90.1 3.6 %copy-start = (f32[4,256,1,1024]{1,3,0,2:T(8,128)S(1)}, f32[4,256,1,1024]{1,3,0,2:T(8,128)}, u32[]{:S(2)}) copy-start(f32[4,256,1,1024]{1,3,0,2:T(8,128)} %copy.57) | copy-start | bytes 12582916
  93.7 1.7 %copy-start.6 = (f32[1024]{0:T(1024)S(1)}, f32[1024]{0:T(1024)}, u32[]{:S(2)}) copy-start(f32[1024]{0:T(1024)} %param.20) | copy-start | bytes 12292

commit v17 on v15

--- a/solution.py
+++ b/solution.py
@@ -258,7 +258,6 @@
     barrier = pltpu.get_barrier_semaphore()
     for target in targets:
         pl.semaphore_signal(barrier, 1, device_id=(seq, target), device_id_type=MESH)
-    pl.semaphore_wait(barrier, 2)
 
     def copy(direction, step, piece):
         return pltpu.make_async_remote_copy(
@@ -299,7 +298,13 @@
                     send_buf[direction, step, piece] = value.astype(send_buf.dtype)
                     copy(direction, step, piece).start()
 
-    run_step(0, True, False)
+    for piece in range(pieces):
+        for direction in range(2):
+            send_buf[direction, 0, piece] = partial(direction, 0, piece).astype(send_buf.dtype)
+    pl.semaphore_wait(barrier, 2)
+    for piece in range(pieces):
+        for direction in range(2):
+            copy(direction, 0, piece).start()
 
     def middle(step, carry):
         run_step(step, False, False)

time: 147 us -> 147 us (level)
  no operation moved by 1% of the time
where the time goes in v17:
time: 147 us; the launch traced here: 146 us
  Pallas kernels  78.5 us (53%)
  local copies, waits for them, and re-layouts  27 us (18%)
  other arithmetic  19.3 us (13%)
  matrix products  15.6 us (11%)
  starting transfers between devices  5.41 us (4%)
    pallas_call x1, Pallas kernels, ring_projection(): pl.pallas_call(functools.partial(ring_kernel, count, pieces), out_shape=j...  52.8 us
    pallas_call x1, Pallas kernels, state_scan(): pl.pallas_call(functools.partial(state_scan_kernel, count), out_shape=jax...  25.8 us
    unnamed x35, local copies, waits for them, and re-layouts  11.1 us
    dot_general x1, matrix products, local(): jnp.einsum('cgjts,csgjp->ctgjp', mixing, x_blocks, preferred_element_type...  8.92 us
    convert_element_type x2, other arithmetic, conv_silu(): return jax.nn.silu(acc).astype(jnp.bfloat16)  5.9 us
    ppermute x2, starting transfers between devices, passed_along(): return lax.ppermute(x, axis, pairs)  5.41 us
    convert_element_type x1, local copies, waits for them, and re-layouts, local(): skip_gain.reshape(groups, per_group)[:, :, None] * x_blocks  3.41 us
    dot_general x1, matrix products, local(): jnp.einsum('csgjp,csgjn->cgjpn', x_blocks, weighted, preferred_element_ty...  3.29 us
  transfers between devices with their start and end apart: 2, of which 0 were waited for; matrix products, arithmetic and copies ran while one was open for 14% of the time, Pallas kernels for 0%

profile of v17, /device:TPU:24, one launch (start us, length us, event | category | flops | bytes accessed | tf_op | source)
XLA Modules:
  0.0 146.3 jit_solution(7695217537722257365)
XLA Ops:
  0.0 0.9 slice.101
  0.9 0.9 copy.44
  1.8 1.9 %collective-permute-start = (bf16[3,1024]{0,1:T(8,128)(2,1)}, bf16[3,1024]{0,1:T(8,128)(2,1)}, u32[]{:S(2)}, u32[]{:S(2)}) collective-permute-start(bf16[3,1024]{0,1:T(8,128)(2,1)} %copy.44), channel_id=1, source_target_pairs={{0,8},{8,16},{16,24},{24,32},{32,40},{40,48},{48,56},{56,64},{64,7... | collective-permute-start | bytes 18440 | tf_op jit(solution)/shard_map/ppermute | solution.py:24
  3.7 1.1 copy.47
  4.8 3.5 %collective-permute-start.1 = (bf16[3,2,1,128]{3,0,2,1:T(4,128)(2,1)S(1)}, bf16[3,2,1,128]{3,0,2,1:T(4,128)(2,1)S(1)}, u32[]{:S(2)}, u32[]{:S(2)}) collective-permute-start(bf16[3,2,1,128]{3,0,2,1:T(4,128)(2,1)S(1)} %slice.133), channel_id=1, source_target_pairs={{0,8},{8,16},{16,24},{24,32},{32,40},{40,48},{48,56},{56,64},{64,7... | collective-permute-start | bytes 4616 | tf_op jit(solution)/shard_map/ppermute | solution.py:24
  8.3 0.7 exponential_negate_fusion
  9.0 1.0 broadcast_multiply_fusion
  10.1 2.3 %reduce-window.6 = f32[4,16,1,2,128]{4,1,2,3,0:T(8,128)S(1)} reduce-window(f32[4,16,1,2,128]{4,1,2,3,0:T(8,128)S(1)} %copy.51, f32[]{:T(128)} %constant.13.clone.1), window={size=1x1x1x1x128 pad=0_0x0_0x0_0x0_0x127_0}, to_apply=%region_0.1 | reduce-window | flops 2080768 | bytes 131076 | tf_op jit(solution)/shard_map/reduce-window
  13.0 0.8 slice_reduce_fusion
  13.9 1.1 fusion.31
  15.1 0.9 fusion.42
  16.1 0.7 fusion.43
  17.4 0.6 iota_compare_fusion
  18.1 2.6 %copy.45 = bf16[1024,1024]{0,1:T(8,128)(2,1)} copy(bf16[1024,1024]{1,0:T(8,128)(2,1)S(1)} %copy-done.2) | data formatting | bytes 4194304 | tf_op args[0]
  22.1 3.9 %copy.67 = bf16[1024,1024]{0,1:T(8,128)(2,1)} copy(bf16[1024,1024]{1,0:T(8,128)(2,1)} %param.13) | data formatting | bytes 4194304 | tf_op args[2]
  26.6 0.7 multiply_convert_fusion.8
  27.7 0.8 convert_element_type.91
  28.5 5.2 %multiply_convert_fusion.5 = bf16[1024,1024]{0,1:T(8,128)(2,1)S(1)} fusion(bf16[1024,1024]{0,1:T(8,128)(2,1)S(1)} %copy-done.1, bf16[3,1024]{0,1:T(8,128)(2,1)} %collective-permute-done, f32[1024]{0:T(1024)S(1)} %bitcast.82, f32[1024]{0:T(1024)S(1)} %bitcast.83, f32[1024]{0:T(1024)S(1)} %bitcast.81, f32[1024]{0:T(1024)S(1)} %bitcast.80), kind=kLoop, calls=%fused_computation.24 | loop fusion | flops 26214400 | bytes 4216832 | tf_op jit(solution)/shard_map/convert_element_type | solution.py:31
  33.7 3.4 %reshape.338 = f32[4,256,1,16,64]{1,0,4,3,2:T(4,128)} reshape(bf16[1024,1024]{0,1:T(8,128)(2,1)S(1)} %multiply_convert_fusion.5) | data formatting | bytes 6291456 | tf_op jit(solution)/shard_map/convert_element_type | solution.py:416
  37.1 2.8 %reshape.324 = bf16[4,256,16,64]{1,0,3,2:T(4,128)(2,1)} reshape(bf16[1024,1024]{0,1:T(8,128)(2,1)S(1)} %multiply_convert_fusion.5) | data formatting | bytes 4194304 | tf_op jit(solution)/shard_map/reshape.26
  39.9 8.9 %bitcast_add_fusion = f32[4,256,1,16,64]{1,4,3,0,2:T(8,128)} fusion(f32[4,256,1,16,64]{1,0,4,3,2:T(4,128)} %reshape.338, f32[4,16,256]{2,1,0:T(8,128)} %copy.55, f32[4,16,256]{2,1,0:T(8,128)S(1)} %reduce_window_sum.44, f32[4,256,256]{2,1,0:T(8,128)S(1)} %fusion.44, pred[256,256]{1,0:T(8,128)(4,1)} %iota_compare_fusion, f32[16]{0:T(128)S(1)} %copy-done.14, ...), kind=kOutput, calls=%fused_computation.18 | convolution fusion | flops 559939584 | bytes 11731008 | tf_op jit(solution)/shard_map/cgjts,csgjp->ctgjp/dot_general | solution.py:391
  48.9 3.3 %fusion.11 = f32[4,16,64,128]{3,2,1,0:T(8,128)S(1)} fusion(f32[4,256,128]{2,1,0:T(8,128)S(1)} %copy-done.4, f32[4,256,16]{1,2,0:T(8,128)S(1)} %copy-done.5, bf16[4,256,16,64]{1,0,3,2:T(4,128)(2,1)S(1)} %copy-done.3), kind=kOutput, calls=%fused_computation.15 | convolution fusion | flops 272629760 | bytes 4784128 | tf_op jit(solution)/shard_map/csgjp,csgjn->cgjpn/dot_general | solution.py:395
  52.3 1.1 fusion.27
  53.4 0.7 broadcast_in_dim.15.decay_ref
  54.0 25.8 %state_scan.1 = f32[16,64,128]{2,1,0:T(8,128)} custom-call(f32[16,64,128]{2,1,0:T(8,128)} %get-tuple-element.9.state_ref, f32[16,128]{1,0:T(8,128)} %broadcast_in_dim.15.decay_ref), custom_call_target="tpu_custom_call" | custom-call | tf_op jit(solution)/shard_map/state_scan/pallas_call | solution.py:227
  79.8 3.1 %fusion.12 = f32[4,256,1,16,64]{1,4,3,0,2:T(8,128)S(1)} fusion(f32[4,256,1,16,64]{1,4,3,0,2:T(8,128)} %bitcast_add_fusion, bf16[4,256,128,1]{2,1,3,0:T(8,128)(2,1)S(1)} %bitcast.72, f32[4,256,16]{1,2,0:T(8,128)S(1)} %copy.61, f32[1,16,64,128]{3,2,1,0:T(8,128)S(1)} %get-tuple-element.10, f32[1,16,64,128]{3,2,1,0:T(8,128)S(1)} %get-tuple-element.11, ...), kind=kOutput, calls=%fused_computation.17 | convolution fusion | flops 273678336 | bytes 10813712 | tf_op jit(solution)/shard_map/ctgn,cgjpn->ctgjp/dot_general | solution.py:424
  82.9 2.8 %copy.66 = f32[4,256,1,16,64]{1,0,4,3,2:T(4,128)S(1)} copy(f32[4,256,1,16,64]{1,4,3,0,2:T(8,128)S(1)} %fusion.12) | data formatting | bytes 8388608 | tf_op jit(solution)/shard_map/add | solution.py:427
  85.7 1.0 copy.70
  87.3 1.3 multiply_reduce_fusion
  88.7 2.9 %fusion.17.normed_ref = bf16[1024,1024]{1,0:T(8,128)(2,1)} fusion(f32[1024]{0:T(1024)S(1)} %copy-done.7, f32[1024]{0:T(1024)S(1)} %add_rsqrt_fusion, f32[1024,1024]{0,1:T(8,128)S(1)} %bitcast.69, bf16[1024,1024]{0,1:T(8,128)(2,1)S(1)} %copy-done), kind=kLoop, calls=%fused_computation.31 | loop fusion | flops 9437184 | bytes 8396800 | tf_op jit(solution)/shard_map/transpose | solution.py:438
  91.6 52.8 %ring_projection.1 = bf16[1024,256]{1,0:T(8,128)(2,1)} custom-call(bf16[1024,1024]{1,0:T(8,128)(2,1)} %fusion.17.normed_ref, bf16[1024,2048]{1,0:T(8,128)(2,1)} %weight_ref.1), custom_call_target="tpu_custom_call" | custom-call | tf_op jit(solution)/shard_map/ring_projection/pallas_call | solution.py:332
  144.4 1.9 %copy.85 = bf16[1024,256]{1,0:T(8,128)(2,1)} copy(bf16[1024,256]{1,0:T(8,128)(2,1)} %ring_projection.1) | data formatting | bytes 1048576
  (62 shorter events, 4.6 us)
Async XLA Ops:
  0.0 18.1 %copy-start.2 = (bf16[1024,1024]{1,0:T(8,128)(2,1)S(1)}, bf16[1024,1024]{1,0:T(8,128)(2,1)}, u32[]{:S(2)}) copy-start(bf16[1024,1024]{1,0:T(8,128)(2,1)} %param.11) | copy-start | bytes 6291460
  1.8 26.7 %collective-permute-start = (bf16[3,1024]{0,1:T(8,128)(2,1)}, bf16[3,1024]{0,1:T(8,128)(2,1)}, u32[]{:S(2)}, u32[]{:S(2)}) collective-permute-start(bf16[3,1024]{0,1:T(8,128)(2,1)} %copy.44), channel_id=1, source_target_pairs={{0,8},{8,16},{16,24},{24,32},{32,40},{40,48},{48,56},{56,64},{64,7... | collective-permute-start | bytes 18440 | tf_op jit(solution)/shard_map/ppermute | solution.py:24
  4.8 21.8 %collective-permute-start.1 = (bf16[3,2,1,128]{3,0,2,1:T(4,128)(2,1)S(1)}, bf16[3,2,1,128]{3,0,2,1:T(4,128)(2,1)S(1)}, u32[]{:S(2)}, u32[]{:S(2)}) collective-permute-start(bf16[3,2,1,128]{3,0,2,1:T(4,128)(2,1)S(1)} %slice.133), channel_id=1, source_target_pairs={{0,8},{8,16},{16,24},{24,32},{32,40},{40,48},{48,56},{56,64},{64,7... | collective-permute-start | bytes 4616 | tf_op jit(solution)/shard_map/ppermute | solution.py:24
  26.0 2.5 %copy-start.1 = (bf16[1024,1024]{0,1:T(8,128)(2,1)S(1)}, bf16[1024,1024]{0,1:T(8,128)(2,1)}, u32[]{:S(2)}) copy-start(bf16[1024,1024]{0,1:T(8,128)(2,1)} %copy.45) | copy-start | bytes 6291460
  33.7 6.2 %copy-start.14 = (f32[16]{0:T(128)S(1)}, f32[16]{0:T(128)}, u32[]{:S(2)}) copy-start(f32[16]{0:T(128)} %param.17) | copy-start | bytes 196
  39.9 8.9 %copy-start.3 = (bf16[4,256,16,64]{1,0,3,2:T(4,128)(2,1)S(1)}, bf16[4,256,16,64]{1,0,3,2:T(4,128)(2,1)}, u32[]{:S(2)}) copy-start(bf16[4,256,16,64]{1,0,3,2:T(4,128)(2,1)} %reshape.324) | copy-start | bytes 6291460
  39.9 8.9 %copy-start.4 = (f32[4,256,128]{2,1,0:T(8,128)S(1)}, f32[4,256,128]{2,1,0:T(8,128)}, u32[]{:S(2)}) copy-start(f32[4,256,128]{2,1,0:T(8,128)} %convert_element_type.91) | copy-start | bytes 1572868
  39.9 8.9 %copy-start.5 = (f32[4,256,16]{1,2,0:T(8,128)S(1)}, f32[4,256,16]{1,2,0:T(8,128)}, u32[]{:S(2)}) copy-start(f32[4,256,16]{1,2,0:T(8,128)} %copy.64) | copy-start | bytes 196612
  48.9 3.4 %copy-start.9 = (f32[16]{0:T(128)S(1)}, f32[16]{0:T(128)}, u32[]{:S(2)}) copy-start(f32[16]{0:T(128)} %get-tuple-element.5) | copy-start | bytes 196
  48.9 3.4 %copy-start.10 = (f32[16]{0:T(128)S(1)}, f32[16]{0:T(128)}, u32[]{:S(2)}) copy-start(f32[16]{0:T(128)} %get-tuple-element.6) | copy-start | bytes 196
  48.9 3.4 %copy-start.11 = (f32[16]{0:T(128)S(1)}, f32[16]{0:T(128)}, u32[]{:S(2)}) copy-start(f32[16]{0:T(128)} %get-tuple-element.7) | copy-start | bytes 196
  48.9 3.4 %copy-start.12 = (f32[16]{0:T(128)S(1)}, f32[16]{0:T(128)}, u32[]{:S(2)}) copy-start(f32[16]{0:T(128)} %get-tuple-element.8) | copy-start | bytes 196
  52.2 1.1 copy-start.8
  52.2 27.6 %copy-start.6 = (f32[4,16]{1,0:T(4,128)S(1)}, f32[4,16]{1,0:T(4,128)}, u32[]{:S(2)}) copy-start(f32[4,16]{1,0:T(4,128)} %subtract_exponential_fusion) | copy-start | bytes 772
  52.2 27.6 %copy-start.13 = (f32[4]{0:T(128)S(1)}, f32[4]{0:T(128)}, u32[]{:S(2)}) copy-start(f32[4]{0:T(128)} %pad.clone) | copy-start | bytes 52
  85.7 1.6 %copy-start = (bf16[1024,1024]{0,1:T(8,128)(2,1)S(1)}, bf16[1024,1024]{0,1:T(8,128)(2,1)}, u32[]{:S(2)}) copy-start(bf16[1024,1024]{0,1:T(8,128)(2,1)} %copy.67) | copy-start | bytes 6291460
  86.8 1.9 %copy-start.7 = (f32[1024]{0:T(1024)S(1)}, f32[1024]{0:T(1024)}, u32[]{:S(2)}) copy-start(f32[1024]{0:T(1024)} %param.20) | copy-start | bytes 12292

commit v18 on v15

--- a/solution.py
+++ b/solution.py
@@ -75,6 +75,8 @@
                 )
 
             peers = peers + valid.astype(jnp.int32)
+    own_s[...] = state_ref[...].astype(jnp.bfloat16)
+    own_d[...] = decay_ref[...]
     pl.semaphore_wait(barrier, peers)
 
     def remote(src, dst, slot, part, target, piece=0):
@@ -83,8 +85,6 @@
             device_id=(target, chan), device_id_type=MESH,
         )
 
-    own_s[...] = state_ref[...].astype(jnp.bfloat16)
-    own_d[...] = decay_ref[...]
     first = [
         lambda t: remote(own_s, pair_s, 0, 0, t),
         lambda t: remote(own_s.at[0:half], pair_s.at[0:half], 0, 0, t),

time: 147 us -> 147 us (level)
  no operation moved by 1% of the time
where the time goes in v18:
time: 147 us
  Pallas kernels  79.1 us (54%)
  local copies, waits for them, and re-layouts  27 us (18%)
  other arithmetic  19.3 us (13%)
  matrix products  15.6 us (11%)
  starting transfers between devices  5.41 us (4%)
    pallas_call x1, Pallas kernels, ring_projection(): pl.pallas_call(functools.partial(ring_kernel, count, pieces), out_shape=j...  53.3 us
    pallas_call x1, Pallas kernels, state_scan(): pl.pallas_call(functools.partial(state_scan_kernel, count), out_shape=jax...  25.7 us
    unnamed x35, local copies, waits for them, and re-layouts  11.1 us
    dot_general x1, matrix products, local(): jnp.einsum('cgjts,csgjp->ctgjp', mixing, x_blocks, preferred_element_type...  8.92 us
    convert_element_type x2, other arithmetic, conv_silu(): return jax.nn.silu(acc).astype(jnp.bfloat16)  5.9 us
    ppermute x2, starting transfers between devices, passed_along(): return lax.ppermute(x, axis, pairs)  5.41 us
    convert_element_type x1, local copies, waits for them, and re-layouts, local(): skip_gain.reshape(groups, per_group)[:, :, None] * x_blocks  3.41 us
    dot_general x1, matrix products, local(): jnp.einsum('csgjp,csgjn->cgjpn', x_blocks, weighted, preferred_element_ty...  3.29 us
  transfers between devices with their start and end apart: 2, of which 0 were waited for; matrix products, arithmetic and copies ran while one was open for 14% of the time, Pallas kernels for 0%

profile of v18, /device:TPU:24, one launch (start us, length us, event | category | flops | bytes accessed | tf_op | source)
XLA Modules:
  0.0 146.8 jit_solution(6478553977240171080)
XLA Ops:
  0.0 0.9 slice.101
  0.9 0.9 copy.44
  1.8 1.9 %collective-permute-start = (bf16[3,1024]{0,1:T(8,128)(2,1)}, bf16[3,1024]{0,1:T(8,128)(2,1)}, u32[]{:S(2)}, u32[]{:S(2)}) collective-permute-start(bf16[3,1024]{0,1:T(8,128)(2,1)} %copy.44), channel_id=1, source_target_pairs={{0,8},{8,16},{16,24},{24,32},{32,40},{40,48},{48,56},{56,64},{64,7... | collective-permute-start | bytes 18440 | tf_op jit(solution)/shard_map/ppermute | solution.py:24
  3.7 1.1 copy.47
  4.8 3.5 %collective-permute-start.1 = (bf16[3,2,1,128]{3,0,2,1:T(4,128)(2,1)S(1)}, bf16[3,2,1,128]{3,0,2,1:T(4,128)(2,1)S(1)}, u32[]{:S(2)}, u32[]{:S(2)}) collective-permute-start(bf16[3,2,1,128]{3,0,2,1:T(4,128)(2,1)S(1)} %slice.133), channel_id=1, source_target_pairs={{0,8},{8,16},{16,24},{24,32},{32,40},{40,48},{48,56},{56,64},{64,7... | collective-permute-start | bytes 4616 | tf_op jit(solution)/shard_map/ppermute | solution.py:24
  8.3 0.7 exponential_negate_fusion
  9.0 1.0 broadcast_multiply_fusion
  10.1 2.3 %reduce-window.6 = f32[4,16,1,2,128]{4,1,2,3,0:T(8,128)S(1)} reduce-window(f32[4,16,1,2,128]{4,1,2,3,0:T(8,128)S(1)} %copy.51, f32[]{:T(128)} %constant.13.clone.1), window={size=1x1x1x1x128 pad=0_0x0_0x0_0x0_0x127_0}, to_apply=%region_0.1 | reduce-window | flops 2080768 | bytes 131076 | tf_op jit(solution)/shard_map/reduce-window
  13.0 0.8 slice_reduce_fusion
  13.9 1.1 fusion.31
  15.1 0.9 fusion.42
  16.1 0.7 fusion.43
  17.4 0.6 iota_compare_fusion
  18.1 2.6 %copy.45 = bf16[1024,1024]{0,1:T(8,128)(2,1)} copy(bf16[1024,1024]{1,0:T(8,128)(2,1)S(1)} %copy-done.2) | data formatting | bytes 4194304 | tf_op args[0]
  22.1 3.9 %copy.67 = bf16[1024,1024]{0,1:T(8,128)(2,1)} copy(bf16[1024,1024]{1,0:T(8,128)(2,1)} %param.13) | data formatting | bytes 4194304 | tf_op args[2]
  26.6 0.7 multiply_convert_fusion.8
  27.7 0.8 convert_element_type.91
  28.5 5.2 %multiply_convert_fusion.5 = bf16[1024,1024]{0,1:T(8,128)(2,1)S(1)} fusion(bf16[1024,1024]{0,1:T(8,128)(2,1)S(1)} %copy-done.1, bf16[3,1024]{0,1:T(8,128)(2,1)} %collective-permute-done, f32[1024]{0:T(1024)S(1)} %bitcast.82, f32[1024]{0:T(1024)S(1)} %bitcast.83, f32[1024]{0:T(1024)S(1)} %bitcast.81, f32[1024]{0:T(1024)S(1)} %bitcast.80), kind=kLoop, calls=%fused_computation.24 | loop fusion | flops 26214400 | bytes 4216832 | tf_op jit(solution)/shard_map/convert_element_type | solution.py:31
  33.7 3.4 %reshape.338 = f32[4,256,1,16,64]{1,0,4,3,2:T(4,128)} reshape(bf16[1024,1024]{0,1:T(8,128)(2,1)S(1)} %multiply_convert_fusion.5) | data formatting | bytes 6291456 | tf_op jit(solution)/shard_map/convert_element_type | solution.py:411
  37.1 2.8 %reshape.324 = bf16[4,256,16,64]{1,0,3,2:T(4,128)(2,1)} reshape(bf16[1024,1024]{0,1:T(8,128)(2,1)S(1)} %multiply_convert_fusion.5) | data formatting | bytes 4194304 | tf_op jit(solution)/shard_map/reshape.26
  39.9 8.9 %bitcast_add_fusion = f32[4,256,1,16,64]{1,4,3,0,2:T(8,128)} fusion(f32[4,256,1,16,64]{1,0,4,3,2:T(4,128)} %reshape.338, f32[4,16,256]{2,1,0:T(8,128)} %copy.55, f32[4,16,256]{2,1,0:T(8,128)S(1)} %reduce_window_sum.44, f32[4,256,256]{2,1,0:T(8,128)S(1)} %fusion.44, pred[256,256]{1,0:T(8,128)(4,1)} %iota_compare_fusion, f32[16]{0:T(128)S(1)} %copy-done.14, ...), kind=kOutput, calls=%fused_computation.18 | convolution fusion | flops 559939584 | bytes 11731008 | tf_op jit(solution)/shard_map/cgjts,csgjp->ctgjp/dot_general | solution.py:386
  48.9 3.3 %fusion.11 = f32[4,16,64,128]{3,2,1,0:T(8,128)S(1)} fusion(f32[4,256,128]{2,1,0:T(8,128)S(1)} %copy-done.4, f32[4,256,16]{1,2,0:T(8,128)S(1)} %copy-done.5, bf16[4,256,16,64]{1,0,3,2:T(4,128)(2,1)S(1)} %copy-done.3), kind=kOutput, calls=%fused_computation.15 | convolution fusion | flops 272629760 | bytes 4784128 | tf_op jit(solution)/shard_map/csgjp,csgjn->cgjpn/dot_general | solution.py:390
  52.3 1.1 fusion.27
  53.4 0.7 broadcast_in_dim.15.decay_ref
  54.0 25.7 %state_scan.1 = f32[16,64,128]{2,1,0:T(8,128)} custom-call(f32[16,64,128]{2,1,0:T(8,128)} %get-tuple-element.9.state_ref, f32[16,128]{1,0:T(8,128)} %broadcast_in_dim.15.decay_ref), custom_call_target="tpu_custom_call" | custom-call | tf_op jit(solution)/shard_map/state_scan/pallas_call | solution.py:227
  79.8 3.1 %fusion.12 = f32[4,256,1,16,64]{1,4,3,0,2:T(8,128)S(1)} fusion(f32[4,256,1,16,64]{1,4,3,0,2:T(8,128)} %bitcast_add_fusion, bf16[4,256,128,1]{2,1,3,0:T(8,128)(2,1)S(1)} %bitcast.72, f32[4,256,16]{1,2,0:T(8,128)S(1)} %copy.61, f32[1,16,64,128]{3,2,1,0:T(8,128)S(1)} %get-tuple-element.10, f32[1,16,64,128]{3,2,1,0:T(8,128)S(1)} %get-tuple-element.11, ...), kind=kOutput, calls=%fused_computation.17 | convolution fusion | flops 273678336 | bytes 10813712 | tf_op jit(solution)/shard_map/ctgn,cgjpn->ctgjp/dot_general | solution.py:419
  82.9 2.8 %copy.66 = f32[4,256,1,16,64]{1,0,4,3,2:T(4,128)S(1)} copy(f32[4,256,1,16,64]{1,4,3,0,2:T(8,128)S(1)} %fusion.12) | data formatting | bytes 8388608 | tf_op jit(solution)/shard_map/add | solution.py:422
  85.7 1.0 copy.70
  87.3 1.3 multiply_reduce_fusion
  88.7 2.9 %fusion.17.normed_ref = bf16[1024,1024]{1,0:T(8,128)(2,1)} fusion(f32[1024]{0:T(1024)S(1)} %copy-done.7, f32[1024]{0:T(1024)S(1)} %add_rsqrt_fusion, f32[1024,1024]{0,1:T(8,128)S(1)} %bitcast.69, bf16[1024,1024]{0,1:T(8,128)(2,1)S(1)} %copy-done), kind=kLoop, calls=%fused_computation.31 | loop fusion | flops 9437184 | bytes 8396800 | tf_op jit(solution)/shard_map/transpose | solution.py:433
  91.6 53.3 %ring_projection.1 = bf16[1024,256]{1,0:T(8,128)(2,1)} custom-call(bf16[1024,1024]{1,0:T(8,128)(2,1)} %fusion.17.normed_ref, bf16[1024,2048]{1,0:T(8,128)(2,1)} %weight_ref.1), custom_call_target="tpu_custom_call" | custom-call | tf_op jit(solution)/shard_map/ring_projection/pallas_call | solution.py:327
  144.9 1.9 %copy.85 = bf16[1024,256]{1,0:T(8,128)(2,1)} copy(bf16[1024,256]{1,0:T(8,128)(2,1)} %ring_projection.1) | data formatting | bytes 1048576
  (62 shorter events, 4.6 us)
Async XLA Ops:
  0.0 18.1 %copy-start.2 = (bf16[1024,1024]{1,0:T(8,128)(2,1)S(1)}, bf16[1024,1024]{1,0:T(8,128)(2,1)}, u32[]{:S(2)}) copy-start(bf16[1024,1024]{1,0:T(8,128)(2,1)} %param.11) | copy-start | bytes 6291460
  1.8 26.7 %collective-permute-start = (bf16[3,1024]{0,1:T(8,128)(2,1)}, bf16[3,1024]{0,1:T(8,128)(2,1)}, u32[]{:S(2)}, u32[]{:S(2)}) collective-permute-start(bf16[3,1024]{0,1:T(8,128)(2,1)} %copy.44), channel_id=1, source_target_pairs={{0,8},{8,16},{16,24},{24,32},{32,40},{40,48},{48,56},{56,64},{64,7... | collective-permute-start | bytes 18440 | tf_op jit(solution)/shard_map/ppermute | solution.py:24
  4.8 21.8 %collective-permute-start.1 = (bf16[3,2,1,128]{3,0,2,1:T(4,128)(2,1)S(1)}, bf16[3,2,1,128]{3,0,2,1:T(4,128)(2,1)S(1)}, u32[]{:S(2)}, u32[]{:S(2)}) collective-permute-start(bf16[3,2,1,128]{3,0,2,1:T(4,128)(2,1)S(1)} %slice.133), channel_id=1, source_target_pairs={{0,8},{8,16},{16,24},{24,32},{32,40},{40,48},{48,56},{56,64},{64,7... | collective-permute-start | bytes 4616 | tf_op jit(solution)/shard_map/ppermute | solution.py:24
  26.0 2.5 %copy-start.1 = (bf16[1024,1024]{0,1:T(8,128)(2,1)S(1)}, bf16[1024,1024]{0,1:T(8,128)(2,1)}, u32[]{:S(2)}) copy-start(bf16[1024,1024]{0,1:T(8,128)(2,1)} %copy.45) | copy-start | bytes 6291460
  33.7 6.2 %copy-start.14 = (f32[16]{0:T(128)S(1)}, f32[16]{0:T(128)}, u32[]{:S(2)}) copy-start(f32[16]{0:T(128)} %param.17) | copy-start | bytes 196
  39.9 8.9 %copy-start.3 = (bf16[4,256,16,64]{1,0,3,2:T(4,128)(2,1)S(1)}, bf16[4,256,16,64]{1,0,3,2:T(4,128)(2,1)}, u32[]{:S(2)}) copy-start(bf16[4,256,16,64]{1,0,3,2:T(4,128)(2,1)} %reshape.324) | copy-start | bytes 6291460
  39.9 8.9 %copy-start.4 = (f32[4,256,128]{2,1,0:T(8,128)S(1)}, f32[4,256,128]{2,1,0:T(8,128)}, u32[]{:S(2)}) copy-start(f32[4,256,128]{2,1,0:T(8,128)} %convert_element_type.91) | copy-start | bytes 1572868
  39.9 8.9 %copy-start.5 = (f32[4,256,16]{1,2,0:T(8,128)S(1)}, f32[4,256,16]{1,2,0:T(8,128)}, u32[]{:S(2)}) copy-start(f32[4,256,16]{1,2,0:T(8,128)} %copy.64) | copy-start | bytes 196612
  48.9 3.4 %copy-start.9 = (f32[16]{0:T(128)S(1)}, f32[16]{0:T(128)}, u32[]{:S(2)}) copy-start(f32[16]{0:T(128)} %get-tuple-element.5) | copy-start | bytes 196
  48.9 3.4 %copy-start.10 = (f32[16]{0:T(128)S(1)}, f32[16]{0:T(128)}, u32[]{:S(2)}) copy-start(f32[16]{0:T(128)} %get-tuple-element.6) | copy-start | bytes 196
  48.9 3.4 %copy-start.11 = (f32[16]{0:T(128)S(1)}, f32[16]{0:T(128)}, u32[]{:S(2)}) copy-start(f32[16]{0:T(128)} %get-tuple-element.7) | copy-start | bytes 196
  48.9 3.4 %copy-start.12 = (f32[16]{0:T(128)S(1)}, f32[16]{0:T(128)}, u32[]{:S(2)}) copy-start(f32[16]{0:T(128)} %get-tuple-element.8) | copy-start | bytes 196
  52.2 1.1 copy-start.8
  52.2 27.5 %copy-start.6 = (f32[4,16]{1,0:T(4,128)S(1)}, f32[4,16]{1,0:T(4,128)}, u32[]{:S(2)}) copy-start(f32[4,16]{1,0:T(4,128)} %subtract_exponential_fusion) | copy-start | bytes 772
  52.2 27.5 %copy-start.13 = (f32[4]{0:T(128)S(1)}, f32[4]{0:T(128)}, u32[]{:S(2)}) copy-start(f32[4]{0:T(128)} %pad.clone) | copy-start | bytes 52
  85.7 1.6 %copy-start = (bf16[1024,1024]{0,1:T(8,128)(2,1)S(1)}, bf16[1024,1024]{0,1:T(8,128)(2,1)}, u32[]{:S(2)}) copy-start(bf16[1024,1024]{0,1:T(8,128)(2,1)} %copy.67) | copy-start | bytes 6291460
  86.8 1.9 %copy-start.7 = (f32[1024]{0:T(1024)S(1)}, f32[1024]{0:T(1024)}, u32[]{:S(2)}) copy-start(f32[1024]{0:T(1024)} %param.20) | copy-start | bytes 12292

commit v19 on v17

--- a/solution.py
+++ b/solution.py
@@ -75,6 +75,8 @@
                 )
 
             peers = peers + valid.astype(jnp.int32)
+    own_s[...] = state_ref[...].astype(jnp.bfloat16)
+    own_d[...] = decay_ref[...]
     pl.semaphore_wait(barrier, peers)
 
     def remote(src, dst, slot, part, target, piece=0):
@@ -83,8 +85,6 @@
             device_id=(target, chan), device_id_type=MESH,
         )
 
-    own_s[...] = state_ref[...].astype(jnp.bfloat16)
-    own_d[...] = decay_ref[...]
     first = [
         lambda t: remote(own_s, pair_s, 0, 0, t),
         lambda t: remote(own_s.at[0:half], pair_s.at[0:half], 0, 0, t),

time: 147 us -> 147 us (level)
  no operation moved by 1% of the time
where the time goes in v19:
time: 147 us; the launch traced here: 146 us
  Pallas kernels  78.6 us (53%)
  local copies, waits for them, and re-layouts  27 us (18%)
  other arithmetic  19.3 us (13%)
  matrix products  15.6 us (11%)
  starting transfers between devices  5.41 us (4%)
    pallas_call x1, Pallas kernels, ring_projection(): pl.pallas_call(functools.partial(ring_kernel, count, pieces), out_shape=j...  52.9 us
    pallas_call x1, Pallas kernels, state_scan(): pl.pallas_call(functools.partial(state_scan_kernel, count), out_shape=jax...  25.7 us
    unnamed x35, local copies, waits for them, and re-layouts  11.1 us
    dot_general x1, matrix products, local(): jnp.einsum('cgjts,csgjp->ctgjp', mixing, x_blocks, preferred_element_type...  8.92 us
    convert_element_type x2, other arithmetic, conv_silu(): return jax.nn.silu(acc).astype(jnp.bfloat16)  5.9 us
    ppermute x2, starting transfers between devices, passed_along(): return lax.ppermute(x, axis, pairs)  5.41 us
    convert_element_type x1, local copies, waits for them, and re-layouts, local(): skip_gain.reshape(groups, per_group)[:, :, None] * x_blocks  3.41 us
    dot_general x1, matrix products, local(): jnp.einsum('csgjp,csgjn->cgjpn', x_blocks, weighted, preferred_element_ty...  3.29 us
  transfers between devices with their start and end apart: 2, of which 0 were waited for; matrix products, arithmetic and copies ran while one was open for 14% of the time, Pallas kernels for 0%

profile of v19, /device:TPU:24, one launch (start us, length us, event | category | flops | bytes accessed | tf_op | source)
XLA Modules:
  0.0 146.3 jit_solution(13592018698966687366)
XLA Ops:
  0.0 0.9 slice.101
  0.9 0.9 copy.44
  1.8 1.9 %collective-permute-start = (bf16[3,1024]{0,1:T(8,128)(2,1)}, bf16[3,1024]{0,1:T(8,128)(2,1)}, u32[]{:S(2)}, u32[]{:S(2)}) collective-permute-start(bf16[3,1024]{0,1:T(8,128)(2,1)} %copy.44), channel_id=1, source_target_pairs={{0,8},{8,16},{16,24},{24,32},{32,40},{40,48},{48,56},{56,64},{64,7... | collective-permute-start | bytes 18440 | tf_op jit(solution)/shard_map/ppermute | solution.py:24
  3.7 1.1 copy.47
  4.8 3.5 %collective-permute-start.1 = (bf16[3,2,1,128]{3,0,2,1:T(4,128)(2,1)S(1)}, bf16[3,2,1,128]{3,0,2,1:T(4,128)(2,1)S(1)}, u32[]{:S(2)}, u32[]{:S(2)}) collective-permute-start(bf16[3,2,1,128]{3,0,2,1:T(4,128)(2,1)S(1)} %slice.133), channel_id=1, source_target_pairs={{0,8},{8,16},{16,24},{24,32},{32,40},{40,48},{48,56},{56,64},{64,7... | collective-permute-start | bytes 4616 | tf_op jit(solution)/shard_map/ppermute | solution.py:24
  8.3 0.7 exponential_negate_fusion
  9.0 1.0 broadcast_multiply_fusion
  10.1 2.3 %reduce-window.6 = f32[4,16,1,2,128]{4,1,2,3,0:T(8,128)S(1)} reduce-window(f32[4,16,1,2,128]{4,1,2,3,0:T(8,128)S(1)} %copy.51, f32[]{:T(128)} %constant.13.clone.1), window={size=1x1x1x1x128 pad=0_0x0_0x0_0x0_0x127_0}, to_apply=%region_0.1 | reduce-window | flops 2080768 | bytes 131076 | tf_op jit(solution)/shard_map/reduce-window
  13.0 0.8 slice_reduce_fusion
  13.9 1.1 fusion.31
  15.1 0.9 fusion.42
  16.1 0.7 fusion.43
  17.4 0.6 iota_compare_fusion
  18.1 2.6 %copy.45 = bf16[1024,1024]{0,1:T(8,128)(2,1)} copy(bf16[1024,1024]{1,0:T(8,128)(2,1)S(1)} %copy-done.2) | data formatting | bytes 4194304 | tf_op args[0]
  22.1 3.9 %copy.67 = bf16[1024,1024]{0,1:T(8,128)(2,1)} copy(bf16[1024,1024]{1,0:T(8,128)(2,1)} %param.13) | data formatting | bytes 4194304 | tf_op args[2]
  26.6 0.7 multiply_convert_fusion.8
  27.7 0.8 convert_element_type.91
  28.5 5.2 %multiply_convert_fusion.5 = bf16[1024,1024]{0,1:T(8,128)(2,1)S(1)} fusion(bf16[1024,1024]{0,1:T(8,128)(2,1)S(1)} %copy-done.1, bf16[3,1024]{0,1:T(8,128)(2,1)} %collective-permute-done, f32[1024]{0:T(1024)S(1)} %bitcast.82, f32[1024]{0:T(1024)S(1)} %bitcast.83, f32[1024]{0:T(1024)S(1)} %bitcast.81, f32[1024]{0:T(1024)S(1)} %bitcast.80), kind=kLoop, calls=%fused_computation.24 | loop fusion | flops 26214400 | bytes 4216832 | tf_op jit(solution)/shard_map/convert_element_type | solution.py:31
  33.7 3.4 %reshape.338 = f32[4,256,1,16,64]{1,0,4,3,2:T(4,128)} reshape(bf16[1024,1024]{0,1:T(8,128)(2,1)S(1)} %multiply_convert_fusion.5) | data formatting | bytes 6291456 | tf_op jit(solution)/shard_map/convert_element_type | solution.py:416
  37.1 2.8 %reshape.324 = bf16[4,256,16,64]{1,0,3,2:T(4,128)(2,1)} reshape(bf16[1024,1024]{0,1:T(8,128)(2,1)S(1)} %multiply_convert_fusion.5) | data formatting | bytes 4194304 | tf_op jit(solution)/shard_map/reshape.26
  39.9 8.9 %bitcast_add_fusion = f32[4,256,1,16,64]{1,4,3,0,2:T(8,128)} fusion(f32[4,256,1,16,64]{1,0,4,3,2:T(4,128)} %reshape.338, f32[4,16,256]{2,1,0:T(8,128)} %copy.55, f32[4,16,256]{2,1,0:T(8,128)S(1)} %reduce_window_sum.44, f32[4,256,256]{2,1,0:T(8,128)S(1)} %fusion.44, pred[256,256]{1,0:T(8,128)(4,1)} %iota_compare_fusion, f32[16]{0:T(128)S(1)} %copy-done.14, ...), kind=kOutput, calls=%fused_computation.18 | convolution fusion | flops 559939584 | bytes 11731008 | tf_op jit(solution)/shard_map/cgjts,csgjp->ctgjp/dot_general | solution.py:391
  48.9 3.3 %fusion.11 = f32[4,16,64,128]{3,2,1,0:T(8,128)S(1)} fusion(f32[4,256,128]{2,1,0:T(8,128)S(1)} %copy-done.4, f32[4,256,16]{1,2,0:T(8,128)S(1)} %copy-done.5, bf16[4,256,16,64]{1,0,3,2:T(4,128)(2,1)S(1)} %copy-done.3), kind=kOutput, calls=%fused_computation.15 | convolution fusion | flops 272629760 | bytes 4784128 | tf_op jit(solution)/shard_map/csgjp,csgjn->cgjpn/dot_general | solution.py:395
  52.3 1.1 fusion.27
  53.4 0.7 broadcast_in_dim.15.decay_ref
  54.0 25.7 %state_scan.1 = f32[16,64,128]{2,1,0:T(8,128)} custom-call(f32[16,64,128]{2,1,0:T(8,128)} %get-tuple-element.9.state_ref, f32[16,128]{1,0:T(8,128)} %broadcast_in_dim.15.decay_ref), custom_call_target="tpu_custom_call" | custom-call | tf_op jit(solution)/shard_map/state_scan/pallas_call | solution.py:227
  79.8 3.1 %fusion.12 = f32[4,256,1,16,64]{1,4,3,0,2:T(8,128)S(1)} fusion(f32[4,256,1,16,64]{1,4,3,0,2:T(8,128)} %bitcast_add_fusion, bf16[4,256,128,1]{2,1,3,0:T(8,128)(2,1)S(1)} %bitcast.72, f32[4,256,16]{1,2,0:T(8,128)S(1)} %copy.61, f32[1,16,64,128]{3,2,1,0:T(8,128)S(1)} %get-tuple-element.10, f32[1,16,64,128]{3,2,1,0:T(8,128)S(1)} %get-tuple-element.11, ...), kind=kOutput, calls=%fused_computation.17 | convolution fusion | flops 273678336 | bytes 10813712 | tf_op jit(solution)/shard_map/ctgn,cgjpn->ctgjp/dot_general | solution.py:424
  82.9 2.8 %copy.66 = f32[4,256,1,16,64]{1,0,4,3,2:T(4,128)S(1)} copy(f32[4,256,1,16,64]{1,4,3,0,2:T(8,128)S(1)} %fusion.12) | data formatting | bytes 8388608 | tf_op jit(solution)/shard_map/add | solution.py:427
  85.7 1.0 copy.70
  87.3 1.3 multiply_reduce_fusion
  88.7 2.9 %fusion.17.normed_ref = bf16[1024,1024]{1,0:T(8,128)(2,1)} fusion(f32[1024]{0:T(1024)S(1)} %copy-done.7, f32[1024]{0:T(1024)S(1)} %add_rsqrt_fusion, f32[1024,1024]{0,1:T(8,128)S(1)} %bitcast.69, bf16[1024,1024]{0,1:T(8,128)(2,1)S(1)} %copy-done), kind=kLoop, calls=%fused_computation.31 | loop fusion | flops 9437184 | bytes 8396800 | tf_op jit(solution)/shard_map/transpose | solution.py:438
  91.6 52.9 %ring_projection.1 = bf16[1024,256]{1,0:T(8,128)(2,1)} custom-call(bf16[1024,1024]{1,0:T(8,128)(2,1)} %fusion.17.normed_ref, bf16[1024,2048]{1,0:T(8,128)(2,1)} %weight_ref.1), custom_call_target="tpu_custom_call" | custom-call | tf_op jit(solution)/shard_map/ring_projection/pallas_call | solution.py:332
  144.5 1.9 %copy.85 = bf16[1024,256]{1,0:T(8,128)(2,1)} copy(bf16[1024,256]{1,0:T(8,128)(2,1)} %ring_projection.1) | data formatting | bytes 1048576
  (62 shorter events, 4.6 us)
Async XLA Ops:
  0.0 18.1 %copy-start.2 = (bf16[1024,1024]{1,0:T(8,128)(2,1)S(1)}, bf16[1024,1024]{1,0:T(8,128)(2,1)}, u32[]{:S(2)}) copy-start(bf16[1024,1024]{1,0:T(8,128)(2,1)} %param.11) | copy-start | bytes 6291460
  1.8 26.7 %collective-permute-start = (bf16[3,1024]{0,1:T(8,128)(2,1)}, bf16[3,1024]{0,1:T(8,128)(2,1)}, u32[]{:S(2)}, u32[]{:S(2)}) collective-permute-start(bf16[3,1024]{0,1:T(8,128)(2,1)} %copy.44), channel_id=1, source_target_pairs={{0,8},{8,16},{16,24},{24,32},{32,40},{40,48},{48,56},{56,64},{64,7... | collective-permute-start | bytes 18440 | tf_op jit(solution)/shard_map/ppermute | solution.py:24
  4.8 21.8 %collective-permute-start.1 = (bf16[3,2,1,128]{3,0,2,1:T(4,128)(2,1)S(1)}, bf16[3,2,1,128]{3,0,2,1:T(4,128)(2,1)S(1)}, u32[]{:S(2)}, u32[]{:S(2)}) collective-permute-start(bf16[3,2,1,128]{3,0,2,1:T(4,128)(2,1)S(1)} %slice.133), channel_id=1, source_target_pairs={{0,8},{8,16},{16,24},{24,32},{32,40},{40,48},{48,56},{56,64},{64,7... | collective-permute-start | bytes 4616 | tf_op jit(solution)/shard_map/ppermute | solution.py:24
  26.0 2.5 %copy-start.1 = (bf16[1024,1024]{0,1:T(8,128)(2,1)S(1)}, bf16[1024,1024]{0,1:T(8,128)(2,1)}, u32[]{:S(2)}) copy-start(bf16[1024,1024]{0,1:T(8,128)(2,1)} %copy.45) | copy-start | bytes 6291460
  33.7 6.2 %copy-start.14 = (f32[16]{0:T(128)S(1)}, f32[16]{0:T(128)}, u32[]{:S(2)}) copy-start(f32[16]{0:T(128)} %param.17) | copy-start | bytes 196
  39.9 8.9 %copy-start.3 = (bf16[4,256,16,64]{1,0,3,2:T(4,128)(2,1)S(1)}, bf16[4,256,16,64]{1,0,3,2:T(4,128)(2,1)}, u32[]{:S(2)}) copy-start(bf16[4,256,16,64]{1,0,3,2:T(4,128)(2,1)} %reshape.324) | copy-start | bytes 6291460
  39.9 8.9 %copy-start.4 = (f32[4,256,128]{2,1,0:T(8,128)S(1)}, f32[4,256,128]{2,1,0:T(8,128)}, u32[]{:S(2)}) copy-start(f32[4,256,128]{2,1,0:T(8,128)} %convert_element_type.91) | copy-start | bytes 1572868
  39.9 8.9 %copy-start.5 = (f32[4,256,16]{1,2,0:T(8,128)S(1)}, f32[4,256,16]{1,2,0:T(8,128)}, u32[]{:S(2)}) copy-start(f32[4,256,16]{1,2,0:T(8,128)} %copy.64) | copy-start | bytes 196612
  48.9 3.4 %copy-start.9 = (f32[16]{0:T(128)S(1)}, f32[16]{0:T(128)}, u32[]{:S(2)}) copy-start(f32[16]{0:T(128)} %get-tuple-element.5) | copy-start | bytes 196
  48.9 3.4 %copy-start.10 = (f32[16]{0:T(128)S(1)}, f32[16]{0:T(128)}, u32[]{:S(2)}) copy-start(f32[16]{0:T(128)} %get-tuple-element.6) | copy-start | bytes 196
  48.9 3.4 %copy-start.11 = (f32[16]{0:T(128)S(1)}, f32[16]{0:T(128)}, u32[]{:S(2)}) copy-start(f32[16]{0:T(128)} %get-tuple-element.7) | copy-start | bytes 196
  48.9 3.4 %copy-start.12 = (f32[16]{0:T(128)S(1)}, f32[16]{0:T(128)}, u32[]{:S(2)}) copy-start(f32[16]{0:T(128)} %get-tuple-element.8) | copy-start | bytes 196
  52.2 1.1 copy-start.8
  52.2 27.5 %copy-start.6 = (f32[4,16]{1,0:T(4,128)S(1)}, f32[4,16]{1,0:T(4,128)}, u32[]{:S(2)}) copy-start(f32[4,16]{1,0:T(4,128)} %subtract_exponential_fusion) | copy-start | bytes 772
  52.2 27.5 %copy-start.13 = (f32[4]{0:T(128)S(1)}, f32[4]{0:T(128)}, u32[]{:S(2)}) copy-start(f32[4]{0:T(128)} %pad.clone) | copy-start | bytes 52
  85.7 1.6 %copy-start = (bf16[1024,1024]{0,1:T(8,128)(2,1)S(1)}, bf16[1024,1024]{0,1:T(8,128)(2,1)}, u32[]{:S(2)}) copy-start(bf16[1024,1024]{0,1:T(8,128)(2,1)} %copy.67) | copy-start | bytes 6291460
  86.8 1.9 %copy-start.7 = (f32[1024]{0:T(1024)S(1)}, f32[1024]{0:T(1024)}, u32[]{:S(2)}) copy-start(f32[1024]{0:T(1024)} %param.20) | copy-start | bytes 12292
